TPU v7x, 256 devices: a whole 4x4x8 slice. The times are simulated.
256 devices in a mesh: dp: 2 (over core), ctx: 32 (over z, y), head: 4 (over x).
Axes of the slice: x: 4, y: 4, z: 8, core: 2. Of those that a mesh axis runs over, the one named last changes fastest.
Arguments:
- queries: bfloat16 [2, 32768, 2048], P('dp', 'ctx', 'head'), may hold values from -6 to 6
- keys_raw: bfloat16 [2, 32768, 2048], P('dp', 'ctx', 'head'), may hold values from -0.625 to 0.625
- values: bfloat16 [2, 32768, 2048], P('dp', 'ctx', 'head'), may hold values from -6 to 6
- gates: float32 [2, 16, 32768], P('dp', 'head', 'ctx'), as said below
- lengths: int32 [2, 16], P('dp'), may hold values from 1 to 8192, 32768 in all within a row
- key_gain: float32 [16, 128], P('head'), may hold values from 0.1 to 1.9
- cotangent: bfloat16 [2, 32768, 2048], P('dp', 'ctx', 'head'), may hold values from -6 to 6
Outputs:
- attended: bfloat16 [2, 32768, 2048], P('dp', 'ctx', 'head')
- grad_queries: bfloat16 [2, 32768, 2048], P('dp', 'ctx', 'head')
- grad_keys: bfloat16 [2, 32768, 2048], P('dp', 'ctx', 'head')
- grad_values: bfloat16 [2, 32768, 2048], P('dp', 'ctx', 'head')
- grad_gates: float32 [2, 16, 32768], P('dp', 'head', 'ctx')
- grad_gain: float32 [16, 128], P('head', 'dp')
Inputs may be any that keep to these rules, and one draw needn't show every extreme that they name: Each row of lengths gives its documents in packing order and sums to 32768. `gates`: every entry is negative.
All inputs are finite; a program needn't handle non-finite values.
Results may differ from a plain program's by a relative error of at most 0.009.
Values sent between devices are 32-bit elements; how exact they have to be, the bound alone decides.
A program may use at most 128 MiB of HBM per device.

v0:
```python
import jax
import jax.numpy as jnp
from jax import lax
from jax.sharding import PartitionSpec as P

BLOCK = 512


PRECISE = lax.Precision.HIGHEST


def passed_along(value, axis, steps):
    count = lax.axis_size(axis)
    first, last = (max(0, -steps), min(count, count - steps))
    return lax.ppermute(value, axis, [(source, source + steps) for source in range(first, last)])


def start_flags(doc_lengths, first_pos, num_rows):
    starts = jnp.cumsum(doc_lengths, dtype=jnp.int32) - doc_lengths
    positions = first_pos + jnp.arange(num_rows, dtype=jnp.int32)
    matches = jnp.any(positions[:, None] == starts[None, :], axis=1)
    return matches.astype(jnp.float32)


def make_step(key_gain, head_width):
    q_scale = head_width ** (-0.5)

    def block_step(carried, inputs):
        q_block, k_block, v_block, gate_block, flag_block = inputs
        k_bf = (k_block.astype(jnp.float32) * key_gain[None]).astype(jnp.bfloat16)
        q_float = q_block.astype(jnp.float32) * q_scale
        k_float = lax.optimization_barrier(k_bf).astype(jnp.float32)
        v_float = v_block.astype(jnp.float32)
        segment = jnp.cumsum(flag_block)
        positions = jnp.arange(flag_block.shape[0])
        same_doc = (segment[:, None] == segment[None, :]) & (
            positions[:, None] >= positions[None, :]
        )
        cum_decay = jnp.cumsum(gate_block, axis=1)
        exponent = cum_decay[:, :, None] - cum_decay[:, None, :]
        decays = jnp.where(same_doc[None], jnp.exp(jnp.where(same_doc[None], exponent, 0.0)), 0.0)
        scores = jnp.einsum("thd,shd->hts", q_block, k_bf, preferred_element_type=jnp.float32)
        weights = (scores * q_scale * decays).astype(jnp.bfloat16)
        within = jnp.einsum("hts,she->the", weights, v_block, preferred_element_type=jnp.float32)
        opened = (segment == 0).astype(cum_decay.dtype)
        carry_in = jnp.exp(cum_decay) * opened[None, :]
        across = (
            jnp.einsum("thd,hde->the", q_float, carried, precision=PRECISE) * carry_in.T[:, :, None]
        )
        tail_mask = (segment == segment[-1]).astype(cum_decay.dtype)
        to_end = jnp.exp(cum_decay[:, -1:] - cum_decay) * tail_mask[None, :]
        written = jnp.einsum(
            "shd,she->hde", k_float * to_end.T[:, :, None], v_float, precision=PRECISE
        )
        end_state = carried * carry_in[:, -1][:, None, None] + written
        return (end_state, within + across)

    return block_step


def run_blocks(q_rows, k_rows, v_rows, gate_rows, flags, key_gain, start_state):
    num_rows = q_rows.shape[0]
    head_count = key_gain.shape[0]
    head_width = key_gain.shape[1]
    num_blocks = num_rows // BLOCK

    def to_blocks(tensor):
        return tensor.reshape(num_blocks, BLOCK, head_count, head_width)

    gate_blocks = gate_rows.reshape(head_count, num_blocks, BLOCK).transpose(1, 0, 2)
    flag_blocks = flags.reshape(num_blocks, BLOCK)
    end_state, outputs = lax.scan(
        jax.checkpoint(make_step(key_gain, head_width)),
        start_state,
        (to_blocks(q_rows), to_blocks(k_rows), to_blocks(v_rows), gate_blocks, flag_blocks),
    )
    return (outputs.reshape(num_rows, head_count * head_width), end_state)


def shards(queries, keys_raw, values, gates, lengths, key_gain, cotangent):
    tok_rows = queries.shape[1]
    head_count = key_gain.shape[0]
    head_width = key_gain.shape[1]
    flags = start_flags(lengths[0], lax.axis_index("ctx") * tok_rows, tok_rows)
    q_rows, k_rows, v_rows, gate_rows = (queries[0], keys_raw[0], values[0], gates[0])
    segment = jnp.cumsum(flags)
    opened = (segment == 0).astype(jnp.float32)
    tail_mask = (segment == segment[-1]).astype(jnp.float32)
    cum_decay = jnp.cumsum(gate_rows, axis=1)
    shard_decay = jnp.exp(cum_decay[:, -1]) * opened[-1]
    to_end = jnp.exp(cum_decay[:, -1:] - cum_decay) * tail_mask[None, :]
    k_bf = (
        k_rows.reshape(tok_rows, head_count, head_width).astype(jnp.float32) * key_gain[None]
    ).astype(jnp.bfloat16)
    k_float = lax.optimization_barrier(k_bf).astype(jnp.float32)
    v_float = v_rows.reshape(tok_rows, head_count, head_width).astype(jnp.float32)
    local_end = jnp.einsum(
        "shd,she->hde", k_float * to_end.T[:, :, None], v_float, precision=PRECISE
    )
    ctx_size = lax.axis_size("ctx")

    def relay_forward(step_index, incoming):
        return passed_along(shard_decay[:, None, None] * incoming + local_end, "ctx", 1)

    state_in = lax.fori_loop(0, ctx_size - 1, relay_forward, jnp.zeros_like(local_end))

    def forward(q_part, k_part, v_part, gate_part, gain_part):
        return run_blocks(q_part, k_part, v_part, gate_part, flags, gain_part, state_in)

    (primal, end_state), pullback = jax.vjp(forward, q_rows, k_rows, v_rows, gate_rows, key_gain)
    factor = jnp.exp(cum_decay) * opened[None, :]
    weighted = (
        q_rows.reshape(tok_rows, head_count, head_width).astype(jnp.float32)
        * head_width ** (-0.5)
        * factor.T[:, :, None]
    )
    cot_float = cotangent[0].astype(jnp.float32)
    local_grad = jnp.einsum(
        "thd,the->hde",
        weighted,
        cot_float.reshape(tok_rows, head_count, head_width),
        precision=PRECISE,
    )

    def relay_back(step_index, incoming):
        return passed_along(shard_decay[:, None, None] * incoming + local_grad, "ctx", -1)

    later_grad = lax.fori_loop(0, ctx_size - 1, relay_back, jnp.zeros_like(local_grad))
    grad_q, grad_k, grad_v, grad_a, gain_term = pullback((cot_float, later_grad))
    gain_total = lax.psum(gain_term, "ctx")
    grad_gain = lax.psum_scatter(gain_total, "dp", scatter_dimension=1, tiled=True)
    return (
        primal.astype(jnp.bfloat16)[None],
        grad_q[None],
        grad_k[None],
        grad_v[None],
        grad_a[None],
        grad_gain,
    )


def solution(mesh):
    placed = (
        P("dp", "ctx", "head"),
        P("dp", "ctx", "head"),
        P("dp", "ctx", "head"),
        P("dp", "head", "ctx"),
        P("dp", None),
        P("head", None),
        P("dp", "ctx", "head"),
    )
    return jax.shard_map(
        shards,
        mesh=mesh,
        in_specs=placed,
        out_specs=(
            P("dp", "ctx", "head"),
            P("dp", "ctx", "head"),
            P("dp", "ctx", "head"),
            P("dp", "ctx", "head"),
            P("dp", "head", "ctx"),
            P("head", "dp"),
        ),
        check_vma=False,
    )
```

profile of v0, /device:TPU:2, one launch (start us, length us, event | category | flops | bytes accessed | tf_op | source)
XLA Modules:
  0.0 1009.6 jit_solution(5768768737271364331)
XLA Ops:
  37.1 336.8 %while.62 = (s32[]{:T(128)}, f32[4,128,128]{2,1,0:T(8,128)S(1)}, f32[4]{0:T(128)S(1)}, f32[4,128,128]{2,1,0:T(8,128)S(1)}, s32[]{:T(128)}) while((s32[]{:T(128)}, f32[4,128,128]{2,1,0:T(8,128)S(1)}, f32[4]{0:T(128)S(1)}, f32[4,128,128]{2,1,0:T(8,128)S(1)}, s32[]{:T(128)}) %tuple.140), condition=%wide.region_7.8_spmd, body=%wide.region_6.7_spmd.sunk | while | flops 131074 | bytes 1835125 | solution.py:105
  90.1 6.5 collective-permute-start
  100.6 6.9 collective-permute-start
  112.6 7.1 collective-permute-start
  126.0 7.4 collective-permute-start
  192.0 6.5 collective-permute-start
  202.7 6.8 collective-permute-start
  214.7 7.1 collective-permute-start
  228.3 7.5 collective-permute-start
  304.5 6.8 collective-permute-start
  316.8 7.1 collective-permute-start
  330.5 7.2 collective-permute-start
  373.8 27.3 %while.64 = (s32[]{:T(128)}, f32[4,128,128]{2,1,0:T(8,128)S(1)}, bf16[2,512,4,128]{1,3,2,0:T(8,128)(2,1)}, f32[2,4,128,128]{3,2,1,0:T(8,128)}, f32[2,4,512]{2,1,...) while((s32[]{:T(128)}, f32[4,128,128]{2,1,0:T(8,128)S(1)}, ...), condition=%wide.region_13.14_spmd.clone, body=%wide.region_8.13_spmd.clone.sunk | while | flops 1352081408 | bytes 9343697 | solution.py:72
  404.3 365.5 %while.63 = (s32[]{:T(128)}, f32[4,128,128]{2,1,0:T(8,128)S(1)}, f32[4]{0:T(128)S(1)}, f32[4,128,128]{2,1,0:T(8,128)S(1)}, s32[]{:T(128)}) while((s32[]{:T(128)}, f32[4,128,128]{2,1,0:T(8,128)S(1)}, f32[4]{0:T(128)S(1)}, f32[4,128,128]{2,1,0:T(8,128)S(1)}, s32[]{:T(128)}) %tuple.160), condition=%wide.region_15.16_spmd, body=%wide.region_14.15_spmd.sunk | while | flops 131074 | bytes 1835125 | solution.py:128
  405.7 9.5 collective-permute-done.1
  416.7 9.5 collective-permute-done.1
  427.6 9.7 collective-permute-done.1
  438.7 11.9 %collective-permute-done.1 = f32[4,128,128]{2,1,0:T(8,128)S(1)} collective-permute-done((f32[4,128,128]{2,1,0:T(8,128)S(1)}, f32[4,128,128]{2,1,0:T(8,128)S(1)}, u32[]{:S(2)}, u32[]{:S(2)}) %collective-permute-start.1) | collective-permute-done | bytes 262176 | tf_op jit(solution)/shard_map/while/body/eval_jaxpr/ppermute | solution.py:15
  451.9 12.8 %collective-permute-done.1 = f32[4,128,128]{2,1,0:T(8,128)S(1)} collective-permute-done((f32[4,128,128]{2,1,0:T(8,128)S(1)}, f32[4,128,128]{2,1,0:T(8,128)S(1)}, u32[]{:S(2)}, u32[]{:S(2)}) %collective-permute-start.1) | collective-permute-done | bytes 262176 | tf_op jit(solution)/shard_map/while/body/eval_jaxpr/ppermute | solution.py:15
  466.2 11.3 %collective-permute-done.1 = f32[4,128,128]{2,1,0:T(8,128)S(1)} collective-permute-done((f32[4,128,128]{2,1,0:T(8,128)S(1)}, f32[4,128,128]{2,1,0:T(8,128)S(1)}, u32[]{:S(2)}, u32[]{:S(2)}) %collective-permute-start.1) | collective-permute-done | bytes 262176 | tf_op jit(solution)/shard_map/while/body/eval_jaxpr/ppermute | solution.py:15
  478.8 10.0 collective-permute-done.1
  490.3 10.6 %collective-permute-done.1 = f32[4,128,128]{2,1,0:T(8,128)S(1)} collective-permute-done((f32[4,128,128]{2,1,0:T(8,128)S(1)}, f32[4,128,128]{2,1,0:T(8,128)S(1)}, u32[]{:S(2)}, u32[]{:S(2)}) %collective-permute-start.1) | collective-permute-done | bytes 262176 | tf_op jit(solution)/shard_map/while/body/eval_jaxpr/ppermute | solution.py:15
  502.3 9.8 collective-permute-done.1
  513.5 9.2 collective-permute-done.1
  524.1 8.7 collective-permute-done.1
  534.2 10.4 %collective-permute-done.1 = f32[4,128,128]{2,1,0:T(8,128)S(1)} collective-permute-done((f32[4,128,128]{2,1,0:T(8,128)S(1)}, f32[4,128,128]{2,1,0:T(8,128)S(1)}, u32[]{:S(2)}, u32[]{:S(2)}) %collective-permute-start.1) | collective-permute-done | bytes 262176 | tf_op jit(solution)/shard_map/while/body/eval_jaxpr/ppermute | solution.py:15
  545.9 10.6 %collective-permute-done.1 = f32[4,128,128]{2,1,0:T(8,128)S(1)} collective-permute-done((f32[4,128,128]{2,1,0:T(8,128)S(1)}, f32[4,128,128]{2,1,0:T(8,128)S(1)}, u32[]{:S(2)}, u32[]{:S(2)}) %collective-permute-start.1) | collective-permute-done | bytes 262176 | tf_op jit(solution)/shard_map/while/body/eval_jaxpr/ppermute | solution.py:15
  557.9 9.6 collective-permute-done.1
  568.9 8.1 collective-permute-done.1
  578.5 8.5 collective-permute-done.1
  588.4 9.6 collective-permute-done.1
  599.3 11.3 %collective-permute-done.1 = f32[4,128,128]{2,1,0:T(8,128)S(1)} collective-permute-done((f32[4,128,128]{2,1,0:T(8,128)S(1)}, f32[4,128,128]{2,1,0:T(8,128)S(1)}, u32[]{:S(2)}, u32[]{:S(2)}) %collective-permute-start.1) | collective-permute-done | bytes 262176 | tf_op jit(solution)/shard_map/while/body/eval_jaxpr/ppermute | solution.py:15
  612.0 9.3 collective-permute-done.1
  622.7 10.2 %collective-permute-done.1 = f32[4,128,128]{2,1,0:T(8,128)S(1)} collective-permute-done((f32[4,128,128]{2,1,0:T(8,128)S(1)}, f32[4,128,128]{2,1,0:T(8,128)S(1)}, u32[]{:S(2)}, u32[]{:S(2)}) %collective-permute-start.1) | collective-permute-done | bytes 262176 | tf_op jit(solution)/shard_map/while/body/eval_jaxpr/ppermute | solution.py:15
  634.4 16.1 %collective-permute-done.1 = f32[4,128,128]{2,1,0:T(8,128)S(1)} collective-permute-done((f32[4,128,128]{2,1,0:T(8,128)S(1)}, f32[4,128,128]{2,1,0:T(8,128)S(1)}, u32[]{:S(2)}, u32[]{:S(2)}) %collective-permute-start.1) | collective-permute-done | bytes 262176 | tf_op jit(solution)/shard_map/while/body/eval_jaxpr/ppermute | solution.py:15
  651.9 11.2 %collective-permute-done.1 = f32[4,128,128]{2,1,0:T(8,128)S(1)} collective-permute-done((f32[4,128,128]{2,1,0:T(8,128)S(1)}, f32[4,128,128]{2,1,0:T(8,128)S(1)}, u32[]{:S(2)}, u32[]{:S(2)}) %collective-permute-start.1) | collective-permute-done | bytes 262176 | tf_op jit(solution)/shard_map/while/body/eval_jaxpr/ppermute | solution.py:15
  664.5 12.7 %collective-permute-done.1 = f32[4,128,128]{2,1,0:T(8,128)S(1)} collective-permute-done((f32[4,128,128]{2,1,0:T(8,128)S(1)}, f32[4,128,128]{2,1,0:T(8,128)S(1)}, u32[]{:S(2)}, u32[]{:S(2)}) %collective-permute-start.1) | collective-permute-done | bytes 262176 | tf_op jit(solution)/shard_map/while/body/eval_jaxpr/ppermute | solution.py:15
  678.6 10.0 collective-permute-done.1
  690.0 8.4 collective-permute-done.1
  699.8 10.7 %collective-permute-done.1 = f32[4,128,128]{2,1,0:T(8,128)S(1)} collective-permute-done((f32[4,128,128]{2,1,0:T(8,128)S(1)}, f32[4,128,128]{2,1,0:T(8,128)S(1)}, u32[]{:S(2)}, u32[]{:S(2)}) %collective-permute-start.1) | collective-permute-done | bytes 262176 | tf_op jit(solution)/shard_map/while/body/eval_jaxpr/ppermute | solution.py:15
  711.9 10.4 %collective-permute-done.1 = f32[4,128,128]{2,1,0:T(8,128)S(1)} collective-permute-done((f32[4,128,128]{2,1,0:T(8,128)S(1)}, f32[4,128,128]{2,1,0:T(8,128)S(1)}, u32[]{:S(2)}, u32[]{:S(2)}) %collective-permute-start.1) | collective-permute-done | bytes 262176 | tf_op jit(solution)/shard_map/while/body/eval_jaxpr/ppermute | solution.py:15
  723.8 10.9 %collective-permute-done.1 = f32[4,128,128]{2,1,0:T(8,128)S(1)} collective-permute-done((f32[4,128,128]{2,1,0:T(8,128)S(1)}, f32[4,128,128]{2,1,0:T(8,128)S(1)}, u32[]{:S(2)}, u32[]{:S(2)}) %collective-permute-start.1) | collective-permute-done | bytes 262176 | tf_op jit(solution)/shard_map/while/body/eval_jaxpr/ppermute | solution.py:15
  736.1 9.6 collective-permute-done.1
  747.1 10.2 %collective-permute-done.1 = f32[4,128,128]{2,1,0:T(8,128)S(1)} collective-permute-done((f32[4,128,128]{2,1,0:T(8,128)S(1)}, f32[4,128,128]{2,1,0:T(8,128)S(1)}, u32[]{:S(2)}, u32[]{:S(2)}) %collective-permute-start.1) | collective-permute-done | bytes 262176 | tf_op jit(solution)/shard_map/while/body/eval_jaxpr/ppermute | solution.py:15
  758.7 11.2 %collective-permute-done.1 = f32[4,128,128]{2,1,0:T(8,128)S(1)} collective-permute-done((f32[4,128,128]{2,1,0:T(8,128)S(1)}, f32[4,128,128]{2,1,0:T(8,128)S(1)}, u32[]{:S(2)}, u32[]{:S(2)}) %collective-permute-start.1) | collective-permute-done | bytes 262176 | tf_op jit(solution)/shard_map/while/body/eval_jaxpr/ppermute | solution.py:15
  773.6 85.2 %while.65 = (s32[]{:T(128)}, f32[4,128]{1,0:T(4,128)S(1)}, f32[4,128,128]{2,1,0:T(8,128)S(1)}, bf16[2,512,4,128]{3,2,1,0:T(4,128)(2,1)}, bf16[2,512,4,128]{3,2,1...) while((s32[]{:T(128)}, f32[4,128]{1,0:T(4,128)S(1)}, ...), condition=%wide.region_30.31_spmd.clone, body=%wide.region_16.30_spmd.clone.sunk | while | flops 3394863616 | bytes 116524784 | solution.py:72
  867.9 58.3 %reduce-scatter.4.cloned.1.call-done = f32[64,4]{1,0:T(8,128)} async-done(((f32[128,4]{1,0:T(8,128)}), f32[64,4]{1,0:T(8,128)}) %reduce-scatter.4.cloned.1.call-update) | async-done | bytes 1040
  927.1 75.7 %psum.8 = f32[4,64]{1,0:T(4,128)} all-reduce(f32[4,64]{1,0:T(4,128)S(1)} %copy.251), channel_id=1, replica_groups=mesh['dp'=2,'ctx'=32,'head'=4] {'ctx'}, use_global_device_ids=true, to_apply=%region_31.32 | all-reduce | flops 256 | bytes 2048 | tf_op jit(solution)/shard_map/psum | solution.py:130
  (422 shorter events, 460.6 us)
Async XLA Ops:
  7.2 919.1 %reduce-scatter.4.cloned.1.call-start = ((), (), s32[]{:S(2)}) async-start(), calls=%async_computation.1 | async-start | bytes 98304
  90.1 10.4 %collective-permute-start = (f32[4,128,128]{2,1,0:T(8,128)S(1)}, f32[4,128,128]{2,1,0:T(8,128)S(1)}, u32[]{:S(2)}, u32[]{:S(2)}) collective-permute-start(f32[4,128,128]{2,1,0:T(8,128)S(1)} %multiply_add_fusion.4), channel_id=1, source_target_pairs={{0,4},{4,8},{8,12},{12,16},{16,20},{20,24},{24,28},{28,32},{32,36}... | collective-permute-start | bytes 786440 | tf_op jit(solution)/shard_map/while/body/eval_jaxpr/ppermute | solution.py:15
  100.6 11.9 %collective-permute-start = (f32[4,128,128]{2,1,0:T(8,128)S(1)}, f32[4,128,128]{2,1,0:T(8,128)S(1)}, u32[]{:S(2)}, u32[]{:S(2)}) collective-permute-start(f32[4,128,128]{2,1,0:T(8,128)S(1)} %multiply_add_fusion.4), channel_id=1, source_target_pairs={{0,4},{4,8},{8,12},{12,16},{16,20},{20,24},{24,28},{28,32},{32,36}... | collective-permute-start | bytes 786440 | tf_op jit(solution)/shard_map/while/body/eval_jaxpr/ppermute | solution.py:15
  112.6 13.4 %collective-permute-start = (f32[4,128,128]{2,1,0:T(8,128)S(1)}, f32[4,128,128]{2,1,0:T(8,128)S(1)}, u32[]{:S(2)}, u32[]{:S(2)}) collective-permute-start(f32[4,128,128]{2,1,0:T(8,128)S(1)} %multiply_add_fusion.4), channel_id=1, source_target_pairs={{0,4},{4,8},{8,12},{12,16},{16,20},{20,24},{24,28},{28,32},{32,36}... | collective-permute-start | bytes 786440 | tf_op jit(solution)/shard_map/while/body/eval_jaxpr/ppermute | solution.py:15
  126.0 13.4 %collective-permute-start = (f32[4,128,128]{2,1,0:T(8,128)S(1)}, f32[4,128,128]{2,1,0:T(8,128)S(1)}, u32[]{:S(2)}, u32[]{:S(2)}) collective-permute-start(f32[4,128,128]{2,1,0:T(8,128)S(1)} %multiply_add_fusion.4), channel_id=1, source_target_pairs={{0,4},{4,8},{8,12},{12,16},{16,20},{20,24},{24,28},{28,32},{32,36}... | collective-permute-start | bytes 786440 | tf_op jit(solution)/shard_map/while/body/eval_jaxpr/ppermute | solution.py:15
  139.5 11.2 %collective-permute-start = (f32[4,128,128]{2,1,0:T(8,128)S(1)}, f32[4,128,128]{2,1,0:T(8,128)S(1)}, u32[]{:S(2)}, u32[]{:S(2)}) collective-permute-start(f32[4,128,128]{2,1,0:T(8,128)S(1)} %multiply_add_fusion.4), channel_id=1, source_target_pairs={{0,4},{4,8},{8,12},{12,16},{16,20},{20,24},{24,28},{28,32},{32,36}... | collective-permute-start | bytes 786440 | tf_op jit(solution)/shard_map/while/body/eval_jaxpr/ppermute | solution.py:15
  160.6 10.4 %collective-permute-start = (f32[4,128,128]{2,1,0:T(8,128)S(1)}, f32[4,128,128]{2,1,0:T(8,128)S(1)}, u32[]{:S(2)}, u32[]{:S(2)}) collective-permute-start(f32[4,128,128]{2,1,0:T(8,128)S(1)} %multiply_add_fusion.4), channel_id=1, source_target_pairs={{0,4},{4,8},{8,12},{12,16},{16,20},{20,24},{24,28},{28,32},{32,36}... | collective-permute-start | bytes 786440 | tf_op jit(solution)/shard_map/while/body/eval_jaxpr/ppermute | solution.py:15
  181.5 10.4 %collective-permute-start = (f32[4,128,128]{2,1,0:T(8,128)S(1)}, f32[4,128,128]{2,1,0:T(8,128)S(1)}, u32[]{:S(2)}, u32[]{:S(2)}) collective-permute-start(f32[4,128,128]{2,1,0:T(8,128)S(1)} %multiply_add_fusion.4), channel_id=1, source_target_pairs={{0,4},{4,8},{8,12},{12,16},{16,20},{20,24},{24,28},{28,32},{32,36}... | collective-permute-start | bytes 786440 | tf_op jit(solution)/shard_map/while/body/eval_jaxpr/ppermute | solution.py:15
  192.0 10.6 %collective-permute-start = (f32[4,128,128]{2,1,0:T(8,128)S(1)}, f32[4,128,128]{2,1,0:T(8,128)S(1)}, u32[]{:S(2)}, u32[]{:S(2)}) collective-permute-start(f32[4,128,128]{2,1,0:T(8,128)S(1)} %multiply_add_fusion.4), channel_id=1, source_target_pairs={{0,4},{4,8},{8,12},{12,16},{16,20},{20,24},{24,28},{28,32},{32,36}... | collective-permute-start | bytes 786440 | tf_op jit(solution)/shard_map/while/body/eval_jaxpr/ppermute | solution.py:15
  202.7 11.9 %collective-permute-start = (f32[4,128,128]{2,1,0:T(8,128)S(1)}, f32[4,128,128]{2,1,0:T(8,128)S(1)}, u32[]{:S(2)}, u32[]{:S(2)}) collective-permute-start(f32[4,128,128]{2,1,0:T(8,128)S(1)} %multiply_add_fusion.4), channel_id=1, source_target_pairs={{0,4},{4,8},{8,12},{12,16},{16,20},{20,24},{24,28},{28,32},{32,36}... | collective-permute-start | bytes 786440 | tf_op jit(solution)/shard_map/while/body/eval_jaxpr/ppermute | solution.py:15
  214.7 13.5 %collective-permute-start = (f32[4,128,128]{2,1,0:T(8,128)S(1)}, f32[4,128,128]{2,1,0:T(8,128)S(1)}, u32[]{:S(2)}, u32[]{:S(2)}) collective-permute-start(f32[4,128,128]{2,1,0:T(8,128)S(1)} %multiply_add_fusion.4), channel_id=1, source_target_pairs={{0,4},{4,8},{8,12},{12,16},{16,20},{20,24},{24,28},{28,32},{32,36}... | collective-permute-start | bytes 786440 | tf_op jit(solution)/shard_map/while/body/eval_jaxpr/ppermute | solution.py:15
  228.3 13.3 %collective-permute-start = (f32[4,128,128]{2,1,0:T(8,128)S(1)}, f32[4,128,128]{2,1,0:T(8,128)S(1)}, u32[]{:S(2)}, u32[]{:S(2)}) collective-permute-start(f32[4,128,128]{2,1,0:T(8,128)S(1)} %multiply_add_fusion.4), channel_id=1, source_target_pairs={{0,4},{4,8},{8,12},{12,16},{16,20},{20,24},{24,28},{28,32},{32,36}... | collective-permute-start | bytes 786440 | tf_op jit(solution)/shard_map/while/body/eval_jaxpr/ppermute | solution.py:15
  241.7 10.8 %collective-permute-start = (f32[4,128,128]{2,1,0:T(8,128)S(1)}, f32[4,128,128]{2,1,0:T(8,128)S(1)}, u32[]{:S(2)}, u32[]{:S(2)}) collective-permute-start(f32[4,128,128]{2,1,0:T(8,128)S(1)} %multiply_add_fusion.4), channel_id=1, source_target_pairs={{0,4},{4,8},{8,12},{12,16},{16,20},{20,24},{24,28},{28,32},{32,36}... | collective-permute-start | bytes 786440 | tf_op jit(solution)/shard_map/while/body/eval_jaxpr/ppermute | solution.py:15
  262.2 10.4 %collective-permute-start = (f32[4,128,128]{2,1,0:T(8,128)S(1)}, f32[4,128,128]{2,1,0:T(8,128)S(1)}, u32[]{:S(2)}, u32[]{:S(2)}) collective-permute-start(f32[4,128,128]{2,1,0:T(8,128)S(1)} %multiply_add_fusion.4), channel_id=1, source_target_pairs={{0,4},{4,8},{8,12},{12,16},{16,20},{20,24},{24,28},{28,32},{32,36}... | collective-permute-start | bytes 786440 | tf_op jit(solution)/shard_map/while/body/eval_jaxpr/ppermute | solution.py:15
  272.7 10.4 %collective-permute-start = (f32[4,128,128]{2,1,0:T(8,128)S(1)}, f32[4,128,128]{2,1,0:T(8,128)S(1)}, u32[]{:S(2)}, u32[]{:S(2)}) collective-permute-start(f32[4,128,128]{2,1,0:T(8,128)S(1)} %multiply_add_fusion.4), channel_id=1, source_target_pairs={{0,4},{4,8},{8,12},{12,16},{16,20},{20,24},{24,28},{28,32},{32,36}... | collective-permute-start | bytes 786440 | tf_op jit(solution)/shard_map/while/body/eval_jaxpr/ppermute | solution.py:15
  283.2 10.4 %collective-permute-start = (f32[4,128,128]{2,1,0:T(8,128)S(1)}, f32[4,128,128]{2,1,0:T(8,128)S(1)}, u32[]{:S(2)}, u32[]{:S(2)}) collective-permute-start(f32[4,128,128]{2,1,0:T(8,128)S(1)} %multiply_add_fusion.4), channel_id=1, source_target_pairs={{0,4},{4,8},{8,12},{12,16},{16,20},{20,24},{24,28},{28,32},{32,36}... | collective-permute-start | bytes 786440 | tf_op jit(solution)/shard_map/while/body/eval_jaxpr/ppermute | solution.py:15
  293.6 10.8 %collective-permute-start = (f32[4,128,128]{2,1,0:T(8,128)S(1)}, f32[4,128,128]{2,1,0:T(8,128)S(1)}, u32[]{:S(2)}, u32[]{:S(2)}) collective-permute-start(f32[4,128,128]{2,1,0:T(8,128)S(1)} %multiply_add_fusion.4), channel_id=1, source_target_pairs={{0,4},{4,8},{8,12},{12,16},{16,20},{20,24},{24,28},{28,32},{32,36}... | collective-permute-start | bytes 786440 | tf_op jit(solution)/shard_map/while/body/eval_jaxpr/ppermute | solution.py:15
  304.5 12.2 %collective-permute-start = (f32[4,128,128]{2,1,0:T(8,128)S(1)}, f32[4,128,128]{2,1,0:T(8,128)S(1)}, u32[]{:S(2)}, u32[]{:S(2)}) collective-permute-start(f32[4,128,128]{2,1,0:T(8,128)S(1)} %multiply_add_fusion.4), channel_id=1, source_target_pairs={{0,4},{4,8},{8,12},{12,16},{16,20},{20,24},{24,28},{28,32},{32,36}... | collective-permute-start | bytes 786440 | tf_op jit(solution)/shard_map/while/body/eval_jaxpr/ppermute | solution.py:15
  316.8 13.6 %collective-permute-start = (f32[4,128,128]{2,1,0:T(8,128)S(1)}, f32[4,128,128]{2,1,0:T(8,128)S(1)}, u32[]{:S(2)}, u32[]{:S(2)}) collective-permute-start(f32[4,128,128]{2,1,0:T(8,128)S(1)} %multiply_add_fusion.4), channel_id=1, source_target_pairs={{0,4},{4,8},{8,12},{12,16},{16,20},{20,24},{24,28},{28,32},{32,36}... | collective-permute-start | bytes 786440 | tf_op jit(solution)/shard_map/while/body/eval_jaxpr/ppermute | solution.py:15
  330.5 12.8 %collective-permute-start = (f32[4,128,128]{2,1,0:T(8,128)S(1)}, f32[4,128,128]{2,1,0:T(8,128)S(1)}, u32[]{:S(2)}, u32[]{:S(2)}) collective-permute-start(f32[4,128,128]{2,1,0:T(8,128)S(1)} %multiply_add_fusion.4), channel_id=1, source_target_pairs={{0,4},{4,8},{8,12},{12,16},{16,20},{20,24},{24,28},{28,32},{32,36}... | collective-permute-start | bytes 786440 | tf_op jit(solution)/shard_map/while/body/eval_jaxpr/ppermute | solution.py:15
  363.5 10.4 %collective-permute-start = (f32[4,128,128]{2,1,0:T(8,128)S(1)}, f32[4,128,128]{2,1,0:T(8,128)S(1)}, u32[]{:S(2)}, u32[]{:S(2)}) collective-permute-start(f32[4,128,128]{2,1,0:T(8,128)S(1)} %multiply_add_fusion.4), channel_id=1, source_target_pairs={{0,4},{4,8},{8,12},{12,16},{16,20},{20,24},{24,28},{28,32},{32,36}... | collective-permute-start | bytes 786440 | tf_op jit(solution)/shard_map/while/body/eval_jaxpr/ppermute | solution.py:15
  404.4 10.8 %collective-permute-start.1 = (f32[4,128,128]{2,1,0:T(8,128)S(1)}, f32[4,128,128]{2,1,0:T(8,128)S(1)}, u32[]{:S(2)}, u32[]{:S(2)}) collective-permute-start(f32[4,128,128]{2,1,0:T(8,128)S(1)} %multiply_add_fusion.5), channel_id=1, source_target_pairs={{4,0},{8,4},{12,8},{16,12},{20,16},{24,20},{28,24},{32,28},{36,32}... | collective-permute-start | bytes 786440 | tf_op jit(solution)/shard_map/while/body/eval_jaxpr/ppermute | solution.py:15
  415.4 10.8 %collective-permute-start.1 = (f32[4,128,128]{2,1,0:T(8,128)S(1)}, f32[4,128,128]{2,1,0:T(8,128)S(1)}, u32[]{:S(2)}, u32[]{:S(2)}) collective-permute-start(f32[4,128,128]{2,1,0:T(8,128)S(1)} %multiply_add_fusion.5), channel_id=1, source_target_pairs={{4,0},{8,4},{12,8},{16,12},{20,16},{24,20},{28,24},{32,28},{36,32}... | collective-permute-start | bytes 786440 | tf_op jit(solution)/shard_map/while/body/eval_jaxpr/ppermute | solution.py:15
  426.3 11.0 %collective-permute-start.1 = (f32[4,128,128]{2,1,0:T(8,128)S(1)}, f32[4,128,128]{2,1,0:T(8,128)S(1)}, u32[]{:S(2)}, u32[]{:S(2)}) collective-permute-start(f32[4,128,128]{2,1,0:T(8,128)S(1)} %multiply_add_fusion.5), channel_id=1, source_target_pairs={{4,0},{8,4},{12,8},{16,12},{20,16},{24,20},{28,24},{32,28},{36,32}... | collective-permute-start | bytes 786440 | tf_op jit(solution)/shard_map/while/body/eval_jaxpr/ppermute | solution.py:15
  437.3 13.2 %collective-permute-start.1 = (f32[4,128,128]{2,1,0:T(8,128)S(1)}, f32[4,128,128]{2,1,0:T(8,128)S(1)}, u32[]{:S(2)}, u32[]{:S(2)}) collective-permute-start(f32[4,128,128]{2,1,0:T(8,128)S(1)} %multiply_add_fusion.5), channel_id=1, source_target_pairs={{4,0},{8,4},{12,8},{16,12},{20,16},{24,20},{28,24},{32,28},{36,32}... | collective-permute-start | bytes 786440 | tf_op jit(solution)/shard_map/while/body/eval_jaxpr/ppermute | solution.py:15
  450.6 14.1 %collective-permute-start.1 = (f32[4,128,128]{2,1,0:T(8,128)S(1)}, f32[4,128,128]{2,1,0:T(8,128)S(1)}, u32[]{:S(2)}, u32[]{:S(2)}) collective-permute-start(f32[4,128,128]{2,1,0:T(8,128)S(1)} %multiply_add_fusion.5), channel_id=1, source_target_pairs={{4,0},{8,4},{12,8},{16,12},{20,16},{24,20},{28,24},{32,28},{36,32}... | collective-permute-start | bytes 786440 | tf_op jit(solution)/shard_map/while/body/eval_jaxpr/ppermute | solution.py:15
  464.8 12.6 %collective-permute-start.1 = (f32[4,128,128]{2,1,0:T(8,128)S(1)}, f32[4,128,128]{2,1,0:T(8,128)S(1)}, u32[]{:S(2)}, u32[]{:S(2)}) collective-permute-start(f32[4,128,128]{2,1,0:T(8,128)S(1)} %multiply_add_fusion.5), channel_id=1, source_target_pairs={{4,0},{8,4},{12,8},{16,12},{20,16},{24,20},{28,24},{32,28},{36,32}... | collective-permute-start | bytes 786440 | tf_op jit(solution)/shard_map/while/body/eval_jaxpr/ppermute | solution.py:15
  477.5 11.3 %collective-permute-start.1 = (f32[4,128,128]{2,1,0:T(8,128)S(1)}, f32[4,128,128]{2,1,0:T(8,128)S(1)}, u32[]{:S(2)}, u32[]{:S(2)}) collective-permute-start(f32[4,128,128]{2,1,0:T(8,128)S(1)} %multiply_add_fusion.5), channel_id=1, source_target_pairs={{4,0},{8,4},{12,8},{16,12},{20,16},{24,20},{28,24},{32,28},{36,32}... | collective-permute-start | bytes 786440 | tf_op jit(solution)/shard_map/while/body/eval_jaxpr/ppermute | solution.py:15
  489.0 11.9 %collective-permute-start.1 = (f32[4,128,128]{2,1,0:T(8,128)S(1)}, f32[4,128,128]{2,1,0:T(8,128)S(1)}, u32[]{:S(2)}, u32[]{:S(2)}) collective-permute-start(f32[4,128,128]{2,1,0:T(8,128)S(1)} %multiply_add_fusion.5), channel_id=1, source_target_pairs={{4,0},{8,4},{12,8},{16,12},{20,16},{24,20},{28,24},{32,28},{36,32}... | collective-permute-start | bytes 786440 | tf_op jit(solution)/shard_map/while/body/eval_jaxpr/ppermute | solution.py:15
  501.0 11.1 %collective-permute-start.1 = (f32[4,128,128]{2,1,0:T(8,128)S(1)}, f32[4,128,128]{2,1,0:T(8,128)S(1)}, u32[]{:S(2)}, u32[]{:S(2)}) collective-permute-start(f32[4,128,128]{2,1,0:T(8,128)S(1)} %multiply_add_fusion.5), channel_id=1, source_target_pairs={{4,0},{8,4},{12,8},{16,12},{20,16},{24,20},{28,24},{32,28},{36,32}... | collective-permute-start | bytes 786440 | tf_op jit(solution)/shard_map/while/body/eval_jaxpr/ppermute | solution.py:15
  512.2 10.5 %collective-permute-start.1 = (f32[4,128,128]{2,1,0:T(8,128)S(1)}, f32[4,128,128]{2,1,0:T(8,128)S(1)}, u32[]{:S(2)}, u32[]{:S(2)}) collective-permute-start(f32[4,128,128]{2,1,0:T(8,128)S(1)} %multiply_add_fusion.5), channel_id=1, source_target_pairs={{4,0},{8,4},{12,8},{16,12},{20,16},{24,20},{28,24},{32,28},{36,32}... | collective-permute-start | bytes 786440 | tf_op jit(solution)/shard_map/while/body/eval_jaxpr/ppermute | solution.py:15
  532.9 11.7 %collective-permute-start.1 = (f32[4,128,128]{2,1,0:T(8,128)S(1)}, f32[4,128,128]{2,1,0:T(8,128)S(1)}, u32[]{:S(2)}, u32[]{:S(2)}) collective-permute-start(f32[4,128,128]{2,1,0:T(8,128)S(1)} %multiply_add_fusion.5), channel_id=1, source_target_pairs={{4,0},{8,4},{12,8},{16,12},{20,16},{24,20},{28,24},{32,28},{36,32}... | collective-permute-start | bytes 786440 | tf_op jit(solution)/shard_map/while/body/eval_jaxpr/ppermute | solution.py:15
  544.6 11.9 %collective-permute-start.1 = (f32[4,128,128]{2,1,0:T(8,128)S(1)}, f32[4,128,128]{2,1,0:T(8,128)S(1)}, u32[]{:S(2)}, u32[]{:S(2)}) collective-permute-start(f32[4,128,128]{2,1,0:T(8,128)S(1)} %multiply_add_fusion.5), channel_id=1, source_target_pairs={{4,0},{8,4},{12,8},{16,12},{20,16},{24,20},{28,24},{32,28},{36,32}... | collective-permute-start | bytes 786440 | tf_op jit(solution)/shard_map/while/body/eval_jaxpr/ppermute | solution.py:15
  556.6 10.9 %collective-permute-start.1 = (f32[4,128,128]{2,1,0:T(8,128)S(1)}, f32[4,128,128]{2,1,0:T(8,128)S(1)}, u32[]{:S(2)}, u32[]{:S(2)}) collective-permute-start(f32[4,128,128]{2,1,0:T(8,128)S(1)} %multiply_add_fusion.5), channel_id=1, source_target_pairs={{4,0},{8,4},{12,8},{16,12},{20,16},{24,20},{28,24},{32,28},{36,32}... | collective-permute-start | bytes 786440 | tf_op jit(solution)/shard_map/while/body/eval_jaxpr/ppermute | solution.py:15
  587.1 10.9 %collective-permute-start.1 = (f32[4,128,128]{2,1,0:T(8,128)S(1)}, f32[4,128,128]{2,1,0:T(8,128)S(1)}, u32[]{:S(2)}, u32[]{:S(2)}) collective-permute-start(f32[4,128,128]{2,1,0:T(8,128)S(1)} %multiply_add_fusion.5), channel_id=1, source_target_pairs={{4,0},{8,4},{12,8},{16,12},{20,16},{24,20},{28,24},{32,28},{36,32}... | collective-permute-start | bytes 786440 | tf_op jit(solution)/shard_map/while/body/eval_jaxpr/ppermute | solution.py:15
  598.0 12.6 %collective-permute-start.1 = (f32[4,128,128]{2,1,0:T(8,128)S(1)}, f32[4,128,128]{2,1,0:T(8,128)S(1)}, u32[]{:S(2)}, u32[]{:S(2)}) collective-permute-start(f32[4,128,128]{2,1,0:T(8,128)S(1)} %multiply_add_fusion.5), channel_id=1, source_target_pairs={{4,0},{8,4},{12,8},{16,12},{20,16},{24,20},{28,24},{32,28},{36,32}... | collective-permute-start | bytes 786440 | tf_op jit(solution)/shard_map/while/body/eval_jaxpr/ppermute | solution.py:15
  610.7 10.6 %collective-permute-start.1 = (f32[4,128,128]{2,1,0:T(8,128)S(1)}, f32[4,128,128]{2,1,0:T(8,128)S(1)}, u32[]{:S(2)}, u32[]{:S(2)}) collective-permute-start(f32[4,128,128]{2,1,0:T(8,128)S(1)} %multiply_add_fusion.5), channel_id=1, source_target_pairs={{4,0},{8,4},{12,8},{16,12},{20,16},{24,20},{28,24},{32,28},{36,32}... | collective-permute-start | bytes 786440 | tf_op jit(solution)/shard_map/while/body/eval_jaxpr/ppermute | solution.py:15
  621.4 11.6 %collective-permute-start.1 = (f32[4,128,128]{2,1,0:T(8,128)S(1)}, f32[4,128,128]{2,1,0:T(8,128)S(1)}, u32[]{:S(2)}, u32[]{:S(2)}) collective-permute-start(f32[4,128,128]{2,1,0:T(8,128)S(1)} %multiply_add_fusion.5), channel_id=1, source_target_pairs={{4,0},{8,4},{12,8},{16,12},{20,16},{24,20},{28,24},{32,28},{36,32}... | collective-permute-start | bytes 786440 | tf_op jit(solution)/shard_map/while/body/eval_jaxpr/ppermute | solution.py:15
  633.1 17.4 %collective-permute-start.1 = (f32[4,128,128]{2,1,0:T(8,128)S(1)}, f32[4,128,128]{2,1,0:T(8,128)S(1)}, u32[]{:S(2)}, u32[]{:S(2)}) collective-permute-start(f32[4,128,128]{2,1,0:T(8,128)S(1)} %multiply_add_fusion.5), channel_id=1, source_target_pairs={{4,0},{8,4},{12,8},{16,12},{20,16},{24,20},{28,24},{32,28},{36,32}... | collective-permute-start | bytes 786440 | tf_op jit(solution)/shard_map/while/body/eval_jaxpr/ppermute | solution.py:15
  650.6 12.5 %collective-permute-start.1 = (f32[4,128,128]{2,1,0:T(8,128)S(1)}, f32[4,128,128]{2,1,0:T(8,128)S(1)}, u32[]{:S(2)}, u32[]{:S(2)}) collective-permute-start(f32[4,128,128]{2,1,0:T(8,128)S(1)} %multiply_add_fusion.5), channel_id=1, source_target_pairs={{4,0},{8,4},{12,8},{16,12},{20,16},{24,20},{28,24},{32,28},{36,32}... | collective-permute-start | bytes 786440 | tf_op jit(solution)/shard_map/while/body/eval_jaxpr/ppermute | solution.py:15
  663.2 14.0 %collective-permute-start.1 = (f32[4,128,128]{2,1,0:T(8,128)S(1)}, f32[4,128,128]{2,1,0:T(8,128)S(1)}, u32[]{:S(2)}, u32[]{:S(2)}) collective-permute-start(f32[4,128,128]{2,1,0:T(8,128)S(1)} %multiply_add_fusion.5), channel_id=1, source_target_pairs={{4,0},{8,4},{12,8},{16,12},{20,16},{24,20},{28,24},{32,28},{36,32}... | collective-permute-start | bytes 786440 | tf_op jit(solution)/shard_map/while/body/eval_jaxpr/ppermute | solution.py:15
  677.3 11.3 %collective-permute-start.1 = (f32[4,128,128]{2,1,0:T(8,128)S(1)}, f32[4,128,128]{2,1,0:T(8,128)S(1)}, u32[]{:S(2)}, u32[]{:S(2)}) collective-permute-start(f32[4,128,128]{2,1,0:T(8,128)S(1)} %multiply_add_fusion.5), channel_id=1, source_target_pairs={{4,0},{8,4},{12,8},{16,12},{20,16},{24,20},{28,24},{32,28},{36,32}... | collective-permute-start | bytes 786440 | tf_op jit(solution)/shard_map/while/body/eval_jaxpr/ppermute | solution.py:15
  698.5 12.1 %collective-permute-start.1 = (f32[4,128,128]{2,1,0:T(8,128)S(1)}, f32[4,128,128]{2,1,0:T(8,128)S(1)}, u32[]{:S(2)}, u32[]{:S(2)}) collective-permute-start(f32[4,128,128]{2,1,0:T(8,128)S(1)} %multiply_add_fusion.5), channel_id=1, source_target_pairs={{4,0},{8,4},{12,8},{16,12},{20,16},{24,20},{28,24},{32,28},{36,32}... | collective-permute-start | bytes 786440 | tf_op jit(solution)/shard_map/while/body/eval_jaxpr/ppermute | solution.py:15
  710.6 11.7 %collective-permute-start.1 = (f32[4,128,128]{2,1,0:T(8,128)S(1)}, f32[4,128,128]{2,1,0:T(8,128)S(1)}, u32[]{:S(2)}, u32[]{:S(2)}) collective-permute-start(f32[4,128,128]{2,1,0:T(8,128)S(1)} %multiply_add_fusion.5), channel_id=1, source_target_pairs={{4,0},{8,4},{12,8},{16,12},{20,16},{24,20},{28,24},{32,28},{36,32}... | collective-permute-start | bytes 786440 | tf_op jit(solution)/shard_map/while/body/eval_jaxpr/ppermute | solution.py:15
  722.5 12.2 %collective-permute-start.1 = (f32[4,128,128]{2,1,0:T(8,128)S(1)}, f32[4,128,128]{2,1,0:T(8,128)S(1)}, u32[]{:S(2)}, u32[]{:S(2)}) collective-permute-start(f32[4,128,128]{2,1,0:T(8,128)S(1)} %multiply_add_fusion.5), channel_id=1, source_target_pairs={{4,0},{8,4},{12,8},{16,12},{20,16},{24,20},{28,24},{32,28},{36,32}... | collective-permute-start | bytes 786440 | tf_op jit(solution)/shard_map/while/body/eval_jaxpr/ppermute | solution.py:15
  734.8 10.9 %collective-permute-start.1 = (f32[4,128,128]{2,1,0:T(8,128)S(1)}, f32[4,128,128]{2,1,0:T(8,128)S(1)}, u32[]{:S(2)}, u32[]{:S(2)}) collective-permute-start(f32[4,128,128]{2,1,0:T(8,128)S(1)} %multiply_add_fusion.5), channel_id=1, source_target_pairs={{4,0},{8,4},{12,8},{16,12},{20,16},{24,20},{28,24},{32,28},{36,32}... | collective-permute-start | bytes 786440 | tf_op jit(solution)/shard_map/while/body/eval_jaxpr/ppermute | solution.py:15
  745.8 11.5 %collective-permute-start.1 = (f32[4,128,128]{2,1,0:T(8,128)S(1)}, f32[4,128,128]{2,1,0:T(8,128)S(1)}, u32[]{:S(2)}, u32[]{:S(2)}) collective-permute-start(f32[4,128,128]{2,1,0:T(8,128)S(1)} %multiply_add_fusion.5), channel_id=1, source_target_pairs={{4,0},{8,4},{12,8},{16,12},{20,16},{24,20},{28,24},{32,28},{36,32}... | collective-permute-start | bytes 786440 | tf_op jit(solution)/shard_map/while/body/eval_jaxpr/ppermute | solution.py:15
  757.4 12.5 %collective-permute-start.1 = (f32[4,128,128]{2,1,0:T(8,128)S(1)}, f32[4,128,128]{2,1,0:T(8,128)S(1)}, u32[]{:S(2)}, u32[]{:S(2)}) collective-permute-start(f32[4,128,128]{2,1,0:T(8,128)S(1)} %multiply_add_fusion.5), channel_id=1, source_target_pairs={{4,0},{8,4},{12,8},{16,12},{20,16},{24,20},{28,24},{32,28},{36,32}... | collective-permute-start | bytes 786440 | tf_op jit(solution)/shard_map/while/body/eval_jaxpr/ppermute | solution.py:15
  (49 other events, 323.3 us)
Sparse Core Ops, SparseCore 0:
  859.7 66.5 reduce-scatter.3
where the time goes:
time: 1010 us
  waiting for transfers between devices  522 us (52%)
  starting transfers between devices  232 us (23%)
  blocking collectives  75.7 us (7%)
  matrix products  65.1 us (6%)
  local copies, waits for them, and re-layouts  63.2 us (6%)
  other arithmetic  35.6 us (4%)
  between operations  14.2 us (1%)
    ppermute x62, waiting for transfers between devices, passed_along(): lax.ppermute(value, axis, [(source, source + steps) for source in range(f...  464 us
    ppermute x62, starting transfers between devices, passed_along(): lax.ppermute(value, axis, [(source, source + steps) for source in range(f...  232 us
    psum x1, blocking collectives, shards(): gain_total = lax.psum(gain_term, 'ctx')  75.7 us
    unnamed x2, waiting for transfers between devices  58.4 us
  transfers between devices with their start and end apart: 63, of which 63 were waited for; matrix products, arithmetic and copies ran while one was open for 1% of the time, Pallas kernels for 0%

commit v1 on v0

--- a/solution.py
+++ b/solution.py
@@ -13,6 +13,51 @@
     count = lax.axis_size(axis)
     first, last = (max(0, -steps), min(count, count - steps))
     return lax.ppermute(value, axis, [(source, source + steps) for source in range(first, last)])
+
+
+def local_incoming_grad(q_rows, cot_rows, cum_decay, opened, head_count, head_width):
+    tok_rows = q_rows.shape[0]
+    factor = jnp.exp(cum_decay) * opened[None, :]
+    weighted = (
+        q_rows.reshape(tok_rows, head_count, head_width).astype(jnp.float32)
+        * head_width ** (-0.5)
+        * factor.T[:, :, None]
+    )
+    cot_float = cot_rows.astype(jnp.float32)
+    return jnp.einsum(
+        "thd,the->hde",
+        weighted,
+        cot_float.reshape(tok_rows, head_count, head_width),
+        precision=PRECISE,
+    )
+
+
+def pack(decay, term):
+    lane = jnp.broadcast_to(decay[:, None, None], (term.shape[0], 1, term.shape[2]))
+    return jnp.concatenate([term, lane], axis=1)
+
+
+def both_scans(decay, fwd_term, bwd_term, count):
+    rows = fwd_term.shape[1]
+    scans = []
+    for term in (fwd_term, bwd_term):
+        scans.append([decay, term, jnp.ones_like(decay), jnp.zeros_like(term)])
+    shift = 1
+    while shift < count:
+        got = [
+            passed_along(pack(agg_a, agg_b), "ctx", shift * sign)
+            for (agg_a, agg_b, _, _), sign in zip(scans, (1, -1))
+        ]
+        for index, received in enumerate(got):
+            agg_a, agg_b, ex_a, ex_b = scans[index]
+            r_b, r_a = received[:, :rows], received[:, rows, 0]
+            ex_b = ex_a[:, None, None] * r_b + ex_b
+            ex_a = ex_a * r_a
+            agg_b = agg_a[:, None, None] * r_b + agg_b
+            agg_a = agg_a * r_a
+            scans[index] = [agg_a, agg_b, ex_a, ex_b]
+        shift *= 2
+    return scans[0][3], scans[1][3]
 
 
 def start_flags(doc_lengths, first_pos, num_rows):
@@ -98,34 +143,14 @@
         "shd,she->hde", k_float * to_end.T[:, :, None], v_float, precision=PRECISE
     )
     ctx_size = lax.axis_size("ctx")
-
-    def relay_forward(step_index, incoming):
-        return passed_along(shard_decay[:, None, None] * incoming + local_end, "ctx", 1)
-
-    state_in = lax.fori_loop(0, ctx_size - 1, relay_forward, jnp.zeros_like(local_end))
+    local_grad = local_incoming_grad(q_rows, cotangent[0], cum_decay, opened, head_count, head_width)
+    state_in, later_grad = both_scans(shard_decay, local_end, local_grad, ctx_size)
 
     def forward(q_part, k_part, v_part, gate_part, gain_part):
         return run_blocks(q_part, k_part, v_part, gate_part, flags, gain_part, state_in)
 
     (primal, end_state), pullback = jax.vjp(forward, q_rows, k_rows, v_rows, gate_rows, key_gain)
-    factor = jnp.exp(cum_decay) * opened[None, :]
-    weighted = (
-        q_rows.reshape(tok_rows, head_count, head_width).astype(jnp.float32)
-        * head_width ** (-0.5)
-        * factor.T[:, :, None]
-    )
     cot_float = cotangent[0].astype(jnp.float32)
-    local_grad = jnp.einsum(
-        "thd,the->hde",
-        weighted,
-        cot_float.reshape(tok_rows, head_count, head_width),
-        precision=PRECISE,
-    )
-
-    def relay_back(step_index, incoming):
-        return passed_along(shard_decay[:, None, None] * incoming + local_grad, "ctx", -1)
-
-    later_grad = lax.fori_loop(0, ctx_size - 1, relay_back, jnp.zeros_like(local_grad))
     grad_q, grad_k, grad_v, grad_a, gain_term = pullback((cot_float, later_grad))
     gain_total = lax.psum(gain_term, "ctx")
     grad_gain = lax.psum_scatter(gain_total, "dp", scatter_dimension=1, tiled=True)

time: 1010 us -> 339 us (0.34)
  waiting for transfers between devices: 522 us -> 30 us
  starting transfers between devices: 232 us -> 49.5 us
    ppermute x62 -> x10, waiting for transfers between devices: 464 us -> 25.9 us  [passed_along(): lax.ppermute(value, axis, [(source, source + steps) for source in range(f...]
    ppermute x62 -> x10, starting transfers between devices: 232 us -> 49.4 us  [passed_along(): lax.ppermute(value, axis, [(source, source + steps) for source in range(f...]
    unnamed x2, waiting for transfers between devices: 58.4 us -> 4.13 us
  transfers between devices with their start and end apart: 63 -> 11, of which waited for: 63 -> 7; matrix products, arithmetic and copies ran while one was open for 1% -> 7% of each run, Pallas kernels for 0% -> 0%
where the time goes in v1:
time: 339 us; the launch traced here: 338 us
  blocking collectives  75.7 us (22%)
  matrix products  66.1 us (19%)
  local copies, waits for them, and re-layouts  61.3 us (18%)
  starting transfers between devices  49.5 us (15%)
  other arithmetic  39.9 us (12%)
  waiting for transfers between devices  30 us (9%)
  between operations  14.5 us (4%)
    psum x1, blocking collectives, shards(): gain_total = lax.psum(gain_term, 'ctx')  75.7 us
    ppermute x10, starting transfers between devices, passed_along(): lax.ppermute(value, axis, [(source, source + steps) for source in range(f...  49.4 us
    ppermute x10, waiting for transfers between devices, passed_along(): lax.ppermute(value, axis, [(source, source + steps) for source in range(f...  25.9 us
    another operation x27, other arithmetic  20.1 us
    dot_general x6, matrix products, block_step(): jnp.einsum('hts,she->the', weights, v_block, preferred_element_type=jnp.f...  19.2 us
    dot_general x8, matrix products, block_step(): jnp.einsum('thd,hde->the', q_float, carried, precision=PRECISE)  15.6 us
    dot_general x6, matrix products, block_step(): jnp.einsum('thd,shd->hts', q_block, k_bf, preferred_element_type=jnp.floa...  14.5 us
    dot_general x6, matrix products, block_step(): jnp.einsum('shd,she->hde', k_float * to_end.T[:, :, None], v_float, preci...  11.3 us
  transfers between devices with their start and end apart: 11, of which 7 were waited for; matrix products, arithmetic and copies ran while one was open for 7% of the time, Pallas kernels for 0%

profile of v1, /device:TPU:2, one launch (start us, length us, event | category | flops | bytes accessed | tf_op | source)
XLA Modules:
  0.0 337.6 jit_solution(13439850530653654449)
XLA Ops:
  14.0 2.1 reshape.632
  19.1 2.7 multiply_convert_fusion.6
  21.8 2.1 reshape_squeeze.17
  24.7 2.5 fusion.107
  27.2 2.9 fusion.109
  31.5 4.6 %collective-permute-start = (f32[4,129,128]{2,1,0:T(8,128)S(1)}, f32[4,129,128]{2,1,0:T(8,128)S(1)}, u32[]{:S(2)}, u32[]{:S(2)}) collective-permute-start(f32[4,129,128]{2,1,0:T(8,128)S(1)} %get-tuple-element.803), channel_id=1, source_target_pairs={{0,4},{4,8},{8,12},{12,16},{16,20},{20,24},{24,28},{28,32},{32,36}... | collective-permute-start | bytes 792584 | tf_op jit(solution)/shard_map/ppermute | solution.py:15
  36.9 3.7 %collective-permute-done.5 = f32[4,129,128]{2,1,0:T(8,128)S(1)} collective-permute-done((f32[4,129,128]{2,1,0:T(8,128)S(1)}, f32[4,129,128]{2,1,0:T(8,128)S(1)}, u32[]{:S(2)}, u32[]{:S(2)}) %collective-permute-start.5) | collective-permute-done | bytes 264224 | tf_op jit(solution)/shard_map/ppermute | solution.py:15
  43.1 6.0 %collective-permute-start.1 = (f32[4,129,128]{2,1,0:T(8,128)S(1)}, f32[4,129,128]{2,1,0:T(8,128)S(1)}, u32[]{:S(2)}, u32[]{:S(2)}) collective-permute-start(f32[4,129,128]{2,1,0:T(8,128)S(1)} %pad_maximum_fusion.2), channel_id=1, source_target_pairs={{0,8},{4,12},{8,16},{12,20},{16,24},{20,28},{24,32},{28,36},{32,40... | collective-permute-start | bytes 792584 | tf_op jit(solution)/shard_map/ppermute | solution.py:15
  50.5 3.3 collective-permute-done.1
  53.8 8.4 %collective-permute-done.6 = f32[4,129,128]{2,1,0:T(8,128)S(1)} collective-permute-done((f32[4,129,128]{2,1,0:T(8,128)S(1)}, f32[4,129,128]{2,1,0:T(8,128)S(1)}, u32[]{:S(2)}, u32[]{:S(2)}) %collective-permute-start.6) | collective-permute-done | bytes 264224 | tf_op jit(solution)/shard_map/ppermute | solution.py:15
  64.7 8.0 %collective-permute-start.2 = (f32[4,129,128]{2,1,0:T(8,128)S(1)}, f32[4,129,128]{2,1,0:T(8,128)S(1)}, u32[]{:S(2)}, u32[]{:S(2)}) collective-permute-start(f32[4,129,128]{2,1,0:T(8,128)S(1)} %pad_maximum_fusion.3), channel_id=1, source_target_pairs={{0,16},{4,20},{8,24},{12,28},{16,32},{20,36},{24,40},{28,44},{32,4... | collective-permute-start | bytes 792584 | tf_op jit(solution)/shard_map/ppermute | solution.py:15
  72.7 4.7 %collective-permute-done.7 = f32[4,129,128]{2,1,0:T(8,128)S(1)} collective-permute-done((f32[4,129,128]{2,1,0:T(8,128)S(1)}, f32[4,129,128]{2,1,0:T(8,128)S(1)}, u32[]{:S(2)}, u32[]{:S(2)}) %collective-permute-start.7) | collective-permute-done | bytes 264224 | tf_op jit(solution)/shard_map/ppermute | solution.py:15
  79.4 5.6 %collective-permute-start.3 = (f32[4,129,128]{2,1,0:T(8,128)S(1)}, f32[4,129,128]{2,1,0:T(8,128)S(1)}, u32[]{:S(2)}, u32[]{:S(2)}) collective-permute-start(f32[4,129,128]{2,1,0:T(8,128)S(1)} %pad_maximum_fusion.4), channel_id=1, source_target_pairs={{0,32},{4,36},{8,40},{12,44},{16,48},{20,52},{24,56},{28,60},{32,6... | collective-permute-start | bytes 792584 | tf_op jit(solution)/shard_map/ppermute | solution.py:15
  85.1 4.7 %collective-permute-done.8 = f32[4,129,128]{2,1,0:T(8,128)S(1)} collective-permute-done((f32[4,129,128]{2,1,0:T(8,128)S(1)}, f32[4,129,128]{2,1,0:T(8,128)S(1)}, u32[]{:S(2)}, u32[]{:S(2)}) %collective-permute-start.8) | collective-permute-done | bytes 264224 | tf_op jit(solution)/shard_map/ppermute | solution.py:15
  93.2 18.7 %collective-permute-start.4 = (f32[4,129,128]{2,1,0:T(8,128)}, f32[4,129,128]{2,1,0:T(8,128)}, u32[]{:S(2)}, u32[]{:S(2)}) collective-permute-start(f32[4,129,128]{2,1,0:T(8,128)} %pad_maximum_fusion.5), channel_id=1, source_target_pairs={{0,64},{4,68},{8,72},{12,76},{16,80},{20,84},{24,88},{28,92},{32,9... | collective-permute-start | bytes 792584 | tf_op jit(solution)/shard_map/ppermute | solution.py:15
  112.9 2.1 reshape_squeeze.20
  116.2 1.7 reshape.642
  119.3 2.3 copy.237
  124.5 27.3 %while.42 = (s32[]{:T(128)}, f32[4,128,128]{2,1,0:T(8,128)S(1)}, bf16[2,512,4,128]{1,3,2,0:T(8,128)(2,1)}, f32[2,4,128,128]{3,2,1,0:T(8,128)}, f32[2,4,512]{2,1,...) while((s32[]{:T(128)}, f32[4,128,128]{2,1,0:T(8,128)S(1)}, ...), condition=%wide.region_11.12_spmd.clone, body=%wide.region_6.11_spmd.clone.sunk | while | flops 1352081408 | bytes 9343697 | solution.py:117
  127.8 3.3 fusion.203
  132.6 3.0 fusion.204
  135.8 2.4 convolution_add_fusion.4
  141.5 3.3 fusion.203
  146.3 3.0 fusion.204
  149.4 2.4 convolution_add_fusion.4
  155.6 85.3 %while.43 = (s32[]{:T(128)}, f32[4,128]{1,0:T(4,128)S(1)}, f32[4,128,128]{2,1,0:T(8,128)S(1)}, bf16[2,512,4,128]{3,2,1,0:T(4,128)(2,1)}, bf16[2,512,4,128]{3,2,1...) while((s32[]{:T(128)}, f32[4,128]{1,0:T(4,128)S(1)}, ...), condition=%wide.region_26.27_spmd.clone, body=%wide.region_12.26_spmd.clone.sunk | while | flops 3394863616 | bytes 116524784 | solution.py:117
  158.9 1.9 dynamic-slice_bitcast_fusion.13
  166.3 1.9 fusion.222
  169.2 2.5 fusion.225
  171.7 3.2 fusion.226
  175.0 3.8 %fusion.232 = bf16[4,128,512]{2,1,0:T(8,128)(2,1)S(1)} fusion(f32[4,512,512]{2,1,0:T(8,128)} %copy-done, f32[4,512]{1,0:T(4,128)S(1)} %bitcast.355, pred[512,512]{1,0:T(8,128)(4,1)S(1)} %fusion.224, f32[512,4,128]{0,2,1:T(8,128)S(1)} %bitcast.341), kind=kOutput, calls=%fused_computation.81.clone.1 | convolution fusion | flops 274726912 | bytes 6037504 | tf_op jit(solution)/shard_map/transpose(jvp())/while/body/eval_jaxpr/checkpoint/hts,she->the/dot_general | solution.py:89
  182.0 1.9 convolution_add_fusion.5
  184.0 3.3 fusion.230
  187.3 1.8 fusion.231
  192.8 5.0 %reduce-window.150 = f32[4,4,128]{2,1,0:T(4,128)S(1)} reduce-window(f32[4,4,128]{2,1,0:T(4,128)S(1)} %reshape.693, f32[]{:T(128)} %constant.142.clone.1..sunk.1), window={size=1x1x128 pad=0_0x0_0x0_127}, to_apply=%region_24.24 | reduce-window | flops 260096 | bytes 16388 | tf_op jit(solution)/shard_map/reduce-window.60
  201.6 1.9 dynamic-slice_bitcast_fusion.13
  208.9 1.9 fusion.222
  211.8 2.5 fusion.225
  214.4 3.2 fusion.226
  217.6 3.8 %fusion.232 = bf16[4,128,512]{2,1,0:T(8,128)(2,1)S(1)} fusion(f32[4,512,512]{2,1,0:T(8,128)} %copy-done, f32[4,512]{1,0:T(4,128)S(1)} %bitcast.355, pred[512,512]{1,0:T(8,128)(4,1)S(1)} %fusion.224, f32[512,4,128]{0,2,1:T(8,128)S(1)} %bitcast.341), kind=kOutput, calls=%fused_computation.81.clone.1 | convolution fusion | flops 274726912 | bytes 6037504 | tf_op jit(solution)/shard_map/transpose(jvp())/while/body/eval_jaxpr/checkpoint/hts,she->the/dot_general | solution.py:89
  224.7 1.9 convolution_add_fusion.5
  226.6 3.3 fusion.230
  230.0 1.8 fusion.231
  235.5 5.0 %reduce-window.150 = f32[4,4,128]{2,1,0:T(4,128)S(1)} reduce-window(f32[4,4,128]{2,1,0:T(4,128)S(1)} %reshape.693, f32[]{:T(128)} %constant.142.clone.1..sunk.1), window={size=1x1x128 pad=0_0x0_0x0_127}, to_apply=%region_24.24 | reduce-window | flops 260096 | bytes 16388 | tf_op jit(solution)/shard_map/reduce-window.60
  241.8 2.5 copy.239
  244.3 2.2 convert_element_type.302
  250.1 4.1 %reduce-scatter.4.cloned.1.call-done = f32[64,4]{1,0:T(8,128)} async-done(((f32[128,4]{1,0:T(8,128)}), f32[64,4]{1,0:T(8,128)}) %reduce-scatter.4.cloned.1.call-update) | async-done | bytes 1040
  255.0 75.7 %psum.8 = f32[4,64]{1,0:T(4,128)} all-reduce(f32[4,64]{1,0:T(4,128)S(1)} %copy.265), channel_id=1, replica_groups=mesh['dp'=2,'ctx'=32,'head'=4] {'ctx'}, use_global_device_ids=true, to_apply=%region_27.28 | all-reduce | flops 256 | bytes 2048 | tf_op jit(solution)/shard_map/psum | solution.py:155
  (315 shorter events, 83.7 us)
Async XLA Ops:
  7.2 10.2 %copy-start.7 = (bf16[1,1024,512]{2,1,0:T(8,128)(2,1)S(1)}, bf16[1,1024,512]{2,1,0:T(8,128)(2,1)}, u32[]{:S(2)}) copy-start(bf16[1,1024,512]{2,1,0:T(8,128)(2,1)} %param.12) | copy-start | bytes 3145732
  7.2 247.0 %reduce-scatter.4.cloned.1.call-start = ((), (), s32[]{:S(2)}) async-start(), calls=%async_computation.1 | async-start | bytes 98304
  12.5 6.5 %copy-start.32 = (f32[4,128]{1,0:T(4,128)S(1)}, f32[4,128]{1,0:T(4,128)}, u32[]{:S(2)}) copy-start(f32[4,128]{1,0:T(4,128)} %param.16) | copy-start | bytes 6148
  27.2 13.4 %copy-start.18 = (f32[4,128,128]{2,1,0:T(8,128)}, f32[4,128,128]{2,1,0:T(8,128)S(1)}, u32[]{:S(2)}) copy-start(f32[4,128,128]{2,1,0:T(8,128)S(1)} %fusion.107) | copy-start | bytes 786436
  30.2 10.3 %collective-permute-start.5 = (f32[4,129,128]{2,1,0:T(8,128)S(1)}, f32[4,129,128]{2,1,0:T(8,128)S(1)}, u32[]{:S(2)}, u32[]{:S(2)}) collective-permute-start(f32[4,129,128]{2,1,0:T(8,128)S(1)} %get-tuple-element.802), channel_id=1, source_target_pairs={{4,0},{8,4},{12,8},{16,12},{20,16},{24,20},{28,24},{32,28},{36,32}... | collective-permute-start | bytes 792584 | tf_op jit(solution)/shard_map/ppermute | solution.py:15
  31.5 10.2 %collective-permute-start = (f32[4,129,128]{2,1,0:T(8,128)S(1)}, f32[4,129,128]{2,1,0:T(8,128)S(1)}, u32[]{:S(2)}, u32[]{:S(2)}) collective-permute-start(f32[4,129,128]{2,1,0:T(8,128)S(1)} %get-tuple-element.803), channel_id=1, source_target_pairs={{0,4},{4,8},{8,12},{12,16},{16,20},{20,24},{24,28},{28,32},{32,36}... | collective-permute-start | bytes 792584 | tf_op jit(solution)/shard_map/ppermute | solution.py:15
  40.5 37.1 %copy-start.19 = (f32[4,129,128]{2,1,0:T(8,128)}, f32[4,129,128]{2,1,0:T(8,128)S(1)}, u32[]{:S(2)}) copy-start(f32[4,129,128]{2,1,0:T(8,128)S(1)} %collective-permute-done.5) | copy-start | bytes 792580
  41.7 35.9 %copy-start.21 = (f32[4,129,128]{2,1,0:T(8,128)}, f32[4,129,128]{2,1,0:T(8,128)S(1)}, u32[]{:S(2)}) copy-start(f32[4,129,128]{2,1,0:T(8,128)S(1)} %collective-permute-done) | copy-start | bytes 792580
  43.1 10.7 %collective-permute-start.1 = (f32[4,129,128]{2,1,0:T(8,128)S(1)}, f32[4,129,128]{2,1,0:T(8,128)S(1)}, u32[]{:S(2)}, u32[]{:S(2)}) collective-permute-start(f32[4,129,128]{2,1,0:T(8,128)S(1)} %pad_maximum_fusion.2), channel_id=1, source_target_pairs={{0,8},{4,12},{8,16},{12,20},{16,24},{20,28},{24,32},{28,36},{32,40... | collective-permute-start | bytes 792584 | tf_op jit(solution)/shard_map/ppermute | solution.py:15
  49.2 13.0 %collective-permute-start.6 = (f32[4,129,128]{2,1,0:T(8,128)S(1)}, f32[4,129,128]{2,1,0:T(8,128)S(1)}, u32[]{:S(2)}, u32[]{:S(2)}) collective-permute-start(f32[4,129,128]{2,1,0:T(8,128)S(1)} %pad_maximum_fusion.6), channel_id=1, source_target_pairs={{8,0},{12,4},{16,8},{20,12},{24,16},{28,20},{32,24},{36,28},{40,32... | collective-permute-start | bytes 792584 | tf_op jit(solution)/shard_map/ppermute | solution.py:15
  53.8 10.8 %copy-start.27 = (f32[4,129,128]{2,1,0:T(8,128)}, f32[4,129,128]{2,1,0:T(8,128)S(1)}, u32[]{:S(2)}) copy-start(f32[4,129,128]{2,1,0:T(8,128)S(1)} %collective-permute-done.1) | copy-start | bytes 792580
  63.2 14.1 %collective-permute-start.7 = (f32[4,129,128]{2,1,0:T(8,128)S(1)}, f32[4,129,128]{2,1,0:T(8,128)S(1)}, u32[]{:S(2)}, u32[]{:S(2)}) collective-permute-start(f32[4,129,128]{2,1,0:T(8,128)S(1)} %pad_maximum_fusion.7), channel_id=1, source_target_pairs={{16,0},{20,4},{24,8},{28,12},{32,16},{36,20},{40,24},{44,28},{48,3... | collective-permute-start | bytes 792584 | tf_op jit(solution)/shard_map/ppermute | solution.py:15
  64.7 14.4 %collective-permute-start.2 = (f32[4,129,128]{2,1,0:T(8,128)S(1)}, f32[4,129,128]{2,1,0:T(8,128)S(1)}, u32[]{:S(2)}, u32[]{:S(2)}) collective-permute-start(f32[4,129,128]{2,1,0:T(8,128)S(1)} %pad_maximum_fusion.3), channel_id=1, source_target_pairs={{0,16},{4,20},{8,24},{12,28},{16,32},{20,36},{24,40},{28,44},{32,4... | collective-permute-start | bytes 792584 | tf_op jit(solution)/shard_map/ppermute | solution.py:15
  77.3 15.8 %copy-start.23 = (f32[4,129,128]{2,1,0:T(8,128)}, f32[4,129,128]{2,1,0:T(8,128)S(1)}, u32[]{:S(2)}) copy-start(f32[4,129,128]{2,1,0:T(8,128)S(1)} %collective-permute-done.7) | copy-start | bytes 792580
  77.7 37.4 %copy-start.8 = (bf16[1,1024,512]{2,1,0:T(8,128)(2,1)S(1)}, bf16[1,1024,512]{2,1,0:T(8,128)(2,1)}, u32[]{:S(2)}) copy-start(bf16[1,1024,512]{2,1,0:T(8,128)(2,1)} %param.11) | copy-start | bytes 3145732
  77.7 12.1 %collective-permute-start.8 = (f32[4,129,128]{2,1,0:T(8,128)S(1)}, f32[4,129,128]{2,1,0:T(8,128)S(1)}, u32[]{:S(2)}, u32[]{:S(2)}) collective-permute-start(f32[4,129,128]{2,1,0:T(8,128)S(1)} %pad_maximum_fusion.8), channel_id=1, source_target_pairs={{32,0},{36,4},{40,8},{44,12},{48,16},{52,20},{56,24},{60,28},{64,3... | collective-permute-start | bytes 792584 | tf_op jit(solution)/shard_map/ppermute | solution.py:15
  79.1 14.0 %copy-start.25 = (f32[4,129,128]{2,1,0:T(8,128)}, f32[4,129,128]{2,1,0:T(8,128)S(1)}, u32[]{:S(2)}) copy-start(f32[4,129,128]{2,1,0:T(8,128)S(1)} %collective-permute-done.2) | copy-start | bytes 792580
  79.4 12.6 %collective-permute-start.3 = (f32[4,129,128]{2,1,0:T(8,128)S(1)}, f32[4,129,128]{2,1,0:T(8,128)S(1)}, u32[]{:S(2)}, u32[]{:S(2)}) collective-permute-start(f32[4,129,128]{2,1,0:T(8,128)S(1)} %pad_maximum_fusion.4), channel_id=1, source_target_pairs={{0,32},{4,36},{8,40},{12,44},{16,48},{20,52},{24,56},{28,60},{32,6... | collective-permute-start | bytes 792584 | tf_op jit(solution)/shard_map/ppermute | solution.py:15
  89.7 3.4 %copy-start.29 = (f32[4,129,128]{2,1,0:T(8,128)}, f32[4,129,128]{2,1,0:T(8,128)S(1)}, u32[]{:S(2)}) copy-start(f32[4,129,128]{2,1,0:T(8,128)S(1)} %collective-permute-done.8) | copy-start | bytes 792580
  90.0 26.2 %copy-start.9 = (bf16[1,1024,512]{2,1,0:T(8,128)(2,1)S(1)}, bf16[1,1024,512]{2,1,0:T(8,128)(2,1)}, u32[]{:S(2)}) copy-start(bf16[1,1024,512]{2,1,0:T(8,128)(2,1)} %param.17) | copy-start | bytes 3145732
  90.8 32.0 %collective-permute-start.9 = (f32[4,129,128]{2,1,0:T(8,128)}, f32[4,129,128]{2,1,0:T(8,128)}, u32[]{:S(2)}, u32[]{:S(2)}) collective-permute-start(f32[4,129,128]{2,1,0:T(8,128)} %pad_maximum_fusion.9), channel_id=1, source_target_pairs={{64,0},{68,4},{72,8},{76,12},{80,16},{84,20},{88,24},{92,28},{96,3... | collective-permute-start | bytes 792584 | tf_op jit(solution)/shard_map/ppermute | solution.py:15
  93.2 29.6 %collective-permute-start.4 = (f32[4,129,128]{2,1,0:T(8,128)}, f32[4,129,128]{2,1,0:T(8,128)}, u32[]{:S(2)}, u32[]{:S(2)}) collective-permute-start(f32[4,129,128]{2,1,0:T(8,128)} %pad_maximum_fusion.5), channel_id=1, source_target_pairs={{0,64},{4,68},{8,72},{12,76},{16,80},{20,84},{24,88},{28,92},{32,9... | collective-permute-start | bytes 792584 | tf_op jit(solution)/shard_map/ppermute | solution.py:15
  116.1 5.5 %copy-start.17 = (bf16[2,512,4,128]{3,2,1,0:T(4,128)(2,1)S(1)}, bf16[2,512,4,128]{3,2,1,0:T(4,128)(2,1)}, u32[]{:S(2)}) copy-start(bf16[2,512,4,128]{3,2,1,0:T(4,128)(2,1)} %reshape_squeeze.21) | copy-start | bytes 3145732
  117.8 4.9 %copy-start.20 = (f32[4,129,128]{2,1,0:T(8,128)S(1)}, f32[4,129,128]{2,1,0:T(8,128)}, u32[]{:S(2)}) copy-start(f32[4,129,128]{2,1,0:T(8,128)} %copy-done.19) | copy-start | bytes 792580
  117.8 4.9 %copy-start.22 = (f32[4,129,128]{2,1,0:T(8,128)S(1)}, f32[4,129,128]{2,1,0:T(8,128)}, u32[]{:S(2)}) copy-start(f32[4,129,128]{2,1,0:T(8,128)} %copy-done.21) | copy-start | bytes 792580
  117.8 5.0 %copy-start.24 = (f32[4,129,128]{2,1,0:T(8,128)S(1)}, f32[4,129,128]{2,1,0:T(8,128)}, u32[]{:S(2)}) copy-start(f32[4,129,128]{2,1,0:T(8,128)} %copy-done.23) | copy-start | bytes 792580
  117.8 5.0 %copy-start.26 = (f32[4,129,128]{2,1,0:T(8,128)S(1)}, f32[4,129,128]{2,1,0:T(8,128)}, u32[]{:S(2)}) copy-start(f32[4,129,128]{2,1,0:T(8,128)} %copy-done.25) | copy-start | bytes 792580
  119.3 5.1 %copy-start.31 = (f32[1,4,1024]{2,1,0:T(4,128)S(1)}, f32[1,4,1024]{2,1,0:T(4,128)}, u32[]{:S(2)}) copy-start(f32[1,4,1024]{2,1,0:T(4,128)} %param.14) | copy-start | bytes 49156
  155.6 5.2 %copy-start.3 = (bf16[2,512,4,128]{3,1,2,0:T(8,128)(2,1)}, bf16[2,512,4,128]{3,1,2,0:T(8,128)(2,1)S(1)}, u32[]{:S(2)}) copy-start(bf16[2,512,4,128]{3,1,2,0:T(8,128)(2,1)S(1)} %get-tuple-element.1097) | copy-start | bytes 3145732 | tf_op jit(solution)/shard_map/transpose(jvp())/while
  155.6 5.2 %copy-start.5 = (f32[2,512,4,128]{3,2,1,0:T(4,128)S(1)}, f32[2,512,4,128]{3,2,1,0:T(4,128)}, u32[]{:S(2)}) copy-start(f32[2,512,4,128]{3,2,1,0:T(4,128)} %get-tuple-element.1101) | copy-start | bytes 6291460 | tf_op jit(solution)/shard_map/transpose(jvp())/while
  161.3 7.9 %copy-start.1 = (bf16[512,4,128]{2,0,1:T(8,128)(2,1)S(1)}, bf16[512,4,128]{2,0,1:T(8,128)(2,1)}, u32[]{:S(2)}) copy-start(bf16[512,4,128]{2,0,1:T(8,128)(2,1)} %dynamic-slice_bitcast_fusion.13) | copy-start | bytes 1572868 | tf_op jit(solution)/shard_map/transpose(jvp())/while
  171.7 3.2 copy-start.34
  183.9 5.2 %copy-start.6 = (bf16[1,512,4,128]{3,1,2,0:T(8,128)(2,1)S(1)}, bf16[1,512,4,128]{3,1,2,0:T(8,128)(2,1)}, u32[]{:S(2)}) copy-start(bf16[1,512,4,128]{3,1,2,0:T(8,128)(2,1)} %get-tuple-element.1012) | copy-start | bytes 1572868 | tf_op jit(solution)/shard_map/transpose(jvp())/while
  183.9 5.2 %copy-start.10 = (bf16[2,512,4,128]{3,2,1,0:T(4,128)(2,1)S(1)}, bf16[2,512,4,128]{3,2,1,0:T(4,128)(2,1)}, u32[]{:S(2)}) copy-start(bf16[2,512,4,128]{3,2,1,0:T(4,128)(2,1)} %get-tuple-element.1073) | copy-start | bytes 3145732 | tf_op jit(solution)/shard_map/transpose(jvp())/while
  184.0 5.2 %copy-start.13 = (bf16[2,512,4,128]{3,2,1,0:T(4,128)(2,1)S(1)}, bf16[2,512,4,128]{3,2,1,0:T(4,128)(2,1)}, u32[]{:S(2)}) copy-start(bf16[2,512,4,128]{3,2,1,0:T(4,128)(2,1)} %get-tuple-element.1074) | copy-start | bytes 3145732 | tf_op jit(solution)/shard_map/transpose(jvp())/while
  189.2 9.1 %copy-start.4 = (bf16[2,512,4,128]{3,1,2,0:T(8,128)(2,1)S(1)}, bf16[2,512,4,128]{3,1,2,0:T(8,128)(2,1)}, u32[]{:S(2)}) copy-start(bf16[2,512,4,128]{3,1,2,0:T(8,128)(2,1)} %copy-done.3) | copy-start | bytes 3145732 | tf_op jit(solution)/shard_map/transpose(jvp())/while
  198.3 5.2 %copy-start.3 = (bf16[2,512,4,128]{3,1,2,0:T(8,128)(2,1)}, bf16[2,512,4,128]{3,1,2,0:T(8,128)(2,1)S(1)}, u32[]{:S(2)}) copy-start(bf16[2,512,4,128]{3,1,2,0:T(8,128)(2,1)S(1)} %get-tuple-element.1097) | copy-start | bytes 3145732 | tf_op jit(solution)/shard_map/transpose(jvp())/while
  198.3 5.2 %copy-start.5 = (f32[2,512,4,128]{3,2,1,0:T(4,128)S(1)}, f32[2,512,4,128]{3,2,1,0:T(4,128)}, u32[]{:S(2)}) copy-start(f32[2,512,4,128]{3,2,1,0:T(4,128)} %get-tuple-element.1101) | copy-start | bytes 6291460 | tf_op jit(solution)/shard_map/transpose(jvp())/while
  203.9 7.9 %copy-start.1 = (bf16[512,4,128]{2,0,1:T(8,128)(2,1)S(1)}, bf16[512,4,128]{2,0,1:T(8,128)(2,1)}, u32[]{:S(2)}) copy-start(bf16[512,4,128]{2,0,1:T(8,128)(2,1)} %dynamic-slice_bitcast_fusion.13) | copy-start | bytes 1572868 | tf_op jit(solution)/shard_map/transpose(jvp())/while
  214.4 3.2 copy-start.34
  226.6 5.2 %copy-start.6 = (bf16[1,512,4,128]{3,1,2,0:T(8,128)(2,1)S(1)}, bf16[1,512,4,128]{3,1,2,0:T(8,128)(2,1)}, u32[]{:S(2)}) copy-start(bf16[1,512,4,128]{3,1,2,0:T(8,128)(2,1)} %get-tuple-element.1012) | copy-start | bytes 1572868 | tf_op jit(solution)/shard_map/transpose(jvp())/while
  226.6 5.2 %copy-start.10 = (bf16[2,512,4,128]{3,2,1,0:T(4,128)(2,1)S(1)}, bf16[2,512,4,128]{3,2,1,0:T(4,128)(2,1)}, u32[]{:S(2)}) copy-start(bf16[2,512,4,128]{3,2,1,0:T(4,128)(2,1)} %get-tuple-element.1073) | copy-start | bytes 3145732 | tf_op jit(solution)/shard_map/transpose(jvp())/while
  226.6 5.2 %copy-start.13 = (bf16[2,512,4,128]{3,2,1,0:T(4,128)(2,1)S(1)}, bf16[2,512,4,128]{3,2,1,0:T(4,128)(2,1)}, u32[]{:S(2)}) copy-start(bf16[2,512,4,128]{3,2,1,0:T(4,128)(2,1)} %get-tuple-element.1074) | copy-start | bytes 3145732 | tf_op jit(solution)/shard_map/transpose(jvp())/while
  231.8 9.1 %copy-start.4 = (bf16[2,512,4,128]{3,1,2,0:T(8,128)(2,1)S(1)}, bf16[2,512,4,128]{3,1,2,0:T(8,128)(2,1)}, u32[]{:S(2)}) copy-start(bf16[2,512,4,128]{3,1,2,0:T(8,128)(2,1)} %copy-done.3) | copy-start | bytes 3145732 | tf_op jit(solution)/shard_map/transpose(jvp())/while
  241.0 7.9 %copy-start.33 = (f32[2,4,512]{2,1,0:T(4,128)}, f32[2,4,512]{2,1,0:T(4,128)S(1)}, u32[]{:S(2)}) copy-start(f32[2,4,512]{2,1,0:T(4,128)S(1)} %get-tuple-element.443) | copy-start | bytes 49156
  241.0 5.5 %copy-start.12 = (bf16[2,512,4,128]{3,2,1,0:T(4,128)(2,1)S(1)}, bf16[2,512,4,128]{3,2,1,0:T(4,128)(2,1)}, u32[]{:S(2)}) copy-start(bf16[2,512,4,128]{3,2,1,0:T(4,128)(2,1)} %get-tuple-element.440) | copy-start | bytes 3145732
  241.0 6.7 %copy-start.15 = (bf16[2,512,4,128]{3,2,1,0:T(4,128)(2,1)S(1)}, bf16[2,512,4,128]{3,2,1,0:T(4,128)(2,1)}, u32[]{:S(2)}) copy-start(bf16[2,512,4,128]{3,2,1,0:T(4,128)(2,1)} %get-tuple-element.441) | copy-start | bytes 3145732
  241.8 7.1 %copy-start.16 = (bf16[2,512,4,128]{3,2,1,0:T(4,128)(2,1)S(1)}, bf16[2,512,4,128]{3,2,1,0:T(4,128)(2,1)}, u32[]{:S(2)}) copy-start(bf16[2,512,4,128]{3,2,1,0:T(4,128)(2,1)} %get-tuple-element.442) | copy-start | bytes 3145732
  (10 other events, 17.7 us)
Sparse Core Ops, SparseCore 0:
  241.9 12.2 reduce-scatter.3

commit v2 on v1

--- a/solution.py
+++ b/solution.py
@@ -152,8 +152,8 @@
     (primal, end_state), pullback = jax.vjp(forward, q_rows, k_rows, v_rows, gate_rows, key_gain)
     cot_float = cotangent[0].astype(jnp.float32)
     grad_q, grad_k, grad_v, grad_a, gain_term = pullback((cot_float, later_grad))
-    gain_total = lax.psum(gain_term, "ctx")
-    grad_gain = lax.psum_scatter(gain_total, "dp", scatter_dimension=1, tiled=True)
+    gain_half = lax.psum_scatter(gain_term, "dp", scatter_dimension=1, tiled=True)
+    grad_gain = jnp.sum(lax.all_gather(gain_half, "ctx"), axis=0)
     return (
         primal.astype(jnp.bfloat16)[None],
         grad_q[None],

time: 339 us -> 314 us (0.926)
  blocking collectives: 75.7 us -> 49.7 us
    psum x1 -> x0, blocking collectives: 75.7 us -> none  [shards(): gain_total = lax.psum(gain_term, 'ctx')]
    all_gather x0 -> x1, blocking collectives: none -> 49.7 us  [shards(): grad_gain = jnp.sum(lax.all_gather(gain_half, 'ctx'), axis=0)]
where the time goes in v2:
time: 314 us; the launch traced here: 312 us
  matrix products  66.1 us (21%)
  local copies, waits for them, and re-layouts  61.3 us (20%)
  blocking collectives  49.7 us (16%)
  starting transfers between devices  49.5 us (16%)
  other arithmetic  40.6 us (13%)
  waiting for transfers between devices  30 us (10%)
  between operations  14.5 us (5%)
    all_gather x1, blocking collectives, shards(): grad_gain = jnp.sum(lax.all_gather(gain_half, 'ctx'), axis=0)  49.7 us
    ppermute x10, starting transfers between devices, passed_along(): lax.ppermute(value, axis, [(source, source + steps) for source in range(f...  49.4 us
    ppermute x10, waiting for transfers between devices, passed_along(): lax.ppermute(value, axis, [(source, source + steps) for source in range(f...  25.9 us
    another operation x27, other arithmetic  20.1 us
    dot_general x6, matrix products, block_step(): jnp.einsum('hts,she->the', weights, v_block, preferred_element_type=jnp.f...  19.2 us
    dot_general x8, matrix products, block_step(): jnp.einsum('thd,hde->the', q_float, carried, precision=PRECISE)  15.6 us
    dot_general x6, matrix products, block_step(): jnp.einsum('thd,shd->hts', q_block, k_bf, preferred_element_type=jnp.floa...  14.5 us
    dot_general x6, matrix products, block_step(): jnp.einsum('shd,she->hde', k_float * to_end.T[:, :, None], v_float, preci...  11.3 us
  transfers between devices with their start and end apart: 11, of which 7 were waited for; matrix products, arithmetic and copies ran while one was open for 7% of the time, Pallas kernels for 0%

profile of v2, /device:TPU:2, one launch (start us, length us, event | category | flops | bytes accessed | tf_op | source)
XLA Modules:
  0.0 312.2 jit_solution(373349398668020199)
XLA Ops:
  14.0 2.1 reshape.632
  19.1 2.7 multiply_convert_fusion.6
  21.8 2.1 reshape_squeeze.17
  24.7 2.5 fusion.107
  27.2 2.9 fusion.109
  31.5 4.6 %collective-permute-start = (f32[4,129,128]{2,1,0:T(8,128)S(1)}, f32[4,129,128]{2,1,0:T(8,128)S(1)}, u32[]{:S(2)}, u32[]{:S(2)}) collective-permute-start(f32[4,129,128]{2,1,0:T(8,128)S(1)} %get-tuple-element.803), channel_id=1, source_target_pairs={{0,4},{4,8},{8,12},{12,16},{16,20},{20,24},{24,28},{28,32},{32,36}... | collective-permute-start | bytes 792584 | tf_op jit(solution)/shard_map/ppermute | solution.py:15
  36.9 3.7 %collective-permute-done.5 = f32[4,129,128]{2,1,0:T(8,128)S(1)} collective-permute-done((f32[4,129,128]{2,1,0:T(8,128)S(1)}, f32[4,129,128]{2,1,0:T(8,128)S(1)}, u32[]{:S(2)}, u32[]{:S(2)}) %collective-permute-start.5) | collective-permute-done | bytes 264224 | tf_op jit(solution)/shard_map/ppermute | solution.py:15
  43.1 6.0 %collective-permute-start.1 = (f32[4,129,128]{2,1,0:T(8,128)S(1)}, f32[4,129,128]{2,1,0:T(8,128)S(1)}, u32[]{:S(2)}, u32[]{:S(2)}) collective-permute-start(f32[4,129,128]{2,1,0:T(8,128)S(1)} %pad_maximum_fusion.2), channel_id=1, source_target_pairs={{0,8},{4,12},{8,16},{12,20},{16,24},{20,28},{24,32},{28,36},{32,40... | collective-permute-start | bytes 792584 | tf_op jit(solution)/shard_map/ppermute | solution.py:15
  50.5 3.3 %collective-permute-done.1 = f32[4,129,128]{2,1,0:T(8,128)S(1)} collective-permute-done((f32[4,129,128]{2,1,0:T(8,128)S(1)}, f32[4,129,128]{2,1,0:T(8,128)S(1)}, u32[]{:S(2)}, u32[]{:S(2)}) %collective-permute-start.1) | collective-permute-done | bytes 264224 | tf_op jit(solution)/shard_map/ppermute | solution.py:15
  53.8 8.4 %collective-permute-done.6 = f32[4,129,128]{2,1,0:T(8,128)S(1)} collective-permute-done((f32[4,129,128]{2,1,0:T(8,128)S(1)}, f32[4,129,128]{2,1,0:T(8,128)S(1)}, u32[]{:S(2)}, u32[]{:S(2)}) %collective-permute-start.6) | collective-permute-done | bytes 264224 | tf_op jit(solution)/shard_map/ppermute | solution.py:15
  64.7 8.0 %collective-permute-start.2 = (f32[4,129,128]{2,1,0:T(8,128)S(1)}, f32[4,129,128]{2,1,0:T(8,128)S(1)}, u32[]{:S(2)}, u32[]{:S(2)}) collective-permute-start(f32[4,129,128]{2,1,0:T(8,128)S(1)} %pad_maximum_fusion.3), channel_id=1, source_target_pairs={{0,16},{4,20},{8,24},{12,28},{16,32},{20,36},{24,40},{28,44},{32,4... | collective-permute-start | bytes 792584 | tf_op jit(solution)/shard_map/ppermute | solution.py:15
  72.7 4.7 %collective-permute-done.7 = f32[4,129,128]{2,1,0:T(8,128)S(1)} collective-permute-done((f32[4,129,128]{2,1,0:T(8,128)S(1)}, f32[4,129,128]{2,1,0:T(8,128)S(1)}, u32[]{:S(2)}, u32[]{:S(2)}) %collective-permute-start.7) | collective-permute-done | bytes 264224 | tf_op jit(solution)/shard_map/ppermute | solution.py:15
  79.4 5.6 %collective-permute-start.3 = (f32[4,129,128]{2,1,0:T(8,128)S(1)}, f32[4,129,128]{2,1,0:T(8,128)S(1)}, u32[]{:S(2)}, u32[]{:S(2)}) collective-permute-start(f32[4,129,128]{2,1,0:T(8,128)S(1)} %pad_maximum_fusion.4), channel_id=1, source_target_pairs={{0,32},{4,36},{8,40},{12,44},{16,48},{20,52},{24,56},{28,60},{32,6... | collective-permute-start | bytes 792584 | tf_op jit(solution)/shard_map/ppermute | solution.py:15
  85.1 4.7 %collective-permute-done.8 = f32[4,129,128]{2,1,0:T(8,128)S(1)} collective-permute-done((f32[4,129,128]{2,1,0:T(8,128)S(1)}, f32[4,129,128]{2,1,0:T(8,128)S(1)}, u32[]{:S(2)}, u32[]{:S(2)}) %collective-permute-start.8) | collective-permute-done | bytes 264224 | tf_op jit(solution)/shard_map/ppermute | solution.py:15
  93.2 18.7 %collective-permute-start.4 = (f32[4,129,128]{2,1,0:T(8,128)}, f32[4,129,128]{2,1,0:T(8,128)}, u32[]{:S(2)}, u32[]{:S(2)}) collective-permute-start(f32[4,129,128]{2,1,0:T(8,128)} %pad_maximum_fusion.5), channel_id=1, source_target_pairs={{0,64},{4,68},{8,72},{12,76},{16,80},{20,84},{24,88},{28,92},{32,9... | collective-permute-start | bytes 792584 | tf_op jit(solution)/shard_map/ppermute | solution.py:15
  112.9 2.1 reshape_squeeze.20
  116.2 1.7 reshape.642
  119.3 2.3 copy.237
  124.5 27.3 %while.42 = (s32[]{:T(128)}, f32[4,128,128]{2,1,0:T(8,128)S(1)}, bf16[2,512,4,128]{1,3,2,0:T(8,128)(2,1)}, f32[2,4,128,128]{3,2,1,0:T(8,128)}, f32[2,4,512]{2,1,...) while((s32[]{:T(128)}, f32[4,128,128]{2,1,0:T(8,128)S(1)}, ...), condition=%wide.region_11.12_spmd.clone, body=%wide.region_6.11_spmd.clone.sunk | while | flops 1352081408 | bytes 9343697 | solution.py:117
  127.8 3.3 %fusion.203 = f32[512,4,128]{0,2,1:T(8,128)S(1)} fusion(bf16[512,4,128]{2,0,1:T(8,128)(2,1)S(1)} %fusion.201, f32[4,512]{1,0:T(4,128)S(1)} %bitcast.358, pred[512,512]{1,0:T(8,128)(4,1)S(1)} %fusion.202, bf16[2,512,4,128]{3,1,2,0:T(8,128)(2,1)} %get-tuple-element.1049, s32[]{:T(128)S(6)} %copy.340, bf16[2,512,4,128]{3,1,2,0:T(8,128)(2,1)} %get-tuple-element.1048), kind=kOutput, calls=%fused_computation.3.clone.1 | convolution fusion | flops 543162368 | bytes 2900992 | tf_op jit(solution)/shard_map/jvp()/while/body/eval_jaxpr/hts,she->the/dot_general | solution.py:89
  132.6 3.0 fusion.204
  135.8 2.4 convolution_add_fusion.4
  141.5 3.3 %fusion.203 = f32[512,4,128]{0,2,1:T(8,128)S(1)} fusion(bf16[512,4,128]{2,0,1:T(8,128)(2,1)S(1)} %fusion.201, f32[4,512]{1,0:T(4,128)S(1)} %bitcast.358, pred[512,512]{1,0:T(8,128)(4,1)S(1)} %fusion.202, bf16[2,512,4,128]{3,1,2,0:T(8,128)(2,1)} %get-tuple-element.1049, s32[]{:T(128)S(6)} %copy.340, bf16[2,512,4,128]{3,1,2,0:T(8,128)(2,1)} %get-tuple-element.1048), kind=kOutput, calls=%fused_computation.3.clone.1 | convolution fusion | flops 543162368 | bytes 2900992 | tf_op jit(solution)/shard_map/jvp()/while/body/eval_jaxpr/hts,she->the/dot_general | solution.py:89
  146.3 3.0 fusion.204
  149.4 2.4 convolution_add_fusion.4
  155.6 85.3 %while.43 = (s32[]{:T(128)}, f32[4,128]{1,0:T(4,128)S(1)}, f32[4,128,128]{2,1,0:T(8,128)S(1)}, bf16[2,512,4,128]{3,2,1,0:T(4,128)(2,1)}, bf16[2,512,4,128]{3,2,1...) while((s32[]{:T(128)}, f32[4,128]{1,0:T(4,128)S(1)}, ...), condition=%wide.region_26.27_spmd.clone, body=%wide.region_12.26_spmd.clone.sunk | while | flops 3394863616 | bytes 116524784 | solution.py:117
  158.9 1.9 dynamic-slice_bitcast_fusion.13
  166.3 1.9 fusion.222
  169.2 2.5 fusion.225
  171.7 3.2 %fusion.226 = (bf16[1,512,4,128]{3,1,2,0:T(8,128)(2,1)}, f32[4,128]{1,0:T(4,128)S(1)}) fusion(f32[4,128]{1,0:T(4,128)S(1)} %get-tuple-element.994, bf16[512,4,128]{2,0,1:T(8,128)(2,1)S(1)} %copy-done.2, bf16[512,4,128]{2,0,1:T(8,128)(2,1)S(1)} %get-tuple-element.1001, bf16[512,4,128]{2,0,1:T(8,128)(2,1)S(1)} %dynamic-slice_bitcast_fusion.11, ...), kind=kOutput, calls=%fused_computation.110.clone.1 | convolution fusion | flops 276823552 | bytes 4468736 | tf_op jit(solution)/shard_map/transpose(jvp())/while/body/eval_jaxpr/checkpoint/thd,shd->hts/dot_general | solution.py:87
  175.0 3.8 %fusion.232 = bf16[4,128,512]{2,1,0:T(8,128)(2,1)S(1)} fusion(f32[4,512,512]{2,1,0:T(8,128)} %copy-done, f32[4,512]{1,0:T(4,128)S(1)} %bitcast.356, pred[512,512]{1,0:T(8,128)(4,1)S(1)} %fusion.224, f32[512,4,128]{0,2,1:T(8,128)S(1)} %bitcast.342), kind=kOutput, calls=%fused_computation.81.clone.1 | convolution fusion | flops 274726912 | bytes 6037504 | tf_op jit(solution)/shard_map/transpose(jvp())/while/body/eval_jaxpr/checkpoint/hts,she->the/dot_general | solution.py:89
  182.0 1.9 convolution_add_fusion.5
  184.0 3.3 %fusion.230 = bf16[4,512,128]{2,1,0:T(8,128)(2,1)S(1)} fusion(bf16[512,4,128]{2,0,1:T(8,128)(2,1)S(1)} %fusion.221, bf16[4,512,512]{2,1,0:T(8,128)(2,1)} %copy-done.34, f32[4,512]{1,0:T(4,128)S(1)} %bitcast.357, pred[512,512]{1,0:T(8,128)(4,1)S(1)} %fusion.224), kind=kOutput, calls=%fused_computation.85.clone.1 | convolution fusion | flops 274989056 | bytes 3416064 | tf_op jit(solution)/shard_map/transpose(jvp())/while/body/eval_jaxpr/checkpoint/thd,shd->hts/dot_general | solution.py:87
  187.3 1.8 fusion.231
  192.8 5.0 %reduce-window.150 = f32[4,4,128]{2,1,0:T(4,128)S(1)} reduce-window(f32[4,4,128]{2,1,0:T(4,128)S(1)} %reshape.697, f32[]{:T(128)} %constant.142.clone.1..sunk.1), window={size=1x1x128 pad=0_0x0_0x0_127}, to_apply=%region_24.24 | reduce-window | flops 260096 | bytes 16388 | tf_op jit(solution)/shard_map/reduce-window.60
  201.6 1.9 dynamic-slice_bitcast_fusion.13
  208.9 1.9 fusion.222
  211.8 2.5 fusion.225
  214.4 3.2 %fusion.226 = (bf16[1,512,4,128]{3,1,2,0:T(8,128)(2,1)}, f32[4,128]{1,0:T(4,128)S(1)}) fusion(f32[4,128]{1,0:T(4,128)S(1)} %get-tuple-element.994, bf16[512,4,128]{2,0,1:T(8,128)(2,1)S(1)} %copy-done.2, bf16[512,4,128]{2,0,1:T(8,128)(2,1)S(1)} %get-tuple-element.1001, bf16[512,4,128]{2,0,1:T(8,128)(2,1)S(1)} %dynamic-slice_bitcast_fusion.11, ...), kind=kOutput, calls=%fused_computation.110.clone.1 | convolution fusion | flops 276823552 | bytes 4468736 | tf_op jit(solution)/shard_map/transpose(jvp())/while/body/eval_jaxpr/checkpoint/thd,shd->hts/dot_general | solution.py:87
  217.6 3.8 %fusion.232 = bf16[4,128,512]{2,1,0:T(8,128)(2,1)S(1)} fusion(f32[4,512,512]{2,1,0:T(8,128)} %copy-done, f32[4,512]{1,0:T(4,128)S(1)} %bitcast.356, pred[512,512]{1,0:T(8,128)(4,1)S(1)} %fusion.224, f32[512,4,128]{0,2,1:T(8,128)S(1)} %bitcast.342), kind=kOutput, calls=%fused_computation.81.clone.1 | convolution fusion | flops 274726912 | bytes 6037504 | tf_op jit(solution)/shard_map/transpose(jvp())/while/body/eval_jaxpr/checkpoint/hts,she->the/dot_general | solution.py:89
  224.7 1.9 convolution_add_fusion.5
  226.6 3.3 %fusion.230 = bf16[4,512,128]{2,1,0:T(8,128)(2,1)S(1)} fusion(bf16[512,4,128]{2,0,1:T(8,128)(2,1)S(1)} %fusion.221, bf16[4,512,512]{2,1,0:T(8,128)(2,1)} %copy-done.34, f32[4,512]{1,0:T(4,128)S(1)} %bitcast.357, pred[512,512]{1,0:T(8,128)(4,1)S(1)} %fusion.224), kind=kOutput, calls=%fused_computation.85.clone.1 | convolution fusion | flops 274989056 | bytes 3416064 | tf_op jit(solution)/shard_map/transpose(jvp())/while/body/eval_jaxpr/checkpoint/thd,shd->hts/dot_general | solution.py:87
  230.0 1.8 fusion.231
  235.5 5.0 %reduce-window.150 = f32[4,4,128]{2,1,0:T(4,128)S(1)} reduce-window(f32[4,4,128]{2,1,0:T(4,128)S(1)} %reshape.697, f32[]{:T(128)} %constant.142.clone.1..sunk.1), window={size=1x1x128 pad=0_0x0_0x0_127}, to_apply=%region_24.24 | reduce-window | flops 260096 | bytes 16388 | tf_op jit(solution)/shard_map/reduce-window.60
  241.8 2.5 copy.239
  244.3 2.2 convert_element_type.302
  250.1 4.1 %reduce-scatter.4.cloned.1.call-done = f32[64,4]{1,0:T(8,128)} async-done(((f32[128,4]{1,0:T(8,128)}), f32[64,4]{1,0:T(8,128)}) %reduce-scatter.4.cloned.1.call-update) | async-done | bytes 1040
  255.0 49.7 %all-gather.1 = f32[32,4,64]{2,1,0:T(4,128)S(1)} all-gather(f32[1,4,64]{2,1,0:T(4,128)S(1)} %bitcast.374), channel_id=2, replica_groups=mesh['dp'=2,'ctx'=32,'head'=4] {'ctx'}, dimensions={0}, use_global_device_ids=true | all-gather | bytes 33792 | tf_op jit(solution)/shard_map/all_gather | solution.py:156
  (316 shorter events, 84.3 us)
Async XLA Ops:
  7.2 10.2 %copy-start.7 = (bf16[1,1024,512]{2,1,0:T(8,128)(2,1)S(1)}, bf16[1,1024,512]{2,1,0:T(8,128)(2,1)}, u32[]{:S(2)}) copy-start(bf16[1,1024,512]{2,1,0:T(8,128)(2,1)} %param.12) | copy-start | bytes 3145732
  7.2 247.0 %reduce-scatter.4.cloned.1.call-start = ((), (), s32[]{:S(2)}) async-start(), calls=%async_computation.1 | async-start | bytes 98304
  12.5 6.5 %copy-start.32 = (f32[4,128]{1,0:T(4,128)S(1)}, f32[4,128]{1,0:T(4,128)}, u32[]{:S(2)}) copy-start(f32[4,128]{1,0:T(4,128)} %param.16) | copy-start | bytes 6148
  27.2 13.4 %copy-start.18 = (f32[4,128,128]{2,1,0:T(8,128)}, f32[4,128,128]{2,1,0:T(8,128)S(1)}, u32[]{:S(2)}) copy-start(f32[4,128,128]{2,1,0:T(8,128)S(1)} %fusion.107) | copy-start | bytes 786436
  30.2 10.3 %collective-permute-start.5 = (f32[4,129,128]{2,1,0:T(8,128)S(1)}, f32[4,129,128]{2,1,0:T(8,128)S(1)}, u32[]{:S(2)}, u32[]{:S(2)}) collective-permute-start(f32[4,129,128]{2,1,0:T(8,128)S(1)} %get-tuple-element.802), channel_id=1, source_target_pairs={{4,0},{8,4},{12,8},{16,12},{20,16},{24,20},{28,24},{32,28},{36,32}... | collective-permute-start | bytes 792584 | tf_op jit(solution)/shard_map/ppermute | solution.py:15
  31.5 10.2 %collective-permute-start = (f32[4,129,128]{2,1,0:T(8,128)S(1)}, f32[4,129,128]{2,1,0:T(8,128)S(1)}, u32[]{:S(2)}, u32[]{:S(2)}) collective-permute-start(f32[4,129,128]{2,1,0:T(8,128)S(1)} %get-tuple-element.803), channel_id=1, source_target_pairs={{0,4},{4,8},{8,12},{12,16},{16,20},{20,24},{24,28},{28,32},{32,36}... | collective-permute-start | bytes 792584 | tf_op jit(solution)/shard_map/ppermute | solution.py:15
  40.5 37.1 %copy-start.19 = (f32[4,129,128]{2,1,0:T(8,128)}, f32[4,129,128]{2,1,0:T(8,128)S(1)}, u32[]{:S(2)}) copy-start(f32[4,129,128]{2,1,0:T(8,128)S(1)} %collective-permute-done.5) | copy-start | bytes 792580
  41.7 35.9 %copy-start.21 = (f32[4,129,128]{2,1,0:T(8,128)}, f32[4,129,128]{2,1,0:T(8,128)S(1)}, u32[]{:S(2)}) copy-start(f32[4,129,128]{2,1,0:T(8,128)S(1)} %collective-permute-done) | copy-start | bytes 792580
  43.1 10.7 %collective-permute-start.1 = (f32[4,129,128]{2,1,0:T(8,128)S(1)}, f32[4,129,128]{2,1,0:T(8,128)S(1)}, u32[]{:S(2)}, u32[]{:S(2)}) collective-permute-start(f32[4,129,128]{2,1,0:T(8,128)S(1)} %pad_maximum_fusion.2), channel_id=1, source_target_pairs={{0,8},{4,12},{8,16},{12,20},{16,24},{20,28},{24,32},{28,36},{32,40... | collective-permute-start | bytes 792584 | tf_op jit(solution)/shard_map/ppermute | solution.py:15
  49.2 13.0 %collective-permute-start.6 = (f32[4,129,128]{2,1,0:T(8,128)S(1)}, f32[4,129,128]{2,1,0:T(8,128)S(1)}, u32[]{:S(2)}, u32[]{:S(2)}) collective-permute-start(f32[4,129,128]{2,1,0:T(8,128)S(1)} %pad_maximum_fusion.6), channel_id=1, source_target_pairs={{8,0},{12,4},{16,8},{20,12},{24,16},{28,20},{32,24},{36,28},{40,32... | collective-permute-start | bytes 792584 | tf_op jit(solution)/shard_map/ppermute | solution.py:15
  53.8 10.8 %copy-start.27 = (f32[4,129,128]{2,1,0:T(8,128)}, f32[4,129,128]{2,1,0:T(8,128)S(1)}, u32[]{:S(2)}) copy-start(f32[4,129,128]{2,1,0:T(8,128)S(1)} %collective-permute-done.1) | copy-start | bytes 792580
  63.2 14.1 %collective-permute-start.7 = (f32[4,129,128]{2,1,0:T(8,128)S(1)}, f32[4,129,128]{2,1,0:T(8,128)S(1)}, u32[]{:S(2)}, u32[]{:S(2)}) collective-permute-start(f32[4,129,128]{2,1,0:T(8,128)S(1)} %pad_maximum_fusion.7), channel_id=1, source_target_pairs={{16,0},{20,4},{24,8},{28,12},{32,16},{36,20},{40,24},{44,28},{48,3... | collective-permute-start | bytes 792584 | tf_op jit(solution)/shard_map/ppermute | solution.py:15
  64.7 14.4 %collective-permute-start.2 = (f32[4,129,128]{2,1,0:T(8,128)S(1)}, f32[4,129,128]{2,1,0:T(8,128)S(1)}, u32[]{:S(2)}, u32[]{:S(2)}) collective-permute-start(f32[4,129,128]{2,1,0:T(8,128)S(1)} %pad_maximum_fusion.3), channel_id=1, source_target_pairs={{0,16},{4,20},{8,24},{12,28},{16,32},{20,36},{24,40},{28,44},{32,4... | collective-permute-start | bytes 792584 | tf_op jit(solution)/shard_map/ppermute | solution.py:15
  77.3 15.8 %copy-start.23 = (f32[4,129,128]{2,1,0:T(8,128)}, f32[4,129,128]{2,1,0:T(8,128)S(1)}, u32[]{:S(2)}) copy-start(f32[4,129,128]{2,1,0:T(8,128)S(1)} %collective-permute-done.7) | copy-start | bytes 792580
  77.7 37.4 %copy-start.8 = (bf16[1,1024,512]{2,1,0:T(8,128)(2,1)S(1)}, bf16[1,1024,512]{2,1,0:T(8,128)(2,1)}, u32[]{:S(2)}) copy-start(bf16[1,1024,512]{2,1,0:T(8,128)(2,1)} %param.11) | copy-start | bytes 3145732
  77.7 12.1 %collective-permute-start.8 = (f32[4,129,128]{2,1,0:T(8,128)S(1)}, f32[4,129,128]{2,1,0:T(8,128)S(1)}, u32[]{:S(2)}, u32[]{:S(2)}) collective-permute-start(f32[4,129,128]{2,1,0:T(8,128)S(1)} %pad_maximum_fusion.8), channel_id=1, source_target_pairs={{32,0},{36,4},{40,8},{44,12},{48,16},{52,20},{56,24},{60,28},{64,3... | collective-permute-start | bytes 792584 | tf_op jit(solution)/shard_map/ppermute | solution.py:15
  79.1 14.0 %copy-start.25 = (f32[4,129,128]{2,1,0:T(8,128)}, f32[4,129,128]{2,1,0:T(8,128)S(1)}, u32[]{:S(2)}) copy-start(f32[4,129,128]{2,1,0:T(8,128)S(1)} %collective-permute-done.2) | copy-start | bytes 792580
  79.4 12.6 %collective-permute-start.3 = (f32[4,129,128]{2,1,0:T(8,128)S(1)}, f32[4,129,128]{2,1,0:T(8,128)S(1)}, u32[]{:S(2)}, u32[]{:S(2)}) collective-permute-start(f32[4,129,128]{2,1,0:T(8,128)S(1)} %pad_maximum_fusion.4), channel_id=1, source_target_pairs={{0,32},{4,36},{8,40},{12,44},{16,48},{20,52},{24,56},{28,60},{32,6... | collective-permute-start | bytes 792584 | tf_op jit(solution)/shard_map/ppermute | solution.py:15
  89.7 3.4 %copy-start.29 = (f32[4,129,128]{2,1,0:T(8,128)}, f32[4,129,128]{2,1,0:T(8,128)S(1)}, u32[]{:S(2)}) copy-start(f32[4,129,128]{2,1,0:T(8,128)S(1)} %collective-permute-done.8) | copy-start | bytes 792580
  90.0 26.2 %copy-start.9 = (bf16[1,1024,512]{2,1,0:T(8,128)(2,1)S(1)}, bf16[1,1024,512]{2,1,0:T(8,128)(2,1)}, u32[]{:S(2)}) copy-start(bf16[1,1024,512]{2,1,0:T(8,128)(2,1)} %param.17) | copy-start | bytes 3145732
  90.8 32.0 %collective-permute-start.9 = (f32[4,129,128]{2,1,0:T(8,128)}, f32[4,129,128]{2,1,0:T(8,128)}, u32[]{:S(2)}, u32[]{:S(2)}) collective-permute-start(f32[4,129,128]{2,1,0:T(8,128)} %pad_maximum_fusion.9), channel_id=1, source_target_pairs={{64,0},{68,4},{72,8},{76,12},{80,16},{84,20},{88,24},{92,28},{96,3... | collective-permute-start | bytes 792584 | tf_op jit(solution)/shard_map/ppermute | solution.py:15
  93.2 29.6 %collective-permute-start.4 = (f32[4,129,128]{2,1,0:T(8,128)}, f32[4,129,128]{2,1,0:T(8,128)}, u32[]{:S(2)}, u32[]{:S(2)}) collective-permute-start(f32[4,129,128]{2,1,0:T(8,128)} %pad_maximum_fusion.5), channel_id=1, source_target_pairs={{0,64},{4,68},{8,72},{12,76},{16,80},{20,84},{24,88},{28,92},{32,9... | collective-permute-start | bytes 792584 | tf_op jit(solution)/shard_map/ppermute | solution.py:15
  116.1 5.5 %copy-start.17 = (bf16[2,512,4,128]{3,2,1,0:T(4,128)(2,1)S(1)}, bf16[2,512,4,128]{3,2,1,0:T(4,128)(2,1)}, u32[]{:S(2)}) copy-start(bf16[2,512,4,128]{3,2,1,0:T(4,128)(2,1)} %reshape_squeeze.21) | copy-start | bytes 3145732
  117.8 4.9 %copy-start.20 = (f32[4,129,128]{2,1,0:T(8,128)S(1)}, f32[4,129,128]{2,1,0:T(8,128)}, u32[]{:S(2)}) copy-start(f32[4,129,128]{2,1,0:T(8,128)} %copy-done.19) | copy-start | bytes 792580
  117.8 4.9 %copy-start.22 = (f32[4,129,128]{2,1,0:T(8,128)S(1)}, f32[4,129,128]{2,1,0:T(8,128)}, u32[]{:S(2)}) copy-start(f32[4,129,128]{2,1,0:T(8,128)} %copy-done.21) | copy-start | bytes 792580
  117.8 5.0 %copy-start.24 = (f32[4,129,128]{2,1,0:T(8,128)S(1)}, f32[4,129,128]{2,1,0:T(8,128)}, u32[]{:S(2)}) copy-start(f32[4,129,128]{2,1,0:T(8,128)} %copy-done.23) | copy-start | bytes 792580
  117.8 5.0 %copy-start.26 = (f32[4,129,128]{2,1,0:T(8,128)S(1)}, f32[4,129,128]{2,1,0:T(8,128)}, u32[]{:S(2)}) copy-start(f32[4,129,128]{2,1,0:T(8,128)} %copy-done.25) | copy-start | bytes 792580
  119.3 5.1 %copy-start.31 = (f32[1,4,1024]{2,1,0:T(4,128)S(1)}, f32[1,4,1024]{2,1,0:T(4,128)}, u32[]{:S(2)}) copy-start(f32[1,4,1024]{2,1,0:T(4,128)} %param.14) | copy-start | bytes 49156
  155.6 5.2 %copy-start.3 = (bf16[2,512,4,128]{3,1,2,0:T(8,128)(2,1)}, bf16[2,512,4,128]{3,1,2,0:T(8,128)(2,1)S(1)}, u32[]{:S(2)}) copy-start(bf16[2,512,4,128]{3,1,2,0:T(8,128)(2,1)S(1)} %get-tuple-element.1097) | copy-start | bytes 3145732 | tf_op jit(solution)/shard_map/transpose(jvp())/while
  155.6 5.2 %copy-start.5 = (f32[2,512,4,128]{3,2,1,0:T(4,128)S(1)}, f32[2,512,4,128]{3,2,1,0:T(4,128)}, u32[]{:S(2)}) copy-start(f32[2,512,4,128]{3,2,1,0:T(4,128)} %get-tuple-element.1101) | copy-start | bytes 6291460 | tf_op jit(solution)/shard_map/transpose(jvp())/while
  161.3 7.9 %copy-start.1 = (bf16[512,4,128]{2,0,1:T(8,128)(2,1)S(1)}, bf16[512,4,128]{2,0,1:T(8,128)(2,1)}, u32[]{:S(2)}) copy-start(bf16[512,4,128]{2,0,1:T(8,128)(2,1)} %dynamic-slice_bitcast_fusion.13) | copy-start | bytes 1572868 | tf_op jit(solution)/shard_map/transpose(jvp())/while
  171.7 3.2 %copy-start.34 = (bf16[4,512,512]{2,1,0:T(8,128)(2,1)}, bf16[4,512,512]{2,1,0:T(8,128)(2,1)S(1)}, u32[]{:S(2)}) copy-start(bf16[4,512,512]{2,1,0:T(8,128)(2,1)S(1)} %get-tuple-element.1004) | copy-start | bytes 6291460 | tf_op jit(solution)/shard_map/transpose(jvp())/while
  183.9 5.2 %copy-start.6 = (bf16[1,512,4,128]{3,1,2,0:T(8,128)(2,1)S(1)}, bf16[1,512,4,128]{3,1,2,0:T(8,128)(2,1)}, u32[]{:S(2)}) copy-start(bf16[1,512,4,128]{3,1,2,0:T(8,128)(2,1)} %get-tuple-element.1012) | copy-start | bytes 1572868 | tf_op jit(solution)/shard_map/transpose(jvp())/while
  183.9 5.2 %copy-start.10 = (bf16[2,512,4,128]{3,2,1,0:T(4,128)(2,1)S(1)}, bf16[2,512,4,128]{3,2,1,0:T(4,128)(2,1)}, u32[]{:S(2)}) copy-start(bf16[2,512,4,128]{3,2,1,0:T(4,128)(2,1)} %get-tuple-element.1073) | copy-start | bytes 3145732 | tf_op jit(solution)/shard_map/transpose(jvp())/while
  184.0 5.2 %copy-start.13 = (bf16[2,512,4,128]{3,2,1,0:T(4,128)(2,1)S(1)}, bf16[2,512,4,128]{3,2,1,0:T(4,128)(2,1)}, u32[]{:S(2)}) copy-start(bf16[2,512,4,128]{3,2,1,0:T(4,128)(2,1)} %get-tuple-element.1074) | copy-start | bytes 3145732 | tf_op jit(solution)/shard_map/transpose(jvp())/while
  189.2 9.1 %copy-start.4 = (bf16[2,512,4,128]{3,1,2,0:T(8,128)(2,1)S(1)}, bf16[2,512,4,128]{3,1,2,0:T(8,128)(2,1)}, u32[]{:S(2)}) copy-start(bf16[2,512,4,128]{3,1,2,0:T(8,128)(2,1)} %copy-done.3) | copy-start | bytes 3145732 | tf_op jit(solution)/shard_map/transpose(jvp())/while
  198.3 5.2 %copy-start.3 = (bf16[2,512,4,128]{3,1,2,0:T(8,128)(2,1)}, bf16[2,512,4,128]{3,1,2,0:T(8,128)(2,1)S(1)}, u32[]{:S(2)}) copy-start(bf16[2,512,4,128]{3,1,2,0:T(8,128)(2,1)S(1)} %get-tuple-element.1097) | copy-start | bytes 3145732 | tf_op jit(solution)/shard_map/transpose(jvp())/while
  198.3 5.2 %copy-start.5 = (f32[2,512,4,128]{3,2,1,0:T(4,128)S(1)}, f32[2,512,4,128]{3,2,1,0:T(4,128)}, u32[]{:S(2)}) copy-start(f32[2,512,4,128]{3,2,1,0:T(4,128)} %get-tuple-element.1101) | copy-start | bytes 6291460 | tf_op jit(solution)/shard_map/transpose(jvp())/while
  203.9 7.9 %copy-start.1 = (bf16[512,4,128]{2,0,1:T(8,128)(2,1)S(1)}, bf16[512,4,128]{2,0,1:T(8,128)(2,1)}, u32[]{:S(2)}) copy-start(bf16[512,4,128]{2,0,1:T(8,128)(2,1)} %dynamic-slice_bitcast_fusion.13) | copy-start | bytes 1572868 | tf_op jit(solution)/shard_map/transpose(jvp())/while
  214.4 3.2 %copy-start.34 = (bf16[4,512,512]{2,1,0:T(8,128)(2,1)}, bf16[4,512,512]{2,1,0:T(8,128)(2,1)S(1)}, u32[]{:S(2)}) copy-start(bf16[4,512,512]{2,1,0:T(8,128)(2,1)S(1)} %get-tuple-element.1004) | copy-start | bytes 6291460 | tf_op jit(solution)/shard_map/transpose(jvp())/while
  226.6 5.2 %copy-start.6 = (bf16[1,512,4,128]{3,1,2,0:T(8,128)(2,1)S(1)}, bf16[1,512,4,128]{3,1,2,0:T(8,128)(2,1)}, u32[]{:S(2)}) copy-start(bf16[1,512,4,128]{3,1,2,0:T(8,128)(2,1)} %get-tuple-element.1012) | copy-start | bytes 1572868 | tf_op jit(solution)/shard_map/transpose(jvp())/while
  226.6 5.2 %copy-start.10 = (bf16[2,512,4,128]{3,2,1,0:T(4,128)(2,1)S(1)}, bf16[2,512,4,128]{3,2,1,0:T(4,128)(2,1)}, u32[]{:S(2)}) copy-start(bf16[2,512,4,128]{3,2,1,0:T(4,128)(2,1)} %get-tuple-element.1073) | copy-start | bytes 3145732 | tf_op jit(solution)/shard_map/transpose(jvp())/while
  226.6 5.2 %copy-start.13 = (bf16[2,512,4,128]{3,2,1,0:T(4,128)(2,1)S(1)}, bf16[2,512,4,128]{3,2,1,0:T(4,128)(2,1)}, u32[]{:S(2)}) copy-start(bf16[2,512,4,128]{3,2,1,0:T(4,128)(2,1)} %get-tuple-element.1074) | copy-start | bytes 3145732 | tf_op jit(solution)/shard_map/transpose(jvp())/while
  231.8 9.1 %copy-start.4 = (bf16[2,512,4,128]{3,1,2,0:T(8,128)(2,1)S(1)}, bf16[2,512,4,128]{3,1,2,0:T(8,128)(2,1)}, u32[]{:S(2)}) copy-start(bf16[2,512,4,128]{3,1,2,0:T(8,128)(2,1)} %copy-done.3) | copy-start | bytes 3145732 | tf_op jit(solution)/shard_map/transpose(jvp())/while
  241.0 7.9 %copy-start.33 = (f32[2,4,512]{2,1,0:T(4,128)}, f32[2,4,512]{2,1,0:T(4,128)S(1)}, u32[]{:S(2)}) copy-start(f32[2,4,512]{2,1,0:T(4,128)S(1)} %get-tuple-element.443) | copy-start | bytes 49156
  241.0 5.5 %copy-start.12 = (bf16[2,512,4,128]{3,2,1,0:T(4,128)(2,1)S(1)}, bf16[2,512,4,128]{3,2,1,0:T(4,128)(2,1)}, u32[]{:S(2)}) copy-start(bf16[2,512,4,128]{3,2,1,0:T(4,128)(2,1)} %get-tuple-element.440) | copy-start | bytes 3145732
  241.0 6.7 %copy-start.15 = (bf16[2,512,4,128]{3,2,1,0:T(4,128)(2,1)S(1)}, bf16[2,512,4,128]{3,2,1,0:T(4,128)(2,1)}, u32[]{:S(2)}) copy-start(bf16[2,512,4,128]{3,2,1,0:T(4,128)(2,1)} %get-tuple-element.441) | copy-start | bytes 3145732
  241.8 7.1 %copy-start.16 = (bf16[2,512,4,128]{3,2,1,0:T(4,128)(2,1)S(1)}, bf16[2,512,4,128]{3,2,1,0:T(4,128)(2,1)}, u32[]{:S(2)}) copy-start(bf16[2,512,4,128]{3,2,1,0:T(4,128)(2,1)} %get-tuple-element.442) | copy-start | bytes 3145732
  (10 other events, 17.7 us)
Sparse Core Ops, SparseCore 0:
  241.9 12.2 reduce-scatter.3

commit v3 on v2

--- a/solution.py
+++ b/solution.py
@@ -2,6 +2,8 @@
 import jax.numpy as jnp
 from jax import lax
 from jax.sharding import PartitionSpec as P
+from jax.experimental import pallas as pl
+from jax.experimental.pallas import tpu as pltpu
 
 BLOCK = 512
 
@@ -60,6 +62,67 @@
     return scans[0][3], scans[1][3]
 
 
+def gain_sum_kernel(part_ref, total_ref, slots, send_sem, recv_sem):
+    count = slots.shape[0]
+    me = lax.axis_index("ctx")
+    row, col = lax.axis_index("dp"), lax.axis_index("head")
+
+    def peer_of(step):
+        return lax.rem(me + step, count)
+
+    barrier = pltpu.get_barrier_semaphore()
+    for step in range(1, count):
+        pl.semaphore_signal(
+            barrier, inc=1, device_id=(row, peer_of(step), col), device_id_type=pl.DeviceIdType.MESH
+        )
+    pl.semaphore_wait(barrier, count - 1)
+
+    copies = []
+    for step in range(1, count):
+        peer = peer_of(step)
+        copy = pltpu.make_async_remote_copy(
+            src_ref=part_ref,
+            dst_ref=slots.at[me],
+            send_sem=send_sem.at[peer],
+            recv_sem=recv_sem.at[me],
+            device_id=(row, peer, col),
+            device_id_type=pl.DeviceIdType.MESH,
+        )
+        copy.start()
+        copies.append(copy)
+    slots[me] = part_ref[...]
+    for step in range(1, count):
+        copies[step - 1].wait_send()
+        source = lax.rem(me + count - step, count)
+        pltpu.make_async_remote_copy(
+            src_ref=part_ref,
+            dst_ref=slots.at[source],
+            send_sem=send_sem.at[source],
+            recv_sem=recv_sem.at[source],
+            device_id=(row, source, col),
+            device_id_type=pl.DeviceIdType.MESH,
+        ).wait_recv()
+    total = slots[0]
+    for index in range(1, count):
+        total = total + slots[index]
+    total_ref[...] = total
+
+
+def gain_sum(part, count):
+    return pl.pallas_call(
+        gain_sum_kernel,
+        out_shape=jax.ShapeDtypeStruct(part.shape, part.dtype),
+        in_specs=[pl.BlockSpec(memory_space=pltpu.VMEM)],
+        out_specs=pl.BlockSpec(memory_space=pltpu.VMEM),
+        scratch_shapes=[
+            pltpu.VMEM((count,) + part.shape, part.dtype),
+            pltpu.SemaphoreType.DMA((count,)),
+            pltpu.SemaphoreType.DMA((count,)),
+        ],
+        compiler_params=pltpu.CompilerParams(collective_id=0, has_side_effects=True),
+    )(part)
+
+
 def start_flags(doc_lengths, first_pos, num_rows):
     starts = jnp.cumsum(doc_lengths, dtype=jnp.int32) - doc_lengths
     positions = first_pos + jnp.arange(num_rows, dtype=jnp.int32)
@@ -153,7 +216,7 @@
     cot_float = cotangent[0].astype(jnp.float32)
     grad_q, grad_k, grad_v, grad_a, gain_term = pullback((cot_float, later_grad))
     gain_half = lax.psum_scatter(gain_term, "dp", scatter_dimension=1, tiled=True)
-    grad_gain = jnp.sum(lax.all_gather(gain_half, "ctx"), axis=0)
+    grad_gain = gain_sum(gain_half, ctx_size)
     return (
         primal.astype(jnp.bfloat16)[None],
         grad_q[None],

time: 314 us -> 279 us (0.89)
  blocking collectives: 49.7 us -> 0 us
  Pallas kernels: 0 us -> 13.6 us
    all_gather x1 -> x0, blocking collectives: 49.7 us -> none  [shards(): grad_gain = jnp.sum(lax.all_gather(gain_half, 'ctx'), axis=0)]
    pallas_call x0 -> x1, Pallas kernels: none -> 13.6 us  [gain_sum(): pl.pallas_call(gain_sum_kernel, out_shape=jax.ShapeDtypeStruct(part.shape...]
    unnamed x54 -> x55, local copies, waits for them, and re-layouts: 7.38 us -> 9.22 us
  transfers between devices with their start and end apart: 11 -> 11, of which waited for: 7 -> 7; matrix products, arithmetic and copies ran while one was open for 7% -> 8% of each run, Pallas kernels for 0% -> 0%
where the time goes in v3:
time: 279 us; the launch traced here: 277 us
  matrix products  66.1 us (24%)
  local copies, waits for them, and re-layouts  63.1 us (23%)
  starting transfers between devices  49.5 us (18%)
  other arithmetic  39.9 us (14%)
  waiting for transfers between devices  30 us (11%)
  between operations  14.5 us (5%)
  Pallas kernels  13.6 us (5%)
    ppermute x10, starting transfers between devices, passed_along(): lax.ppermute(value, axis, [(source, source + steps) for source in range(f...  49.4 us
    ppermute x10, waiting for transfers between devices, passed_along(): lax.ppermute(value, axis, [(source, source + steps) for source in range(f...  25.9 us
    another operation x27, other arithmetic  20.1 us
    dot_general x6, matrix products, block_step(): jnp.einsum('hts,she->the', weights, v_block, preferred_element_type=jnp.f...  19.2 us
    dot_general x8, matrix products, block_step(): jnp.einsum('thd,hde->the', q_float, carried, precision=PRECISE)  15.6 us
    dot_general x6, matrix products, block_step(): jnp.einsum('thd,shd->hts', q_block, k_bf, preferred_element_type=jnp.floa...  14.5 us
    pallas_call x1, Pallas kernels, gain_sum(): pl.pallas_call(gain_sum_kernel, out_shape=jax.ShapeDtypeStruct(part.shape...  13.6 us
    dot_general x6, matrix products, block_step(): jnp.einsum('shd,she->hde', k_float * to_end.T[:, :, None], v_float, preci...  11.3 us
  transfers between devices with their start and end apart: 11, of which 7 were waited for; matrix products, arithmetic and copies ran while one was open for 8% of the time, Pallas kernels for 0%

profile of v3, /device:TPU:2, one launch (start us, length us, event | category | flops | bytes accessed | tf_op | source)
XLA Modules:
  0.0 277.3 jit_solution(13440324715931615434)
XLA Ops:
  14.0 2.1 reshape.632
  19.1 2.7 multiply_convert_fusion.6
  21.8 2.1 reshape_squeeze.17
  24.7 2.5 fusion.107
  27.2 2.9 %fusion.109 = f32[4,128,128]{2,1,0:T(8,128)S(1)} fusion(bf16[1024,4,128]{0,2,1:T(8,128)(2,1)} %multiply_convert_fusion.6, bf16[1024,4,128]{2,1,0:T(4,128)(2,1)} %reshape_squeeze.17, f32[1024,4]{0,1:T(4,128)S(1)} %get-tuple-element.795), kind=kOutput, calls=%fused_computation.161 | convolution fusion | flops 806354944 | bytes 2375680 | tf_op jit(solution)/shard_map/shd,she->hde/dot_general | solution.py:205
  31.5 4.6 %collective-permute-start = (f32[4,129,128]{2,1,0:T(8,128)S(1)}, f32[4,129,128]{2,1,0:T(8,128)S(1)}, u32[]{:S(2)}, u32[]{:S(2)}) collective-permute-start(f32[4,129,128]{2,1,0:T(8,128)S(1)} %get-tuple-element.803), channel_id=1, source_target_pairs={{0,4},{4,8},{8,12},{12,16},{16,20},{20,24},{24,28},{28,32},{32,36}... | collective-permute-start | bytes 792584 | tf_op jit(solution)/shard_map/ppermute | solution.py:17
  36.9 3.7 %collective-permute-done.5 = f32[4,129,128]{2,1,0:T(8,128)S(1)} collective-permute-done((f32[4,129,128]{2,1,0:T(8,128)S(1)}, f32[4,129,128]{2,1,0:T(8,128)S(1)}, u32[]{:S(2)}, u32[]{:S(2)}) %collective-permute-start.5) | collective-permute-done | bytes 264224 | tf_op jit(solution)/shard_map/ppermute | solution.py:17
  43.1 6.0 %collective-permute-start.1 = (f32[4,129,128]{2,1,0:T(8,128)S(1)}, f32[4,129,128]{2,1,0:T(8,128)S(1)}, u32[]{:S(2)}, u32[]{:S(2)}) collective-permute-start(f32[4,129,128]{2,1,0:T(8,128)S(1)} %pad_maximum_fusion.2), channel_id=1, source_target_pairs={{0,8},{4,12},{8,16},{12,20},{16,24},{20,28},{24,32},{28,36},{32,40... | collective-permute-start | bytes 792584 | tf_op jit(solution)/shard_map/ppermute | solution.py:17
  50.5 3.3 %collective-permute-done.1 = f32[4,129,128]{2,1,0:T(8,128)S(1)} collective-permute-done((f32[4,129,128]{2,1,0:T(8,128)S(1)}, f32[4,129,128]{2,1,0:T(8,128)S(1)}, u32[]{:S(2)}, u32[]{:S(2)}) %collective-permute-start.1) | collective-permute-done | bytes 264224 | tf_op jit(solution)/shard_map/ppermute | solution.py:17
  53.8 8.4 %collective-permute-done.6 = f32[4,129,128]{2,1,0:T(8,128)S(1)} collective-permute-done((f32[4,129,128]{2,1,0:T(8,128)S(1)}, f32[4,129,128]{2,1,0:T(8,128)S(1)}, u32[]{:S(2)}, u32[]{:S(2)}) %collective-permute-start.6) | collective-permute-done | bytes 264224 | tf_op jit(solution)/shard_map/ppermute | solution.py:17
  64.7 8.0 %collective-permute-start.2 = (f32[4,129,128]{2,1,0:T(8,128)S(1)}, f32[4,129,128]{2,1,0:T(8,128)S(1)}, u32[]{:S(2)}, u32[]{:S(2)}) collective-permute-start(f32[4,129,128]{2,1,0:T(8,128)S(1)} %pad_maximum_fusion.3), channel_id=1, source_target_pairs={{0,16},{4,20},{8,24},{12,28},{16,32},{20,36},{24,40},{28,44},{32,4... | collective-permute-start | bytes 792584 | tf_op jit(solution)/shard_map/ppermute | solution.py:17
  72.7 4.7 %collective-permute-done.7 = f32[4,129,128]{2,1,0:T(8,128)S(1)} collective-permute-done((f32[4,129,128]{2,1,0:T(8,128)S(1)}, f32[4,129,128]{2,1,0:T(8,128)S(1)}, u32[]{:S(2)}, u32[]{:S(2)}) %collective-permute-start.7) | collective-permute-done | bytes 264224 | tf_op jit(solution)/shard_map/ppermute | solution.py:17
  79.4 5.6 %collective-permute-start.3 = (f32[4,129,128]{2,1,0:T(8,128)S(1)}, f32[4,129,128]{2,1,0:T(8,128)S(1)}, u32[]{:S(2)}, u32[]{:S(2)}) collective-permute-start(f32[4,129,128]{2,1,0:T(8,128)S(1)} %pad_maximum_fusion.4), channel_id=1, source_target_pairs={{0,32},{4,36},{8,40},{12,44},{16,48},{20,52},{24,56},{28,60},{32,6... | collective-permute-start | bytes 792584 | tf_op jit(solution)/shard_map/ppermute | solution.py:17
  85.1 4.7 %collective-permute-done.8 = f32[4,129,128]{2,1,0:T(8,128)S(1)} collective-permute-done((f32[4,129,128]{2,1,0:T(8,128)S(1)}, f32[4,129,128]{2,1,0:T(8,128)S(1)}, u32[]{:S(2)}, u32[]{:S(2)}) %collective-permute-start.8) | collective-permute-done | bytes 264224 | tf_op jit(solution)/shard_map/ppermute | solution.py:17
  93.2 18.7 %collective-permute-start.4 = (f32[4,129,128]{2,1,0:T(8,128)}, f32[4,129,128]{2,1,0:T(8,128)}, u32[]{:S(2)}, u32[]{:S(2)}) collective-permute-start(f32[4,129,128]{2,1,0:T(8,128)} %pad_maximum_fusion.5), channel_id=1, source_target_pairs={{0,64},{4,68},{8,72},{12,76},{16,80},{20,84},{24,88},{28,92},{32,9... | collective-permute-start | bytes 792584 | tf_op jit(solution)/shard_map/ppermute | solution.py:17
  112.9 2.1 reshape_squeeze.20
  116.2 1.7 reshape.642
  119.3 2.3 copy.237
  124.5 27.3 %while.42 = (s32[]{:T(128)}, f32[4,128,128]{2,1,0:T(8,128)S(1)}, bf16[2,512,4,128]{1,3,2,0:T(8,128)(2,1)}, f32[2,4,128,128]{3,2,1,0:T(8,128)}, f32[2,4,512]{2,1,...) while((s32[]{:T(128)}, f32[4,128,128]{2,1,0:T(8,128)S(1)}, ...), condition=%wide.region_11.12_spmd.clone, body=%wide.region_6.11_spmd.clone.sunk | while | flops 1352081408 | bytes 9343697 | solution.py:180
  127.8 3.3 %fusion.203 = f32[512,4,128]{0,2,1:T(8,128)S(1)} fusion(bf16[512,4,128]{2,0,1:T(8,128)(2,1)S(1)} %fusion.201, f32[4,512]{1,0:T(4,128)S(1)} %bitcast.357, pred[512,512]{1,0:T(8,128)(4,1)S(1)} %fusion.202, bf16[2,512,4,128]{3,1,2,0:T(8,128)(2,1)} %get-tuple-element.1049, s32[]{:T(128)S(6)} %copy.340, bf16[2,512,4,128]{3,1,2,0:T(8,128)(2,1)} %get-tuple-element.1048), kind=kOutput, calls=%fused_computation.3.clone.1 | convolution fusion | flops 543162368 | bytes 2900992 | tf_op jit(solution)/shard_map/jvp()/while/body/eval_jaxpr/hts,she->the/dot_general | solution.py:152
  132.6 3.0 %fusion.204 = bf16[2,512,4,128]{1,3,2,0:T(8,128)(2,1)} fusion(bf16[2,512,4,128]{1,3,2,0:T(8,128)(2,1)} %get-tuple-element.1030, s32[]{:T(128)S(6)} %copy.340, f32[512,4,128]{0,2,1:T(8,128)S(1)} %fusion.203, f32[4,128,128]{2,1,0:T(8,128)S(1)} %get-tuple-element.1029, f32[512,4]{0,1:T(4,128)S(1)} %bitcast.349, ...), kind=kOutput, calls=%fused_computation.8.clone.1 | convolution fusion | flops 403701760 | bytes 2892800 | tf_op jit(solution)/shard_map/jvp()/while/body/eval_jaxpr/thd,hde->the/dot_general | solution.py:156
  135.8 2.4 convolution_add_fusion.4
  141.5 3.3 %fusion.203 = f32[512,4,128]{0,2,1:T(8,128)S(1)} fusion(bf16[512,4,128]{2,0,1:T(8,128)(2,1)S(1)} %fusion.201, f32[4,512]{1,0:T(4,128)S(1)} %bitcast.357, pred[512,512]{1,0:T(8,128)(4,1)S(1)} %fusion.202, bf16[2,512,4,128]{3,1,2,0:T(8,128)(2,1)} %get-tuple-element.1049, s32[]{:T(128)S(6)} %copy.340, bf16[2,512,4,128]{3,1,2,0:T(8,128)(2,1)} %get-tuple-element.1048), kind=kOutput, calls=%fused_computation.3.clone.1 | convolution fusion | flops 543162368 | bytes 2900992 | tf_op jit(solution)/shard_map/jvp()/while/body/eval_jaxpr/hts,she->the/dot_general | solution.py:152
  146.3 3.0 %fusion.204 = bf16[2,512,4,128]{1,3,2,0:T(8,128)(2,1)} fusion(bf16[2,512,4,128]{1,3,2,0:T(8,128)(2,1)} %get-tuple-element.1030, s32[]{:T(128)S(6)} %copy.340, f32[512,4,128]{0,2,1:T(8,128)S(1)} %fusion.203, f32[4,128,128]{2,1,0:T(8,128)S(1)} %get-tuple-element.1029, f32[512,4]{0,1:T(4,128)S(1)} %bitcast.349, ...), kind=kOutput, calls=%fused_computation.8.clone.1 | convolution fusion | flops 403701760 | bytes 2892800 | tf_op jit(solution)/shard_map/jvp()/while/body/eval_jaxpr/thd,hde->the/dot_general | solution.py:156
  149.4 2.4 convolution_add_fusion.4
  155.6 85.3 %while.43 = (s32[]{:T(128)}, f32[4,128]{1,0:T(4,128)S(1)}, f32[4,128,128]{2,1,0:T(8,128)S(1)}, bf16[2,512,4,128]{3,2,1,0:T(4,128)(2,1)}, bf16[2,512,4,128]{3,2,1...) while((s32[]{:T(128)}, f32[4,128]{1,0:T(4,128)S(1)}, ...), condition=%wide.region_26.27_spmd.clone, body=%wide.region_12.26_spmd.clone.sunk | while | flops 3394863616 | bytes 116524784 | solution.py:180
  158.9 1.9 dynamic-slice_bitcast_fusion.13
  166.3 1.9 fusion.222
  169.2 2.5 fusion.225
  171.7 3.2 %fusion.226 = (bf16[1,512,4,128]{3,1,2,0:T(8,128)(2,1)}, f32[4,128]{1,0:T(4,128)S(1)}) fusion(f32[4,128]{1,0:T(4,128)S(1)} %get-tuple-element.994, bf16[512,4,128]{2,0,1:T(8,128)(2,1)S(1)} %copy-done.2, bf16[512,4,128]{2,0,1:T(8,128)(2,1)S(1)} %get-tuple-element.1001, bf16[512,4,128]{2,0,1:T(8,128)(2,1)S(1)} %dynamic-slice_bitcast_fusion.11, ...), kind=kOutput, calls=%fused_computation.110.clone.1 | convolution fusion | flops 276823552 | bytes 4468736 | tf_op jit(solution)/shard_map/transpose(jvp())/while/body/eval_jaxpr/checkpoint/thd,shd->hts/dot_general | solution.py:150
  175.0 3.8 %fusion.232 = bf16[4,128,512]{2,1,0:T(8,128)(2,1)S(1)} fusion(f32[4,512,512]{2,1,0:T(8,128)} %copy-done, f32[4,512]{1,0:T(4,128)S(1)} %bitcast.355, pred[512,512]{1,0:T(8,128)(4,1)S(1)} %fusion.224, f32[512,4,128]{0,2,1:T(8,128)S(1)} %bitcast.341), kind=kOutput, calls=%fused_computation.81.clone.1 | convolution fusion | flops 274726912 | bytes 6037504 | tf_op jit(solution)/shard_map/transpose(jvp())/while/body/eval_jaxpr/checkpoint/hts,she->the/dot_general | solution.py:152
  182.0 1.9 convolution_add_fusion.5
  184.0 3.3 %fusion.230 = bf16[4,512,128]{2,1,0:T(8,128)(2,1)S(1)} fusion(bf16[512,4,128]{2,0,1:T(8,128)(2,1)S(1)} %fusion.221, bf16[4,512,512]{2,1,0:T(8,128)(2,1)} %copy-done.34, f32[4,512]{1,0:T(4,128)S(1)} %bitcast.356, pred[512,512]{1,0:T(8,128)(4,1)S(1)} %fusion.224), kind=kOutput, calls=%fused_computation.85.clone.1 | convolution fusion | flops 274989056 | bytes 3416064 | tf_op jit(solution)/shard_map/transpose(jvp())/while/body/eval_jaxpr/checkpoint/thd,shd->hts/dot_general | solution.py:150
  187.3 1.8 fusion.231
  192.8 5.0 %reduce-window.150 = f32[4,4,128]{2,1,0:T(4,128)S(1)} reduce-window(f32[4,4,128]{2,1,0:T(4,128)S(1)} %reshape.693, f32[]{:T(128)} %constant.142.clone.1..sunk.1), window={size=1x1x128 pad=0_0x0_0x0_127}, to_apply=%region_24.24 | reduce-window | flops 260096 | bytes 16388 | tf_op jit(solution)/shard_map/reduce-window.60
  201.6 1.9 dynamic-slice_bitcast_fusion.13
  208.9 1.9 fusion.222
  211.8 2.5 fusion.225
  214.4 3.2 %fusion.226 = (bf16[1,512,4,128]{3,1,2,0:T(8,128)(2,1)}, f32[4,128]{1,0:T(4,128)S(1)}) fusion(f32[4,128]{1,0:T(4,128)S(1)} %get-tuple-element.994, bf16[512,4,128]{2,0,1:T(8,128)(2,1)S(1)} %copy-done.2, bf16[512,4,128]{2,0,1:T(8,128)(2,1)S(1)} %get-tuple-element.1001, bf16[512,4,128]{2,0,1:T(8,128)(2,1)S(1)} %dynamic-slice_bitcast_fusion.11, ...), kind=kOutput, calls=%fused_computation.110.clone.1 | convolution fusion | flops 276823552 | bytes 4468736 | tf_op jit(solution)/shard_map/transpose(jvp())/while/body/eval_jaxpr/checkpoint/thd,shd->hts/dot_general | solution.py:150
  217.6 3.8 %fusion.232 = bf16[4,128,512]{2,1,0:T(8,128)(2,1)S(1)} fusion(f32[4,512,512]{2,1,0:T(8,128)} %copy-done, f32[4,512]{1,0:T(4,128)S(1)} %bitcast.355, pred[512,512]{1,0:T(8,128)(4,1)S(1)} %fusion.224, f32[512,4,128]{0,2,1:T(8,128)S(1)} %bitcast.341), kind=kOutput, calls=%fused_computation.81.clone.1 | convolution fusion | flops 274726912 | bytes 6037504 | tf_op jit(solution)/shard_map/transpose(jvp())/while/body/eval_jaxpr/checkpoint/hts,she->the/dot_general | solution.py:152
  224.7 1.9 convolution_add_fusion.5
  226.6 3.3 %fusion.230 = bf16[4,512,128]{2,1,0:T(8,128)(2,1)S(1)} fusion(bf16[512,4,128]{2,0,1:T(8,128)(2,1)S(1)} %fusion.221, bf16[4,512,512]{2,1,0:T(8,128)(2,1)} %copy-done.34, f32[4,512]{1,0:T(4,128)S(1)} %bitcast.356, pred[512,512]{1,0:T(8,128)(4,1)S(1)} %fusion.224), kind=kOutput, calls=%fused_computation.85.clone.1 | convolution fusion | flops 274989056 | bytes 3416064 | tf_op jit(solution)/shard_map/transpose(jvp())/while/body/eval_jaxpr/checkpoint/thd,shd->hts/dot_general | solution.py:150
  230.0 1.8 fusion.231
  235.5 5.0 %reduce-window.150 = f32[4,4,128]{2,1,0:T(4,128)S(1)} reduce-window(f32[4,4,128]{2,1,0:T(4,128)S(1)} %reshape.693, f32[]{:T(128)} %constant.142.clone.1..sunk.1), window={size=1x1x128 pad=0_0x0_0x0_127}, to_apply=%region_24.24 | reduce-window | flops 260096 | bytes 16388 | tf_op jit(solution)/shard_map/reduce-window.60
  241.8 2.5 copy.239
  244.3 2.2 convert_element_type.302
  250.1 4.1 %reduce-scatter.4.cloned.1.call-done = f32[64,4]{1,0:T(8,128)} async-done(((f32[128,4]{1,0:T(8,128)}), f32[64,4]{1,0:T(8,128)}) %reduce-scatter.4.cloned.1.call-update) | async-done | bytes 1040
  255.6 13.6 %shard_map.118 = f32[4,64]{1,0:T(4,128)} custom-call(f32[4,64]{1,0:T(4,128)} %copy.265.part_ref), custom_call_target="tpu_custom_call" | custom-call | tf_op jit(solution)/shard_map/pallas_call | solution.py:112
  (316 shorter events, 85.5 us)
Async XLA Ops:
  7.2 10.2 %copy-start.7 = (bf16[1,1024,512]{2,1,0:T(8,128)(2,1)S(1)}, bf16[1,1024,512]{2,1,0:T(8,128)(2,1)}, u32[]{:S(2)}) copy-start(bf16[1,1024,512]{2,1,0:T(8,128)(2,1)} %param.12) | copy-start | bytes 3145732
  7.2 247.0 %reduce-scatter.4.cloned.1.call-start = ((), (), s32[]{:S(2)}) async-start(), calls=%async_computation.1 | async-start | bytes 98304
  12.5 6.5 %copy-start.32 = (f32[4,128]{1,0:T(4,128)S(1)}, f32[4,128]{1,0:T(4,128)}, u32[]{:S(2)}) copy-start(f32[4,128]{1,0:T(4,128)} %param.16) | copy-start | bytes 6148
  27.2 13.4 %copy-start.18 = (f32[4,128,128]{2,1,0:T(8,128)}, f32[4,128,128]{2,1,0:T(8,128)S(1)}, u32[]{:S(2)}) copy-start(f32[4,128,128]{2,1,0:T(8,128)S(1)} %fusion.107) | copy-start | bytes 786436
  30.2 10.3 %collective-permute-start.5 = (f32[4,129,128]{2,1,0:T(8,128)S(1)}, f32[4,129,128]{2,1,0:T(8,128)S(1)}, u32[]{:S(2)}, u32[]{:S(2)}) collective-permute-start(f32[4,129,128]{2,1,0:T(8,128)S(1)} %get-tuple-element.802), channel_id=1, source_target_pairs={{4,0},{8,4},{12,8},{16,12},{20,16},{24,20},{28,24},{32,28},{36,32}... | collective-permute-start | bytes 792584 | tf_op jit(solution)/shard_map/ppermute | solution.py:17
  31.5 10.2 %collective-permute-start = (f32[4,129,128]{2,1,0:T(8,128)S(1)}, f32[4,129,128]{2,1,0:T(8,128)S(1)}, u32[]{:S(2)}, u32[]{:S(2)}) collective-permute-start(f32[4,129,128]{2,1,0:T(8,128)S(1)} %get-tuple-element.803), channel_id=1, source_target_pairs={{0,4},{4,8},{8,12},{12,16},{16,20},{20,24},{24,28},{28,32},{32,36}... | collective-permute-start | bytes 792584 | tf_op jit(solution)/shard_map/ppermute | solution.py:17
  40.5 37.1 %copy-start.19 = (f32[4,129,128]{2,1,0:T(8,128)}, f32[4,129,128]{2,1,0:T(8,128)S(1)}, u32[]{:S(2)}) copy-start(f32[4,129,128]{2,1,0:T(8,128)S(1)} %collective-permute-done.5) | copy-start | bytes 792580
  41.7 35.9 %copy-start.21 = (f32[4,129,128]{2,1,0:T(8,128)}, f32[4,129,128]{2,1,0:T(8,128)S(1)}, u32[]{:S(2)}) copy-start(f32[4,129,128]{2,1,0:T(8,128)S(1)} %collective-permute-done) | copy-start | bytes 792580
  43.1 10.7 %collective-permute-start.1 = (f32[4,129,128]{2,1,0:T(8,128)S(1)}, f32[4,129,128]{2,1,0:T(8,128)S(1)}, u32[]{:S(2)}, u32[]{:S(2)}) collective-permute-start(f32[4,129,128]{2,1,0:T(8,128)S(1)} %pad_maximum_fusion.2), channel_id=1, source_target_pairs={{0,8},{4,12},{8,16},{12,20},{16,24},{20,28},{24,32},{28,36},{32,40... | collective-permute-start | bytes 792584 | tf_op jit(solution)/shard_map/ppermute | solution.py:17
  49.2 13.0 %collective-permute-start.6 = (f32[4,129,128]{2,1,0:T(8,128)S(1)}, f32[4,129,128]{2,1,0:T(8,128)S(1)}, u32[]{:S(2)}, u32[]{:S(2)}) collective-permute-start(f32[4,129,128]{2,1,0:T(8,128)S(1)} %pad_maximum_fusion.6), channel_id=1, source_target_pairs={{8,0},{12,4},{16,8},{20,12},{24,16},{28,20},{32,24},{36,28},{40,32... | collective-permute-start | bytes 792584 | tf_op jit(solution)/shard_map/ppermute | solution.py:17
  53.8 10.8 %copy-start.27 = (f32[4,129,128]{2,1,0:T(8,128)}, f32[4,129,128]{2,1,0:T(8,128)S(1)}, u32[]{:S(2)}) copy-start(f32[4,129,128]{2,1,0:T(8,128)S(1)} %collective-permute-done.1) | copy-start | bytes 792580
  63.2 14.1 %collective-permute-start.7 = (f32[4,129,128]{2,1,0:T(8,128)S(1)}, f32[4,129,128]{2,1,0:T(8,128)S(1)}, u32[]{:S(2)}, u32[]{:S(2)}) collective-permute-start(f32[4,129,128]{2,1,0:T(8,128)S(1)} %pad_maximum_fusion.7), channel_id=1, source_target_pairs={{16,0},{20,4},{24,8},{28,12},{32,16},{36,20},{40,24},{44,28},{48,3... | collective-permute-start | bytes 792584 | tf_op jit(solution)/shard_map/ppermute | solution.py:17
  64.7 14.4 %collective-permute-start.2 = (f32[4,129,128]{2,1,0:T(8,128)S(1)}, f32[4,129,128]{2,1,0:T(8,128)S(1)}, u32[]{:S(2)}, u32[]{:S(2)}) collective-permute-start(f32[4,129,128]{2,1,0:T(8,128)S(1)} %pad_maximum_fusion.3), channel_id=1, source_target_pairs={{0,16},{4,20},{8,24},{12,28},{16,32},{20,36},{24,40},{28,44},{32,4... | collective-permute-start | bytes 792584 | tf_op jit(solution)/shard_map/ppermute | solution.py:17
  77.3 15.8 %copy-start.23 = (f32[4,129,128]{2,1,0:T(8,128)}, f32[4,129,128]{2,1,0:T(8,128)S(1)}, u32[]{:S(2)}) copy-start(f32[4,129,128]{2,1,0:T(8,128)S(1)} %collective-permute-done.7) | copy-start | bytes 792580
  77.7 37.4 %copy-start.8 = (bf16[1,1024,512]{2,1,0:T(8,128)(2,1)S(1)}, bf16[1,1024,512]{2,1,0:T(8,128)(2,1)}, u32[]{:S(2)}) copy-start(bf16[1,1024,512]{2,1,0:T(8,128)(2,1)} %param.11) | copy-start | bytes 3145732
  77.7 12.1 %collective-permute-start.8 = (f32[4,129,128]{2,1,0:T(8,128)S(1)}, f32[4,129,128]{2,1,0:T(8,128)S(1)}, u32[]{:S(2)}, u32[]{:S(2)}) collective-permute-start(f32[4,129,128]{2,1,0:T(8,128)S(1)} %pad_maximum_fusion.8), channel_id=1, source_target_pairs={{32,0},{36,4},{40,8},{44,12},{48,16},{52,20},{56,24},{60,28},{64,3... | collective-permute-start | bytes 792584 | tf_op jit(solution)/shard_map/ppermute | solution.py:17
  79.1 14.0 %copy-start.25 = (f32[4,129,128]{2,1,0:T(8,128)}, f32[4,129,128]{2,1,0:T(8,128)S(1)}, u32[]{:S(2)}) copy-start(f32[4,129,128]{2,1,0:T(8,128)S(1)} %collective-permute-done.2) | copy-start | bytes 792580
  79.4 12.6 %collective-permute-start.3 = (f32[4,129,128]{2,1,0:T(8,128)S(1)}, f32[4,129,128]{2,1,0:T(8,128)S(1)}, u32[]{:S(2)}, u32[]{:S(2)}) collective-permute-start(f32[4,129,128]{2,1,0:T(8,128)S(1)} %pad_maximum_fusion.4), channel_id=1, source_target_pairs={{0,32},{4,36},{8,40},{12,44},{16,48},{20,52},{24,56},{28,60},{32,6... | collective-permute-start | bytes 792584 | tf_op jit(solution)/shard_map/ppermute | solution.py:17
  89.7 3.4 %copy-start.29 = (f32[4,129,128]{2,1,0:T(8,128)}, f32[4,129,128]{2,1,0:T(8,128)S(1)}, u32[]{:S(2)}) copy-start(f32[4,129,128]{2,1,0:T(8,128)S(1)} %collective-permute-done.8) | copy-start | bytes 792580
  90.0 26.2 %copy-start.9 = (bf16[1,1024,512]{2,1,0:T(8,128)(2,1)S(1)}, bf16[1,1024,512]{2,1,0:T(8,128)(2,1)}, u32[]{:S(2)}) copy-start(bf16[1,1024,512]{2,1,0:T(8,128)(2,1)} %param.17) | copy-start | bytes 3145732
  90.8 32.0 %collective-permute-start.9 = (f32[4,129,128]{2,1,0:T(8,128)}, f32[4,129,128]{2,1,0:T(8,128)}, u32[]{:S(2)}, u32[]{:S(2)}) collective-permute-start(f32[4,129,128]{2,1,0:T(8,128)} %pad_maximum_fusion.9), channel_id=1, source_target_pairs={{64,0},{68,4},{72,8},{76,12},{80,16},{84,20},{88,24},{92,28},{96,3... | collective-permute-start | bytes 792584 | tf_op jit(solution)/shard_map/ppermute | solution.py:17
  93.2 29.6 %collective-permute-start.4 = (f32[4,129,128]{2,1,0:T(8,128)}, f32[4,129,128]{2,1,0:T(8,128)}, u32[]{:S(2)}, u32[]{:S(2)}) collective-permute-start(f32[4,129,128]{2,1,0:T(8,128)} %pad_maximum_fusion.5), channel_id=1, source_target_pairs={{0,64},{4,68},{8,72},{12,76},{16,80},{20,84},{24,88},{28,92},{32,9... | collective-permute-start | bytes 792584 | tf_op jit(solution)/shard_map/ppermute | solution.py:17
  116.1 5.5 %copy-start.17 = (bf16[2,512,4,128]{3,2,1,0:T(4,128)(2,1)S(1)}, bf16[2,512,4,128]{3,2,1,0:T(4,128)(2,1)}, u32[]{:S(2)}) copy-start(bf16[2,512,4,128]{3,2,1,0:T(4,128)(2,1)} %reshape_squeeze.21) | copy-start | bytes 3145732
  117.8 4.9 %copy-start.20 = (f32[4,129,128]{2,1,0:T(8,128)S(1)}, f32[4,129,128]{2,1,0:T(8,128)}, u32[]{:S(2)}) copy-start(f32[4,129,128]{2,1,0:T(8,128)} %copy-done.19) | copy-start | bytes 792580
  117.8 4.9 %copy-start.22 = (f32[4,129,128]{2,1,0:T(8,128)S(1)}, f32[4,129,128]{2,1,0:T(8,128)}, u32[]{:S(2)}) copy-start(f32[4,129,128]{2,1,0:T(8,128)} %copy-done.21) | copy-start | bytes 792580
  117.8 5.0 %copy-start.24 = (f32[4,129,128]{2,1,0:T(8,128)S(1)}, f32[4,129,128]{2,1,0:T(8,128)}, u32[]{:S(2)}) copy-start(f32[4,129,128]{2,1,0:T(8,128)} %copy-done.23) | copy-start | bytes 792580
  117.8 5.0 %copy-start.26 = (f32[4,129,128]{2,1,0:T(8,128)S(1)}, f32[4,129,128]{2,1,0:T(8,128)}, u32[]{:S(2)}) copy-start(f32[4,129,128]{2,1,0:T(8,128)} %copy-done.25) | copy-start | bytes 792580
  119.3 5.1 %copy-start.31 = (f32[1,4,1024]{2,1,0:T(4,128)S(1)}, f32[1,4,1024]{2,1,0:T(4,128)}, u32[]{:S(2)}) copy-start(f32[1,4,1024]{2,1,0:T(4,128)} %param.14) | copy-start | bytes 49156
  155.6 5.2 %copy-start.3 = (bf16[2,512,4,128]{3,1,2,0:T(8,128)(2,1)}, bf16[2,512,4,128]{3,1,2,0:T(8,128)(2,1)S(1)}, u32[]{:S(2)}) copy-start(bf16[2,512,4,128]{3,1,2,0:T(8,128)(2,1)S(1)} %get-tuple-element.1097) | copy-start | bytes 3145732 | tf_op jit(solution)/shard_map/transpose(jvp())/while
  155.6 5.2 %copy-start.5 = (f32[2,512,4,128]{3,2,1,0:T(4,128)S(1)}, f32[2,512,4,128]{3,2,1,0:T(4,128)}, u32[]{:S(2)}) copy-start(f32[2,512,4,128]{3,2,1,0:T(4,128)} %get-tuple-element.1101) | copy-start | bytes 6291460 | tf_op jit(solution)/shard_map/transpose(jvp())/while
  161.3 7.9 %copy-start.1 = (bf16[512,4,128]{2,0,1:T(8,128)(2,1)S(1)}, bf16[512,4,128]{2,0,1:T(8,128)(2,1)}, u32[]{:S(2)}) copy-start(bf16[512,4,128]{2,0,1:T(8,128)(2,1)} %dynamic-slice_bitcast_fusion.13) | copy-start | bytes 1572868 | tf_op jit(solution)/shard_map/transpose(jvp())/while
  171.7 3.2 %copy-start.34 = (bf16[4,512,512]{2,1,0:T(8,128)(2,1)}, bf16[4,512,512]{2,1,0:T(8,128)(2,1)S(1)}, u32[]{:S(2)}) copy-start(bf16[4,512,512]{2,1,0:T(8,128)(2,1)S(1)} %get-tuple-element.1004) | copy-start | bytes 6291460 | tf_op jit(solution)/shard_map/transpose(jvp())/while
  183.9 5.2 %copy-start.6 = (bf16[1,512,4,128]{3,1,2,0:T(8,128)(2,1)S(1)}, bf16[1,512,4,128]{3,1,2,0:T(8,128)(2,1)}, u32[]{:S(2)}) copy-start(bf16[1,512,4,128]{3,1,2,0:T(8,128)(2,1)} %get-tuple-element.1012) | copy-start | bytes 1572868 | tf_op jit(solution)/shard_map/transpose(jvp())/while
  183.9 5.2 %copy-start.10 = (bf16[2,512,4,128]{3,2,1,0:T(4,128)(2,1)S(1)}, bf16[2,512,4,128]{3,2,1,0:T(4,128)(2,1)}, u32[]{:S(2)}) copy-start(bf16[2,512,4,128]{3,2,1,0:T(4,128)(2,1)} %get-tuple-element.1073) | copy-start | bytes 3145732 | tf_op jit(solution)/shard_map/transpose(jvp())/while
  184.0 5.2 %copy-start.13 = (bf16[2,512,4,128]{3,2,1,0:T(4,128)(2,1)S(1)}, bf16[2,512,4,128]{3,2,1,0:T(4,128)(2,1)}, u32[]{:S(2)}) copy-start(bf16[2,512,4,128]{3,2,1,0:T(4,128)(2,1)} %get-tuple-element.1074) | copy-start | bytes 3145732 | tf_op jit(solution)/shard_map/transpose(jvp())/while
  189.2 9.1 %copy-start.4 = (bf16[2,512,4,128]{3,1,2,0:T(8,128)(2,1)S(1)}, bf16[2,512,4,128]{3,1,2,0:T(8,128)(2,1)}, u32[]{:S(2)}) copy-start(bf16[2,512,4,128]{3,1,2,0:T(8,128)(2,1)} %copy-done.3) | copy-start | bytes 3145732 | tf_op jit(solution)/shard_map/transpose(jvp())/while
  198.3 5.2 %copy-start.3 = (bf16[2,512,4,128]{3,1,2,0:T(8,128)(2,1)}, bf16[2,512,4,128]{3,1,2,0:T(8,128)(2,1)S(1)}, u32[]{:S(2)}) copy-start(bf16[2,512,4,128]{3,1,2,0:T(8,128)(2,1)S(1)} %get-tuple-element.1097) | copy-start | bytes 3145732 | tf_op jit(solution)/shard_map/transpose(jvp())/while
  198.3 5.2 %copy-start.5 = (f32[2,512,4,128]{3,2,1,0:T(4,128)S(1)}, f32[2,512,4,128]{3,2,1,0:T(4,128)}, u32[]{:S(2)}) copy-start(f32[2,512,4,128]{3,2,1,0:T(4,128)} %get-tuple-element.1101) | copy-start | bytes 6291460 | tf_op jit(solution)/shard_map/transpose(jvp())/while
  203.9 7.9 %copy-start.1 = (bf16[512,4,128]{2,0,1:T(8,128)(2,1)S(1)}, bf16[512,4,128]{2,0,1:T(8,128)(2,1)}, u32[]{:S(2)}) copy-start(bf16[512,4,128]{2,0,1:T(8,128)(2,1)} %dynamic-slice_bitcast_fusion.13) | copy-start | bytes 1572868 | tf_op jit(solution)/shard_map/transpose(jvp())/while
  214.4 3.2 %copy-start.34 = (bf16[4,512,512]{2,1,0:T(8,128)(2,1)}, bf16[4,512,512]{2,1,0:T(8,128)(2,1)S(1)}, u32[]{:S(2)}) copy-start(bf16[4,512,512]{2,1,0:T(8,128)(2,1)S(1)} %get-tuple-element.1004) | copy-start | bytes 6291460 | tf_op jit(solution)/shard_map/transpose(jvp())/while
  226.6 5.2 %copy-start.6 = (bf16[1,512,4,128]{3,1,2,0:T(8,128)(2,1)S(1)}, bf16[1,512,4,128]{3,1,2,0:T(8,128)(2,1)}, u32[]{:S(2)}) copy-start(bf16[1,512,4,128]{3,1,2,0:T(8,128)(2,1)} %get-tuple-element.1012) | copy-start | bytes 1572868 | tf_op jit(solution)/shard_map/transpose(jvp())/while
  226.6 5.2 %copy-start.10 = (bf16[2,512,4,128]{3,2,1,0:T(4,128)(2,1)S(1)}, bf16[2,512,4,128]{3,2,1,0:T(4,128)(2,1)}, u32[]{:S(2)}) copy-start(bf16[2,512,4,128]{3,2,1,0:T(4,128)(2,1)} %get-tuple-element.1073) | copy-start | bytes 3145732 | tf_op jit(solution)/shard_map/transpose(jvp())/while
  226.6 5.2 %copy-start.13 = (bf16[2,512,4,128]{3,2,1,0:T(4,128)(2,1)S(1)}, bf16[2,512,4,128]{3,2,1,0:T(4,128)(2,1)}, u32[]{:S(2)}) copy-start(bf16[2,512,4,128]{3,2,1,0:T(4,128)(2,1)} %get-tuple-element.1074) | copy-start | bytes 3145732 | tf_op jit(solution)/shard_map/transpose(jvp())/while
  231.8 9.1 %copy-start.4 = (bf16[2,512,4,128]{3,1,2,0:T(8,128)(2,1)S(1)}, bf16[2,512,4,128]{3,1,2,0:T(8,128)(2,1)}, u32[]{:S(2)}) copy-start(bf16[2,512,4,128]{3,1,2,0:T(8,128)(2,1)} %copy-done.3) | copy-start | bytes 3145732 | tf_op jit(solution)/shard_map/transpose(jvp())/while
  241.0 7.9 %copy-start.33 = (f32[2,4,512]{2,1,0:T(4,128)}, f32[2,4,512]{2,1,0:T(4,128)S(1)}, u32[]{:S(2)}) copy-start(f32[2,4,512]{2,1,0:T(4,128)S(1)} %get-tuple-element.443) | copy-start | bytes 49156
  241.0 5.5 %copy-start.12 = (bf16[2,512,4,128]{3,2,1,0:T(4,128)(2,1)S(1)}, bf16[2,512,4,128]{3,2,1,0:T(4,128)(2,1)}, u32[]{:S(2)}) copy-start(bf16[2,512,4,128]{3,2,1,0:T(4,128)(2,1)} %get-tuple-element.440) | copy-start | bytes 3145732
  241.0 6.7 %copy-start.15 = (bf16[2,512,4,128]{3,2,1,0:T(4,128)(2,1)S(1)}, bf16[2,512,4,128]{3,2,1,0:T(4,128)(2,1)}, u32[]{:S(2)}) copy-start(bf16[2,512,4,128]{3,2,1,0:T(4,128)(2,1)} %get-tuple-element.441) | copy-start | bytes 3145732
  241.8 7.1 %copy-start.16 = (bf16[2,512,4,128]{3,2,1,0:T(4,128)(2,1)S(1)}, bf16[2,512,4,128]{3,2,1,0:T(4,128)(2,1)}, u32[]{:S(2)}) copy-start(bf16[2,512,4,128]{3,2,1,0:T(4,128)(2,1)} %get-tuple-element.442) | copy-start | bytes 3145732
  (10 other events, 17.7 us)
Sparse Core Ops, SparseCore 0:
  241.9 12.2 reduce-scatter.3

commit v4 on v3

--- a/solution.py
+++ b/solution.py
@@ -123,6 +123,110 @@
     )(part)
 
 
+def scan_kernel(fwd_ref, bwd_ref, fwd_out, bwd_out, aggs, exs, slots, send_sem, recv_sem):
+    count = lax.axis_size("ctx")
+    me = lax.axis_index("ctx")
+    row, col = lax.axis_index("dp"), lax.axis_index("head")
+    rows = fwd_out.shape[1]
+    shifts = []
+    shift = 1
+    while shift < count:
+        shifts.append(shift)
+        shift *= 2
+
+    def device(index):
+        return (row, index, col)
+
+    barrier = pltpu.get_barrier_semaphore()
+    for shift in shifts:
+        for peer, present in ((me + shift, me + shift < count), (me - shift, me >= shift)):
+            @pl.when(present)
+            def _():
+                pl.semaphore_signal(
+                    barrier, inc=1, device_id=device(peer), device_id_type=pl.DeviceIdType.MESH
+                )
+
+    def at_least(bound):
+        span = (count - 1) // bound + 1
+        return (me // bound + span - 1) // span
+
+    peers = 0
+    for shift in shifts:
+        peers = peers + at_least(shift) + 1 - at_least(count - shift)
+    pl.semaphore_wait(barrier, peers)
+
+    aggs[0] = fwd_ref[...]
+    aggs[1] = bwd_ref[...]
+    exs[...] = jnp.zeros_like(exs)
+    exs[:, :, rows:, :] = jnp.ones_like(exs[:, :, rows:, :])
+
+    for round_index, shift in enumerate(shifts):
+        sends = (me + shift < count, me >= shift)
+        targets = (me + shift, me - shift)
+        sources = (me - shift, me + shift)
+
+        def copy_of(side, peer):
+            return pltpu.make_async_remote_copy(
+                src_ref=aggs.at[side],
+                dst_ref=slots.at[side, round_index],
+                send_sem=send_sem.at[side, round_index],
+                recv_sem=recv_sem.at[side, round_index],
+                device_id=device(peer),
+                device_id_type=pl.DeviceIdType.MESH,
+            )
+
+        for side in range(2):
+            @pl.when(sends[side])
+            def _():
+                copy_of(side, targets[side]).start()
+
+        for side in range(2):
+            @pl.when(sends[side])
+            def _():
+                copy_of(side, targets[side]).wait_send()
+
+        for side in range(2):
+            @pl.when(sends[1 - side])
+            def _():
+                copy_of(side, sources[side]).wait_recv()
+                got = slots[side, round_index]
+                ex = exs[side]
+                agg = aggs[side]
+                ex_a = ex[:, rows:rows + 1, :]
+                agg_a = agg[:, rows:rows + 1, :]
+                exs[side, :, :rows, :] = ex_a * got[:, :rows, :] + ex[:, :rows, :]
+                exs[side, :, rows:, :] = ex[:, rows:, :] * got[:, rows:, :]
+                aggs[side, :, :rows, :] = agg_a * got[:, :rows, :] + agg[:, :rows, :]
+                aggs[side, :, rows:, :] = agg[:, rows:, :] * got[:, rows:, :]
+
+    fwd_out[...] = exs[0, :, :rows, :]
+    bwd_out[...] = exs[1, :, :rows, :]
+
+
+def both_scans_kernel(decay, fwd_term, bwd_term, count):
+    heads, rows, width = fwd_term.shape
+    rounds = max(1, (count - 1).bit_length())
+    lane = jnp.broadcast_to(decay[:, None, None], (heads, 8, width))
+    fwd = jnp.concatenate([fwd_term, lane], axis=1)
+    bwd = jnp.concatenate([bwd_term, lane], axis=1)
+    packed = fwd.shape
+    out = jax.ShapeDtypeStruct(fwd_term.shape, jnp.float32)
+    return pl.pallas_call(
+        scan_kernel,
+        out_shape=(out, out),
+        in_specs=[pl.BlockSpec(memory_space=pltpu.VMEM)] * 2,
+        out_specs=(pl.BlockSpec(memory_space=pltpu.VMEM),) * 2,
+        scratch_shapes=[
+            pltpu.VMEM((2,) + packed, jnp.float32),
+            pltpu.VMEM((2,) + packed, jnp.float32),
+            pltpu.VMEM((2, rounds) + packed, jnp.float32),
+            pltpu.SemaphoreType.DMA((2, rounds)),
+            pltpu.SemaphoreType.DMA((2, rounds)),
+        ],
+        compiler_params=pltpu.CompilerParams(collective_id=1, has_side_effects=True),
+    )(fwd, bwd)
+
+
 def start_flags(doc_lengths, first_pos, num_rows):
     starts = jnp.cumsum(doc_lengths, dtype=jnp.int32) - doc_lengths
     positions = first_pos + jnp.arange(num_rows, dtype=jnp.int32)
@@ -207,7 +311,7 @@
     )
     ctx_size = lax.axis_size("ctx")
     local_grad = local_incoming_grad(q_rows, cotangent[0], cum_decay, opened, head_count, head_width)
-    state_in, later_grad = both_scans(shard_decay, local_end, local_grad, ctx_size)
+    state_in, later_grad = both_scans_kernel(shard_decay, local_end, local_grad, ctx_size)
 
     def forward(q_part, k_part, v_part, gate_part, gain_part):
         return run_blocks(q_part, k_part, v_part, gate_part, flags, gain_part, state_in)

time: 279 us -> 260 us (0.932)
  Pallas kernels: 13.6 us -> 80.8 us
  starting transfers between devices: 49.5 us -> 0.04 us
  waiting for transfers between devices: 30 us -> 2.87 us
  other arithmetic: 39.9 us -> 32.4 us
    pallas_call x0 -> x1, Pallas kernels: none -> 67.2 us  [both_scans_kernel(): pl.pallas_call(scan_kernel, out_shape=(out, out), in_specs=[pl.BlockSpec(...]
    ppermute x10 -> x0, starting transfers between devices: 49.4 us -> none  [passed_along(): lax.ppermute(value, axis, [(source, source + steps) for source in range(f...]
    ppermute x10 -> x0, waiting for transfers between devices: 25.9 us -> none  [passed_along(): lax.ppermute(value, axis, [(source, source + steps) for source in range(f...]
    add x8 -> x0, other arithmetic: 3.36 us -> none  [the longest x7 1.73 us: both_scans(): agg_b = agg_a[:, None, None] * r_b + agg_b]
    unnamed x55 -> x31, local copies, waits for them, and re-layouts: 9.22 us -> 9.84 us
  transfers between devices with their start and end apart: 11 -> 1, of which waited for: 7 -> 1; matrix products, arithmetic and copies ran while one was open for 8% -> 3% of each run, Pallas kernels for 0% -> 0%
where the time goes in v4:
time: 260 us; the launch traced here: 258 us
  Pallas kernels  80.8 us (31%)
  matrix products  64.5 us (25%)
  local copies, waits for them, and re-layouts  63 us (24%)
  other arithmetic  32.4 us (12%)
  between operations  14.3 us (6%)
  waiting for transfers between devices  2.87 us (1%)
    pallas_call x1, Pallas kernels, both_scans_kernel(): pl.pallas_call(scan_kernel, out_shape=(out, out), in_specs=[pl.BlockSpec(...  67.2 us
    another operation x27, other arithmetic  19.4 us
    dot_general x6, matrix products, block_step(): jnp.einsum('hts,she->the', weights, v_block, preferred_element_type=jnp.f...  19.2 us
    dot_general x8, matrix products, block_step(): jnp.einsum('thd,hde->the', q_float, carried, precision=PRECISE)  15.6 us
    dot_general x6, matrix products, block_step(): jnp.einsum('thd,shd->hts', q_block, k_bf, preferred_element_type=jnp.floa...  14.5 us
    pallas_call x1, Pallas kernels, gain_sum(): pl.pallas_call(gain_sum_kernel, out_shape=jax.ShapeDtypeStruct(part.shape...  13.6 us
    dot_general x6, matrix products, block_step(): jnp.einsum('shd,she->hde', k_float * to_end.T[:, :, None], v_float, preci...  11.3 us
    squeeze x10, local copies, waits for them, and re-layouts, run_blocks(): lax.scan(jax.checkpoint(make_step(key_gain, head_width)), start_state, (t...  10.2 us
  transfers between devices with their start and end apart: 1, of which 1 were waited for; matrix products, arithmetic and copies ran while one was open for 3% of the time, Pallas kernels for 0%

profile of v4, /device:TPU:2, one launch (start us, length us, event | category | flops | bytes accessed | tf_op | source)
XLA Modules:
  0.0 258.5 jit_solution(13267310609685024308)
XLA Ops:
  7.3 2.7 %copy.248 = f32[1,1024,512]{1,2,0:T(8,128)} copy(bf16[1,1024,512]{2,1,0:T(8,128)(2,1)} %param.12) | data formatting | bytes 3145728 | tf_op jit(solution)/shard_map/convert_element_type | solution.py:305
  10.0 2.2 reshape_squeeze.19
  16.1 2.1 reshape.588
  18.2 2.7 %reshape.598 = f32[2,512,4,128]{3,2,1,0:T(4,128)} reshape(bf16[1,1024,512]{2,1,0:T(8,128)(2,1)} %param.17) | data formatting | bytes 3145728 | tf_op jit(solution)/shard_map/convert_element_type | solution.py:28
  25.4 2.7 %multiply_convert_fusion.6 = bf16[1024,4,128]{0,2,1:T(8,128)(2,1)} fusion(f32[1024,4,128]{0,2,1:T(8,128)} %bitcast.342, f32[4,128]{1,0:T(4,128)S(1)} %copy-done.19), kind=kLoop, calls=%fused_computation.164 | loop fusion | flops 1048576 | bytes 3147776 | tf_op jit(solution)/shard_map/convert_element_type | solution.py:306
  28.1 1.4 copy.225
  29.5 2.6 copy.226
  32.1 2.3 copy.227
  35.2 2.5 fusion.107
  37.7 1.3 fusion.109
  39.9 67.2 %shard_map.118 = (f32[4,128,128]{2,1,0:T(8,128)S(1)}, f32[4,128,128]{2,1,0:T(8,128)S(1)}) custom-call(f32[4,136,128]{2,1,0:T(8,128)} %get-tuple-element.773.fwd_ref, f32[4,136,128]{2,1,0:T(8,128)} %get-tuple-element.772.bwd_ref), custom_call_target="tpu_custom_call" | custom-call | tf_op jit(solution)/shard_map/pallas_call | solution.py:214
  107.1 27.4 %while.42 = (s32[]{:T(128)}, f32[4,128,128]{2,1,0:T(8,128)S(1)}, bf16[2,512,4,128]{1,3,2,0:T(8,128)(2,1)}, f32[2,4,128,128]{3,2,1,0:T(8,128)}, f32[2,4,512]{2,1,...) while((s32[]{:T(128)}, f32[4,128,128]{2,1,0:T(8,128)S(1)}, ...), condition=%wide.region_11.12_spmd.clone, body=%wide.region_6.11_spmd.clone.sunk | while | flops 1352081408 | bytes 9343697 | solution.py:284
  110.5 3.3 %fusion.191 = f32[512,4,128]{0,2,1:T(8,128)S(1)} fusion(bf16[512,4,128]{2,0,1:T(8,128)(2,1)S(1)} %fusion.189, f32[4,512]{1,0:T(4,128)S(1)} %bitcast.353, pred[512,512]{1,0:T(8,128)(4,1)S(1)} %fusion.190, bf16[2,512,4,128]{3,1,2,0:T(8,128)(2,1)} %get-tuple-element.1015, s32[]{:T(128)S(6)} %copy.326, bf16[2,512,4,128]{3,1,2,0:T(8,128)(2,1)} %get-tuple-element.1014), kind=kOutput, calls=%fused_computation.3.clone.1 | convolution fusion | flops 543162368 | bytes 2900992 | tf_op jit(solution)/shard_map/jvp()/while/body/eval_jaxpr/hts,she->the/dot_general | solution.py:256
  115.3 3.0 %fusion.192 = bf16[2,512,4,128]{1,3,2,0:T(8,128)(2,1)} fusion(bf16[2,512,4,128]{1,3,2,0:T(8,128)(2,1)} %get-tuple-element.996, s32[]{:T(128)S(6)} %copy.326, f32[512,4,128]{0,2,1:T(8,128)S(1)} %fusion.191, f32[4,128,128]{2,1,0:T(8,128)S(1)} %get-tuple-element.995, f32[512,4]{0,1:T(4,128)S(1)} %bitcast.345, ...), kind=kOutput, calls=%fused_computation.8.clone.1 | convolution fusion | flops 403701760 | bytes 2892800 | tf_op jit(solution)/shard_map/jvp()/while/body/eval_jaxpr/thd,hde->the/dot_general | solution.py:260
  118.4 2.4 convolution_add_fusion.4
  124.2 3.3 %fusion.191 = f32[512,4,128]{0,2,1:T(8,128)S(1)} fusion(bf16[512,4,128]{2,0,1:T(8,128)(2,1)S(1)} %fusion.189, f32[4,512]{1,0:T(4,128)S(1)} %bitcast.353, pred[512,512]{1,0:T(8,128)(4,1)S(1)} %fusion.190, bf16[2,512,4,128]{3,1,2,0:T(8,128)(2,1)} %get-tuple-element.1015, s32[]{:T(128)S(6)} %copy.326, bf16[2,512,4,128]{3,1,2,0:T(8,128)(2,1)} %get-tuple-element.1014), kind=kOutput, calls=%fused_computation.3.clone.1 | convolution fusion | flops 543162368 | bytes 2900992 | tf_op jit(solution)/shard_map/jvp()/while/body/eval_jaxpr/hts,she->the/dot_general | solution.py:256
  129.0 3.0 %fusion.192 = bf16[2,512,4,128]{1,3,2,0:T(8,128)(2,1)} fusion(bf16[2,512,4,128]{1,3,2,0:T(8,128)(2,1)} %get-tuple-element.996, s32[]{:T(128)S(6)} %copy.326, f32[512,4,128]{0,2,1:T(8,128)S(1)} %fusion.191, f32[4,128,128]{2,1,0:T(8,128)S(1)} %get-tuple-element.995, f32[512,4]{0,1:T(4,128)S(1)} %bitcast.345, ...), kind=kOutput, calls=%fused_computation.8.clone.1 | convolution fusion | flops 403701760 | bytes 2892800 | tf_op jit(solution)/shard_map/jvp()/while/body/eval_jaxpr/thd,hde->the/dot_general | solution.py:260
  132.1 2.4 convolution_add_fusion.4
  135.7 1.2 broadcast.246.clone2
  138.2 85.1 %while.43 = (s32[]{:T(128)}, f32[4,128]{1,0:T(4,128)S(1)}, f32[4,128,128]{2,1,0:T(8,128)S(1)}, bf16[2,512,4,128]{3,2,1,0:T(4,128)(2,1)}, bf16[2,512,4,128]{3,2,1...) while((s32[]{:T(128)}, f32[4,128]{1,0:T(4,128)S(1)}, ...), condition=%wide.region_26.27_spmd.clone, body=%wide.region_12.26_spmd.clone.sunk | while | flops 3394863616 | bytes 116524784 | solution.py:284
  138.2 1.3 dynamic-slice_bitcast_fusion.10
  141.5 1.9 dynamic-slice_bitcast_fusion.13
  148.9 1.9 fusion.210
  151.8 2.5 fusion.213
  154.3 3.2 %fusion.214 = (bf16[1,512,4,128]{3,1,2,0:T(8,128)(2,1)}, f32[4,128]{1,0:T(4,128)S(1)}) fusion(f32[4,128]{1,0:T(4,128)S(1)} %get-tuple-element.960, bf16[512,4,128]{2,0,1:T(8,128)(2,1)S(1)} %copy-done.2, bf16[512,4,128]{2,0,1:T(8,128)(2,1)S(1)} %get-tuple-element.967, bf16[512,4,128]{2,0,1:T(8,128)(2,1)S(1)} %dynamic-slice_bitcast_fusion.11, ...), kind=kOutput, calls=%fused_computation.110.clone.1 | convolution fusion | flops 276823552 | bytes 4468736 | tf_op jit(solution)/shard_map/transpose(jvp())/while/body/eval_jaxpr/checkpoint/thd,shd->hts/dot_general | solution.py:254
  157.6 3.8 %fusion.220 = bf16[4,128,512]{2,1,0:T(8,128)(2,1)S(1)} fusion(f32[4,512,512]{2,1,0:T(8,128)} %copy-done, f32[4,512]{1,0:T(4,128)S(1)} %bitcast.351, pred[512,512]{1,0:T(8,128)(4,1)S(1)} %fusion.212, f32[512,4,128]{0,2,1:T(8,128)S(1)} %bitcast.337), kind=kOutput, calls=%fused_computation.81.clone.1 | convolution fusion | flops 274726912 | bytes 6037504 | tf_op jit(solution)/shard_map/transpose(jvp())/while/body/eval_jaxpr/checkpoint/hts,she->the/dot_general | solution.py:256
  161.3 1.4 fusion.221
  164.6 1.9 convolution_add_fusion.5
  166.6 3.3 %fusion.218 = bf16[4,512,128]{2,1,0:T(8,128)(2,1)S(1)} fusion(bf16[512,4,128]{2,0,1:T(8,128)(2,1)S(1)} %fusion.209, bf16[4,512,512]{2,1,0:T(8,128)(2,1)} %copy-done.22, f32[4,512]{1,0:T(4,128)S(1)} %bitcast.352, pred[512,512]{1,0:T(8,128)(4,1)S(1)} %fusion.212), kind=kOutput, calls=%fused_computation.85.clone.1 | convolution fusion | flops 274989056 | bytes 3416064 | tf_op jit(solution)/shard_map/transpose(jvp())/while/body/eval_jaxpr/checkpoint/thd,shd->hts/dot_general | solution.py:254
  169.9 1.8 fusion.219
  175.3 5.0 %reduce-window.150 = f32[4,4,128]{2,1,0:T(4,128)S(1)} reduce-window(f32[4,4,128]{2,1,0:T(4,128)S(1)} %reshape.629, f32[]{:T(128)} %constant.142.clone.1..sunk.1), window={size=1x1x128 pad=0_0x0_0x0_127}, to_apply=%region_24.24 | reduce-window | flops 260096 | bytes 16388 | tf_op jit(solution)/shard_map/reduce-window.60
  180.8 1.3 dynamic-slice_bitcast_fusion.10
  184.1 1.9 dynamic-slice_bitcast_fusion.13
  191.5 1.9 fusion.210
  194.3 2.5 fusion.213
  196.9 3.2 %fusion.214 = (bf16[1,512,4,128]{3,1,2,0:T(8,128)(2,1)}, f32[4,128]{1,0:T(4,128)S(1)}) fusion(f32[4,128]{1,0:T(4,128)S(1)} %get-tuple-element.960, bf16[512,4,128]{2,0,1:T(8,128)(2,1)S(1)} %copy-done.2, bf16[512,4,128]{2,0,1:T(8,128)(2,1)S(1)} %get-tuple-element.967, bf16[512,4,128]{2,0,1:T(8,128)(2,1)S(1)} %dynamic-slice_bitcast_fusion.11, ...), kind=kOutput, calls=%fused_computation.110.clone.1 | convolution fusion | flops 276823552 | bytes 4468736 | tf_op jit(solution)/shard_map/transpose(jvp())/while/body/eval_jaxpr/checkpoint/thd,shd->hts/dot_general | solution.py:254
  200.1 3.8 %fusion.220 = bf16[4,128,512]{2,1,0:T(8,128)(2,1)S(1)} fusion(f32[4,512,512]{2,1,0:T(8,128)} %copy-done, f32[4,512]{1,0:T(4,128)S(1)} %bitcast.351, pred[512,512]{1,0:T(8,128)(4,1)S(1)} %fusion.212, f32[512,4,128]{0,2,1:T(8,128)S(1)} %bitcast.337), kind=kOutput, calls=%fused_computation.81.clone.1 | convolution fusion | flops 274726912 | bytes 6037504 | tf_op jit(solution)/shard_map/transpose(jvp())/while/body/eval_jaxpr/checkpoint/hts,she->the/dot_general | solution.py:256
  203.9 1.4 fusion.221
  207.2 1.9 convolution_add_fusion.5
  209.1 3.3 %fusion.218 = bf16[4,512,128]{2,1,0:T(8,128)(2,1)S(1)} fusion(bf16[512,4,128]{2,0,1:T(8,128)(2,1)S(1)} %fusion.209, bf16[4,512,512]{2,1,0:T(8,128)(2,1)} %copy-done.22, f32[4,512]{1,0:T(4,128)S(1)} %bitcast.352, pred[512,512]{1,0:T(8,128)(4,1)S(1)} %fusion.212), kind=kOutput, calls=%fused_computation.85.clone.1 | convolution fusion | flops 274989056 | bytes 3416064 | tf_op jit(solution)/shard_map/transpose(jvp())/while/body/eval_jaxpr/checkpoint/thd,shd->hts/dot_general | solution.py:254
  212.5 1.8 fusion.219
  217.9 5.0 %reduce-window.150 = f32[4,4,128]{2,1,0:T(4,128)S(1)} reduce-window(f32[4,4,128]{2,1,0:T(4,128)S(1)} %reshape.629, f32[]{:T(128)} %constant.142.clone.1..sunk.1), window={size=1x1x128 pad=0_0x0_0x0_127}, to_apply=%region_24.24 | reduce-window | flops 260096 | bytes 16388 | tf_op jit(solution)/shard_map/reduce-window.60
  224.2 2.5 copy.228
  226.7 2.2 convert_element_type.304
  232.5 2.9 %reduce-scatter.4.cloned.1.call-done = f32[64,4]{1,0:T(8,128)} async-done(((f32[128,4]{1,0:T(8,128)}), f32[64,4]{1,0:T(8,128)}) %reduce-scatter.4.cloned.1.call-update) | async-done | bytes 1040
  235.4 1.4 copy.251.part_ref
  236.8 13.6 %shard_map.119 = f32[4,64]{1,0:T(4,128)} custom-call(f32[4,64]{1,0:T(4,128)} %copy.251.part_ref), custom_call_target="tpu_custom_call" | custom-call | tf_op jit(solution)/shard_map/pallas_call | solution.py:112
  250.4 1.3 copy.356
  (238 shorter events, 55.2 us)
Async XLA Ops:
  7.2 5.0 %copy-start.8 = (bf16[1,1024,512]{2,1,0:T(8,128)(2,1)S(1)}, bf16[1,1024,512]{2,1,0:T(8,128)(2,1)}, u32[]{:S(2)}) copy-start(bf16[1,1024,512]{2,1,0:T(8,128)(2,1)} %param.13) | copy-start | bytes 3145732
  7.2 228.2 %reduce-scatter.4.cloned.1.call-start = ((), (), s32[]{:S(2)}) async-start(), calls=%async_computation.1 | async-start | bytes 98304
  7.2 7.1 %copy-start.7 = (bf16[1,1024,512]{2,1,0:T(8,128)(2,1)S(1)}, bf16[1,1024,512]{2,1,0:T(8,128)(2,1)}, u32[]{:S(2)}) copy-start(bf16[1,1024,512]{2,1,0:T(8,128)(2,1)} %param.11) | copy-start | bytes 3145732
  14.9 6.0 %copy-start.21 = (s32[1,16]{1,0:T(1,128)S(1)}, s32[1,16]{1,0:T(1,128)}, u32[]{:S(2)}) copy-start(s32[1,16]{1,0:T(1,128)} %param.15) | copy-start | bytes 196
  14.9 7.5 %copy-start.18 = (f32[1,4,1024]{2,1,0:T(4,128)S(1)}, f32[1,4,1024]{2,1,0:T(4,128)}, u32[]{:S(2)}) copy-start(f32[1,4,1024]{2,1,0:T(4,128)} %param.14) | copy-start | bytes 49156
  14.9 10.4 %copy-start.19 = (f32[4,128]{1,0:T(4,128)S(1)}, f32[4,128]{1,0:T(4,128)}, u32[]{:S(2)}) copy-start(f32[4,128]{1,0:T(4,128)} %param.16) | copy-start | bytes 6148
  29.5 8.2 %copy-start.16 = (bf16[1024,4,128]{2,1,0:T(4,128)(2,1)S(1)}, bf16[1024,4,128]{2,1,0:T(4,128)(2,1)}, u32[]{:S(2)}) copy-start(bf16[1024,4,128]{2,1,0:T(4,128)(2,1)} %reshape_squeeze.17) | copy-start | bytes 3145732
  29.5 8.2 %copy-start.17 = (bf16[1024,4,128]{0,2,1:T(8,128)(2,1)S(1)}, bf16[1024,4,128]{0,2,1:T(8,128)(2,1)}, u32[]{:S(2)}) copy-start(bf16[1024,4,128]{0,2,1:T(8,128)(2,1)} %multiply_convert_fusion.6) | copy-start | bytes 3145732
  138.2 5.2 %copy-start.3 = (bf16[2,512,4,128]{3,1,2,0:T(8,128)(2,1)}, bf16[2,512,4,128]{3,1,2,0:T(8,128)(2,1)S(1)}, u32[]{:S(2)}) copy-start(bf16[2,512,4,128]{3,1,2,0:T(8,128)(2,1)S(1)} %get-tuple-element.1063) | copy-start | bytes 3145732 | tf_op jit(solution)/shard_map/transpose(jvp())/while
  138.2 5.2 %copy-start.5 = (f32[2,512,4,128]{3,2,1,0:T(4,128)S(1)}, f32[2,512,4,128]{3,2,1,0:T(4,128)}, u32[]{:S(2)}) copy-start(f32[2,512,4,128]{3,2,1,0:T(4,128)} %get-tuple-element.1067) | copy-start | bytes 6291460 | tf_op jit(solution)/shard_map/transpose(jvp())/while
  143.9 7.9 %copy-start.1 = (bf16[512,4,128]{2,0,1:T(8,128)(2,1)S(1)}, bf16[512,4,128]{2,0,1:T(8,128)(2,1)}, u32[]{:S(2)}) copy-start(bf16[512,4,128]{2,0,1:T(8,128)(2,1)} %dynamic-slice_bitcast_fusion.13) | copy-start | bytes 1572868 | tf_op jit(solution)/shard_map/transpose(jvp())/while
  151.5 2.8 %copy-start = (f32[4,512,512]{2,1,0:T(8,128)}, f32[4,512,512]{2,1,0:T(8,128)S(1)}, u32[]{:S(2)}) copy-start(f32[4,512,512]{2,1,0:T(8,128)S(1)} %fusion.211) | copy-start | bytes 12582916 | tf_op jit(solution)/shard_map/transpose(jvp())/while
  151.7 2.6 copy-start.2
  154.3 3.2 %copy-start.22 = (bf16[4,512,512]{2,1,0:T(8,128)(2,1)}, bf16[4,512,512]{2,1,0:T(8,128)(2,1)S(1)}, u32[]{:S(2)}) copy-start(bf16[4,512,512]{2,1,0:T(8,128)(2,1)S(1)} %get-tuple-element.970) | copy-start | bytes 6291460 | tf_op jit(solution)/shard_map/transpose(jvp())/while
  166.5 5.2 %copy-start.6 = (bf16[1,512,4,128]{3,1,2,0:T(8,128)(2,1)S(1)}, bf16[1,512,4,128]{3,1,2,0:T(8,128)(2,1)}, u32[]{:S(2)}) copy-start(bf16[1,512,4,128]{3,1,2,0:T(8,128)(2,1)} %get-tuple-element.978) | copy-start | bytes 1572868 | tf_op jit(solution)/shard_map/transpose(jvp())/while
  166.5 5.2 %copy-start.9 = (bf16[2,512,4,128]{3,2,1,0:T(4,128)(2,1)S(1)}, bf16[2,512,4,128]{3,2,1,0:T(4,128)(2,1)}, u32[]{:S(2)}) copy-start(bf16[2,512,4,128]{3,2,1,0:T(4,128)(2,1)} %get-tuple-element.1039) | copy-start | bytes 3145732 | tf_op jit(solution)/shard_map/transpose(jvp())/while
  166.5 5.2 %copy-start.12 = (bf16[2,512,4,128]{3,2,1,0:T(4,128)(2,1)S(1)}, bf16[2,512,4,128]{3,2,1,0:T(4,128)(2,1)}, u32[]{:S(2)}) copy-start(bf16[2,512,4,128]{3,2,1,0:T(4,128)(2,1)} %get-tuple-element.1040) | copy-start | bytes 3145732 | tf_op jit(solution)/shard_map/transpose(jvp())/while
  171.8 9.0 %copy-start.4 = (bf16[2,512,4,128]{3,1,2,0:T(8,128)(2,1)S(1)}, bf16[2,512,4,128]{3,1,2,0:T(8,128)(2,1)}, u32[]{:S(2)}) copy-start(bf16[2,512,4,128]{3,1,2,0:T(8,128)(2,1)} %copy-done.3) | copy-start | bytes 3145732 | tf_op jit(solution)/shard_map/transpose(jvp())/while
  172.7 1.0 copy-start.10
  172.7 1.3 copy-start.13
  180.8 5.2 %copy-start.3 = (bf16[2,512,4,128]{3,1,2,0:T(8,128)(2,1)}, bf16[2,512,4,128]{3,1,2,0:T(8,128)(2,1)S(1)}, u32[]{:S(2)}) copy-start(bf16[2,512,4,128]{3,1,2,0:T(8,128)(2,1)S(1)} %get-tuple-element.1063) | copy-start | bytes 3145732 | tf_op jit(solution)/shard_map/transpose(jvp())/while
  180.8 5.2 %copy-start.5 = (f32[2,512,4,128]{3,2,1,0:T(4,128)S(1)}, f32[2,512,4,128]{3,2,1,0:T(4,128)}, u32[]{:S(2)}) copy-start(f32[2,512,4,128]{3,2,1,0:T(4,128)} %get-tuple-element.1067) | copy-start | bytes 6291460 | tf_op jit(solution)/shard_map/transpose(jvp())/while
  186.5 7.9 %copy-start.1 = (bf16[512,4,128]{2,0,1:T(8,128)(2,1)S(1)}, bf16[512,4,128]{2,0,1:T(8,128)(2,1)}, u32[]{:S(2)}) copy-start(bf16[512,4,128]{2,0,1:T(8,128)(2,1)} %dynamic-slice_bitcast_fusion.13) | copy-start | bytes 1572868 | tf_op jit(solution)/shard_map/transpose(jvp())/while
  194.1 2.8 %copy-start = (f32[4,512,512]{2,1,0:T(8,128)}, f32[4,512,512]{2,1,0:T(8,128)S(1)}, u32[]{:S(2)}) copy-start(f32[4,512,512]{2,1,0:T(8,128)S(1)} %fusion.211) | copy-start | bytes 12582916 | tf_op jit(solution)/shard_map/transpose(jvp())/while
  194.3 2.6 copy-start.2
  196.9 3.2 %copy-start.22 = (bf16[4,512,512]{2,1,0:T(8,128)(2,1)}, bf16[4,512,512]{2,1,0:T(8,128)(2,1)S(1)}, u32[]{:S(2)}) copy-start(bf16[4,512,512]{2,1,0:T(8,128)(2,1)S(1)} %get-tuple-element.970) | copy-start | bytes 6291460 | tf_op jit(solution)/shard_map/transpose(jvp())/while
  209.1 5.2 %copy-start.6 = (bf16[1,512,4,128]{3,1,2,0:T(8,128)(2,1)S(1)}, bf16[1,512,4,128]{3,1,2,0:T(8,128)(2,1)}, u32[]{:S(2)}) copy-start(bf16[1,512,4,128]{3,1,2,0:T(8,128)(2,1)} %get-tuple-element.978) | copy-start | bytes 1572868 | tf_op jit(solution)/shard_map/transpose(jvp())/while
  209.1 5.2 %copy-start.9 = (bf16[2,512,4,128]{3,2,1,0:T(4,128)(2,1)S(1)}, bf16[2,512,4,128]{3,2,1,0:T(4,128)(2,1)}, u32[]{:S(2)}) copy-start(bf16[2,512,4,128]{3,2,1,0:T(4,128)(2,1)} %get-tuple-element.1039) | copy-start | bytes 3145732 | tf_op jit(solution)/shard_map/transpose(jvp())/while
  209.1 5.2 %copy-start.12 = (bf16[2,512,4,128]{3,2,1,0:T(4,128)(2,1)S(1)}, bf16[2,512,4,128]{3,2,1,0:T(4,128)(2,1)}, u32[]{:S(2)}) copy-start(bf16[2,512,4,128]{3,2,1,0:T(4,128)(2,1)} %get-tuple-element.1040) | copy-start | bytes 3145732 | tf_op jit(solution)/shard_map/transpose(jvp())/while
  214.3 9.0 %copy-start.4 = (bf16[2,512,4,128]{3,1,2,0:T(8,128)(2,1)S(1)}, bf16[2,512,4,128]{3,1,2,0:T(8,128)(2,1)}, u32[]{:S(2)}) copy-start(bf16[2,512,4,128]{3,1,2,0:T(8,128)(2,1)} %copy-done.3) | copy-start | bytes 3145732 | tf_op jit(solution)/shard_map/transpose(jvp())/while
  215.2 1.0 copy-start.10
  215.3 1.3 copy-start.13
  223.4 7.9 %copy-start.20 = (f32[2,4,512]{2,1,0:T(4,128)}, f32[2,4,512]{2,1,0:T(4,128)S(1)}, u32[]{:S(2)}) copy-start(f32[2,4,512]{2,1,0:T(4,128)S(1)} %get-tuple-element.447) | copy-start | bytes 49156
  223.4 5.5 %copy-start.11 = (bf16[2,512,4,128]{3,2,1,0:T(4,128)(2,1)S(1)}, bf16[2,512,4,128]{3,2,1,0:T(4,128)(2,1)}, u32[]{:S(2)}) copy-start(bf16[2,512,4,128]{3,2,1,0:T(4,128)(2,1)} %get-tuple-element.444) | copy-start | bytes 3145732
  223.4 6.7 %copy-start.14 = (bf16[2,512,4,128]{3,2,1,0:T(4,128)(2,1)S(1)}, bf16[2,512,4,128]{3,2,1,0:T(4,128)(2,1)}, u32[]{:S(2)}) copy-start(bf16[2,512,4,128]{3,2,1,0:T(4,128)(2,1)} %get-tuple-element.445) | copy-start | bytes 3145732
  224.2 7.1 %copy-start.15 = (bf16[2,512,4,128]{3,2,1,0:T(4,128)(2,1)S(1)}, bf16[2,512,4,128]{3,2,1,0:T(4,128)(2,1)}, u32[]{:S(2)}) copy-start(bf16[2,512,4,128]{3,2,1,0:T(4,128)(2,1)} %get-tuple-element.446) | copy-start | bytes 3145732
Sparse Core Ops, SparseCore 0:
  224.3 11.0 reduce-scatter.3

commit v5 on v4

--- a/solution.py
+++ b/solution.py
@@ -282,7 +282,7 @@
     gate_blocks = gate_rows.reshape(head_count, num_blocks, BLOCK).transpose(1, 0, 2)
     flag_blocks = flags.reshape(num_blocks, BLOCK)
     end_state, outputs = lax.scan(
-        jax.checkpoint(make_step(key_gain, head_width)),
+        make_step(key_gain, head_width),
         start_state,
         (to_blocks(q_rows), to_blocks(k_rows), to_blocks(v_rows), gate_blocks, flag_blocks),
     )

time: 260 us -> 298 us (1.15)
  matrix products: 64.5 us -> 78.9 us
  other arithmetic: 32.4 us -> 45.8 us
  local copies, waits for them, and re-layouts: 63 us -> 72.1 us
    while x52 -> x118, local copies, waits for them, and re-layouts: 2.74 us -> 20.3 us
    dynamic_update_slice x0 -> x14, other arithmetic: none -> 16.5 us  [run_blocks(): lax.scan(make_step(key_gain, head_width), start_state, (to_blocks(q_rows)...]
    squeeze x10 -> x0, local copies, waits for them, and re-layouts: 10.2 us -> none  [run_blocks(): lax.scan(jax.checkpoint(make_step(key_gain, head_width)), start_state, (t...]
    dynamic_slice x10 -> x14, local copies, waits for them, and re-layouts: 0.92 us -> 9.84 us  [run_blocks(): lax.scan(make_step(key_gain, head_width), start_state, (to_blocks(q_rows)...]
    dot_general x6, matrix products: 11.3 us -> 18.5 us  [block_step(): jnp.einsum('shd,she->hde', k_float * to_end.T[:, :, None], v_float, preci...]
    dot_general x6, matrix products: 14.5 us -> 21.2 us  [block_step(): jnp.einsum('thd,shd->hts', q_block, k_bf, preferred_element_type=jnp.floa...]
    unnamed x31 -> x34, local copies, waits for them, and re-layouts: 9.84 us -> 5.84 us
    another operation x27 -> x38, other arithmetic: 19.4 us -> 16.1 us
where the time goes in v5:
time: 298 us; the launch traced here: 296 us
  Pallas kernels  80.8 us (27%)
  matrix products  78.9 us (26%)
  local copies, waits for them, and re-layouts  72.1 us (24%)
  other arithmetic  45.8 us (15%)
  between operations  14.3 us (5%)
  waiting for transfers between devices  3.54 us (1%)
    pallas_call x1, Pallas kernels, both_scans_kernel(): pl.pallas_call(scan_kernel, out_shape=(out, out), in_specs=[pl.BlockSpec(...  67.2 us
    dot_general x6, matrix products, block_step(): jnp.einsum('thd,shd->hts', q_block, k_bf, preferred_element_type=jnp.floa...  21.2 us
    dot_general x6, matrix products, block_step(): jnp.einsum('hts,she->the', weights, v_block, preferred_element_type=jnp.f...  21.1 us
    while x118, local copies, waits for them, and re-layouts  20.3 us
    dot_general x6, matrix products, block_step(): jnp.einsum('shd,she->hde', k_float * to_end.T[:, :, None], v_float, preci...  18.5 us
    dynamic_update_slice x14, other arithmetic, run_blocks(): lax.scan(make_step(key_gain, head_width), start_state, (to_blocks(q_rows)...  16.5 us
    another operation x38, other arithmetic  16.1 us
    dot_general x6, matrix products, block_step(): jnp.einsum('thd,hde->the', q_float, carried, precision=PRECISE)  14 us
  transfers between devices with their start and end apart: 1, of which 1 were waited for; matrix products, arithmetic and copies ran while one was open for 3% of the time, Pallas kernels for 0%

profile of v5, /device:TPU:2, one launch (start us, length us, event | category | flops | bytes accessed | tf_op | source)
XLA Modules:
  0.0 296.3 jit_solution(12200425200891362321)
XLA Ops:
  7.2 2.3 reshape_squeeze.17
  10.6 1.6 copy.166
  13.4 1.7 copy.165
  21.9 2.8 multiply_convert_fusion.3
  28.5 2.9 fusion.123
  33.6 67.2 %shard_map.118 = (f32[4,128,128]{2,1,0:T(8,128)S(1)}, f32[4,128,128]{2,1,0:T(8,128)S(1)}) custom-call(f32[4,136,128]{2,1,0:T(8,128)} %get-tuple-element.1670.fwd_ref, f32[4,136,128]{2,1,0:T(8,128)} %get-tuple-element.1669.bwd_ref), custom_call_target="tpu_custom_call" | custom-call | tf_op jit(solution)/shard_map/pallas_call | solution.py:214
  100.9 69.9 %while.83 = (s32[]{:T(128)}, f32[4,128,128]{2,1,0:T(8,128)S(1)}, bf16[2,512,4,128]{1,3,2,0:T(8,128)(2,1)}, f32[2,512,4,128]{3,1,2,0:T(8,128)}, pred[2,4,512,512]...) while((s32[]{:T(128)}, f32[4,128,128]{2,1,0:T(8,128)S(1)}, ...), condition=%wide.region_11.12_spmd.clone, body=%wide.region_6.11_spmd.clone.sunk | while | flops 1364937216 | bytes 221041584 | solution.py:284
  106.3 3.8 %bitcast_dynamic-update-slice_fusion.13 = (f32[2,4,512,512]{3,2,1,0:T(8,128)}, f32[4,512,512]{2,1,0:T(8,128)S(1)}) fusion(f32[2,4,512,512]{3,2,1,0:T(8,128)} %get-tuple-element.2142, s32[]{:T(128)} %get-tuple-element.2134, bf16[512,4,128]{2,0,1:T(8,128)(2,1)S(1)} %fusion.181, bf16[2,512,4,128]{3,1,2,0:T(8,128)(2,1)} %get-tuple-element.2193), kind=kOutput, calls=%fused_computation.1.clone.1 | convolution fusion | flops 269484032 | bytes 9438208 | tf_op jit(solution)/shard_map/jvp()/while/body/eval_jaxpr/thd,shd->hts/dot_general | solution.py:254
  110.1 2.3 bitcast_dynamic-update-slice_fusion.12
  113.8 3.2 %fusion.186 = bf16[2,512,4,128]{1,3,2,0:T(8,128)(2,1)S(1)} fusion(bf16[2,512,4,128]{1,3,2,0:T(8,128)(2,1)S(1)} %copy-done.34, s32[]{:T(128)} %get-tuple-element.2134, f32[4,512,128]{1,2,0:T(8,128)S(1)} %get-tuple-element.2042, f32[512,4]{0,1:T(4,128)S(1)} %bitcast.457, bf16[2,512,4,128]{3,1,2,0:T(8,128)(2,1)} %get-tuple-element.2192, ...), kind=kOutput, calls=%fused_computation.14.clone.1 | convolution fusion | flops 275251200 | bytes 7103488 | tf_op jit(solution)/shard_map/jvp()/while/body/eval_jaxpr/hts,she->the/dot_general | solution.py:256
  118.4 2.8 select_dynamic-update-slice_fusion.2
  123.6 2.1 copy-done.15
  127.2 2.8 fusion.184
  133.2 2.7 convert_dynamic-update-slice_fusion.3
  141.2 3.9 %bitcast_dynamic-update-slice_fusion.13 = (f32[2,4,512,512]{3,2,1,0:T(8,128)}, f32[4,512,512]{2,1,0:T(8,128)S(1)}) fusion(f32[2,4,512,512]{3,2,1,0:T(8,128)} %get-tuple-element.2142, s32[]{:T(128)} %get-tuple-element.2134, bf16[512,4,128]{2,0,1:T(8,128)(2,1)S(1)} %fusion.181, bf16[2,512,4,128]{3,1,2,0:T(8,128)(2,1)} %get-tuple-element.2193), kind=kOutput, calls=%fused_computation.1.clone.1 | convolution fusion | flops 269484032 | bytes 9438208 | tf_op jit(solution)/shard_map/jvp()/while/body/eval_jaxpr/thd,shd->hts/dot_general | solution.py:254
  145.1 2.3 bitcast_dynamic-update-slice_fusion.12
  148.8 3.2 %fusion.186 = bf16[2,512,4,128]{1,3,2,0:T(8,128)(2,1)S(1)} fusion(bf16[2,512,4,128]{1,3,2,0:T(8,128)(2,1)S(1)} %copy-done.34, s32[]{:T(128)} %get-tuple-element.2134, f32[4,512,128]{1,2,0:T(8,128)S(1)} %get-tuple-element.2042, f32[512,4]{0,1:T(4,128)S(1)} %bitcast.457, bf16[2,512,4,128]{3,1,2,0:T(8,128)(2,1)} %get-tuple-element.2192, ...), kind=kOutput, calls=%fused_computation.14.clone.1 | convolution fusion | flops 275251200 | bytes 7103488 | tf_op jit(solution)/shard_map/jvp()/while/body/eval_jaxpr/hts,she->the/dot_general | solution.py:256
  153.4 2.8 select_dynamic-update-slice_fusion.2
  158.6 2.1 copy-done.15
  162.2 2.8 fusion.184
  168.1 2.7 convert_dynamic-update-slice_fusion.3
  175.2 86.1 %while.84 = (s32[]{:T(128)}, f32[4,128]{1,0:T(4,128)S(1)}, f32[4,128,128]{2,1,0:T(8,128)S(1)}, bf16[2,512,4,128]{3,2,1,0:T(4,128)(2,1)}, bf16[2,512,4,128]{3,2,1...) while((s32[]{:T(128)}, f32[4,128]{1,0:T(4,128)S(1)}, ...), condition=%wide.region_22.23_spmd.clone, body=%wide.region_12.22_spmd.clone.sunk | while | flops 2704036352 | bytes 121648944 | solution.py:284
  175.2 4.2 %fusion.202 = (f32[512,4]{0,1:T(4,128)S(1)}, bf16[512,4,128]{2,0,1:T(8,128)(2,1)}) fusion(f32[2,512,4,128]{3,1,2,0:T(8,128)} %get-tuple-element.2286, s32[]{:T(128)S(6)} %sub.190, f32[512,4]{0,1:T(4,128)S(1)} %dynamic-slice_bitcast_fusion.4, f32[4,128,128]{2,1,0:T(8,128)S(1)} %get-tuple-element.2232, f32[2,512,4,128]{3,1,2,0:T(8,128)} %get-tuple-element.2276), kind=kOutput, calls=%fused_computation.114.clone.1 | convolution fusion | flops 403699712 | bytes 2900992 | tf_op jit(solution)/shard_map/transpose(jvp())/while/body/eval_jaxpr/shd,she->hde/dot_general | solution.py:264
  179.7 1.5 copy-done.9
  181.2 5.2 %fusion.203 = (f32[4,512]{1,0:T(4,128)S(1)}, f32[4,512]{1,0:T(4,128)S(1)}, bf16[4,512,512]{2,1,0:T(8,128)(2,1)S(1)}) fusion(f32[2,4,512,512]{3,2,1,0:T(8,128)} %get-tuple-element.2294, s32[]{:T(128)S(6)} %sub.190, f32[2,4,512,512]{3,2,1,0:T(8,128)} %get-tuple-element.2293, pred[2,4,512,512]{3,2,1,0:T(32,128)(4,1)S(1)} %copy-done.9, ...), kind=kOutput, calls=%fused_computation.177.clone.1 | convolution fusion | flops 275771392 | bytes 13124608 | tf_op jit(solution)/shard_map/transpose(jvp())/while/body/eval_jaxpr/hts,she->the/dot_general | solution.py:256
  187.5 2.5 copy.259
  190.0 1.6 fusion.210
  192.0 5.0 %reduce-window.99 = f32[4,4,128]{2,1,0:T(4,128)S(1)} reduce-window(f32[4,4,128]{2,1,0:T(4,128)S(1)} %reshape.595, f32[]{:T(128)} %constant.203.clone.1..sunk.1), window={size=1x1x128 pad=0_0x0_0x0_127}, to_apply=%region_20.20 | reduce-window | flops 260096 | bytes 16388 | tf_op jit(solution)/shard_map/reduce-window.37
  198.1 3.2 %fusion.206 = bf16[4,512,128]{2,1,0:T(8,128)(2,1)S(1)} fusion(bf16[4,512,512]{2,1,0:T(8,128)(2,1)S(1)} %get-tuple-element.2093, f32[2,4,512,512]{3,2,1,0:T(8,128)} %get-tuple-element.2274, s32[]{:T(128)S(6)} %sub.190, bf16[2,512,4,128]{3,1,2,0:T(8,128)(2,1)} %get-tuple-element.2281), kind=kOutput, calls=%fused_computation.98.clone.1 | convolution fusion | flops 271843328 | bytes 7341056 | tf_op jit(solution)/shard_map/transpose(jvp())/while/body/eval_jaxpr/thd,shd->hts/dot_general | solution.py:254
  202.5 3.6 %fusion.204 = (bf16[1,512,4,128]{3,1,2,0:T(8,128)(2,1)S(1)}, f32[4,128]{1,0:T(4,128)S(1)}) fusion(f32[4,128]{1,0:T(4,128)S(1)} %bitcast.452, f32[2,512,4,128]{3,1,2,0:T(8,128)S(1)} %copy-done.8, s32[]{:T(128)S(6)} %sub.190, bf16[512,4,128]{2,0,1:T(8,128)(2,1)S(1)} %copy-done.1, bf16[2,512,4,128]{3,1,2,0:T(8,128)(2,1)} %get-tuple-element.2275, ...), kind=kOutput, calls=%fused_computation.130.clone.1 | convolution fusion | flops 273415680 | bytes 8918528 | tf_op jit(solution)/shard_map/transpose(jvp())/while/body/eval_jaxpr/thd,shd->hts/dot_general | solution.py:254
  209.0 2.1 fusion.208
  211.1 2.3 fusion.209
  214.7 3.5 %convolution_add_fusion.2 = f32[4,128,128]{2,1,0:T(8,128)S(1)} fusion(f32[2,512,4,128]{3,1,2,0:T(8,128)} %get-tuple-element.2279, s32[]{:T(128)S(6)} %sub.190, f32[1,512,4,128]{3,2,1,0:T(4,128)S(1)} %constant_dynamic-slice_fusion.17, f32[512,4]{0,1:T(4,128)S(1)} %dynamic-slice_bitcast_fusion.5, f32[4,128,128]{2,1,0:T(8,128)S(1)} %get-tuple-element.2232, ...), kind=kOutput, calls=%fused_computation.107.clone.1 | convolution fusion | flops 403046400 | bytes 2629652 | tf_op jit(solution)/shard_map/transpose(jvp())/while/body/eval_jaxpr/thd,hde->the/dot_general | solution.py:260
  218.2 4.2 %fusion.202 = (f32[512,4]{0,1:T(4,128)S(1)}, bf16[512,4,128]{2,0,1:T(8,128)(2,1)}) fusion(f32[2,512,4,128]{3,1,2,0:T(8,128)} %get-tuple-element.2286, s32[]{:T(128)S(6)} %sub.190, f32[512,4]{0,1:T(4,128)S(1)} %dynamic-slice_bitcast_fusion.4, f32[4,128,128]{2,1,0:T(8,128)S(1)} %get-tuple-element.2232, f32[2,512,4,128]{3,1,2,0:T(8,128)} %get-tuple-element.2276), kind=kOutput, calls=%fused_computation.114.clone.1 | convolution fusion | flops 403699712 | bytes 2900992 | tf_op jit(solution)/shard_map/transpose(jvp())/while/body/eval_jaxpr/shd,she->hde/dot_general | solution.py:264
  222.7 1.5 copy-done.9
  224.2 5.2 %fusion.203 = (f32[4,512]{1,0:T(4,128)S(1)}, f32[4,512]{1,0:T(4,128)S(1)}, bf16[4,512,512]{2,1,0:T(8,128)(2,1)S(1)}) fusion(f32[2,4,512,512]{3,2,1,0:T(8,128)} %get-tuple-element.2294, s32[]{:T(128)S(6)} %sub.190, f32[2,4,512,512]{3,2,1,0:T(8,128)} %get-tuple-element.2293, pred[2,4,512,512]{3,2,1,0:T(32,128)(4,1)S(1)} %copy-done.9, ...), kind=kOutput, calls=%fused_computation.177.clone.1 | convolution fusion | flops 275771392 | bytes 13124608 | tf_op jit(solution)/shard_map/transpose(jvp())/while/body/eval_jaxpr/hts,she->the/dot_general | solution.py:256
  230.5 2.5 copy.259
  233.1 1.6 fusion.210
  235.1 5.0 %reduce-window.99 = f32[4,4,128]{2,1,0:T(4,128)S(1)} reduce-window(f32[4,4,128]{2,1,0:T(4,128)S(1)} %reshape.595, f32[]{:T(128)} %constant.203.clone.1..sunk.1), window={size=1x1x128 pad=0_0x0_0x0_127}, to_apply=%region_20.20 | reduce-window | flops 260096 | bytes 16388 | tf_op jit(solution)/shard_map/reduce-window.37
  241.1 3.2 %fusion.206 = bf16[4,512,128]{2,1,0:T(8,128)(2,1)S(1)} fusion(bf16[4,512,512]{2,1,0:T(8,128)(2,1)S(1)} %get-tuple-element.2093, f32[2,4,512,512]{3,2,1,0:T(8,128)} %get-tuple-element.2274, s32[]{:T(128)S(6)} %sub.190, bf16[2,512,4,128]{3,1,2,0:T(8,128)(2,1)} %get-tuple-element.2281), kind=kOutput, calls=%fused_computation.98.clone.1 | convolution fusion | flops 271843328 | bytes 7341056 | tf_op jit(solution)/shard_map/transpose(jvp())/while/body/eval_jaxpr/thd,shd->hts/dot_general | solution.py:254
  245.6 3.6 %fusion.204 = (bf16[1,512,4,128]{3,1,2,0:T(8,128)(2,1)S(1)}, f32[4,128]{1,0:T(4,128)S(1)}) fusion(f32[4,128]{1,0:T(4,128)S(1)} %bitcast.452, f32[2,512,4,128]{3,1,2,0:T(8,128)S(1)} %copy-done.8, s32[]{:T(128)S(6)} %sub.190, bf16[512,4,128]{2,0,1:T(8,128)(2,1)S(1)} %copy-done.1, bf16[2,512,4,128]{3,1,2,0:T(8,128)(2,1)} %get-tuple-element.2275, ...), kind=kOutput, calls=%fused_computation.130.clone.1 | convolution fusion | flops 273415680 | bytes 8918528 | tf_op jit(solution)/shard_map/transpose(jvp())/while/body/eval_jaxpr/thd,shd->hts/dot_general | solution.py:254
  252.0 2.1 fusion.208
  254.1 2.3 fusion.209
  257.7 3.5 %convolution_add_fusion.2 = f32[4,128,128]{2,1,0:T(8,128)S(1)} fusion(f32[2,512,4,128]{3,1,2,0:T(8,128)} %get-tuple-element.2279, s32[]{:T(128)S(6)} %sub.190, f32[1,512,4,128]{3,2,1,0:T(4,128)S(1)} %constant_dynamic-slice_fusion.17, f32[512,4]{0,1:T(4,128)S(1)} %dynamic-slice_bitcast_fusion.5, f32[4,128,128]{2,1,0:T(8,128)S(1)} %get-tuple-element.2232, ...), kind=kOutput, calls=%fused_computation.107.clone.1 | convolution fusion | flops 403046400 | bytes 2629652 | tf_op jit(solution)/shard_map/transpose(jvp())/while/body/eval_jaxpr/thd,hde->the/dot_general | solution.py:260
  262.0 2.2 reshape.560
  265.5 2.2 reshape.562
  269.7 3.5 %reduce-scatter.4.cloned.1.call-done = f32[64,4]{1,0:T(8,128)} async-done(((f32[128,4]{1,0:T(8,128)}), f32[64,4]{1,0:T(8,128)}) %reduce-scatter.4.cloned.1.call-update) | async-done | bytes 1040
  274.6 13.6 %shard_map.119 = f32[4,64]{1,0:T(4,128)} custom-call(f32[4,64]{1,0:T(4,128)} %copy.168.part_ref), custom_call_target="tpu_custom_call" | custom-call | tf_op jit(solution)/shard_map/pallas_call | solution.py:112
  (320 shorter events, 72.0 us)
Async XLA Ops:
  7.2 266.0 %reduce-scatter.4.cloned.1.call-start = ((), (), s32[]{:S(2)}) async-start(), calls=%async_computation.1 | async-start | bytes 98304
  7.2 3.4 %copy-start.22 = (bf16[1,1024,512]{2,1,0:T(8,128)(2,1)S(1)}, bf16[1,1024,512]{2,1,0:T(8,128)(2,1)}, u32[]{:S(2)}) copy-start(bf16[1,1024,512]{2,1,0:T(8,128)(2,1)} %param.11) | copy-start | bytes 3145732
  17.3 4.6 %copy-start.37 = (f32[4,128]{1,0:T(4,128)S(1)}, f32[4,128]{1,0:T(4,128)}, u32[]{:S(2)}) copy-start(f32[4,128]{1,0:T(4,128)} %param.16) | copy-start | bytes 6148
  18.0 7.4 %copy-start.26 = (bf16[2,512,4,128]{3,2,1,0:T(4,128)(2,1)S(1)}, bf16[2,512,4,128]{3,2,1,0:T(4,128)(2,1)}, u32[]{:S(2)}) copy-start(bf16[2,512,4,128]{3,2,1,0:T(4,128)(2,1)} %reshape_squeeze.20) | copy-start | bytes 3145732
  21.9 4.5 %copy-start.27 = (bf16[2,512,4,128]{3,2,1,0:T(4,128)(2,1)S(1)}, bf16[2,512,4,128]{3,2,1,0:T(4,128)(2,1)}, u32[]{:S(2)}) copy-start(bf16[2,512,4,128]{3,2,1,0:T(4,128)(2,1)} %reshape_squeeze.21) | copy-start | bytes 3145732
  26.5 4.9 %copy-start.28 = (bf16[1024,4,128]{2,1,0:T(4,128)(2,1)S(1)}, bf16[1024,4,128]{2,1,0:T(4,128)(2,1)}, u32[]{:S(2)}) copy-start(bf16[1024,4,128]{2,1,0:T(4,128)(2,1)} %reshape.559) | copy-start | bytes 3145732
  27.6 3.8 %copy-start.21 = (f32[1,1024,512]{1,2,0:T(8,128)S(1)}, f32[1,1024,512]{1,2,0:T(8,128)}, u32[]{:S(2)}) copy-start(f32[1,1024,512]{1,2,0:T(8,128)} %copy.166) | copy-start | bytes 6291460
  106.3 3.9 %copy-start.10 = (f32[2,512,4,128]{1,3,2,0:T(8,128)S(1)}, f32[2,512,4,128]{1,3,2,0:T(8,128)}, u32[]{:S(2)}) copy-start(f32[2,512,4,128]{1,3,2,0:T(8,128)} %get-tuple-element.2149) | copy-start | bytes 6291460 | tf_op jit(solution)/shard_map/jvp()/while
  106.3 7.5 %copy-start.34 = (bf16[2,512,4,128]{1,3,2,0:T(8,128)(2,1)S(1)}, bf16[2,512,4,128]{1,3,2,0:T(8,128)(2,1)}, u32[]{:S(2)}) copy-start(bf16[2,512,4,128]{1,3,2,0:T(8,128)(2,1)} %get-tuple-element.2136) | copy-start | bytes 3145732 | tf_op jit(solution)/shard_map/jvp()/while
  110.1 8.3 %slice-start = ((s8[8388608]{0:T(1024)(128)(4,1)}), s8[4194304]{0:T(1024)(128)(4,1)S(1)}, s32[]{:S(2)}) async-start(s8[8388608]{0:T(1024)(128)(4,1)} %bitcast.441), calls=%async_computation.2 | async-start | bytes 8388608 | tf_op jit(solution)/shard_map/jvp()/while
  113.8 3.3 %copy-start.2 = (bf16[2,4,512,512]{3,2,1,0:T(8,128)(2,1)S(1)}, bf16[2,4,512,512]{3,2,1,0:T(8,128)(2,1)}, u32[]{:S(2)}) copy-start(bf16[2,4,512,512]{3,2,1,0:T(8,128)(2,1)} %get-tuple-element.2143) | copy-start | bytes 12582916 | tf_op jit(solution)/shard_map/jvp()/while
  113.8 4.6 %slice-start.1 = ((s8[8388608]{0:T(1024)(128)(4,1)}), s8[4194304]{0:T(1024)(128)(4,1)S(1)}, s32[]{:S(2)}) async-start(s8[8388608]{0:T(1024)(128)(4,1)} %bitcast.441), calls=%async_computation.3 | async-start | bytes 8388608 | tf_op jit(solution)/shard_map/jvp()/while
  118.4 4.1 %copy-start.3 = (bf16[2,4,512,512]{3,2,1,0:T(8,128)(2,1)}, bf16[2,4,512,512]{3,2,1,0:T(8,128)(2,1)S(1)}, u32[]{:S(2)}) copy-start(bf16[2,4,512,512]{3,2,1,0:T(8,128)(2,1)S(1)} %bitcast_dynamic-update-slice_fusion.14) | copy-start | bytes 12582916 | tf_op jit(solution)/shard_map/jvp()/while
  118.4 4.2 %copy-start.6 = (f32[2,512,4,128]{3,1,2,0:T(8,128)S(1)}, f32[2,512,4,128]{3,1,2,0:T(8,128)}, u32[]{:S(2)}) copy-start(f32[2,512,4,128]{3,1,2,0:T(8,128)} %get-tuple-element.2137) | copy-start | bytes 6291460 | tf_op jit(solution)/shard_map/jvp()/while
  118.4 5.2 %copy-start.13 = (f32[2,512,4,128]{3,1,2,0:T(8,128)S(1)}, f32[2,512,4,128]{3,1,2,0:T(8,128)}, u32[]{:S(2)}) copy-start(f32[2,512,4,128]{3,1,2,0:T(8,128)} %get-tuple-element.2155) | copy-start | bytes 6291460 | tf_op jit(solution)/shard_map/jvp()/while
  118.4 7.4 %copy-start.15 = (f32[2,512,4,128]{3,1,2,0:T(8,128)S(1)}, f32[2,512,4,128]{3,1,2,0:T(8,128)}, u32[]{:S(2)}) copy-start(f32[2,512,4,128]{3,1,2,0:T(8,128)} %get-tuple-element.2153) | copy-start | bytes 6291460 | tf_op jit(solution)/shard_map/jvp()/while
  122.5 7.5 %copy-start = (f32[2,4,512,512]{3,2,1,0:T(8,128)}, f32[2,4,512,512]{3,2,1,0:T(8,128)S(1)}, u32[]{:S(2)}) copy-start(f32[2,4,512,512]{3,2,1,0:T(8,128)S(1)} %get-tuple-element.2170) | copy-start | bytes 25165828 | tf_op jit(solution)/shard_map/jvp()/while
  126.2 3.9 %copy-start.7 = (f32[2,512,4,128]{3,1,2,0:T(8,128)}, f32[2,512,4,128]{3,1,2,0:T(8,128)S(1)}, u32[]{:S(2)}) copy-start(f32[2,512,4,128]{3,1,2,0:T(8,128)S(1)} %get-tuple-element.2168) | copy-start | bytes 6291460 | tf_op jit(solution)/shard_map/jvp()/while
  126.2 3.9 %copy-start.14 = (f32[2,512,4,128]{3,1,2,0:T(8,128)}, f32[2,512,4,128]{3,1,2,0:T(8,128)S(1)}, u32[]{:S(2)}) copy-start(f32[2,512,4,128]{3,1,2,0:T(8,128)S(1)} %get-tuple-element.2186) | copy-start | bytes 6291460 | tf_op jit(solution)/shard_map/jvp()/while
  126.2 3.9 %copy-start.16 = (f32[2,512,4,128]{3,1,2,0:T(8,128)}, f32[2,512,4,128]{3,1,2,0:T(8,128)S(1)}, u32[]{:S(2)}) copy-start(f32[2,512,4,128]{3,1,2,0:T(8,128)S(1)} %get-tuple-element.2184) | copy-start | bytes 6291460 | tf_op jit(solution)/shard_map/jvp()/while
  141.2 3.9 %copy-start.10 = (f32[2,512,4,128]{1,3,2,0:T(8,128)S(1)}, f32[2,512,4,128]{1,3,2,0:T(8,128)}, u32[]{:S(2)}) copy-start(f32[2,512,4,128]{1,3,2,0:T(8,128)} %get-tuple-element.2149) | copy-start | bytes 6291460 | tf_op jit(solution)/shard_map/jvp()/while
  141.2 7.6 %copy-start.34 = (bf16[2,512,4,128]{1,3,2,0:T(8,128)(2,1)S(1)}, bf16[2,512,4,128]{1,3,2,0:T(8,128)(2,1)}, u32[]{:S(2)}) copy-start(bf16[2,512,4,128]{1,3,2,0:T(8,128)(2,1)} %get-tuple-element.2136) | copy-start | bytes 3145732 | tf_op jit(solution)/shard_map/jvp()/while
  145.1 8.3 %slice-start = ((s8[8388608]{0:T(1024)(128)(4,1)}), s8[4194304]{0:T(1024)(128)(4,1)S(1)}, s32[]{:S(2)}) async-start(s8[8388608]{0:T(1024)(128)(4,1)} %bitcast.441), calls=%async_computation.2 | async-start | bytes 8388608 | tf_op jit(solution)/shard_map/jvp()/while
  148.8 3.3 %copy-start.2 = (bf16[2,4,512,512]{3,2,1,0:T(8,128)(2,1)S(1)}, bf16[2,4,512,512]{3,2,1,0:T(8,128)(2,1)}, u32[]{:S(2)}) copy-start(bf16[2,4,512,512]{3,2,1,0:T(8,128)(2,1)} %get-tuple-element.2143) | copy-start | bytes 12582916 | tf_op jit(solution)/shard_map/jvp()/while
  148.8 4.6 %slice-start.1 = ((s8[8388608]{0:T(1024)(128)(4,1)}), s8[4194304]{0:T(1024)(128)(4,1)S(1)}, s32[]{:S(2)}) async-start(s8[8388608]{0:T(1024)(128)(4,1)} %bitcast.441), calls=%async_computation.3 | async-start | bytes 8388608 | tf_op jit(solution)/shard_map/jvp()/while
  153.3 4.1 %copy-start.3 = (bf16[2,4,512,512]{3,2,1,0:T(8,128)(2,1)}, bf16[2,4,512,512]{3,2,1,0:T(8,128)(2,1)S(1)}, u32[]{:S(2)}) copy-start(bf16[2,4,512,512]{3,2,1,0:T(8,128)(2,1)S(1)} %bitcast_dynamic-update-slice_fusion.14) | copy-start | bytes 12582916 | tf_op jit(solution)/shard_map/jvp()/while
  153.4 4.2 %copy-start.6 = (f32[2,512,4,128]{3,1,2,0:T(8,128)S(1)}, f32[2,512,4,128]{3,1,2,0:T(8,128)}, u32[]{:S(2)}) copy-start(f32[2,512,4,128]{3,1,2,0:T(8,128)} %get-tuple-element.2137) | copy-start | bytes 6291460 | tf_op jit(solution)/shard_map/jvp()/while
  153.4 5.2 %copy-start.13 = (f32[2,512,4,128]{3,1,2,0:T(8,128)S(1)}, f32[2,512,4,128]{3,1,2,0:T(8,128)}, u32[]{:S(2)}) copy-start(f32[2,512,4,128]{3,1,2,0:T(8,128)} %get-tuple-element.2155) | copy-start | bytes 6291460 | tf_op jit(solution)/shard_map/jvp()/while
  153.4 7.4 %copy-start.15 = (f32[2,512,4,128]{3,1,2,0:T(8,128)S(1)}, f32[2,512,4,128]{3,1,2,0:T(8,128)}, u32[]{:S(2)}) copy-start(f32[2,512,4,128]{3,1,2,0:T(8,128)} %get-tuple-element.2153) | copy-start | bytes 6291460 | tf_op jit(solution)/shard_map/jvp()/while
  157.5 7.5 %copy-start = (f32[2,4,512,512]{3,2,1,0:T(8,128)}, f32[2,4,512,512]{3,2,1,0:T(8,128)S(1)}, u32[]{:S(2)}) copy-start(f32[2,4,512,512]{3,2,1,0:T(8,128)S(1)} %get-tuple-element.2170) | copy-start | bytes 25165828 | tf_op jit(solution)/shard_map/jvp()/while
  161.1 3.9 %copy-start.7 = (f32[2,512,4,128]{3,1,2,0:T(8,128)}, f32[2,512,4,128]{3,1,2,0:T(8,128)S(1)}, u32[]{:S(2)}) copy-start(f32[2,512,4,128]{3,1,2,0:T(8,128)S(1)} %get-tuple-element.2168) | copy-start | bytes 6291460 | tf_op jit(solution)/shard_map/jvp()/while
  161.1 3.9 %copy-start.14 = (f32[2,512,4,128]{3,1,2,0:T(8,128)}, f32[2,512,4,128]{3,1,2,0:T(8,128)S(1)}, u32[]{:S(2)}) copy-start(f32[2,512,4,128]{3,1,2,0:T(8,128)S(1)} %get-tuple-element.2186) | copy-start | bytes 6291460 | tf_op jit(solution)/shard_map/jvp()/while
  161.2 3.9 %copy-start.16 = (f32[2,512,4,128]{3,1,2,0:T(8,128)}, f32[2,512,4,128]{3,1,2,0:T(8,128)S(1)}, u32[]{:S(2)}) copy-start(f32[2,512,4,128]{3,1,2,0:T(8,128)S(1)} %get-tuple-element.2184) | copy-start | bytes 6291460 | tf_op jit(solution)/shard_map/jvp()/while
  175.2 4.5 %copy-start.4 = (f32[2,512,4,128]{3,2,1,0:T(4,128)}, f32[2,512,4,128]{3,2,1,0:T(4,128)S(1)}, u32[]{:S(2)}) copy-start(f32[2,512,4,128]{3,2,1,0:T(4,128)S(1)} %get-tuple-element.2272) | copy-start | bytes 6291460 | tf_op jit(solution)/shard_map/transpose(jvp())/while
  181.2 5.2 %copy-start.12 = (f32[2,512,4,128]{1,3,2,0:T(8,128)S(1)}, f32[2,512,4,128]{1,3,2,0:T(8,128)}, u32[]{:S(2)}) copy-start(f32[2,512,4,128]{1,3,2,0:T(8,128)} %get-tuple-element.2289) | copy-start | bytes 6291460 | tf_op jit(solution)/shard_map/transpose(jvp())/while
  198.1 3.2 %copy-start.20 = (f32[2,4,128,128]{3,2,1,0:T(8,128)S(1)}, f32[2,4,128,128]{3,2,1,0:T(8,128)}, u32[]{:S(2)}) copy-start(f32[2,4,128,128]{3,2,1,0:T(8,128)} %get-tuple-element.2282) | copy-start | bytes 1572868 | tf_op jit(solution)/shard_map/transpose(jvp())/while
  198.1 4.4 %copy-start.8 = (f32[2,512,4,128]{3,1,2,0:T(8,128)S(1)}, f32[2,512,4,128]{3,1,2,0:T(8,128)}, u32[]{:S(2)}) copy-start(f32[2,512,4,128]{3,1,2,0:T(8,128)} %get-tuple-element.2271) | copy-start | bytes 6291460 | tf_op jit(solution)/shard_map/transpose(jvp())/while
  202.5 3.6 %copy-start.29 = (bf16[2,512,4,128]{3,2,1,0:T(4,128)(2,1)S(1)}, bf16[2,512,4,128]{3,2,1,0:T(4,128)(2,1)}, u32[]{:S(2)}) copy-start(bf16[2,512,4,128]{3,2,1,0:T(4,128)(2,1)} %get-tuple-element.2233) | copy-start | bytes 3145732 | tf_op jit(solution)/shard_map/transpose(jvp())/while
  202.5 3.6 %copy-start.31 = (bf16[2,512,4,128]{3,2,1,0:T(4,128)(2,1)S(1)}, bf16[2,512,4,128]{3,2,1,0:T(4,128)(2,1)}, u32[]{:S(2)}) copy-start(bf16[2,512,4,128]{3,2,1,0:T(4,128)(2,1)} %get-tuple-element.2234) | copy-start | bytes 3145732 | tf_op jit(solution)/shard_map/transpose(jvp())/while
  214.7 3.5 %copy-start.5 = (f32[2,512,4,128]{3,2,1,0:T(4,128)S(1)}, f32[2,512,4,128]{3,2,1,0:T(4,128)}, u32[]{:S(2)}) copy-start(f32[2,512,4,128]{3,2,1,0:T(4,128)} %copy-done.4) | copy-start | bytes 6291460 | tf_op jit(solution)/shard_map/transpose(jvp())/while
  218.2 4.5 %copy-start.4 = (f32[2,512,4,128]{3,2,1,0:T(4,128)}, f32[2,512,4,128]{3,2,1,0:T(4,128)S(1)}, u32[]{:S(2)}) copy-start(f32[2,512,4,128]{3,2,1,0:T(4,128)S(1)} %get-tuple-element.2272) | copy-start | bytes 6291460 | tf_op jit(solution)/shard_map/transpose(jvp())/while
  224.2 5.2 %copy-start.12 = (f32[2,512,4,128]{1,3,2,0:T(8,128)S(1)}, f32[2,512,4,128]{1,3,2,0:T(8,128)}, u32[]{:S(2)}) copy-start(f32[2,512,4,128]{1,3,2,0:T(8,128)} %get-tuple-element.2289) | copy-start | bytes 6291460 | tf_op jit(solution)/shard_map/transpose(jvp())/while
  241.1 3.2 %copy-start.20 = (f32[2,4,128,128]{3,2,1,0:T(8,128)S(1)}, f32[2,4,128,128]{3,2,1,0:T(8,128)}, u32[]{:S(2)}) copy-start(f32[2,4,128,128]{3,2,1,0:T(8,128)} %get-tuple-element.2282) | copy-start | bytes 1572868 | tf_op jit(solution)/shard_map/transpose(jvp())/while
  241.1 4.4 %copy-start.8 = (f32[2,512,4,128]{3,1,2,0:T(8,128)S(1)}, f32[2,512,4,128]{3,1,2,0:T(8,128)}, u32[]{:S(2)}) copy-start(f32[2,512,4,128]{3,1,2,0:T(8,128)} %get-tuple-element.2271) | copy-start | bytes 6291460 | tf_op jit(solution)/shard_map/transpose(jvp())/while
  245.6 3.6 %copy-start.29 = (bf16[2,512,4,128]{3,2,1,0:T(4,128)(2,1)S(1)}, bf16[2,512,4,128]{3,2,1,0:T(4,128)(2,1)}, u32[]{:S(2)}) copy-start(bf16[2,512,4,128]{3,2,1,0:T(4,128)(2,1)} %get-tuple-element.2233) | copy-start | bytes 3145732 | tf_op jit(solution)/shard_map/transpose(jvp())/while
  245.6 3.6 %copy-start.31 = (bf16[2,512,4,128]{3,2,1,0:T(4,128)(2,1)S(1)}, bf16[2,512,4,128]{3,2,1,0:T(4,128)(2,1)}, u32[]{:S(2)}) copy-start(bf16[2,512,4,128]{3,2,1,0:T(4,128)(2,1)} %get-tuple-element.2234) | copy-start | bytes 3145732 | tf_op jit(solution)/shard_map/transpose(jvp())/while
  257.7 3.5 %copy-start.5 = (f32[2,512,4,128]{3,2,1,0:T(4,128)S(1)}, f32[2,512,4,128]{3,2,1,0:T(4,128)}, u32[]{:S(2)}) copy-start(f32[2,512,4,128]{3,2,1,0:T(4,128)} %copy-done.4) | copy-start | bytes 6291460 | tf_op jit(solution)/shard_map/transpose(jvp())/while
  264.3 3.4 %copy-start.36 = (bf16[2,512,4,128]{1,3,2,0:T(8,128)(2,1)S(1)}, bf16[2,512,4,128]{1,3,2,0:T(8,128)(2,1)}, u32[]{:S(2)}) copy-start(bf16[2,512,4,128]{1,3,2,0:T(8,128)(2,1)} %get-tuple-element.1091) | copy-start | bytes 3145732
  (24 other events, 41.3 us)
Sparse Core Ops, SparseCore 0:
  262.1 11.0 reduce-scatter.3

commit v6 on v4

--- a/solution.py
+++ b/solution.py
@@ -62,26 +62,43 @@
     return scans[0][3], scans[1][3]
 
 
-def gain_sum_kernel(part_ref, total_ref, slots, send_sem, recv_sem):
+def gain_sum_kernel(part_ref, total_ref, pair_slot, slots, pair_sem, send_sem, recv_sem):
     count = slots.shape[0]
     me = lax.axis_index("ctx")
     row, col = lax.axis_index("dp"), lax.axis_index("head")
+    other = 1 - row
 
     def peer_of(step):
         return lax.rem(me + step, count)
 
     barrier = pltpu.get_barrier_semaphore()
+    pl.semaphore_signal(
+        barrier, inc=1, device_id=(other, me, col), device_id_type=pl.DeviceIdType.MESH
+    )
     for step in range(1, count):
         pl.semaphore_signal(
             barrier, inc=1, device_id=(row, peer_of(step), col), device_id_type=pl.DeviceIdType.MESH
         )
-    pl.semaphore_wait(barrier, count - 1)
+    pl.semaphore_wait(barrier, count)
+
+    pair = pltpu.make_async_remote_copy(
+        src_ref=part_ref.at[other],
+        dst_ref=pair_slot,
+        send_sem=pair_sem.at[0],
+        recv_sem=pair_sem.at[1],
+        device_id=(other, me, col),
+        device_id_type=pl.DeviceIdType.MESH,
+    )
+    pair.start()
+    pair.wait_send()
+    pair.wait_recv()
+    slots[me] = part_ref[row] + pair_slot[...]
 
     copies = []
     for step in range(1, count):
         peer = peer_of(step)
         copy = pltpu.make_async_remote_copy(
-            src_ref=part_ref,
+            src_ref=slots.at[me],
             dst_ref=slots.at[me],
             send_sem=send_sem.at[peer],
             recv_sem=recv_sem.at[me],
@@ -90,12 +107,11 @@
         )
         copy.start()
         copies.append(copy)
-    slots[me] = part_ref[...]
     for step in range(1, count):
         copies[step - 1].wait_send()
         source = lax.rem(me + count - step, count)
         pltpu.make_async_remote_copy(
-            src_ref=part_ref,
+            src_ref=slots.at[source],
             dst_ref=slots.at[source],
             send_sem=send_sem.at[source],
             recv_sem=recv_sem.at[source],
@@ -109,18 +125,23 @@
 
 
 def gain_sum(part, count):
+    heads, width = part.shape
+    halves = part.reshape(heads, 2, width // 2).transpose(1, 0, 2)
+    shape = halves.shape[1:]
     return pl.pallas_call(
         gain_sum_kernel,
-        out_shape=jax.ShapeDtypeStruct(part.shape, part.dtype),
+        out_shape=jax.ShapeDtypeStruct(shape, part.dtype),
         in_specs=[pl.BlockSpec(memory_space=pltpu.VMEM)],
         out_specs=pl.BlockSpec(memory_space=pltpu.VMEM),
         scratch_shapes=[
-            pltpu.VMEM((count,) + part.shape, part.dtype),
+            pltpu.VMEM(shape, part.dtype),
+            pltpu.VMEM((count,) + shape, part.dtype),
+            pltpu.SemaphoreType.DMA((2,)),
             pltpu.SemaphoreType.DMA((count,)),
             pltpu.SemaphoreType.DMA((count,)),
         ],
         compiler_params=pltpu.CompilerParams(collective_id=0, has_side_effects=True),
-    )(part)
+    )(halves)
 
 
 def scan_kernel(fwd_ref, bwd_ref, fwd_out, bwd_out, aggs, exs, slots, send_sem, recv_sem):
@@ -319,8 +340,7 @@
     (primal, end_state), pullback = jax.vjp(forward, q_rows, k_rows, v_rows, gate_rows, key_gain)
     cot_float = cotangent[0].astype(jnp.float32)
     grad_q, grad_k, grad_v, grad_a, gain_term = pullback((cot_float, later_grad))
-    gain_half = lax.psum_scatter(gain_term, "dp", scatter_dimension=1, tiled=True)
-    grad_gain = gain_sum(gain_half, ctx_size)
+    grad_gain = gain_sum(gain_term, ctx_size)
     return (
         primal.astype(jnp.bfloat16)[None],
         grad_q[None],

time: 260 us -> 243 us (0.935)
  between operations: 14.3 us -> 0.83 us
  waiting for transfers between devices: 2.87 us -> 0 us
    unnamed x2 -> x0, waiting for transfers between devices: 2.87 us -> none
    unnamed x31 -> x21, local copies, waits for them, and re-layouts: 9.84 us -> 8.32 us
  transfers between devices with their start and end apart: 1 -> 0, of which waited for: 1 -> 0; matrix products, arithmetic and copies ran while one was open for 3% -> 0% of each run, Pallas kernels for 0% -> 0%
where the time goes in v6:
time: 243 us; the launch traced here: 241 us
  Pallas kernels  80.9 us (33%)
  matrix products  65.6 us (27%)
  local copies, waits for them, and re-layouts  60.6 us (25%)
  other arithmetic  32.1 us (13%)
    pallas_call x1, Pallas kernels, both_scans_kernel(): pl.pallas_call(scan_kernel, out_shape=(out, out), in_specs=[pl.BlockSpec(...  67.2 us
    another operation x27, other arithmetic  20 us
    dot_general x6, matrix products, block_step(): jnp.einsum('hts,she->the', weights, v_block, preferred_element_type=jnp.f...  19.2 us
    dot_general x8, matrix products, block_step(): jnp.einsum('thd,hde->the', q_float, carried, precision=PRECISE)  15.6 us
    dot_general x6, matrix products, block_step(): jnp.einsum('thd,shd->hts', q_block, k_bf, preferred_element_type=jnp.floa...  14.5 us
    pallas_call x1, Pallas kernels, gain_sum(): pl.pallas_call(gain_sum_kernel, out_shape=jax.ShapeDtypeStruct(shape, par...  13.7 us
    dot_general x6, matrix products, block_step(): jnp.einsum('shd,she->hde', k_float * to_end.T[:, :, None], v_float, preci...  11.3 us
    squeeze x10, local copies, waits for them, and re-layouts, run_blocks(): lax.scan(jax.checkpoint(make_step(key_gain, head_width)), start_state, (t...  10.2 us

profile of v6, /device:TPU:2, one launch (start us, length us, event | category | flops | bytes accessed | tf_op | source)
XLA Modules:
  0.0 240.7 jit_solution(3769154643077457730)
XLA Ops:
  6.6 1.6 copy.255
  8.2 2.1 reshape.591
  11.6 2.5 %fusion.107 = f32[4,128,128]{2,1,0:T(8,128)S(1)} fusion(f32[1024,4,128]{0,2,1:T(8,128)S(1)} %bitcast.342, bf16[1024,4,128]{2,1,0:T(4,128)(2,1)} %reshape.591, f32[1024,4]{0,1:T(4,128)S(1)} %get-tuple-element.774), kind=kOutput, calls=%fused_computation.159 | convolution fusion | flops 805830656 | bytes 3424256 | tf_op jit(solution)/shard_map/thd,the->hde/dot_general | solution.py:29
  15.8 1.3 reshape_squeeze.17
  17.2 2.5 %fusion.109 = f32[4,128,128]{2,1,0:T(8,128)S(1)} fusion(bf16[1024,4,128]{0,2,1:T(8,128)(2,1)} %multiply_convert_fusion.6, bf16[1024,4,128]{2,1,0:T(4,128)(2,1)S(1)} %reshape_squeeze.17, f32[1024,4]{0,1:T(4,128)S(1)} %get-tuple-element.775), kind=kOutput, calls=%fused_computation.161 | convolution fusion | flops 806354944 | bytes 2375680 | tf_op jit(solution)/shard_map/shd,she->hde/dot_general | solution.py:330
  20.6 67.2 %shard_map.118 = (f32[4,128,128]{2,1,0:T(8,128)S(1)}, f32[4,128,128]{2,1,0:T(8,128)S(1)}) custom-call(f32[4,136,128]{2,1,0:T(8,128)} %get-tuple-element.773.fwd_ref, f32[4,136,128]{2,1,0:T(8,128)} %get-tuple-element.772.bwd_ref), custom_call_target="tpu_custom_call" | custom-call | tf_op jit(solution)/shard_map/pallas_call | solution.py:235
  88.9 1.4 copy.230
  90.4 2.1 reshape_squeeze.20
  92.5 2.3 copy.231
  96.0 2.4 %copy.232 = bf16[2,512,4,128]{3,1,2,0:T(8,128)(2,1)} copy(bf16[2,512,4,128]{3,2,1,0:T(4,128)(2,1)} %reshape_squeeze.21) | data formatting | bytes 2097152
  98.4 27.3 %while.42 = (s32[]{:T(128)}, f32[4,128,128]{2,1,0:T(8,128)S(1)}, bf16[2,512,4,128]{1,3,2,0:T(8,128)(2,1)}, f32[2,4,128,128]{3,2,1,0:T(8,128)}, f32[2,4,512]{2,1,...) while((s32[]{:T(128)}, f32[4,128,128]{2,1,0:T(8,128)S(1)}, ...), condition=%wide.region_11.12_spmd.clone, body=%wide.region_6.11_spmd.clone.sunk | while | flops 1352081408 | bytes 9343697 | solution.py:305
  101.7 3.3 %fusion.191 = f32[512,4,128]{0,2,1:T(8,128)S(1)} fusion(bf16[512,4,128]{2,0,1:T(8,128)(2,1)S(1)} %fusion.189, f32[4,512]{1,0:T(4,128)S(1)} %bitcast.354, pred[512,512]{1,0:T(8,128)(4,1)S(1)} %fusion.190, bf16[2,512,4,128]{3,1,2,0:T(8,128)(2,1)} %get-tuple-element.1015, s32[]{:T(128)S(6)} %copy.332, bf16[2,512,4,128]{3,1,2,0:T(8,128)(2,1)} %get-tuple-element.1014), kind=kOutput, calls=%fused_computation.3.clone.1 | convolution fusion | flops 543162368 | bytes 2900992 | tf_op jit(solution)/shard_map/jvp()/while/body/eval_jaxpr/hts,she->the/dot_general | solution.py:277
  106.5 3.0 %fusion.192 = bf16[2,512,4,128]{1,3,2,0:T(8,128)(2,1)} fusion(bf16[2,512,4,128]{1,3,2,0:T(8,128)(2,1)} %get-tuple-element.996, s32[]{:T(128)S(6)} %copy.332, f32[512,4,128]{0,2,1:T(8,128)S(1)} %fusion.191, f32[4,128,128]{2,1,0:T(8,128)S(1)} %get-tuple-element.995, f32[512,4]{0,1:T(4,128)S(1)} %bitcast.346, ...), kind=kOutput, calls=%fused_computation.8.clone.1 | convolution fusion | flops 403701760 | bytes 2892800 | tf_op jit(solution)/shard_map/jvp()/while/body/eval_jaxpr/thd,hde->the/dot_general | solution.py:281
  109.7 2.4 convolution_add_fusion.4
  115.4 3.3 %fusion.191 = f32[512,4,128]{0,2,1:T(8,128)S(1)} fusion(bf16[512,4,128]{2,0,1:T(8,128)(2,1)S(1)} %fusion.189, f32[4,512]{1,0:T(4,128)S(1)} %bitcast.354, pred[512,512]{1,0:T(8,128)(4,1)S(1)} %fusion.190, bf16[2,512,4,128]{3,1,2,0:T(8,128)(2,1)} %get-tuple-element.1015, s32[]{:T(128)S(6)} %copy.332, bf16[2,512,4,128]{3,1,2,0:T(8,128)(2,1)} %get-tuple-element.1014), kind=kOutput, calls=%fused_computation.3.clone.1 | convolution fusion | flops 543162368 | bytes 2900992 | tf_op jit(solution)/shard_map/jvp()/while/body/eval_jaxpr/hts,she->the/dot_general | solution.py:277
  120.2 3.0 %fusion.192 = bf16[2,512,4,128]{1,3,2,0:T(8,128)(2,1)} fusion(bf16[2,512,4,128]{1,3,2,0:T(8,128)(2,1)} %get-tuple-element.996, s32[]{:T(128)S(6)} %copy.332, f32[512,4,128]{0,2,1:T(8,128)S(1)} %fusion.191, f32[4,128,128]{2,1,0:T(8,128)S(1)} %get-tuple-element.995, f32[512,4]{0,1:T(4,128)S(1)} %bitcast.346, ...), kind=kOutput, calls=%fused_computation.8.clone.1 | convolution fusion | flops 403701760 | bytes 2892800 | tf_op jit(solution)/shard_map/jvp()/while/body/eval_jaxpr/thd,hde->the/dot_general | solution.py:281
  123.3 2.4 convolution_add_fusion.4
  125.7 1.8 copy.233
  128.8 1.7 reshape.602
  131.7 1.2 broadcast.246.clone2
  132.9 1.2 broadcast.246.clone2.1
  134.2 85.1 %while.43 = (s32[]{:T(128)}, f32[4,128]{1,0:T(4,128)S(1)}, f32[4,128,128]{2,1,0:T(8,128)S(1)}, bf16[2,512,4,128]{3,2,1,0:T(4,128)(2,1)}, bf16[2,512,4,128]{3,2,1...) while((s32[]{:T(128)}, f32[4,128]{1,0:T(4,128)S(1)}, ...), condition=%wide.region_26.27_spmd.clone, body=%wide.region_12.26_spmd.clone.sunk | while | flops 3394863616 | bytes 116524784 | solution.py:305
  134.2 1.3 dynamic-slice_bitcast_fusion.10
  137.4 1.9 dynamic-slice_bitcast_fusion.13
  144.8 1.9 fusion.210
  147.7 2.5 %fusion.213 = (f32[4,512]{1,0:T(4,128)S(1)}, f32[4,512]{1,0:T(4,128)S(1)}, bf16[4,512,512]{2,1,0:T(8,128)(2,1)S(1)}) fusion(f32[4,512]{1,0:T(4,128)S(1)} %bitcast.350, f32[4,512,512]{2,1,0:T(8,128)S(1)} %fusion.211, pred[512,512]{1,0:T(8,128)(4,1)S(1)} %fusion.212, bf16[512,4,128]{2,0,1:T(8,128)(2,1)S(1)} %copy-done.1, f32[512,4,128]{0,2,1:T(8,128)S(1)} %bitcast.337), kind=kOutput, calls=%fused_computation.107.clone.1 | convolution fusion | flops 278917120 | bytes 8151040 | tf_op jit(solution)/shard_map/transpose(jvp())/while/body/eval_jaxpr/checkpoint/hts,she->the/dot_general | solution.py:277
  150.3 3.2 %fusion.214 = (bf16[1,512,4,128]{3,1,2,0:T(8,128)(2,1)}, f32[4,128]{1,0:T(4,128)S(1)}) fusion(f32[4,128]{1,0:T(4,128)S(1)} %get-tuple-element.960, bf16[512,4,128]{2,0,1:T(8,128)(2,1)S(1)} %copy-done.2, bf16[512,4,128]{2,0,1:T(8,128)(2,1)S(1)} %get-tuple-element.967, bf16[512,4,128]{2,0,1:T(8,128)(2,1)S(1)} %dynamic-slice_bitcast_fusion.11, ...), kind=kOutput, calls=%fused_computation.110.clone.1 | convolution fusion | flops 276823552 | bytes 4468736 | tf_op jit(solution)/shard_map/transpose(jvp())/while/body/eval_jaxpr/checkpoint/thd,shd->hts/dot_general | solution.py:275
  153.5 3.8 %fusion.220 = bf16[4,128,512]{2,1,0:T(8,128)(2,1)S(1)} fusion(f32[4,512,512]{2,1,0:T(8,128)} %copy-done, f32[4,512]{1,0:T(4,128)S(1)} %bitcast.352, pred[512,512]{1,0:T(8,128)(4,1)S(1)} %fusion.212, f32[512,4,128]{0,2,1:T(8,128)S(1)} %bitcast.338), kind=kOutput, calls=%fused_computation.81.clone.1 | convolution fusion | flops 274726912 | bytes 6037504 | tf_op jit(solution)/shard_map/transpose(jvp())/while/body/eval_jaxpr/checkpoint/hts,she->the/dot_general | solution.py:277
  157.3 1.4 fusion.221
  160.5 1.9 convolution_add_fusion.5
  162.5 3.3 %fusion.218 = bf16[4,512,128]{2,1,0:T(8,128)(2,1)S(1)} fusion(bf16[512,4,128]{2,0,1:T(8,128)(2,1)S(1)} %fusion.209, bf16[4,512,512]{2,1,0:T(8,128)(2,1)} %copy-done.18, f32[4,512]{1,0:T(4,128)S(1)} %bitcast.353, pred[512,512]{1,0:T(8,128)(4,1)S(1)} %fusion.212), kind=kOutput, calls=%fused_computation.85.clone.1 | convolution fusion | flops 274989056 | bytes 3416064 | tf_op jit(solution)/shard_map/transpose(jvp())/while/body/eval_jaxpr/checkpoint/thd,shd->hts/dot_general | solution.py:275
  165.8 1.8 fusion.219
  171.2 5.0 %reduce-window.150 = f32[4,4,128]{2,1,0:T(4,128)S(1)} reduce-window(f32[4,4,128]{2,1,0:T(4,128)S(1)} %reshape.631, f32[]{:T(128)} %constant.142.clone.1..sunk.1), window={size=1x1x128 pad=0_0x0_0x0_127}, to_apply=%region_24.24 | reduce-window | flops 260096 | bytes 16388 | tf_op jit(solution)/shard_map/reduce-window.60
  176.8 1.3 dynamic-slice_bitcast_fusion.10
  180.0 1.9 dynamic-slice_bitcast_fusion.13
  187.4 1.9 fusion.210
  190.2 2.5 %fusion.213 = (f32[4,512]{1,0:T(4,128)S(1)}, f32[4,512]{1,0:T(4,128)S(1)}, bf16[4,512,512]{2,1,0:T(8,128)(2,1)S(1)}) fusion(f32[4,512]{1,0:T(4,128)S(1)} %bitcast.350, f32[4,512,512]{2,1,0:T(8,128)S(1)} %fusion.211, pred[512,512]{1,0:T(8,128)(4,1)S(1)} %fusion.212, bf16[512,4,128]{2,0,1:T(8,128)(2,1)S(1)} %copy-done.1, f32[512,4,128]{0,2,1:T(8,128)S(1)} %bitcast.337), kind=kOutput, calls=%fused_computation.107.clone.1 | convolution fusion | flops 278917120 | bytes 8151040 | tf_op jit(solution)/shard_map/transpose(jvp())/while/body/eval_jaxpr/checkpoint/hts,she->the/dot_general | solution.py:277
  192.8 3.2 %fusion.214 = (bf16[1,512,4,128]{3,1,2,0:T(8,128)(2,1)}, f32[4,128]{1,0:T(4,128)S(1)}) fusion(f32[4,128]{1,0:T(4,128)S(1)} %get-tuple-element.960, bf16[512,4,128]{2,0,1:T(8,128)(2,1)S(1)} %copy-done.2, bf16[512,4,128]{2,0,1:T(8,128)(2,1)S(1)} %get-tuple-element.967, bf16[512,4,128]{2,0,1:T(8,128)(2,1)S(1)} %dynamic-slice_bitcast_fusion.11, ...), kind=kOutput, calls=%fused_computation.110.clone.1 | convolution fusion | flops 276823552 | bytes 4468736 | tf_op jit(solution)/shard_map/transpose(jvp())/while/body/eval_jaxpr/checkpoint/thd,shd->hts/dot_general | solution.py:275
  196.0 3.8 %fusion.220 = bf16[4,128,512]{2,1,0:T(8,128)(2,1)S(1)} fusion(f32[4,512,512]{2,1,0:T(8,128)} %copy-done, f32[4,512]{1,0:T(4,128)S(1)} %bitcast.352, pred[512,512]{1,0:T(8,128)(4,1)S(1)} %fusion.212, f32[512,4,128]{0,2,1:T(8,128)S(1)} %bitcast.338), kind=kOutput, calls=%fused_computation.81.clone.1 | convolution fusion | flops 274726912 | bytes 6037504 | tf_op jit(solution)/shard_map/transpose(jvp())/while/body/eval_jaxpr/checkpoint/hts,she->the/dot_general | solution.py:277
  199.8 1.4 fusion.221
  203.1 1.9 convolution_add_fusion.5
  205.0 3.3 %fusion.218 = bf16[4,512,128]{2,1,0:T(8,128)(2,1)S(1)} fusion(bf16[512,4,128]{2,0,1:T(8,128)(2,1)S(1)} %fusion.209, bf16[4,512,512]{2,1,0:T(8,128)(2,1)} %copy-done.18, f32[4,512]{1,0:T(4,128)S(1)} %bitcast.353, pred[512,512]{1,0:T(8,128)(4,1)S(1)} %fusion.212), kind=kOutput, calls=%fused_computation.85.clone.1 | convolution fusion | flops 274989056 | bytes 3416064 | tf_op jit(solution)/shard_map/transpose(jvp())/while/body/eval_jaxpr/checkpoint/thd,shd->hts/dot_general | solution.py:275
  208.4 1.8 fusion.219
  213.8 5.0 %reduce-window.150 = f32[4,4,128]{2,1,0:T(4,128)S(1)} reduce-window(f32[4,4,128]{2,1,0:T(4,128)S(1)} %reshape.631, f32[]{:T(128)} %constant.142.clone.1..sunk.1), window={size=1x1x128 pad=0_0x0_0x0_127}, to_apply=%region_24.24 | reduce-window | flops 260096 | bytes 16388 | tf_op jit(solution)/shard_map/reduce-window.60
  219.3 2.3 reshape.592
  221.7 2.2 reshape.593
  225.8 13.7 %shard_map.119 = f32[4,64]{1,0:T(4,128)} custom-call(f32[2,4,64]{2,1,0:T(4,128)} %bitcast.368), custom_call_target="tpu_custom_call" | custom-call | tf_op jit(solution)/shard_map/pallas_call | solution.py:131
  239.5 1.2 copy.362
  (227 shorter events, 54.7 us)
Async XLA Ops:
  6.6 7.5 %copy-start.7 = (bf16[1,1024,512]{2,1,0:T(8,128)(2,1)S(1)}, bf16[1,1024,512]{2,1,0:T(8,128)(2,1)}, u32[]{:S(2)}) copy-start(bf16[1,1024,512]{2,1,0:T(8,128)(2,1)} %param.12) | copy-start | bytes 3145732
  8.2 6.5 %copy-start.16 = (f32[4,128]{1,0:T(4,128)S(1)}, f32[4,128]{1,0:T(4,128)}, u32[]{:S(2)}) copy-start(f32[4,128]{1,0:T(4,128)} %param.16) | copy-start | bytes 6148
  88.9 5.9 %copy-start.8 = (bf16[1,1024,512]{2,1,0:T(8,128)(2,1)S(1)}, bf16[1,1024,512]{2,1,0:T(8,128)(2,1)}, u32[]{:S(2)}) copy-start(bf16[1,1024,512]{2,1,0:T(8,128)(2,1)} %param.11) | copy-start | bytes 3145732
  90.4 8.0 %copy-start.15 = (f32[1,4,1024]{2,1,0:T(4,128)S(1)}, f32[1,4,1024]{2,1,0:T(4,128)}, u32[]{:S(2)}) copy-start(f32[1,4,1024]{2,1,0:T(4,128)} %param.14) | copy-start | bytes 49156
  125.7 3.0 %copy-start.9 = (bf16[1,1024,512]{2,1,0:T(8,128)(2,1)S(1)}, bf16[1,1024,512]{2,1,0:T(8,128)(2,1)}, u32[]{:S(2)}) copy-start(bf16[1,1024,512]{2,1,0:T(8,128)(2,1)} %param.17) | copy-start | bytes 3145732
  134.2 5.2 %copy-start.3 = (bf16[2,512,4,128]{3,1,2,0:T(8,128)(2,1)}, bf16[2,512,4,128]{3,1,2,0:T(8,128)(2,1)S(1)}, u32[]{:S(2)}) copy-start(bf16[2,512,4,128]{3,1,2,0:T(8,128)(2,1)S(1)} %get-tuple-element.1063) | copy-start | bytes 3145732 | tf_op jit(solution)/shard_map/transpose(jvp())/while
  134.2 5.2 %copy-start.5 = (f32[2,512,4,128]{3,2,1,0:T(4,128)S(1)}, f32[2,512,4,128]{3,2,1,0:T(4,128)}, u32[]{:S(2)}) copy-start(f32[2,512,4,128]{3,2,1,0:T(4,128)} %get-tuple-element.1067) | copy-start | bytes 6291460 | tf_op jit(solution)/shard_map/transpose(jvp())/while
  139.8 7.9 %copy-start.1 = (bf16[512,4,128]{2,0,1:T(8,128)(2,1)S(1)}, bf16[512,4,128]{2,0,1:T(8,128)(2,1)}, u32[]{:S(2)}) copy-start(bf16[512,4,128]{2,0,1:T(8,128)(2,1)} %dynamic-slice_bitcast_fusion.13) | copy-start | bytes 1572868 | tf_op jit(solution)/shard_map/transpose(jvp())/while
  147.4 2.8 %copy-start = (f32[4,512,512]{2,1,0:T(8,128)}, f32[4,512,512]{2,1,0:T(8,128)S(1)}, u32[]{:S(2)}) copy-start(f32[4,512,512]{2,1,0:T(8,128)S(1)} %fusion.211) | copy-start | bytes 12582916 | tf_op jit(solution)/shard_map/transpose(jvp())/while
  147.7 2.6 %copy-start.2 = (bf16[512,4,128]{2,0,1:T(8,128)(2,1)S(1)}, bf16[512,4,128]{2,0,1:T(8,128)(2,1)}, u32[]{:S(2)}) copy-start(bf16[512,4,128]{2,0,1:T(8,128)(2,1)} %dynamic-slice_bitcast_fusion.12) | copy-start | bytes 1572868 | tf_op jit(solution)/shard_map/transpose(jvp())/while
  150.2 3.2 %copy-start.18 = (bf16[4,512,512]{2,1,0:T(8,128)(2,1)}, bf16[4,512,512]{2,1,0:T(8,128)(2,1)S(1)}, u32[]{:S(2)}) copy-start(bf16[4,512,512]{2,1,0:T(8,128)(2,1)S(1)} %get-tuple-element.970) | copy-start | bytes 6291460 | tf_op jit(solution)/shard_map/transpose(jvp())/while
  162.4 5.2 %copy-start.6 = (bf16[1,512,4,128]{3,1,2,0:T(8,128)(2,1)S(1)}, bf16[1,512,4,128]{3,1,2,0:T(8,128)(2,1)}, u32[]{:S(2)}) copy-start(bf16[1,512,4,128]{3,1,2,0:T(8,128)(2,1)} %get-tuple-element.978) | copy-start | bytes 1572868 | tf_op jit(solution)/shard_map/transpose(jvp())/while
  162.5 5.2 %copy-start.10 = (bf16[2,512,4,128]{3,2,1,0:T(4,128)(2,1)S(1)}, bf16[2,512,4,128]{3,2,1,0:T(4,128)(2,1)}, u32[]{:S(2)}) copy-start(bf16[2,512,4,128]{3,2,1,0:T(4,128)(2,1)} %get-tuple-element.1039) | copy-start | bytes 3145732 | tf_op jit(solution)/shard_map/transpose(jvp())/while
  162.5 5.2 %copy-start.12 = (bf16[2,512,4,128]{3,2,1,0:T(4,128)(2,1)S(1)}, bf16[2,512,4,128]{3,2,1,0:T(4,128)(2,1)}, u32[]{:S(2)}) copy-start(bf16[2,512,4,128]{3,2,1,0:T(4,128)(2,1)} %get-tuple-element.1040) | copy-start | bytes 3145732 | tf_op jit(solution)/shard_map/transpose(jvp())/while
  167.7 9.0 %copy-start.4 = (bf16[2,512,4,128]{3,1,2,0:T(8,128)(2,1)S(1)}, bf16[2,512,4,128]{3,1,2,0:T(8,128)(2,1)}, u32[]{:S(2)}) copy-start(bf16[2,512,4,128]{3,1,2,0:T(8,128)(2,1)} %copy-done.3) | copy-start | bytes 3145732 | tf_op jit(solution)/shard_map/transpose(jvp())/while
  168.6 1.0 copy-start.11
  168.6 1.3 copy-start.13
  176.7 5.2 %copy-start.3 = (bf16[2,512,4,128]{3,1,2,0:T(8,128)(2,1)}, bf16[2,512,4,128]{3,1,2,0:T(8,128)(2,1)S(1)}, u32[]{:S(2)}) copy-start(bf16[2,512,4,128]{3,1,2,0:T(8,128)(2,1)S(1)} %get-tuple-element.1063) | copy-start | bytes 3145732 | tf_op jit(solution)/shard_map/transpose(jvp())/while
  176.7 5.2 %copy-start.5 = (f32[2,512,4,128]{3,2,1,0:T(4,128)S(1)}, f32[2,512,4,128]{3,2,1,0:T(4,128)}, u32[]{:S(2)}) copy-start(f32[2,512,4,128]{3,2,1,0:T(4,128)} %get-tuple-element.1067) | copy-start | bytes 6291460 | tf_op jit(solution)/shard_map/transpose(jvp())/while
  182.4 7.9 %copy-start.1 = (bf16[512,4,128]{2,0,1:T(8,128)(2,1)S(1)}, bf16[512,4,128]{2,0,1:T(8,128)(2,1)}, u32[]{:S(2)}) copy-start(bf16[512,4,128]{2,0,1:T(8,128)(2,1)} %dynamic-slice_bitcast_fusion.13) | copy-start | bytes 1572868 | tf_op jit(solution)/shard_map/transpose(jvp())/while
  190.0 2.8 %copy-start = (f32[4,512,512]{2,1,0:T(8,128)}, f32[4,512,512]{2,1,0:T(8,128)S(1)}, u32[]{:S(2)}) copy-start(f32[4,512,512]{2,1,0:T(8,128)S(1)} %fusion.211) | copy-start | bytes 12582916 | tf_op jit(solution)/shard_map/transpose(jvp())/while
  190.2 2.6 %copy-start.2 = (bf16[512,4,128]{2,0,1:T(8,128)(2,1)S(1)}, bf16[512,4,128]{2,0,1:T(8,128)(2,1)}, u32[]{:S(2)}) copy-start(bf16[512,4,128]{2,0,1:T(8,128)(2,1)} %dynamic-slice_bitcast_fusion.12) | copy-start | bytes 1572868 | tf_op jit(solution)/shard_map/transpose(jvp())/while
  192.8 3.2 %copy-start.18 = (bf16[4,512,512]{2,1,0:T(8,128)(2,1)}, bf16[4,512,512]{2,1,0:T(8,128)(2,1)S(1)}, u32[]{:S(2)}) copy-start(bf16[4,512,512]{2,1,0:T(8,128)(2,1)S(1)} %get-tuple-element.970) | copy-start | bytes 6291460 | tf_op jit(solution)/shard_map/transpose(jvp())/while
  205.0 5.2 %copy-start.6 = (bf16[1,512,4,128]{3,1,2,0:T(8,128)(2,1)S(1)}, bf16[1,512,4,128]{3,1,2,0:T(8,128)(2,1)}, u32[]{:S(2)}) copy-start(bf16[1,512,4,128]{3,1,2,0:T(8,128)(2,1)} %get-tuple-element.978) | copy-start | bytes 1572868 | tf_op jit(solution)/shard_map/transpose(jvp())/while
  205.0 5.2 %copy-start.10 = (bf16[2,512,4,128]{3,2,1,0:T(4,128)(2,1)S(1)}, bf16[2,512,4,128]{3,2,1,0:T(4,128)(2,1)}, u32[]{:S(2)}) copy-start(bf16[2,512,4,128]{3,2,1,0:T(4,128)(2,1)} %get-tuple-element.1039) | copy-start | bytes 3145732 | tf_op jit(solution)/shard_map/transpose(jvp())/while
  205.0 5.2 %copy-start.12 = (bf16[2,512,4,128]{3,2,1,0:T(4,128)(2,1)S(1)}, bf16[2,512,4,128]{3,2,1,0:T(4,128)(2,1)}, u32[]{:S(2)}) copy-start(bf16[2,512,4,128]{3,2,1,0:T(4,128)(2,1)} %get-tuple-element.1040) | copy-start | bytes 3145732 | tf_op jit(solution)/shard_map/transpose(jvp())/while
  210.2 9.1 %copy-start.4 = (bf16[2,512,4,128]{3,1,2,0:T(8,128)(2,1)S(1)}, bf16[2,512,4,128]{3,1,2,0:T(8,128)(2,1)}, u32[]{:S(2)}) copy-start(bf16[2,512,4,128]{3,1,2,0:T(8,128)(2,1)} %copy-done.3) | copy-start | bytes 3145732 | tf_op jit(solution)/shard_map/transpose(jvp())/while
  211.1 1.0 copy-start.11
  211.2 1.3 copy-start.13
  219.3 21.4 %copy-start.17 = (f32[2,4,512]{2,1,0:T(4,128)}, f32[2,4,512]{2,1,0:T(4,128)S(1)}, u32[]{:S(2)}) copy-start(f32[2,4,512]{2,1,0:T(4,128)S(1)} %get-tuple-element.447) | copy-start | bytes 49156
  219.3 4.6 %copy-start.14 = (bf16[2,512,4,128]{3,2,1,0:T(4,128)(2,1)S(1)}, bf16[2,512,4,128]{3,2,1,0:T(4,128)(2,1)}, u32[]{:S(2)}) copy-start(bf16[2,512,4,128]{3,2,1,0:T(4,128)(2,1)} %get-tuple-element.446) | copy-start | bytes 3145732

commit v7 on v6

--- a/solution.py
+++ b/solution.py
@@ -148,12 +148,13 @@
     count = lax.axis_size("ctx")
     me = lax.axis_index("ctx")
     row, col = lax.axis_index("dp"), lax.axis_index("head")
-    rows = fwd_out.shape[1]
+    heads, rows = fwd_out.shape[0], fwd_out.shape[1]
     shifts = []
     shift = 1
     while shift < count:
         shifts.append(shift)
         shift *= 2
+    rounds = len(shifts)
 
     def device(index):
         return (row, index, col)
@@ -176,49 +177,82 @@
         peers = peers + at_least(shift) + 1 - at_least(count - shift)
     pl.semaphore_wait(barrier, peers)
 
-    aggs[0] = fwd_ref[...]
-    aggs[1] = bwd_ref[...]
+    def sends(side, step):
+        return me + shifts[step] < count if side == 0 else me >= shifts[step]
+
+    def target(side, step):
+        return me + shifts[step] if side == 0 else me - shifts[step]
+
+    def source(side, step):
+        return me - shifts[step] if side == 0 else me + shifts[step]
+
+    inputs = (fwd_ref, bwd_ref)
+
+    def held(side, step):
+        return inputs[side] if step == 0 else aggs.at[side, step % 2]
+
+    def copy_of(side, step, head, peer):
+        return pltpu.make_async_remote_copy(
+            src_ref=held(side, step).at[head],
+            dst_ref=slots.at[side, step, head],
+            send_sem=send_sem.at[side, step, head],
+            recv_sem=recv_sem.at[side, step, head],
+            device_id=device(peer),
+            device_id_type=pl.DeviceIdType.MESH,
+        )
+
+    def send(side, step, head):
+        @pl.when(sends(side, step))
+        def _():
+            copy_of(side, step, head, target(side, step)).start()
+
+    def sent(side, step, head):
+        @pl.when(sends(side, step))
+        def _():
+            copy_of(side, step, head, target(side, step)).wait_send()
+
     exs[...] = jnp.zeros_like(exs)
     exs[:, :, rows:, :] = jnp.ones_like(exs[:, :, rows:, :])
-
-    for round_index, shift in enumerate(shifts):
-        sends = (me + shift < count, me >= shift)
-        targets = (me + shift, me - shift)
-        sources = (me - shift, me + shift)
-
-        def copy_of(side, peer):
-            return pltpu.make_async_remote_copy(
-                src_ref=aggs.at[side],
-                dst_ref=slots.at[side, round_index],
-                send_sem=send_sem.at[side, round_index],
-                recv_sem=recv_sem.at[side, round_index],
-                device_id=device(peer),
-                device_id_type=pl.DeviceIdType.MESH,
-            )
-
+    for head in range(heads):
         for side in range(2):
-            @pl.when(sends[side])
-            def _():
-                copy_of(side, targets[side]).start()
-
-        for side in range(2):
-            @pl.when(sends[side])
-            def _():
-                copy_of(side, targets[side]).wait_send()
-
-        for side in range(2):
-            @pl.when(sends[1 - side])
-            def _():
-                copy_of(side, sources[side]).wait_recv()
-                got = slots[side, round_index]
-                ex = exs[side]
-                agg = aggs[side]
-                ex_a = ex[:, rows:rows + 1, :]
-                agg_a = agg[:, rows:rows + 1, :]
-                exs[side, :, :rows, :] = ex_a * got[:, :rows, :] + ex[:, :rows, :]
-                exs[side, :, rows:, :] = ex[:, rows:, :] * got[:, rows:, :]
-                aggs[side, :, :rows, :] = agg_a * got[:, :rows, :] + agg[:, :rows, :]
-                aggs[side, :, rows:, :] = agg[:, rows:, :] * got[:, rows:, :]
+            send(side, 0, head)
+
+    for step in range(rounds):
+        for head in range(heads):
+            for side in range(2):
+                current = held(side, step).at[head]
+                later = aggs.at[side, (step + 1) % 2, head]
+                has_next = step + 1 < rounds
+
+                @pl.when(sends(1 - side, step))
+                def _():
+                    copy_of(side, step, head, source(side, step)).wait_recv()
+                    got = slots[side, step, head]
+                    if has_next:
+                        if step >= 1:
+                            sent(side, step - 1, head)
+                        agg = current[...]
+                        agg_a = agg[rows:rows + 1, :]
+                        later[:rows, :] = agg_a * got[:rows, :] + agg[:rows, :]
+                        later[rows:, :] = agg[rows:, :] * got[rows:, :]
+                    ex = exs[side, head]
+                    ex_a = ex[rows:rows + 1, :]
+                    exs[side, head, :rows, :] = ex_a * got[:rows, :] + ex[:rows, :]
+                    exs[side, head, rows:, :] = ex[rows:, :] * got[rows:, :]
+
+                if has_next:
+                    @pl.when(jnp.logical_not(sends(1 - side, step)))
+                    def _():
+                        if step >= 1:
+                            sent(side, step - 1, head)
+                        later[...] = current[...]
+
+                    send(side, step + 1, head)
+
+    for step in range(max(0, rounds - 2), rounds):
+        for head in range(heads):
+            for side in range(2):
+                sent(side, step, head)
 
     fwd_out[...] = exs[0, :, :rows, :]
     bwd_out[...] = exs[1, :, :rows, :]
@@ -238,11 +272,11 @@
         in_specs=[pl.BlockSpec(memory_space=pltpu.VMEM)] * 2,
         out_specs=(pl.BlockSpec(memory_space=pltpu.VMEM),) * 2,
         scratch_shapes=[
-            pltpu.VMEM((2,) + packed, jnp.float32),
+            pltpu.VMEM((2, 2) + packed, jnp.float32),
             pltpu.VMEM((2,) + packed, jnp.float32),
             pltpu.VMEM((2, rounds) + packed, jnp.float32),
-            pltpu.SemaphoreType.DMA((2, rounds)),
-            pltpu.SemaphoreType.DMA((2, rounds)),
+            pltpu.SemaphoreType.DMA((2, rounds, heads)),
+            pltpu.SemaphoreType.DMA((2, rounds, heads)),
         ],
         compiler_params=pltpu.CompilerParams(collective_id=1, has_side_effects=True),
     )(fwd, bwd)

time: 243 us -> 242 us (level)
  no operation moved by 1% of the time
where the time goes in v7:
time: 242 us; the launch traced here: 241 us
  Pallas kernels  80.7 us (33%)
  matrix products  65.6 us (27%)
  local copies, waits for them, and re-layouts  60.6 us (25%)
  other arithmetic  32.1 us (13%)
    pallas_call x1, Pallas kernels, both_scans_kernel(): pl.pallas_call(scan_kernel, out_shape=(out, out), in_specs=[pl.BlockSpec(...  66.2 us
    another operation x27, other arithmetic  20 us
    dot_general x6, matrix products, block_step(): jnp.einsum('hts,she->the', weights, v_block, preferred_element_type=jnp.f...  19.2 us
    dot_general x8, matrix products, block_step(): jnp.einsum('thd,hde->the', q_float, carried, precision=PRECISE)  15.6 us
    dot_general x6, matrix products, block_step(): jnp.einsum('thd,shd->hts', q_block, k_bf, preferred_element_type=jnp.floa...  14.5 us
    pallas_call x1, Pallas kernels, gain_sum(): pl.pallas_call(gain_sum_kernel, out_shape=jax.ShapeDtypeStruct(shape, par...  14.5 us
    dot_general x6, matrix products, block_step(): jnp.einsum('shd,she->hde', k_float * to_end.T[:, :, None], v_float, preci...  11.3 us
    squeeze x10, local copies, waits for them, and re-layouts, run_blocks(): lax.scan(jax.checkpoint(make_step(key_gain, head_width)), start_state, (t...  10.2 us

profile of v7, /device:TPU:2, one launch (start us, length us, event | category | flops | bytes accessed | tf_op | source)
XLA Modules:
  0.0 240.5 jit_solution(17812725374798291172)
XLA Ops:
  6.6 1.6 copy.255
  8.2 2.1 reshape.591
  11.6 2.5 %fusion.107 = f32[4,128,128]{2,1,0:T(8,128)S(1)} fusion(f32[1024,4,128]{0,2,1:T(8,128)S(1)} %bitcast.342, bf16[1024,4,128]{2,1,0:T(4,128)(2,1)} %reshape.591, f32[1024,4]{0,1:T(4,128)S(1)} %get-tuple-element.774), kind=kOutput, calls=%fused_computation.159 | convolution fusion | flops 805830656 | bytes 3424256 | tf_op jit(solution)/shard_map/thd,the->hde/dot_general | solution.py:29
  15.8 1.3 reshape_squeeze.17
  17.2 2.5 %fusion.109 = f32[4,128,128]{2,1,0:T(8,128)S(1)} fusion(bf16[1024,4,128]{0,2,1:T(8,128)(2,1)} %multiply_convert_fusion.6, bf16[1024,4,128]{2,1,0:T(4,128)(2,1)S(1)} %reshape_squeeze.17, f32[1024,4]{0,1:T(4,128)S(1)} %get-tuple-element.775), kind=kOutput, calls=%fused_computation.161 | convolution fusion | flops 806354944 | bytes 2375680 | tf_op jit(solution)/shard_map/shd,she->hde/dot_general | solution.py:364
  20.6 66.2 %shard_map.118 = (f32[4,128,128]{2,1,0:T(8,128)S(1)}, f32[4,128,128]{2,1,0:T(8,128)S(1)}) custom-call(f32[4,136,128]{2,1,0:T(8,128)} %get-tuple-element.773.fwd_ref, f32[4,136,128]{2,1,0:T(8,128)} %get-tuple-element.772.bwd_ref), custom_call_target="tpu_custom_call" | custom-call | tf_op jit(solution)/shard_map/pallas_call | solution.py:269
  87.9 1.4 copy.230
  89.4 2.1 reshape_squeeze.20
  91.5 2.3 copy.231
  94.9 2.4 %copy.232 = bf16[2,512,4,128]{3,1,2,0:T(8,128)(2,1)} copy(bf16[2,512,4,128]{3,2,1,0:T(4,128)(2,1)} %reshape_squeeze.21) | data formatting | bytes 2097152
  97.4 27.3 %while.42 = (s32[]{:T(128)}, f32[4,128,128]{2,1,0:T(8,128)S(1)}, bf16[2,512,4,128]{1,3,2,0:T(8,128)(2,1)}, f32[2,4,128,128]{3,2,1,0:T(8,128)}, f32[2,4,512]{2,1,...) while((s32[]{:T(128)}, f32[4,128,128]{2,1,0:T(8,128)S(1)}, ...), condition=%wide.region_11.12_spmd.clone, body=%wide.region_6.11_spmd.clone.sunk | while | flops 1352081408 | bytes 9343697 | solution.py:339
  100.7 3.3 %fusion.191 = f32[512,4,128]{0,2,1:T(8,128)S(1)} fusion(bf16[512,4,128]{2,0,1:T(8,128)(2,1)S(1)} %fusion.189, f32[4,512]{1,0:T(4,128)S(1)} %bitcast.354, pred[512,512]{1,0:T(8,128)(4,1)S(1)} %fusion.190, bf16[2,512,4,128]{3,1,2,0:T(8,128)(2,1)} %get-tuple-element.1015, s32[]{:T(128)S(6)} %copy.332, bf16[2,512,4,128]{3,1,2,0:T(8,128)(2,1)} %get-tuple-element.1014), kind=kOutput, calls=%fused_computation.3.clone.1 | convolution fusion | flops 543162368 | bytes 2900992 | tf_op jit(solution)/shard_map/jvp()/while/body/eval_jaxpr/hts,she->the/dot_general | solution.py:311
  105.5 3.0 %fusion.192 = bf16[2,512,4,128]{1,3,2,0:T(8,128)(2,1)} fusion(bf16[2,512,4,128]{1,3,2,0:T(8,128)(2,1)} %get-tuple-element.996, s32[]{:T(128)S(6)} %copy.332, f32[512,4,128]{0,2,1:T(8,128)S(1)} %fusion.191, f32[4,128,128]{2,1,0:T(8,128)S(1)} %get-tuple-element.995, f32[512,4]{0,1:T(4,128)S(1)} %bitcast.346, ...), kind=kOutput, calls=%fused_computation.8.clone.1 | convolution fusion | flops 403701760 | bytes 2892800 | tf_op jit(solution)/shard_map/jvp()/while/body/eval_jaxpr/thd,hde->the/dot_general | solution.py:315
  108.6 2.4 convolution_add_fusion.4
  114.4 3.3 %fusion.191 = f32[512,4,128]{0,2,1:T(8,128)S(1)} fusion(bf16[512,4,128]{2,0,1:T(8,128)(2,1)S(1)} %fusion.189, f32[4,512]{1,0:T(4,128)S(1)} %bitcast.354, pred[512,512]{1,0:T(8,128)(4,1)S(1)} %fusion.190, bf16[2,512,4,128]{3,1,2,0:T(8,128)(2,1)} %get-tuple-element.1015, s32[]{:T(128)S(6)} %copy.332, bf16[2,512,4,128]{3,1,2,0:T(8,128)(2,1)} %get-tuple-element.1014), kind=kOutput, calls=%fused_computation.3.clone.1 | convolution fusion | flops 543162368 | bytes 2900992 | tf_op jit(solution)/shard_map/jvp()/while/body/eval_jaxpr/hts,she->the/dot_general | solution.py:311
  119.2 3.0 %fusion.192 = bf16[2,512,4,128]{1,3,2,0:T(8,128)(2,1)} fusion(bf16[2,512,4,128]{1,3,2,0:T(8,128)(2,1)} %get-tuple-element.996, s32[]{:T(128)S(6)} %copy.332, f32[512,4,128]{0,2,1:T(8,128)S(1)} %fusion.191, f32[4,128,128]{2,1,0:T(8,128)S(1)} %get-tuple-element.995, f32[512,4]{0,1:T(4,128)S(1)} %bitcast.346, ...), kind=kOutput, calls=%fused_computation.8.clone.1 | convolution fusion | flops 403701760 | bytes 2892800 | tf_op jit(solution)/shard_map/jvp()/while/body/eval_jaxpr/thd,hde->the/dot_general | solution.py:315
  122.3 2.4 convolution_add_fusion.4
  124.7 1.8 copy.233
  127.7 1.7 reshape.602
  130.7 1.2 broadcast.246.clone2
  131.9 1.2 broadcast.246.clone2.1
  133.2 85.1 %while.43 = (s32[]{:T(128)}, f32[4,128]{1,0:T(4,128)S(1)}, f32[4,128,128]{2,1,0:T(8,128)S(1)}, bf16[2,512,4,128]{3,2,1,0:T(4,128)(2,1)}, bf16[2,512,4,128]{3,2,1...) while((s32[]{:T(128)}, f32[4,128]{1,0:T(4,128)S(1)}, ...), condition=%wide.region_26.27_spmd.clone, body=%wide.region_12.26_spmd.clone.sunk | while | flops 3394863616 | bytes 116524784 | solution.py:339
  133.2 1.3 dynamic-slice_bitcast_fusion.10
  136.4 1.9 dynamic-slice_bitcast_fusion.13
  143.8 1.9 fusion.210
  146.7 2.5 %fusion.213 = (f32[4,512]{1,0:T(4,128)S(1)}, f32[4,512]{1,0:T(4,128)S(1)}, bf16[4,512,512]{2,1,0:T(8,128)(2,1)S(1)}) fusion(f32[4,512]{1,0:T(4,128)S(1)} %bitcast.350, f32[4,512,512]{2,1,0:T(8,128)S(1)} %fusion.211, pred[512,512]{1,0:T(8,128)(4,1)S(1)} %fusion.212, bf16[512,4,128]{2,0,1:T(8,128)(2,1)S(1)} %copy-done.1, f32[512,4,128]{0,2,1:T(8,128)S(1)} %bitcast.337), kind=kOutput, calls=%fused_computation.107.clone.1 | convolution fusion | flops 278917120 | bytes 8151040 | tf_op jit(solution)/shard_map/transpose(jvp())/while/body/eval_jaxpr/checkpoint/hts,she->the/dot_general | solution.py:311
  149.2 3.2 %fusion.214 = (bf16[1,512,4,128]{3,1,2,0:T(8,128)(2,1)}, f32[4,128]{1,0:T(4,128)S(1)}) fusion(f32[4,128]{1,0:T(4,128)S(1)} %get-tuple-element.960, bf16[512,4,128]{2,0,1:T(8,128)(2,1)S(1)} %copy-done.2, bf16[512,4,128]{2,0,1:T(8,128)(2,1)S(1)} %get-tuple-element.967, bf16[512,4,128]{2,0,1:T(8,128)(2,1)S(1)} %dynamic-slice_bitcast_fusion.11, ...), kind=kOutput, calls=%fused_computation.110.clone.1 | convolution fusion | flops 276823552 | bytes 4468736 | tf_op jit(solution)/shard_map/transpose(jvp())/while/body/eval_jaxpr/checkpoint/thd,shd->hts/dot_general | solution.py:309
  152.5 3.8 %fusion.220 = bf16[4,128,512]{2,1,0:T(8,128)(2,1)S(1)} fusion(f32[4,512,512]{2,1,0:T(8,128)} %copy-done, f32[4,512]{1,0:T(4,128)S(1)} %bitcast.352, pred[512,512]{1,0:T(8,128)(4,1)S(1)} %fusion.212, f32[512,4,128]{0,2,1:T(8,128)S(1)} %bitcast.338), kind=kOutput, calls=%fused_computation.81.clone.1 | convolution fusion | flops 274726912 | bytes 6037504 | tf_op jit(solution)/shard_map/transpose(jvp())/while/body/eval_jaxpr/checkpoint/hts,she->the/dot_general | solution.py:311
  156.2 1.4 fusion.221
  159.5 1.9 convolution_add_fusion.5
  161.5 3.3 %fusion.218 = bf16[4,512,128]{2,1,0:T(8,128)(2,1)S(1)} fusion(bf16[512,4,128]{2,0,1:T(8,128)(2,1)S(1)} %fusion.209, bf16[4,512,512]{2,1,0:T(8,128)(2,1)} %copy-done.18, f32[4,512]{1,0:T(4,128)S(1)} %bitcast.353, pred[512,512]{1,0:T(8,128)(4,1)S(1)} %fusion.212), kind=kOutput, calls=%fused_computation.85.clone.1 | convolution fusion | flops 274989056 | bytes 3416064 | tf_op jit(solution)/shard_map/transpose(jvp())/while/body/eval_jaxpr/checkpoint/thd,shd->hts/dot_general | solution.py:309
  164.8 1.8 fusion.219
  170.2 5.0 %reduce-window.150 = f32[4,4,128]{2,1,0:T(4,128)S(1)} reduce-window(f32[4,4,128]{2,1,0:T(4,128)S(1)} %reshape.631, f32[]{:T(128)} %constant.142.clone.1..sunk.1), window={size=1x1x128 pad=0_0x0_0x0_127}, to_apply=%region_24.24 | reduce-window | flops 260096 | bytes 16388 | tf_op jit(solution)/shard_map/reduce-window.60
  175.7 1.3 dynamic-slice_bitcast_fusion.10
  179.0 1.9 dynamic-slice_bitcast_fusion.13
  186.4 1.9 fusion.210
  189.2 2.5 %fusion.213 = (f32[4,512]{1,0:T(4,128)S(1)}, f32[4,512]{1,0:T(4,128)S(1)}, bf16[4,512,512]{2,1,0:T(8,128)(2,1)S(1)}) fusion(f32[4,512]{1,0:T(4,128)S(1)} %bitcast.350, f32[4,512,512]{2,1,0:T(8,128)S(1)} %fusion.211, pred[512,512]{1,0:T(8,128)(4,1)S(1)} %fusion.212, bf16[512,4,128]{2,0,1:T(8,128)(2,1)S(1)} %copy-done.1, f32[512,4,128]{0,2,1:T(8,128)S(1)} %bitcast.337), kind=kOutput, calls=%fused_computation.107.clone.1 | convolution fusion | flops 278917120 | bytes 8151040 | tf_op jit(solution)/shard_map/transpose(jvp())/while/body/eval_jaxpr/checkpoint/hts,she->the/dot_general | solution.py:311
  191.8 3.2 %fusion.214 = (bf16[1,512,4,128]{3,1,2,0:T(8,128)(2,1)}, f32[4,128]{1,0:T(4,128)S(1)}) fusion(f32[4,128]{1,0:T(4,128)S(1)} %get-tuple-element.960, bf16[512,4,128]{2,0,1:T(8,128)(2,1)S(1)} %copy-done.2, bf16[512,4,128]{2,0,1:T(8,128)(2,1)S(1)} %get-tuple-element.967, bf16[512,4,128]{2,0,1:T(8,128)(2,1)S(1)} %dynamic-slice_bitcast_fusion.11, ...), kind=kOutput, calls=%fused_computation.110.clone.1 | convolution fusion | flops 276823552 | bytes 4468736 | tf_op jit(solution)/shard_map/transpose(jvp())/while/body/eval_jaxpr/checkpoint/thd,shd->hts/dot_general | solution.py:309
  195.0 3.8 %fusion.220 = bf16[4,128,512]{2,1,0:T(8,128)(2,1)S(1)} fusion(f32[4,512,512]{2,1,0:T(8,128)} %copy-done, f32[4,512]{1,0:T(4,128)S(1)} %bitcast.352, pred[512,512]{1,0:T(8,128)(4,1)S(1)} %fusion.212, f32[512,4,128]{0,2,1:T(8,128)S(1)} %bitcast.338), kind=kOutput, calls=%fused_computation.81.clone.1 | convolution fusion | flops 274726912 | bytes 6037504 | tf_op jit(solution)/shard_map/transpose(jvp())/while/body/eval_jaxpr/checkpoint/hts,she->the/dot_general | solution.py:311
  198.8 1.4 fusion.221
  202.1 1.9 convolution_add_fusion.5
  204.0 3.3 %fusion.218 = bf16[4,512,128]{2,1,0:T(8,128)(2,1)S(1)} fusion(bf16[512,4,128]{2,0,1:T(8,128)(2,1)S(1)} %fusion.209, bf16[4,512,512]{2,1,0:T(8,128)(2,1)} %copy-done.18, f32[4,512]{1,0:T(4,128)S(1)} %bitcast.353, pred[512,512]{1,0:T(8,128)(4,1)S(1)} %fusion.212), kind=kOutput, calls=%fused_computation.85.clone.1 | convolution fusion | flops 274989056 | bytes 3416064 | tf_op jit(solution)/shard_map/transpose(jvp())/while/body/eval_jaxpr/checkpoint/thd,shd->hts/dot_general | solution.py:309
  207.4 1.8 fusion.219
  212.8 5.0 %reduce-window.150 = f32[4,4,128]{2,1,0:T(4,128)S(1)} reduce-window(f32[4,4,128]{2,1,0:T(4,128)S(1)} %reshape.631, f32[]{:T(128)} %constant.142.clone.1..sunk.1), window={size=1x1x128 pad=0_0x0_0x0_127}, to_apply=%region_24.24 | reduce-window | flops 260096 | bytes 16388 | tf_op jit(solution)/shard_map/reduce-window.60
  218.3 2.3 reshape.592
  220.6 2.2 reshape.593
  224.8 14.5 %shard_map.119 = f32[4,64]{1,0:T(4,128)} custom-call(f32[2,4,64]{2,1,0:T(4,128)} %bitcast.368), custom_call_target="tpu_custom_call" | custom-call | tf_op jit(solution)/shard_map/pallas_call | solution.py:131
  239.3 1.2 copy.362
  (227 shorter events, 54.7 us)
Async XLA Ops:
  6.6 7.5 %copy-start.7 = (bf16[1,1024,512]{2,1,0:T(8,128)(2,1)S(1)}, bf16[1,1024,512]{2,1,0:T(8,128)(2,1)}, u32[]{:S(2)}) copy-start(bf16[1,1024,512]{2,1,0:T(8,128)(2,1)} %param.12) | copy-start | bytes 3145732
  8.2 6.5 %copy-start.16 = (f32[4,128]{1,0:T(4,128)S(1)}, f32[4,128]{1,0:T(4,128)}, u32[]{:S(2)}) copy-start(f32[4,128]{1,0:T(4,128)} %param.16) | copy-start | bytes 6148
  87.9 5.9 %copy-start.8 = (bf16[1,1024,512]{2,1,0:T(8,128)(2,1)S(1)}, bf16[1,1024,512]{2,1,0:T(8,128)(2,1)}, u32[]{:S(2)}) copy-start(bf16[1,1024,512]{2,1,0:T(8,128)(2,1)} %param.11) | copy-start | bytes 3145732
  89.4 8.0 %copy-start.15 = (f32[1,4,1024]{2,1,0:T(4,128)S(1)}, f32[1,4,1024]{2,1,0:T(4,128)}, u32[]{:S(2)}) copy-start(f32[1,4,1024]{2,1,0:T(4,128)} %param.14) | copy-start | bytes 49156
  124.7 3.0 %copy-start.9 = (bf16[1,1024,512]{2,1,0:T(8,128)(2,1)S(1)}, bf16[1,1024,512]{2,1,0:T(8,128)(2,1)}, u32[]{:S(2)}) copy-start(bf16[1,1024,512]{2,1,0:T(8,128)(2,1)} %param.17) | copy-start | bytes 3145732
  133.2 5.2 %copy-start.3 = (bf16[2,512,4,128]{3,1,2,0:T(8,128)(2,1)}, bf16[2,512,4,128]{3,1,2,0:T(8,128)(2,1)S(1)}, u32[]{:S(2)}) copy-start(bf16[2,512,4,128]{3,1,2,0:T(8,128)(2,1)S(1)} %get-tuple-element.1063) | copy-start | bytes 3145732 | tf_op jit(solution)/shard_map/transpose(jvp())/while
  133.2 5.2 %copy-start.5 = (f32[2,512,4,128]{3,2,1,0:T(4,128)S(1)}, f32[2,512,4,128]{3,2,1,0:T(4,128)}, u32[]{:S(2)}) copy-start(f32[2,512,4,128]{3,2,1,0:T(4,128)} %get-tuple-element.1067) | copy-start | bytes 6291460 | tf_op jit(solution)/shard_map/transpose(jvp())/while
  138.8 7.9 %copy-start.1 = (bf16[512,4,128]{2,0,1:T(8,128)(2,1)S(1)}, bf16[512,4,128]{2,0,1:T(8,128)(2,1)}, u32[]{:S(2)}) copy-start(bf16[512,4,128]{2,0,1:T(8,128)(2,1)} %dynamic-slice_bitcast_fusion.13) | copy-start | bytes 1572868 | tf_op jit(solution)/shard_map/transpose(jvp())/while
  146.4 2.8 %copy-start = (f32[4,512,512]{2,1,0:T(8,128)}, f32[4,512,512]{2,1,0:T(8,128)S(1)}, u32[]{:S(2)}) copy-start(f32[4,512,512]{2,1,0:T(8,128)S(1)} %fusion.211) | copy-start | bytes 12582916 | tf_op jit(solution)/shard_map/transpose(jvp())/while
  146.7 2.6 %copy-start.2 = (bf16[512,4,128]{2,0,1:T(8,128)(2,1)S(1)}, bf16[512,4,128]{2,0,1:T(8,128)(2,1)}, u32[]{:S(2)}) copy-start(bf16[512,4,128]{2,0,1:T(8,128)(2,1)} %dynamic-slice_bitcast_fusion.12) | copy-start | bytes 1572868 | tf_op jit(solution)/shard_map/transpose(jvp())/while
  149.2 3.2 %copy-start.18 = (bf16[4,512,512]{2,1,0:T(8,128)(2,1)}, bf16[4,512,512]{2,1,0:T(8,128)(2,1)S(1)}, u32[]{:S(2)}) copy-start(bf16[4,512,512]{2,1,0:T(8,128)(2,1)S(1)} %get-tuple-element.970) | copy-start | bytes 6291460 | tf_op jit(solution)/shard_map/transpose(jvp())/while
  161.4 5.2 %copy-start.6 = (bf16[1,512,4,128]{3,1,2,0:T(8,128)(2,1)S(1)}, bf16[1,512,4,128]{3,1,2,0:T(8,128)(2,1)}, u32[]{:S(2)}) copy-start(bf16[1,512,4,128]{3,1,2,0:T(8,128)(2,1)} %get-tuple-element.978) | copy-start | bytes 1572868 | tf_op jit(solution)/shard_map/transpose(jvp())/while
  161.4 5.2 %copy-start.10 = (bf16[2,512,4,128]{3,2,1,0:T(4,128)(2,1)S(1)}, bf16[2,512,4,128]{3,2,1,0:T(4,128)(2,1)}, u32[]{:S(2)}) copy-start(bf16[2,512,4,128]{3,2,1,0:T(4,128)(2,1)} %get-tuple-element.1039) | copy-start | bytes 3145732 | tf_op jit(solution)/shard_map/transpose(jvp())/while
  161.4 5.2 %copy-start.12 = (bf16[2,512,4,128]{3,2,1,0:T(4,128)(2,1)S(1)}, bf16[2,512,4,128]{3,2,1,0:T(4,128)(2,1)}, u32[]{:S(2)}) copy-start(bf16[2,512,4,128]{3,2,1,0:T(4,128)(2,1)} %get-tuple-element.1040) | copy-start | bytes 3145732 | tf_op jit(solution)/shard_map/transpose(jvp())/while
  166.7 9.0 %copy-start.4 = (bf16[2,512,4,128]{3,1,2,0:T(8,128)(2,1)S(1)}, bf16[2,512,4,128]{3,1,2,0:T(8,128)(2,1)}, u32[]{:S(2)}) copy-start(bf16[2,512,4,128]{3,1,2,0:T(8,128)(2,1)} %copy-done.3) | copy-start | bytes 3145732 | tf_op jit(solution)/shard_map/transpose(jvp())/while
  167.6 1.0 copy-start.11
  167.6 1.3 copy-start.13
  175.7 5.2 %copy-start.3 = (bf16[2,512,4,128]{3,1,2,0:T(8,128)(2,1)}, bf16[2,512,4,128]{3,1,2,0:T(8,128)(2,1)S(1)}, u32[]{:S(2)}) copy-start(bf16[2,512,4,128]{3,1,2,0:T(8,128)(2,1)S(1)} %get-tuple-element.1063) | copy-start | bytes 3145732 | tf_op jit(solution)/shard_map/transpose(jvp())/while
  175.7 5.2 %copy-start.5 = (f32[2,512,4,128]{3,2,1,0:T(4,128)S(1)}, f32[2,512,4,128]{3,2,1,0:T(4,128)}, u32[]{:S(2)}) copy-start(f32[2,512,4,128]{3,2,1,0:T(4,128)} %get-tuple-element.1067) | copy-start | bytes 6291460 | tf_op jit(solution)/shard_map/transpose(jvp())/while
  181.4 7.9 %copy-start.1 = (bf16[512,4,128]{2,0,1:T(8,128)(2,1)S(1)}, bf16[512,4,128]{2,0,1:T(8,128)(2,1)}, u32[]{:S(2)}) copy-start(bf16[512,4,128]{2,0,1:T(8,128)(2,1)} %dynamic-slice_bitcast_fusion.13) | copy-start | bytes 1572868 | tf_op jit(solution)/shard_map/transpose(jvp())/while
  189.0 2.8 %copy-start = (f32[4,512,512]{2,1,0:T(8,128)}, f32[4,512,512]{2,1,0:T(8,128)S(1)}, u32[]{:S(2)}) copy-start(f32[4,512,512]{2,1,0:T(8,128)S(1)} %fusion.211) | copy-start | bytes 12582916 | tf_op jit(solution)/shard_map/transpose(jvp())/while
  189.2 2.6 %copy-start.2 = (bf16[512,4,128]{2,0,1:T(8,128)(2,1)S(1)}, bf16[512,4,128]{2,0,1:T(8,128)(2,1)}, u32[]{:S(2)}) copy-start(bf16[512,4,128]{2,0,1:T(8,128)(2,1)} %dynamic-slice_bitcast_fusion.12) | copy-start | bytes 1572868 | tf_op jit(solution)/shard_map/transpose(jvp())/while
  191.8 3.2 %copy-start.18 = (bf16[4,512,512]{2,1,0:T(8,128)(2,1)}, bf16[4,512,512]{2,1,0:T(8,128)(2,1)S(1)}, u32[]{:S(2)}) copy-start(bf16[4,512,512]{2,1,0:T(8,128)(2,1)S(1)} %get-tuple-element.970) | copy-start | bytes 6291460 | tf_op jit(solution)/shard_map/transpose(jvp())/while
  204.0 5.2 %copy-start.6 = (bf16[1,512,4,128]{3,1,2,0:T(8,128)(2,1)S(1)}, bf16[1,512,4,128]{3,1,2,0:T(8,128)(2,1)}, u32[]{:S(2)}) copy-start(bf16[1,512,4,128]{3,1,2,0:T(8,128)(2,1)} %get-tuple-element.978) | copy-start | bytes 1572868 | tf_op jit(solution)/shard_map/transpose(jvp())/while
  204.0 5.2 %copy-start.10 = (bf16[2,512,4,128]{3,2,1,0:T(4,128)(2,1)S(1)}, bf16[2,512,4,128]{3,2,1,0:T(4,128)(2,1)}, u32[]{:S(2)}) copy-start(bf16[2,512,4,128]{3,2,1,0:T(4,128)(2,1)} %get-tuple-element.1039) | copy-start | bytes 3145732 | tf_op jit(solution)/shard_map/transpose(jvp())/while
  204.0 5.2 %copy-start.12 = (bf16[2,512,4,128]{3,2,1,0:T(4,128)(2,1)S(1)}, bf16[2,512,4,128]{3,2,1,0:T(4,128)(2,1)}, u32[]{:S(2)}) copy-start(bf16[2,512,4,128]{3,2,1,0:T(4,128)(2,1)} %get-tuple-element.1040) | copy-start | bytes 3145732 | tf_op jit(solution)/shard_map/transpose(jvp())/while
  209.2 9.1 %copy-start.4 = (bf16[2,512,4,128]{3,1,2,0:T(8,128)(2,1)S(1)}, bf16[2,512,4,128]{3,1,2,0:T(8,128)(2,1)}, u32[]{:S(2)}) copy-start(bf16[2,512,4,128]{3,1,2,0:T(8,128)(2,1)} %copy-done.3) | copy-start | bytes 3145732 | tf_op jit(solution)/shard_map/transpose(jvp())/while
  210.1 1.0 copy-start.11
  210.1 1.3 copy-start.13
  218.3 22.2 %copy-start.17 = (f32[2,4,512]{2,1,0:T(4,128)}, f32[2,4,512]{2,1,0:T(4,128)S(1)}, u32[]{:S(2)}) copy-start(f32[2,4,512]{2,1,0:T(4,128)S(1)} %get-tuple-element.447) | copy-start | bytes 49156
  218.3 4.6 %copy-start.14 = (bf16[2,512,4,128]{3,2,1,0:T(4,128)(2,1)S(1)}, bf16[2,512,4,128]{3,2,1,0:T(4,128)(2,1)}, u32[]{:S(2)}) copy-start(bf16[2,512,4,128]{3,2,1,0:T(4,128)(2,1)} %get-tuple-element.446) | copy-start | bytes 3145732

commit v8 on v6

--- a/solution.py
+++ b/solution.py
@@ -62,24 +62,26 @@
     return scans[0][3], scans[1][3]
 
 
-def gain_sum_kernel(part_ref, total_ref, pair_slot, slots, pair_sem, send_sem, recv_sem):
-    count = slots.shape[0]
+def gain_sum_kernel(part_ref, total_ref, pair_slot, accs, slots, pair_sem, send_sem, recv_sem):
+    count = lax.axis_size("ctx")
     me = lax.axis_index("ctx")
     row, col = lax.axis_index("dp"), lax.axis_index("head")
     other = 1 - row
-
-    def peer_of(step):
-        return lax.rem(me + step, count)
+    rounds = slots.shape[0]
+    shifts = [1 << step for step in range(rounds)]
+
+    def partner(shift):
+        return me + shift - 2 * shift * ((me // shift) % 2)
 
     barrier = pltpu.get_barrier_semaphore()
     pl.semaphore_signal(
         barrier, inc=1, device_id=(other, me, col), device_id_type=pl.DeviceIdType.MESH
     )
-    for step in range(1, count):
+    for shift in shifts:
         pl.semaphore_signal(
-            barrier, inc=1, device_id=(row, peer_of(step), col), device_id_type=pl.DeviceIdType.MESH
-        )
-    pl.semaphore_wait(barrier, count)
+            barrier, inc=1, device_id=(row, partner(shift), col), device_id_type=pl.DeviceIdType.MESH
+        )
+    pl.semaphore_wait(barrier, rounds + 1)
 
     pair = pltpu.make_async_remote_copy(
         src_ref=part_ref.at[other],
@@ -92,42 +94,29 @@
     pair.start()
     pair.wait_send()
     pair.wait_recv()
-    slots[me] = part_ref[row] + pair_slot[...]
-
-    copies = []
-    for step in range(1, count):
-        peer = peer_of(step)
+    accs[0] = part_ref[row] + pair_slot[...]
+
+    for step, shift in enumerate(shifts):
         copy = pltpu.make_async_remote_copy(
-            src_ref=slots.at[me],
-            dst_ref=slots.at[me],
-            send_sem=send_sem.at[peer],
-            recv_sem=recv_sem.at[me],
-            device_id=(row, peer, col),
+            src_ref=accs.at[step],
+            dst_ref=slots.at[step],
+            send_sem=send_sem.at[step],
+            recv_sem=recv_sem.at[step],
+            device_id=(row, partner(shift), col),
             device_id_type=pl.DeviceIdType.MESH,
         )
         copy.start()
-        copies.append(copy)
-    for step in range(1, count):
-        copies[step - 1].wait_send()
-        source = lax.rem(me + count - step, count)
-        pltpu.make_async_remote_copy(
-            src_ref=slots.at[source],
-            dst_ref=slots.at[source],
-            send_sem=send_sem.at[source],
-            recv_sem=recv_sem.at[source],
-            device_id=(row, source, col),
-            device_id_type=pl.DeviceIdType.MESH,
-        ).wait_recv()
-    total = slots[0]
-    for index in range(1, count):
-        total = total + slots[index]
-    total_ref[...] = total
+        copy.wait_send()
+        copy.wait_recv()
+        accs[step + 1] = accs[step] + slots[step]
+    total_ref[...] = accs[rounds]
 
 
 def gain_sum(part, count):
     heads, width = part.shape
     halves = part.reshape(heads, 2, width // 2).transpose(1, 0, 2)
     shape = halves.shape[1:]
+    rounds = max(1, (count - 1).bit_length())
     return pl.pallas_call(
         gain_sum_kernel,
         out_shape=jax.ShapeDtypeStruct(shape, part.dtype),
@@ -135,10 +124,11 @@
         out_specs=pl.BlockSpec(memory_space=pltpu.VMEM),
         scratch_shapes=[
             pltpu.VMEM(shape, part.dtype),
-            pltpu.VMEM((count,) + shape, part.dtype),
+            pltpu.VMEM((rounds + 1,) + shape, part.dtype),
+            pltpu.VMEM((rounds,) + shape, part.dtype),
             pltpu.SemaphoreType.DMA((2,)),
-            pltpu.SemaphoreType.DMA((count,)),
-            pltpu.SemaphoreType.DMA((count,)),
+            pltpu.SemaphoreType.DMA((rounds,)),
+            pltpu.SemaphoreType.DMA((rounds,)),
         ],
         compiler_params=pltpu.CompilerParams(collective_id=0, has_side_effects=True),
     )(halves)

time: 243 us -> 249 us (1.025)
  Pallas kernels: 80.9 us -> 88.3 us
    pallas_call x1, Pallas kernels: 13.7 us -> 21.1 us  [gain_sum(): pl.pallas_call(gain_sum_kernel, out_shape=jax.ShapeDtypeStruct(shape, par...]
where the time goes in v8:
time: 249 us; the launch traced here: 248 us
  Pallas kernels  88.3 us (35%)
  matrix products  65.6 us (26%)
  local copies, waits for them, and re-layouts  60.6 us (24%)
  other arithmetic  32.1 us (13%)
    pallas_call x1, Pallas kernels, both_scans_kernel(): pl.pallas_call(scan_kernel, out_shape=(out, out), in_specs=[pl.BlockSpec(...  67.2 us
    pallas_call x1, Pallas kernels, gain_sum(): pl.pallas_call(gain_sum_kernel, out_shape=jax.ShapeDtypeStruct(shape, par...  21.1 us
    another operation x27, other arithmetic  20 us
    dot_general x6, matrix products, block_step(): jnp.einsum('hts,she->the', weights, v_block, preferred_element_type=jnp.f...  19.2 us
    dot_general x8, matrix products, block_step(): jnp.einsum('thd,hde->the', q_float, carried, precision=PRECISE)  15.6 us
    dot_general x6, matrix products, block_step(): jnp.einsum('thd,shd->hts', q_block, k_bf, preferred_element_type=jnp.floa...  14.5 us
    dot_general x6, matrix products, block_step(): jnp.einsum('shd,she->hde', k_float * to_end.T[:, :, None], v_float, preci...  11.3 us
    squeeze x10, local copies, waits for them, and re-layouts, run_blocks(): lax.scan(jax.checkpoint(make_step(key_gain, head_width)), start_state, (t...  10.2 us

profile of v8, /device:TPU:2, one launch (start us, length us, event | category | flops | bytes accessed | tf_op | source)
XLA Modules:
  0.0 248.2 jit_solution(9445112117731595408)
XLA Ops:
  6.6 1.6 copy.255
  8.2 2.1 reshape.591
  11.6 2.5 %fusion.107 = f32[4,128,128]{2,1,0:T(8,128)S(1)} fusion(f32[1024,4,128]{0,2,1:T(8,128)S(1)} %bitcast.342, bf16[1024,4,128]{2,1,0:T(4,128)(2,1)} %reshape.591, f32[1024,4]{0,1:T(4,128)S(1)} %get-tuple-element.774), kind=kOutput, calls=%fused_computation.159 | convolution fusion | flops 805830656 | bytes 3424256 | tf_op jit(solution)/shard_map/thd,the->hde/dot_general | solution.py:29
  15.8 1.3 reshape_squeeze.17
  17.2 2.5 %fusion.109 = f32[4,128,128]{2,1,0:T(8,128)S(1)} fusion(bf16[1024,4,128]{0,2,1:T(8,128)(2,1)} %multiply_convert_fusion.6, bf16[1024,4,128]{2,1,0:T(4,128)(2,1)S(1)} %reshape_squeeze.17, f32[1024,4]{0,1:T(4,128)S(1)} %get-tuple-element.775), kind=kOutput, calls=%fused_computation.161 | convolution fusion | flops 806354944 | bytes 2375680 | tf_op jit(solution)/shard_map/shd,she->hde/dot_general | solution.py:320
  20.6 67.2 %shard_map.118 = (f32[4,128,128]{2,1,0:T(8,128)S(1)}, f32[4,128,128]{2,1,0:T(8,128)S(1)}) custom-call(f32[4,136,128]{2,1,0:T(8,128)} %get-tuple-element.773.fwd_ref, f32[4,136,128]{2,1,0:T(8,128)} %get-tuple-element.772.bwd_ref), custom_call_target="tpu_custom_call" | custom-call | tf_op jit(solution)/shard_map/pallas_call | solution.py:225
  88.9 1.4 copy.230
  90.4 2.1 reshape_squeeze.20
  92.5 2.3 copy.231
  96.0 2.4 copy.232
  98.4 27.3 %while.42 = (s32[]{:T(128)}, f32[4,128,128]{2,1,0:T(8,128)S(1)}, bf16[2,512,4,128]{1,3,2,0:T(8,128)(2,1)}, f32[2,4,128,128]{3,2,1,0:T(8,128)}, f32[2,4,512]{2,1,...) while((s32[]{:T(128)}, f32[4,128,128]{2,1,0:T(8,128)S(1)}, ...), condition=%wide.region_11.12_spmd.clone, body=%wide.region_6.11_spmd.clone.sunk | while | flops 1352081408 | bytes 9343697 | solution.py:295
  101.7 3.3 %fusion.191 = f32[512,4,128]{0,2,1:T(8,128)S(1)} fusion(bf16[512,4,128]{2,0,1:T(8,128)(2,1)S(1)} %fusion.189, f32[4,512]{1,0:T(4,128)S(1)} %bitcast.354, pred[512,512]{1,0:T(8,128)(4,1)S(1)} %fusion.190, bf16[2,512,4,128]{3,1,2,0:T(8,128)(2,1)} %get-tuple-element.1015, s32[]{:T(128)S(6)} %copy.332, bf16[2,512,4,128]{3,1,2,0:T(8,128)(2,1)} %get-tuple-element.1014), kind=kOutput, calls=%fused_computation.3.clone.1 | convolution fusion | flops 543162368 | bytes 2900992 | tf_op jit(solution)/shard_map/jvp()/while/body/eval_jaxpr/hts,she->the/dot_general | solution.py:267
  106.5 3.0 %fusion.192 = bf16[2,512,4,128]{1,3,2,0:T(8,128)(2,1)} fusion(bf16[2,512,4,128]{1,3,2,0:T(8,128)(2,1)} %get-tuple-element.996, s32[]{:T(128)S(6)} %copy.332, f32[512,4,128]{0,2,1:T(8,128)S(1)} %fusion.191, f32[4,128,128]{2,1,0:T(8,128)S(1)} %get-tuple-element.995, f32[512,4]{0,1:T(4,128)S(1)} %bitcast.346, ...), kind=kOutput, calls=%fused_computation.8.clone.1 | convolution fusion | flops 403701760 | bytes 2892800 | tf_op jit(solution)/shard_map/jvp()/while/body/eval_jaxpr/thd,hde->the/dot_general | solution.py:271
  109.7 2.4 convolution_add_fusion.4
  115.4 3.3 %fusion.191 = f32[512,4,128]{0,2,1:T(8,128)S(1)} fusion(bf16[512,4,128]{2,0,1:T(8,128)(2,1)S(1)} %fusion.189, f32[4,512]{1,0:T(4,128)S(1)} %bitcast.354, pred[512,512]{1,0:T(8,128)(4,1)S(1)} %fusion.190, bf16[2,512,4,128]{3,1,2,0:T(8,128)(2,1)} %get-tuple-element.1015, s32[]{:T(128)S(6)} %copy.332, bf16[2,512,4,128]{3,1,2,0:T(8,128)(2,1)} %get-tuple-element.1014), kind=kOutput, calls=%fused_computation.3.clone.1 | convolution fusion | flops 543162368 | bytes 2900992 | tf_op jit(solution)/shard_map/jvp()/while/body/eval_jaxpr/hts,she->the/dot_general | solution.py:267
  120.2 3.0 %fusion.192 = bf16[2,512,4,128]{1,3,2,0:T(8,128)(2,1)} fusion(bf16[2,512,4,128]{1,3,2,0:T(8,128)(2,1)} %get-tuple-element.996, s32[]{:T(128)S(6)} %copy.332, f32[512,4,128]{0,2,1:T(8,128)S(1)} %fusion.191, f32[4,128,128]{2,1,0:T(8,128)S(1)} %get-tuple-element.995, f32[512,4]{0,1:T(4,128)S(1)} %bitcast.346, ...), kind=kOutput, calls=%fused_computation.8.clone.1 | convolution fusion | flops 403701760 | bytes 2892800 | tf_op jit(solution)/shard_map/jvp()/while/body/eval_jaxpr/thd,hde->the/dot_general | solution.py:271
  123.3 2.4 convolution_add_fusion.4
  125.7 1.8 copy.233
  128.8 1.7 reshape.602
  131.7 1.2 broadcast.246.clone2
  132.9 1.2 broadcast.246.clone2.1
  134.2 85.1 %while.43 = (s32[]{:T(128)}, f32[4,128]{1,0:T(4,128)S(1)}, f32[4,128,128]{2,1,0:T(8,128)S(1)}, bf16[2,512,4,128]{3,2,1,0:T(4,128)(2,1)}, bf16[2,512,4,128]{3,2,1...) while((s32[]{:T(128)}, f32[4,128]{1,0:T(4,128)S(1)}, ...), condition=%wide.region_26.27_spmd.clone, body=%wide.region_12.26_spmd.clone.sunk | while | flops 3394863616 | bytes 116524784 | solution.py:295
  134.2 1.3 dynamic-slice_bitcast_fusion.10
  137.4 1.9 dynamic-slice_bitcast_fusion.13
  144.8 1.9 fusion.210
  147.7 2.5 %fusion.213 = (f32[4,512]{1,0:T(4,128)S(1)}, f32[4,512]{1,0:T(4,128)S(1)}, bf16[4,512,512]{2,1,0:T(8,128)(2,1)S(1)}) fusion(f32[4,512]{1,0:T(4,128)S(1)} %bitcast.350, f32[4,512,512]{2,1,0:T(8,128)S(1)} %fusion.211, pred[512,512]{1,0:T(8,128)(4,1)S(1)} %fusion.212, bf16[512,4,128]{2,0,1:T(8,128)(2,1)S(1)} %copy-done.1, f32[512,4,128]{0,2,1:T(8,128)S(1)} %bitcast.337), kind=kOutput, calls=%fused_computation.107.clone.1 | convolution fusion | flops 278917120 | bytes 8151040 | tf_op jit(solution)/shard_map/transpose(jvp())/while/body/eval_jaxpr/checkpoint/hts,she->the/dot_general | solution.py:267
  150.3 3.2 %fusion.214 = (bf16[1,512,4,128]{3,1,2,0:T(8,128)(2,1)}, f32[4,128]{1,0:T(4,128)S(1)}) fusion(f32[4,128]{1,0:T(4,128)S(1)} %get-tuple-element.960, bf16[512,4,128]{2,0,1:T(8,128)(2,1)S(1)} %copy-done.2, bf16[512,4,128]{2,0,1:T(8,128)(2,1)S(1)} %get-tuple-element.967, bf16[512,4,128]{2,0,1:T(8,128)(2,1)S(1)} %dynamic-slice_bitcast_fusion.11, ...), kind=kOutput, calls=%fused_computation.110.clone.1 | convolution fusion | flops 276823552 | bytes 4468736 | tf_op jit(solution)/shard_map/transpose(jvp())/while/body/eval_jaxpr/checkpoint/thd,shd->hts/dot_general | solution.py:265
  153.5 3.8 %fusion.220 = bf16[4,128,512]{2,1,0:T(8,128)(2,1)S(1)} fusion(f32[4,512,512]{2,1,0:T(8,128)} %copy-done, f32[4,512]{1,0:T(4,128)S(1)} %bitcast.352, pred[512,512]{1,0:T(8,128)(4,1)S(1)} %fusion.212, f32[512,4,128]{0,2,1:T(8,128)S(1)} %bitcast.338), kind=kOutput, calls=%fused_computation.81.clone.1 | convolution fusion | flops 274726912 | bytes 6037504 | tf_op jit(solution)/shard_map/transpose(jvp())/while/body/eval_jaxpr/checkpoint/hts,she->the/dot_general | solution.py:267
  157.3 1.4 fusion.221
  160.5 1.9 convolution_add_fusion.5
  162.5 3.3 %fusion.218 = bf16[4,512,128]{2,1,0:T(8,128)(2,1)S(1)} fusion(bf16[512,4,128]{2,0,1:T(8,128)(2,1)S(1)} %fusion.209, bf16[4,512,512]{2,1,0:T(8,128)(2,1)} %copy-done.18, f32[4,512]{1,0:T(4,128)S(1)} %bitcast.353, pred[512,512]{1,0:T(8,128)(4,1)S(1)} %fusion.212), kind=kOutput, calls=%fused_computation.85.clone.1 | convolution fusion | flops 274989056 | bytes 3416064 | tf_op jit(solution)/shard_map/transpose(jvp())/while/body/eval_jaxpr/checkpoint/thd,shd->hts/dot_general | solution.py:265
  165.8 1.8 fusion.219
  171.2 5.0 %reduce-window.150 = f32[4,4,128]{2,1,0:T(4,128)S(1)} reduce-window(f32[4,4,128]{2,1,0:T(4,128)S(1)} %reshape.631, f32[]{:T(128)} %constant.142.clone.1..sunk.1), window={size=1x1x128 pad=0_0x0_0x0_127}, to_apply=%region_24.24 | reduce-window | flops 260096 | bytes 16388 | tf_op jit(solution)/shard_map/reduce-window.60
  176.8 1.3 dynamic-slice_bitcast_fusion.10
  180.0 1.9 dynamic-slice_bitcast_fusion.13
  187.4 1.9 fusion.210
  190.2 2.5 %fusion.213 = (f32[4,512]{1,0:T(4,128)S(1)}, f32[4,512]{1,0:T(4,128)S(1)}, bf16[4,512,512]{2,1,0:T(8,128)(2,1)S(1)}) fusion(f32[4,512]{1,0:T(4,128)S(1)} %bitcast.350, f32[4,512,512]{2,1,0:T(8,128)S(1)} %fusion.211, pred[512,512]{1,0:T(8,128)(4,1)S(1)} %fusion.212, bf16[512,4,128]{2,0,1:T(8,128)(2,1)S(1)} %copy-done.1, f32[512,4,128]{0,2,1:T(8,128)S(1)} %bitcast.337), kind=kOutput, calls=%fused_computation.107.clone.1 | convolution fusion | flops 278917120 | bytes 8151040 | tf_op jit(solution)/shard_map/transpose(jvp())/while/body/eval_jaxpr/checkpoint/hts,she->the/dot_general | solution.py:267
  192.8 3.2 %fusion.214 = (bf16[1,512,4,128]{3,1,2,0:T(8,128)(2,1)}, f32[4,128]{1,0:T(4,128)S(1)}) fusion(f32[4,128]{1,0:T(4,128)S(1)} %get-tuple-element.960, bf16[512,4,128]{2,0,1:T(8,128)(2,1)S(1)} %copy-done.2, bf16[512,4,128]{2,0,1:T(8,128)(2,1)S(1)} %get-tuple-element.967, bf16[512,4,128]{2,0,1:T(8,128)(2,1)S(1)} %dynamic-slice_bitcast_fusion.11, ...), kind=kOutput, calls=%fused_computation.110.clone.1 | convolution fusion | flops 276823552 | bytes 4468736 | tf_op jit(solution)/shard_map/transpose(jvp())/while/body/eval_jaxpr/checkpoint/thd,shd->hts/dot_general | solution.py:265
  196.0 3.8 %fusion.220 = bf16[4,128,512]{2,1,0:T(8,128)(2,1)S(1)} fusion(f32[4,512,512]{2,1,0:T(8,128)} %copy-done, f32[4,512]{1,0:T(4,128)S(1)} %bitcast.352, pred[512,512]{1,0:T(8,128)(4,1)S(1)} %fusion.212, f32[512,4,128]{0,2,1:T(8,128)S(1)} %bitcast.338), kind=kOutput, calls=%fused_computation.81.clone.1 | convolution fusion | flops 274726912 | bytes 6037504 | tf_op jit(solution)/shard_map/transpose(jvp())/while/body/eval_jaxpr/checkpoint/hts,she->the/dot_general | solution.py:267
  199.8 1.4 fusion.221
  203.1 1.9 convolution_add_fusion.5
  205.0 3.3 %fusion.218 = bf16[4,512,128]{2,1,0:T(8,128)(2,1)S(1)} fusion(bf16[512,4,128]{2,0,1:T(8,128)(2,1)S(1)} %fusion.209, bf16[4,512,512]{2,1,0:T(8,128)(2,1)} %copy-done.18, f32[4,512]{1,0:T(4,128)S(1)} %bitcast.353, pred[512,512]{1,0:T(8,128)(4,1)S(1)} %fusion.212), kind=kOutput, calls=%fused_computation.85.clone.1 | convolution fusion | flops 274989056 | bytes 3416064 | tf_op jit(solution)/shard_map/transpose(jvp())/while/body/eval_jaxpr/checkpoint/thd,shd->hts/dot_general | solution.py:265
  208.4 1.8 fusion.219
  213.8 5.0 %reduce-window.150 = f32[4,4,128]{2,1,0:T(4,128)S(1)} reduce-window(f32[4,4,128]{2,1,0:T(4,128)S(1)} %reshape.631, f32[]{:T(128)} %constant.142.clone.1..sunk.1), window={size=1x1x128 pad=0_0x0_0x0_127}, to_apply=%region_24.24 | reduce-window | flops 260096 | bytes 16388 | tf_op jit(solution)/shard_map/reduce-window.60
  219.3 2.3 reshape.592
  221.7 2.2 reshape.593
  225.8 21.1 %shard_map.119 = f32[4,64]{1,0:T(4,128)} custom-call(f32[2,4,64]{2,1,0:T(4,128)} %bitcast.368), custom_call_target="tpu_custom_call" | custom-call | tf_op jit(solution)/shard_map/pallas_call | solution.py:120
  246.9 1.2 copy.362
  (227 shorter events, 54.7 us)
Async XLA Ops:
  6.6 7.5 %copy-start.7 = (bf16[1,1024,512]{2,1,0:T(8,128)(2,1)S(1)}, bf16[1,1024,512]{2,1,0:T(8,128)(2,1)}, u32[]{:S(2)}) copy-start(bf16[1,1024,512]{2,1,0:T(8,128)(2,1)} %param.12) | copy-start | bytes 3145732
  8.2 6.5 %copy-start.16 = (f32[4,128]{1,0:T(4,128)S(1)}, f32[4,128]{1,0:T(4,128)}, u32[]{:S(2)}) copy-start(f32[4,128]{1,0:T(4,128)} %param.16) | copy-start | bytes 6148
  88.9 5.9 %copy-start.8 = (bf16[1,1024,512]{2,1,0:T(8,128)(2,1)S(1)}, bf16[1,1024,512]{2,1,0:T(8,128)(2,1)}, u32[]{:S(2)}) copy-start(bf16[1,1024,512]{2,1,0:T(8,128)(2,1)} %param.11) | copy-start | bytes 3145732
  90.4 8.0 %copy-start.15 = (f32[1,4,1024]{2,1,0:T(4,128)S(1)}, f32[1,4,1024]{2,1,0:T(4,128)}, u32[]{:S(2)}) copy-start(f32[1,4,1024]{2,1,0:T(4,128)} %param.14) | copy-start | bytes 49156
  125.7 3.0 %copy-start.9 = (bf16[1,1024,512]{2,1,0:T(8,128)(2,1)S(1)}, bf16[1,1024,512]{2,1,0:T(8,128)(2,1)}, u32[]{:S(2)}) copy-start(bf16[1,1024,512]{2,1,0:T(8,128)(2,1)} %param.17) | copy-start | bytes 3145732
  134.2 5.2 %copy-start.3 = (bf16[2,512,4,128]{3,1,2,0:T(8,128)(2,1)}, bf16[2,512,4,128]{3,1,2,0:T(8,128)(2,1)S(1)}, u32[]{:S(2)}) copy-start(bf16[2,512,4,128]{3,1,2,0:T(8,128)(2,1)S(1)} %get-tuple-element.1063) | copy-start | bytes 3145732 | tf_op jit(solution)/shard_map/transpose(jvp())/while
  134.2 5.2 %copy-start.5 = (f32[2,512,4,128]{3,2,1,0:T(4,128)S(1)}, f32[2,512,4,128]{3,2,1,0:T(4,128)}, u32[]{:S(2)}) copy-start(f32[2,512,4,128]{3,2,1,0:T(4,128)} %get-tuple-element.1067) | copy-start | bytes 6291460 | tf_op jit(solution)/shard_map/transpose(jvp())/while
  139.8 7.9 %copy-start.1 = (bf16[512,4,128]{2,0,1:T(8,128)(2,1)S(1)}, bf16[512,4,128]{2,0,1:T(8,128)(2,1)}, u32[]{:S(2)}) copy-start(bf16[512,4,128]{2,0,1:T(8,128)(2,1)} %dynamic-slice_bitcast_fusion.13) | copy-start | bytes 1572868 | tf_op jit(solution)/shard_map/transpose(jvp())/while
  147.4 2.8 %copy-start = (f32[4,512,512]{2,1,0:T(8,128)}, f32[4,512,512]{2,1,0:T(8,128)S(1)}, u32[]{:S(2)}) copy-start(f32[4,512,512]{2,1,0:T(8,128)S(1)} %fusion.211) | copy-start | bytes 12582916 | tf_op jit(solution)/shard_map/transpose(jvp())/while
  147.7 2.6 %copy-start.2 = (bf16[512,4,128]{2,0,1:T(8,128)(2,1)S(1)}, bf16[512,4,128]{2,0,1:T(8,128)(2,1)}, u32[]{:S(2)}) copy-start(bf16[512,4,128]{2,0,1:T(8,128)(2,1)} %dynamic-slice_bitcast_fusion.12) | copy-start | bytes 1572868 | tf_op jit(solution)/shard_map/transpose(jvp())/while
  150.2 3.2 %copy-start.18 = (bf16[4,512,512]{2,1,0:T(8,128)(2,1)}, bf16[4,512,512]{2,1,0:T(8,128)(2,1)S(1)}, u32[]{:S(2)}) copy-start(bf16[4,512,512]{2,1,0:T(8,128)(2,1)S(1)} %get-tuple-element.970) | copy-start | bytes 6291460 | tf_op jit(solution)/shard_map/transpose(jvp())/while
  162.4 5.2 %copy-start.6 = (bf16[1,512,4,128]{3,1,2,0:T(8,128)(2,1)S(1)}, bf16[1,512,4,128]{3,1,2,0:T(8,128)(2,1)}, u32[]{:S(2)}) copy-start(bf16[1,512,4,128]{3,1,2,0:T(8,128)(2,1)} %get-tuple-element.978) | copy-start | bytes 1572868 | tf_op jit(solution)/shard_map/transpose(jvp())/while
  162.5 5.2 %copy-start.10 = (bf16[2,512,4,128]{3,2,1,0:T(4,128)(2,1)S(1)}, bf16[2,512,4,128]{3,2,1,0:T(4,128)(2,1)}, u32[]{:S(2)}) copy-start(bf16[2,512,4,128]{3,2,1,0:T(4,128)(2,1)} %get-tuple-element.1039) | copy-start | bytes 3145732 | tf_op jit(solution)/shard_map/transpose(jvp())/while
  162.5 5.2 %copy-start.12 = (bf16[2,512,4,128]{3,2,1,0:T(4,128)(2,1)S(1)}, bf16[2,512,4,128]{3,2,1,0:T(4,128)(2,1)}, u32[]{:S(2)}) copy-start(bf16[2,512,4,128]{3,2,1,0:T(4,128)(2,1)} %get-tuple-element.1040) | copy-start | bytes 3145732 | tf_op jit(solution)/shard_map/transpose(jvp())/while
  167.7 9.0 %copy-start.4 = (bf16[2,512,4,128]{3,1,2,0:T(8,128)(2,1)S(1)}, bf16[2,512,4,128]{3,1,2,0:T(8,128)(2,1)}, u32[]{:S(2)}) copy-start(bf16[2,512,4,128]{3,1,2,0:T(8,128)(2,1)} %copy-done.3) | copy-start | bytes 3145732 | tf_op jit(solution)/shard_map/transpose(jvp())/while
  168.6 1.0 copy-start.11
  168.6 1.3 copy-start.13
  176.7 5.2 %copy-start.3 = (bf16[2,512,4,128]{3,1,2,0:T(8,128)(2,1)}, bf16[2,512,4,128]{3,1,2,0:T(8,128)(2,1)S(1)}, u32[]{:S(2)}) copy-start(bf16[2,512,4,128]{3,1,2,0:T(8,128)(2,1)S(1)} %get-tuple-element.1063) | copy-start | bytes 3145732 | tf_op jit(solution)/shard_map/transpose(jvp())/while
  176.7 5.2 %copy-start.5 = (f32[2,512,4,128]{3,2,1,0:T(4,128)S(1)}, f32[2,512,4,128]{3,2,1,0:T(4,128)}, u32[]{:S(2)}) copy-start(f32[2,512,4,128]{3,2,1,0:T(4,128)} %get-tuple-element.1067) | copy-start | bytes 6291460 | tf_op jit(solution)/shard_map/transpose(jvp())/while
  182.4 7.9 %copy-start.1 = (bf16[512,4,128]{2,0,1:T(8,128)(2,1)S(1)}, bf16[512,4,128]{2,0,1:T(8,128)(2,1)}, u32[]{:S(2)}) copy-start(bf16[512,4,128]{2,0,1:T(8,128)(2,1)} %dynamic-slice_bitcast_fusion.13) | copy-start | bytes 1572868 | tf_op jit(solution)/shard_map/transpose(jvp())/while
  190.0 2.8 %copy-start = (f32[4,512,512]{2,1,0:T(8,128)}, f32[4,512,512]{2,1,0:T(8,128)S(1)}, u32[]{:S(2)}) copy-start(f32[4,512,512]{2,1,0:T(8,128)S(1)} %fusion.211) | copy-start | bytes 12582916 | tf_op jit(solution)/shard_map/transpose(jvp())/while
  190.2 2.6 %copy-start.2 = (bf16[512,4,128]{2,0,1:T(8,128)(2,1)S(1)}, bf16[512,4,128]{2,0,1:T(8,128)(2,1)}, u32[]{:S(2)}) copy-start(bf16[512,4,128]{2,0,1:T(8,128)(2,1)} %dynamic-slice_bitcast_fusion.12) | copy-start | bytes 1572868 | tf_op jit(solution)/shard_map/transpose(jvp())/while
  192.8 3.2 %copy-start.18 = (bf16[4,512,512]{2,1,0:T(8,128)(2,1)}, bf16[4,512,512]{2,1,0:T(8,128)(2,1)S(1)}, u32[]{:S(2)}) copy-start(bf16[4,512,512]{2,1,0:T(8,128)(2,1)S(1)} %get-tuple-element.970) | copy-start | bytes 6291460 | tf_op jit(solution)/shard_map/transpose(jvp())/while
  205.0 5.2 %copy-start.6 = (bf16[1,512,4,128]{3,1,2,0:T(8,128)(2,1)S(1)}, bf16[1,512,4,128]{3,1,2,0:T(8,128)(2,1)}, u32[]{:S(2)}) copy-start(bf16[1,512,4,128]{3,1,2,0:T(8,128)(2,1)} %get-tuple-element.978) | copy-start | bytes 1572868 | tf_op jit(solution)/shard_map/transpose(jvp())/while
  205.0 5.2 %copy-start.10 = (bf16[2,512,4,128]{3,2,1,0:T(4,128)(2,1)S(1)}, bf16[2,512,4,128]{3,2,1,0:T(4,128)(2,1)}, u32[]{:S(2)}) copy-start(bf16[2,512,4,128]{3,2,1,0:T(4,128)(2,1)} %get-tuple-element.1039) | copy-start | bytes 3145732 | tf_op jit(solution)/shard_map/transpose(jvp())/while
  205.0 5.2 %copy-start.12 = (bf16[2,512,4,128]{3,2,1,0:T(4,128)(2,1)S(1)}, bf16[2,512,4,128]{3,2,1,0:T(4,128)(2,1)}, u32[]{:S(2)}) copy-start(bf16[2,512,4,128]{3,2,1,0:T(4,128)(2,1)} %get-tuple-element.1040) | copy-start | bytes 3145732 | tf_op jit(solution)/shard_map/transpose(jvp())/while
  210.2 9.1 %copy-start.4 = (bf16[2,512,4,128]{3,1,2,0:T(8,128)(2,1)S(1)}, bf16[2,512,4,128]{3,1,2,0:T(8,128)(2,1)}, u32[]{:S(2)}) copy-start(bf16[2,512,4,128]{3,1,2,0:T(8,128)(2,1)} %copy-done.3) | copy-start | bytes 3145732 | tf_op jit(solution)/shard_map/transpose(jvp())/while
  211.1 1.0 copy-start.11
  211.2 1.3 copy-start.13
  219.3 28.9 %copy-start.17 = (f32[2,4,512]{2,1,0:T(4,128)}, f32[2,4,512]{2,1,0:T(4,128)S(1)}, u32[]{:S(2)}) copy-start(f32[2,4,512]{2,1,0:T(4,128)S(1)} %get-tuple-element.447) | copy-start | bytes 49156
  219.3 4.6 %copy-start.14 = (bf16[2,512,4,128]{3,2,1,0:T(4,128)(2,1)S(1)}, bf16[2,512,4,128]{3,2,1,0:T(4,128)(2,1)}, u32[]{:S(2)}) copy-start(bf16[2,512,4,128]{3,2,1,0:T(4,128)(2,1)} %get-tuple-element.446) | copy-start | bytes 3145732

commit v9 on v6

--- a/solution.py
+++ b/solution.py
@@ -8,7 +8,7 @@
 BLOCK = 512
 
 
-PRECISE = lax.Precision.HIGHEST
+PRECISE = lax.Precision.HIGH
 
 
 def passed_along(value, axis, steps):

time: 243 us -> 235 us (0.967)
  matrix products: 65.6 us -> 57.7 us
    dot_general x8, matrix products: 15.6 us -> 10.3 us  [block_step(): jnp.einsum('thd,hde->the', q_float, carried, precision=PRECISE)]
where the time goes in v9:
time: 235 us; the launch traced here: 233 us
  Pallas kernels  80.6 us (34%)
  local copies, waits for them, and re-layouts  60.6 us (26%)
  matrix products  57.7 us (25%)
  other arithmetic  32.1 us (14%)
    pallas_call x1, Pallas kernels, both_scans_kernel(): pl.pallas_call(scan_kernel, out_shape=(out, out), in_specs=[pl.BlockSpec(...  67 us
    another operation x27, other arithmetic  20 us
    dot_general x6, matrix products, block_step(): jnp.einsum('hts,she->the', weights, v_block, preferred_element_type=jnp.f...  19.2 us
    dot_general x6, matrix products, block_step(): jnp.einsum('thd,shd->hts', q_block, k_bf, preferred_element_type=jnp.floa...  14.5 us
    pallas_call x1, Pallas kernels, gain_sum(): pl.pallas_call(gain_sum_kernel, out_shape=jax.ShapeDtypeStruct(shape, par...  13.6 us
    dot_general x8, matrix products, block_step(): jnp.einsum('thd,hde->the', q_float, carried, precision=PRECISE)  10.3 us
    squeeze x10, local copies, waits for them, and re-layouts, run_blocks(): lax.scan(jax.checkpoint(make_step(key_gain, head_width)), start_state, (t...  10.2 us
    dot_general x6, matrix products, block_step(): jnp.einsum('shd,she->hde', k_float * to_end.T[:, :, None], v_float, preci...  9.62 us

profile of v9, /device:TPU:2, one launch (start us, length us, event | category | flops | bytes accessed | tf_op | source)
XLA Modules:
  0.0 232.6 jit_solution(17626117469094585143)
XLA Ops:
  6.6 1.6 copy.255
  8.2 2.1 reshape.591
  11.6 2.0 fusion.107
  15.4 1.3 reshape_squeeze.17
  16.7 2.1 fusion.109
  19.6 67.0 %shard_map.118 = (f32[4,128,128]{2,1,0:T(8,128)S(1)}, f32[4,128,128]{2,1,0:T(8,128)S(1)}) custom-call(f32[4,136,128]{2,1,0:T(8,128)} %get-tuple-element.773.fwd_ref, f32[4,136,128]{2,1,0:T(8,128)} %get-tuple-element.772.bwd_ref), custom_call_target="tpu_custom_call" | custom-call | tf_op jit(solution)/shard_map/pallas_call | solution.py:235
  87.8 1.4 copy.230
  89.2 2.1 reshape_squeeze.20
  91.4 2.3 %copy.231 = bf16[2,512,4,128]{3,1,2,0:T(8,128)(2,1)} copy(bf16[2,512,4,128]{3,2,1,0:T(4,128)(2,1)} %reshape_squeeze.20) | data formatting | bytes 2097152
  94.8 2.4 %copy.232 = bf16[2,512,4,128]{3,1,2,0:T(8,128)(2,1)} copy(bf16[2,512,4,128]{3,2,1,0:T(4,128)(2,1)} %reshape_squeeze.21) | data formatting | bytes 2097152
  97.2 25.8 %while.42 = (s32[]{:T(128)}, f32[4,128,128]{2,1,0:T(8,128)S(1)}, bf16[2,512,4,128]{1,3,2,0:T(8,128)(2,1)}, f32[2,4,128,128]{3,2,1,0:T(8,128)}, f32[2,4,512]{2,1,...) while((s32[]{:T(128)}, f32[4,128,128]{2,1,0:T(8,128)S(1)}, ...), condition=%wide.region_11.12_spmd.clone, body=%wide.region_6.11_spmd.clone.sunk | while | flops 949428288 | bytes 9343697 | solution.py:305
  98.1 1.2 reduce-window.144
  100.6 3.3 %fusion.191 = f32[512,4,128]{0,2,1:T(8,128)S(1)} fusion(bf16[512,4,128]{2,0,1:T(8,128)(2,1)S(1)} %fusion.189, f32[4,512]{1,0:T(4,128)S(1)} %bitcast.354, pred[512,512]{1,0:T(8,128)(4,1)S(1)} %fusion.190, bf16[2,512,4,128]{3,1,2,0:T(8,128)(2,1)} %get-tuple-element.1015, s32[]{:T(128)S(6)} %copy.332, bf16[2,512,4,128]{3,1,2,0:T(8,128)(2,1)} %get-tuple-element.1014), kind=kOutput, calls=%fused_computation.3.clone.1 | convolution fusion | flops 543162368 | bytes 2900992 | tf_op jit(solution)/shard_map/jvp()/while/body/eval_jaxpr/hts,she->the/dot_general | solution.py:277
  105.4 2.5 %fusion.192 = bf16[2,512,4,128]{1,3,2,0:T(8,128)(2,1)} fusion(bf16[2,512,4,128]{1,3,2,0:T(8,128)(2,1)} %get-tuple-element.996, s32[]{:T(128)S(6)} %copy.332, f32[512,4,128]{0,2,1:T(8,128)S(1)} %fusion.191, f32[4,128,128]{2,1,0:T(8,128)S(1)} %get-tuple-element.995, f32[512,4]{0,1:T(4,128)S(1)} %bitcast.346, ...), kind=kOutput, calls=%fused_computation.8.clone.1 | convolution fusion | flops 202375168 | bytes 2892800 | tf_op jit(solution)/shard_map/jvp()/while/body/eval_jaxpr/thd,hde->the/dot_general | solution.py:281
  108.0 2.1 convolution_add_fusion.4
  111.0 1.2 reduce-window.144
  113.5 3.3 %fusion.191 = f32[512,4,128]{0,2,1:T(8,128)S(1)} fusion(bf16[512,4,128]{2,0,1:T(8,128)(2,1)S(1)} %fusion.189, f32[4,512]{1,0:T(4,128)S(1)} %bitcast.354, pred[512,512]{1,0:T(8,128)(4,1)S(1)} %fusion.190, bf16[2,512,4,128]{3,1,2,0:T(8,128)(2,1)} %get-tuple-element.1015, s32[]{:T(128)S(6)} %copy.332, bf16[2,512,4,128]{3,1,2,0:T(8,128)(2,1)} %get-tuple-element.1014), kind=kOutput, calls=%fused_computation.3.clone.1 | convolution fusion | flops 543162368 | bytes 2900992 | tf_op jit(solution)/shard_map/jvp()/while/body/eval_jaxpr/hts,she->the/dot_general | solution.py:277
  118.3 2.5 %fusion.192 = bf16[2,512,4,128]{1,3,2,0:T(8,128)(2,1)} fusion(bf16[2,512,4,128]{1,3,2,0:T(8,128)(2,1)} %get-tuple-element.996, s32[]{:T(128)S(6)} %copy.332, f32[512,4,128]{0,2,1:T(8,128)S(1)} %fusion.191, f32[4,128,128]{2,1,0:T(8,128)S(1)} %get-tuple-element.995, f32[512,4]{0,1:T(4,128)S(1)} %bitcast.346, ...), kind=kOutput, calls=%fused_computation.8.clone.1 | convolution fusion | flops 202375168 | bytes 2892800 | tf_op jit(solution)/shard_map/jvp()/while/body/eval_jaxpr/thd,hde->the/dot_general | solution.py:281
  120.9 2.1 convolution_add_fusion.4
  123.0 1.8 copy.233
  124.8 1.2 convert_element_type.304
  126.1 1.7 reshape.602
  127.7 1.2 broadcast.246.clone
  129.0 1.2 broadcast.246.clone2
  130.2 1.2 broadcast.246.clone2.1
  131.5 79.7 %while.43 = (s32[]{:T(128)}, f32[4,128]{1,0:T(4,128)S(1)}, f32[4,128,128]{2,1,0:T(8,128)S(1)}, bf16[2,512,4,128]{3,2,1,0:T(4,128)(2,1)}, bf16[2,512,4,128]{3,2,1...) while((s32[]{:T(128)}, f32[4,128]{1,0:T(4,128)S(1)}, ...), condition=%wide.region_26.27_spmd.clone, body=%wide.region_12.26_spmd.clone.sunk | while | flops 2388230656 | bytes 116524784 | solution.py:305
  131.5 1.3 dynamic-slice_bitcast_fusion.10
  134.8 1.9 dynamic-slice_bitcast_fusion.13
  140.2 1.2 reduce-window.148
  142.1 1.8 fusion.210
  144.9 2.5 %fusion.213 = (f32[4,512]{1,0:T(4,128)S(1)}, f32[4,512]{1,0:T(4,128)S(1)}, bf16[4,512,512]{2,1,0:T(8,128)(2,1)S(1)}) fusion(f32[4,512]{1,0:T(4,128)S(1)} %bitcast.350, f32[4,512,512]{2,1,0:T(8,128)S(1)} %fusion.211, pred[512,512]{1,0:T(8,128)(4,1)S(1)} %fusion.212, bf16[512,4,128]{2,0,1:T(8,128)(2,1)S(1)} %copy-done.1, f32[512,4,128]{0,2,1:T(8,128)S(1)} %bitcast.337), kind=kOutput, calls=%fused_computation.107.clone.1 | convolution fusion | flops 278917120 | bytes 8151040 | tf_op jit(solution)/shard_map/transpose(jvp())/while/body/eval_jaxpr/checkpoint/hts,she->the/dot_general | solution.py:277
  147.4 3.2 %fusion.214 = (bf16[1,512,4,128]{3,1,2,0:T(8,128)(2,1)}, f32[4,128]{1,0:T(4,128)S(1)}) fusion(f32[4,128]{1,0:T(4,128)S(1)} %get-tuple-element.960, bf16[512,4,128]{2,0,1:T(8,128)(2,1)S(1)} %copy-done.2, bf16[512,4,128]{2,0,1:T(8,128)(2,1)S(1)} %get-tuple-element.967, bf16[512,4,128]{2,0,1:T(8,128)(2,1)S(1)} %dynamic-slice_bitcast_fusion.11, ...), kind=kOutput, calls=%fused_computation.110.clone.1 | convolution fusion | flops 276823552 | bytes 4468736 | tf_op jit(solution)/shard_map/transpose(jvp())/while/body/eval_jaxpr/checkpoint/thd,shd->hts/dot_general | solution.py:275
  150.6 3.8 %fusion.220 = bf16[4,128,512]{2,1,0:T(8,128)(2,1)S(1)} fusion(f32[4,512,512]{2,1,0:T(8,128)} %copy-done, f32[4,512]{1,0:T(4,128)S(1)} %bitcast.352, pred[512,512]{1,0:T(8,128)(4,1)S(1)} %fusion.212, f32[512,4,128]{0,2,1:T(8,128)S(1)} %bitcast.338), kind=kOutput, calls=%fused_computation.81.clone.1 | convolution fusion | flops 274726912 | bytes 6037504 | tf_op jit(solution)/shard_map/transpose(jvp())/while/body/eval_jaxpr/checkpoint/hts,she->the/dot_general | solution.py:277
  157.9 3.3 %fusion.218 = bf16[4,512,128]{2,1,0:T(8,128)(2,1)S(1)} fusion(bf16[512,4,128]{2,0,1:T(8,128)(2,1)S(1)} %fusion.209, bf16[4,512,512]{2,1,0:T(8,128)(2,1)} %copy-done.18, f32[4,512]{1,0:T(4,128)S(1)} %bitcast.353, pred[512,512]{1,0:T(8,128)(4,1)S(1)} %fusion.212), kind=kOutput, calls=%fused_computation.85.clone.1 | convolution fusion | flops 274989056 | bytes 3416064 | tf_op jit(solution)/shard_map/transpose(jvp())/while/body/eval_jaxpr/checkpoint/thd,shd->hts/dot_general | solution.py:275
  165.8 5.0 %reduce-window.150 = f32[4,4,128]{2,1,0:T(4,128)S(1)} reduce-window(f32[4,4,128]{2,1,0:T(4,128)S(1)} %reshape.631, f32[]{:T(128)} %constant.142.clone.1..sunk.1), window={size=1x1x128 pad=0_0x0_0x0_127}, to_apply=%region_24.24 | reduce-window | flops 260096 | bytes 16388 | tf_op jit(solution)/shard_map/reduce-window.60
  171.4 1.3 dynamic-slice_bitcast_fusion.10
  174.6 1.9 dynamic-slice_bitcast_fusion.13
  180.1 1.2 reduce-window.148
  182.0 1.8 fusion.210
  184.7 2.5 %fusion.213 = (f32[4,512]{1,0:T(4,128)S(1)}, f32[4,512]{1,0:T(4,128)S(1)}, bf16[4,512,512]{2,1,0:T(8,128)(2,1)S(1)}) fusion(f32[4,512]{1,0:T(4,128)S(1)} %bitcast.350, f32[4,512,512]{2,1,0:T(8,128)S(1)} %fusion.211, pred[512,512]{1,0:T(8,128)(4,1)S(1)} %fusion.212, bf16[512,4,128]{2,0,1:T(8,128)(2,1)S(1)} %copy-done.1, f32[512,4,128]{0,2,1:T(8,128)S(1)} %bitcast.337), kind=kOutput, calls=%fused_computation.107.clone.1 | convolution fusion | flops 278917120 | bytes 8151040 | tf_op jit(solution)/shard_map/transpose(jvp())/while/body/eval_jaxpr/checkpoint/hts,she->the/dot_general | solution.py:277
  187.3 3.2 %fusion.214 = (bf16[1,512,4,128]{3,1,2,0:T(8,128)(2,1)}, f32[4,128]{1,0:T(4,128)S(1)}) fusion(f32[4,128]{1,0:T(4,128)S(1)} %get-tuple-element.960, bf16[512,4,128]{2,0,1:T(8,128)(2,1)S(1)} %copy-done.2, bf16[512,4,128]{2,0,1:T(8,128)(2,1)S(1)} %get-tuple-element.967, bf16[512,4,128]{2,0,1:T(8,128)(2,1)S(1)} %dynamic-slice_bitcast_fusion.11, ...), kind=kOutput, calls=%fused_computation.110.clone.1 | convolution fusion | flops 276823552 | bytes 4468736 | tf_op jit(solution)/shard_map/transpose(jvp())/while/body/eval_jaxpr/checkpoint/thd,shd->hts/dot_general | solution.py:275
  190.5 3.8 %fusion.220 = bf16[4,128,512]{2,1,0:T(8,128)(2,1)S(1)} fusion(f32[4,512,512]{2,1,0:T(8,128)} %copy-done, f32[4,512]{1,0:T(4,128)S(1)} %bitcast.352, pred[512,512]{1,0:T(8,128)(4,1)S(1)} %fusion.212, f32[512,4,128]{0,2,1:T(8,128)S(1)} %bitcast.338), kind=kOutput, calls=%fused_computation.81.clone.1 | convolution fusion | flops 274726912 | bytes 6037504 | tf_op jit(solution)/shard_map/transpose(jvp())/while/body/eval_jaxpr/checkpoint/hts,she->the/dot_general | solution.py:277
  197.8 3.3 %fusion.218 = bf16[4,512,128]{2,1,0:T(8,128)(2,1)S(1)} fusion(bf16[512,4,128]{2,0,1:T(8,128)(2,1)S(1)} %fusion.209, bf16[4,512,512]{2,1,0:T(8,128)(2,1)} %copy-done.18, f32[4,512]{1,0:T(4,128)S(1)} %bitcast.353, pred[512,512]{1,0:T(8,128)(4,1)S(1)} %fusion.212), kind=kOutput, calls=%fused_computation.85.clone.1 | convolution fusion | flops 274989056 | bytes 3416064 | tf_op jit(solution)/shard_map/transpose(jvp())/while/body/eval_jaxpr/checkpoint/thd,shd->hts/dot_general | solution.py:275
  205.7 5.0 %reduce-window.150 = f32[4,4,128]{2,1,0:T(4,128)S(1)} reduce-window(f32[4,4,128]{2,1,0:T(4,128)S(1)} %reshape.631, f32[]{:T(128)} %constant.142.clone.1..sunk.1), window={size=1x1x128 pad=0_0x0_0x0_127}, to_apply=%region_24.24 | reduce-window | flops 260096 | bytes 16388 | tf_op jit(solution)/shard_map/reduce-window.60
  211.2 2.3 %reshape.592 = bf16[1,1024,512]{2,1,0:T(8,128)(2,1)} reshape(bf16[2,512,4,128]{3,2,1,0:T(4,128)(2,1)} %get-tuple-element.444) | data formatting | bytes 2097152 | tf_op jit(solution)/shard_map/broadcast_in_dim;transpose(jvp())/reshape | solution.py:346
  213.6 2.2 reshape.593
  217.7 13.6 %shard_map.119 = f32[4,64]{1,0:T(4,128)} custom-call(f32[2,4,64]{2,1,0:T(4,128)} %bitcast.368), custom_call_target="tpu_custom_call" | custom-call | tf_op jit(solution)/shard_map/pallas_call | solution.py:131
  231.3 1.2 copy.362
  (227 shorter events, 52.4 us)
Async XLA Ops:
  6.6 7.1 %copy-start.7 = (bf16[1,1024,512]{2,1,0:T(8,128)(2,1)S(1)}, bf16[1,1024,512]{2,1,0:T(8,128)(2,1)}, u32[]{:S(2)}) copy-start(bf16[1,1024,512]{2,1,0:T(8,128)(2,1)} %param.12) | copy-start | bytes 3145732
  8.2 6.0 %copy-start.16 = (f32[4,128]{1,0:T(4,128)S(1)}, f32[4,128]{1,0:T(4,128)}, u32[]{:S(2)}) copy-start(f32[4,128]{1,0:T(4,128)} %param.16) | copy-start | bytes 6148
  87.8 5.9 %copy-start.8 = (bf16[1,1024,512]{2,1,0:T(8,128)(2,1)S(1)}, bf16[1,1024,512]{2,1,0:T(8,128)(2,1)}, u32[]{:S(2)}) copy-start(bf16[1,1024,512]{2,1,0:T(8,128)(2,1)} %param.11) | copy-start | bytes 3145732
  89.2 8.0 %copy-start.15 = (f32[1,4,1024]{2,1,0:T(4,128)S(1)}, f32[1,4,1024]{2,1,0:T(4,128)}, u32[]{:S(2)}) copy-start(f32[1,4,1024]{2,1,0:T(4,128)} %param.14) | copy-start | bytes 49156
  123.0 3.0 %copy-start.9 = (bf16[1,1024,512]{2,1,0:T(8,128)(2,1)S(1)}, bf16[1,1024,512]{2,1,0:T(8,128)(2,1)}, u32[]{:S(2)}) copy-start(bf16[1,1024,512]{2,1,0:T(8,128)(2,1)} %param.17) | copy-start | bytes 3145732
  131.5 5.2 %copy-start.3 = (bf16[2,512,4,128]{3,1,2,0:T(8,128)(2,1)}, bf16[2,512,4,128]{3,1,2,0:T(8,128)(2,1)S(1)}, u32[]{:S(2)}) copy-start(bf16[2,512,4,128]{3,1,2,0:T(8,128)(2,1)S(1)} %get-tuple-element.1063) | copy-start | bytes 3145732 | tf_op jit(solution)/shard_map/transpose(jvp())/while
  131.5 5.2 %copy-start.5 = (f32[2,512,4,128]{3,2,1,0:T(4,128)S(1)}, f32[2,512,4,128]{3,2,1,0:T(4,128)}, u32[]{:S(2)}) copy-start(f32[2,512,4,128]{3,2,1,0:T(4,128)} %get-tuple-element.1067) | copy-start | bytes 6291460 | tf_op jit(solution)/shard_map/transpose(jvp())/while
  137.1 7.7 %copy-start.1 = (bf16[512,4,128]{2,0,1:T(8,128)(2,1)S(1)}, bf16[512,4,128]{2,0,1:T(8,128)(2,1)}, u32[]{:S(2)}) copy-start(bf16[512,4,128]{2,0,1:T(8,128)(2,1)} %dynamic-slice_bitcast_fusion.13) | copy-start | bytes 1572868 | tf_op jit(solution)/shard_map/transpose(jvp())/while
  144.6 2.8 %copy-start = (f32[4,512,512]{2,1,0:T(8,128)}, f32[4,512,512]{2,1,0:T(8,128)S(1)}, u32[]{:S(2)}) copy-start(f32[4,512,512]{2,1,0:T(8,128)S(1)} %fusion.211) | copy-start | bytes 12582916 | tf_op jit(solution)/shard_map/transpose(jvp())/while
  144.8 2.6 %copy-start.2 = (bf16[512,4,128]{2,0,1:T(8,128)(2,1)S(1)}, bf16[512,4,128]{2,0,1:T(8,128)(2,1)}, u32[]{:S(2)}) copy-start(bf16[512,4,128]{2,0,1:T(8,128)(2,1)} %dynamic-slice_bitcast_fusion.12) | copy-start | bytes 1572868 | tf_op jit(solution)/shard_map/transpose(jvp())/while
  147.4 3.2 %copy-start.18 = (bf16[4,512,512]{2,1,0:T(8,128)(2,1)}, bf16[4,512,512]{2,1,0:T(8,128)(2,1)S(1)}, u32[]{:S(2)}) copy-start(bf16[4,512,512]{2,1,0:T(8,128)(2,1)S(1)} %get-tuple-element.970) | copy-start | bytes 6291460 | tf_op jit(solution)/shard_map/transpose(jvp())/while
  157.9 4.4 %copy-start.6 = (bf16[1,512,4,128]{3,1,2,0:T(8,128)(2,1)S(1)}, bf16[1,512,4,128]{3,1,2,0:T(8,128)(2,1)}, u32[]{:S(2)}) copy-start(bf16[1,512,4,128]{3,1,2,0:T(8,128)(2,1)} %get-tuple-element.978) | copy-start | bytes 1572868 | tf_op jit(solution)/shard_map/transpose(jvp())/while
  157.9 4.4 %copy-start.10 = (bf16[2,512,4,128]{3,2,1,0:T(4,128)(2,1)S(1)}, bf16[2,512,4,128]{3,2,1,0:T(4,128)(2,1)}, u32[]{:S(2)}) copy-start(bf16[2,512,4,128]{3,2,1,0:T(4,128)(2,1)} %get-tuple-element.1039) | copy-start | bytes 3145732 | tf_op jit(solution)/shard_map/transpose(jvp())/while
  157.9 4.4 %copy-start.12 = (bf16[2,512,4,128]{3,2,1,0:T(4,128)(2,1)S(1)}, bf16[2,512,4,128]{3,2,1,0:T(4,128)(2,1)}, u32[]{:S(2)}) copy-start(bf16[2,512,4,128]{3,2,1,0:T(4,128)(2,1)} %get-tuple-element.1040) | copy-start | bytes 3145732 | tf_op jit(solution)/shard_map/transpose(jvp())/while
  162.3 9.0 %copy-start.4 = (bf16[2,512,4,128]{3,1,2,0:T(8,128)(2,1)S(1)}, bf16[2,512,4,128]{3,1,2,0:T(8,128)(2,1)}, u32[]{:S(2)}) copy-start(bf16[2,512,4,128]{3,1,2,0:T(8,128)(2,1)} %copy-done.3) | copy-start | bytes 3145732 | tf_op jit(solution)/shard_map/transpose(jvp())/while
  163.2 1.0 copy-start.11
  163.2 1.3 copy-start.13
  171.3 5.2 %copy-start.3 = (bf16[2,512,4,128]{3,1,2,0:T(8,128)(2,1)}, bf16[2,512,4,128]{3,1,2,0:T(8,128)(2,1)S(1)}, u32[]{:S(2)}) copy-start(bf16[2,512,4,128]{3,1,2,0:T(8,128)(2,1)S(1)} %get-tuple-element.1063) | copy-start | bytes 3145732 | tf_op jit(solution)/shard_map/transpose(jvp())/while
  171.4 5.2 %copy-start.5 = (f32[2,512,4,128]{3,2,1,0:T(4,128)S(1)}, f32[2,512,4,128]{3,2,1,0:T(4,128)}, u32[]{:S(2)}) copy-start(f32[2,512,4,128]{3,2,1,0:T(4,128)} %get-tuple-element.1067) | copy-start | bytes 6291460 | tf_op jit(solution)/shard_map/transpose(jvp())/while
  177.0 7.7 %copy-start.1 = (bf16[512,4,128]{2,0,1:T(8,128)(2,1)S(1)}, bf16[512,4,128]{2,0,1:T(8,128)(2,1)}, u32[]{:S(2)}) copy-start(bf16[512,4,128]{2,0,1:T(8,128)(2,1)} %dynamic-slice_bitcast_fusion.13) | copy-start | bytes 1572868 | tf_op jit(solution)/shard_map/transpose(jvp())/while
  184.5 2.8 %copy-start = (f32[4,512,512]{2,1,0:T(8,128)}, f32[4,512,512]{2,1,0:T(8,128)S(1)}, u32[]{:S(2)}) copy-start(f32[4,512,512]{2,1,0:T(8,128)S(1)} %fusion.211) | copy-start | bytes 12582916 | tf_op jit(solution)/shard_map/transpose(jvp())/while
  184.7 2.6 %copy-start.2 = (bf16[512,4,128]{2,0,1:T(8,128)(2,1)S(1)}, bf16[512,4,128]{2,0,1:T(8,128)(2,1)}, u32[]{:S(2)}) copy-start(bf16[512,4,128]{2,0,1:T(8,128)(2,1)} %dynamic-slice_bitcast_fusion.12) | copy-start | bytes 1572868 | tf_op jit(solution)/shard_map/transpose(jvp())/while
  187.3 3.2 %copy-start.18 = (bf16[4,512,512]{2,1,0:T(8,128)(2,1)}, bf16[4,512,512]{2,1,0:T(8,128)(2,1)S(1)}, u32[]{:S(2)}) copy-start(bf16[4,512,512]{2,1,0:T(8,128)(2,1)S(1)} %get-tuple-element.970) | copy-start | bytes 6291460 | tf_op jit(solution)/shard_map/transpose(jvp())/while
  197.7 4.4 %copy-start.6 = (bf16[1,512,4,128]{3,1,2,0:T(8,128)(2,1)S(1)}, bf16[1,512,4,128]{3,1,2,0:T(8,128)(2,1)}, u32[]{:S(2)}) copy-start(bf16[1,512,4,128]{3,1,2,0:T(8,128)(2,1)} %get-tuple-element.978) | copy-start | bytes 1572868 | tf_op jit(solution)/shard_map/transpose(jvp())/while
  197.7 4.4 %copy-start.10 = (bf16[2,512,4,128]{3,2,1,0:T(4,128)(2,1)S(1)}, bf16[2,512,4,128]{3,2,1,0:T(4,128)(2,1)}, u32[]{:S(2)}) copy-start(bf16[2,512,4,128]{3,2,1,0:T(4,128)(2,1)} %get-tuple-element.1039) | copy-start | bytes 3145732 | tf_op jit(solution)/shard_map/transpose(jvp())/while
  197.7 4.4 %copy-start.12 = (bf16[2,512,4,128]{3,2,1,0:T(4,128)(2,1)S(1)}, bf16[2,512,4,128]{3,2,1,0:T(4,128)(2,1)}, u32[]{:S(2)}) copy-start(bf16[2,512,4,128]{3,2,1,0:T(4,128)(2,1)} %get-tuple-element.1040) | copy-start | bytes 3145732 | tf_op jit(solution)/shard_map/transpose(jvp())/while
  202.1 9.1 %copy-start.4 = (bf16[2,512,4,128]{3,1,2,0:T(8,128)(2,1)S(1)}, bf16[2,512,4,128]{3,1,2,0:T(8,128)(2,1)}, u32[]{:S(2)}) copy-start(bf16[2,512,4,128]{3,1,2,0:T(8,128)(2,1)} %copy-done.3) | copy-start | bytes 3145732 | tf_op jit(solution)/shard_map/transpose(jvp())/while
  203.1 1.0 copy-start.11
  203.1 1.3 copy-start.13
  211.2 21.3 %copy-start.17 = (f32[2,4,512]{2,1,0:T(4,128)}, f32[2,4,512]{2,1,0:T(4,128)S(1)}, u32[]{:S(2)}) copy-start(f32[2,4,512]{2,1,0:T(4,128)S(1)} %get-tuple-element.447) | copy-start | bytes 49156
  211.2 4.6 %copy-start.14 = (bf16[2,512,4,128]{3,2,1,0:T(4,128)(2,1)S(1)}, bf16[2,512,4,128]{3,2,1,0:T(4,128)(2,1)}, u32[]{:S(2)}) copy-start(bf16[2,512,4,128]{3,2,1,0:T(4,128)(2,1)} %get-tuple-element.446) | copy-start | bytes 3145732

commit v10 on v8

--- a/solution.py
+++ b/solution.py
@@ -8,7 +8,7 @@
 BLOCK = 512
 
 
-PRECISE = lax.Precision.HIGHEST
+PRECISE = lax.Precision.HIGH
 
 
 def passed_along(value, axis, steps):
@@ -62,26 +62,38 @@
     return scans[0][3], scans[1][3]
 
 
-def gain_sum_kernel(part_ref, total_ref, pair_slot, accs, slots, pair_sem, send_sem, recv_sem):
-    count = lax.axis_size("ctx")
+def gain_sum_kernel(part_ref, total_ref, pair_slot, near, far, pair_sem, send_sem, recv_sem):
+    group = near.shape[0]
+    outer = far.shape[0]
     me = lax.axis_index("ctx")
     row, col = lax.axis_index("dp"), lax.axis_index("head")
     other = 1 - row
-    rounds = slots.shape[0]
-    shifts = [1 << step for step in range(rounds)]
-
-    def partner(shift):
-        return me + shift - 2 * shift * ((me // shift) % 2)
+    inner, upper = me % group, me // group
+
+    def near_peer(index):
+        return upper * group + index
+
+    def far_peer(index):
+        return index * group + inner
+
+    def device(index):
+        return (row, index, col)
 
     barrier = pltpu.get_barrier_semaphore()
     pl.semaphore_signal(
         barrier, inc=1, device_id=(other, me, col), device_id_type=pl.DeviceIdType.MESH
     )
-    for shift in shifts:
+    for step in range(1, group):
         pl.semaphore_signal(
-            barrier, inc=1, device_id=(row, partner(shift), col), device_id_type=pl.DeviceIdType.MESH
+            barrier, inc=1, device_id=device(near_peer((inner + step) % group)),
+            device_id_type=pl.DeviceIdType.MESH,
         )
-    pl.semaphore_wait(barrier, rounds + 1)
+    for step in range(1, outer):
+        pl.semaphore_signal(
+            barrier, inc=1, device_id=device(far_peer((upper + step) % outer)),
+            device_id_type=pl.DeviceIdType.MESH,
+        )
+    pl.semaphore_wait(barrier, group + outer - 1)
 
     pair = pltpu.make_async_remote_copy(
         src_ref=part_ref.at[other],
@@ -94,29 +106,52 @@
     pair.start()
     pair.wait_send()
     pair.wait_recv()
-    accs[0] = part_ref[row] + pair_slot[...]
-
-    for step, shift in enumerate(shifts):
-        copy = pltpu.make_async_remote_copy(
-            src_ref=accs.at[step],
-            dst_ref=slots.at[step],
-            send_sem=send_sem.at[step],
-            recv_sem=recv_sem.at[step],
-            device_id=(row, partner(shift), col),
-            device_id_type=pl.DeviceIdType.MESH,
-        )
-        copy.start()
-        copy.wait_send()
-        copy.wait_recv()
-        accs[step + 1] = accs[step] + slots[step]
-    total_ref[...] = accs[rounds]
+    near[inner] = part_ref[row] + pair_slot[...]
+
+    for level, (slots, size, position, peer_at) in enumerate(
+        ((near, group, inner, near_peer), (far, outer, upper, far_peer))
+    ):
+        if level == 1:
+            total = near[0]
+            for index in range(1, group):
+                total = total + near[index]
+            far[upper] = total
+        copies = []
+        for step in range(1, size):
+            peer = peer_at((position + step) % size)
+            copy = pltpu.make_async_remote_copy(
+                src_ref=slots.at[position],
+                dst_ref=slots.at[position],
+                send_sem=send_sem.at[level, (position + step) % size],
+                recv_sem=recv_sem.at[level, position],
+                device_id=device(peer),
+                device_id_type=pl.DeviceIdType.MESH,
+            )
+            copy.start()
+            copies.append(copy)
+        for step in range(1, size):
+            copies[step - 1].wait_send()
+            source = (position + size - step) % size
+            pltpu.make_async_remote_copy(
+                src_ref=slots.at[source],
+                dst_ref=slots.at[source],
+                send_sem=send_sem.at[level, source],
+                recv_sem=recv_sem.at[level, source],
+                device_id=device(peer_at(source)),
+                device_id_type=pl.DeviceIdType.MESH,
+            ).wait_recv()
+    total = far[0]
+    for index in range(1, outer):
+        total = total + far[index]
+    total_ref[...] = total
 
 
 def gain_sum(part, count):
     heads, width = part.shape
     halves = part.reshape(heads, 2, width // 2).transpose(1, 0, 2)
     shape = halves.shape[1:]
-    rounds = max(1, (count - 1).bit_length())
+    group = 4 if count % 4 == 0 else count
+    outer = count // group
     return pl.pallas_call(
         gain_sum_kernel,
         out_shape=jax.ShapeDtypeStruct(shape, part.dtype),
@@ -124,11 +159,11 @@
         out_specs=pl.BlockSpec(memory_space=pltpu.VMEM),
         scratch_shapes=[
             pltpu.VMEM(shape, part.dtype),
-            pltpu.VMEM((rounds + 1,) + shape, part.dtype),
-            pltpu.VMEM((rounds,) + shape, part.dtype),
+            pltpu.VMEM((group,) + shape, part.dtype),
+            pltpu.VMEM((outer,) + shape, part.dtype),
             pltpu.SemaphoreType.DMA((2,)),
-            pltpu.SemaphoreType.DMA((rounds,)),
-            pltpu.SemaphoreType.DMA((rounds,)),
+            pltpu.SemaphoreType.DMA((2, max(group, outer))),
+            pltpu.SemaphoreType.DMA((2, max(group, outer))),
         ],
         compiler_params=pltpu.CompilerParams(collective_id=0, has_side_effects=True),
     )(halves)

time: 249 us -> 235 us (0.944)
  matrix products: 65.6 us -> 57.7 us
  Pallas kernels: 88.3 us -> 81.7 us
    pallas_call x1, Pallas kernels: 21.1 us -> 14.7 us  [gain_sum(): pl.pallas_call(gain_sum_kernel, out_shape=jax.ShapeDtypeStruct(shape, par...]
    dot_general x8, matrix products: 15.6 us -> 10.3 us  [block_step(): jnp.einsum('thd,hde->the', q_float, carried, precision=PRECISE)]
where the time goes in v10:
time: 235 us; the launch traced here: 234 us
  Pallas kernels  81.7 us (35%)
  local copies, waits for them, and re-layouts  60.6 us (26%)
  matrix products  57.7 us (25%)
  other arithmetic  32.1 us (14%)
    pallas_call x1, Pallas kernels, both_scans_kernel(): pl.pallas_call(scan_kernel, out_shape=(out, out), in_specs=[pl.BlockSpec(...  67 us
    another operation x27, other arithmetic  20 us
    dot_general x6, matrix products, block_step(): jnp.einsum('hts,she->the', weights, v_block, preferred_element_type=jnp.f...  19.2 us
    pallas_call x1, Pallas kernels, gain_sum(): pl.pallas_call(gain_sum_kernel, out_shape=jax.ShapeDtypeStruct(shape, par...  14.7 us
    dot_general x6, matrix products, block_step(): jnp.einsum('thd,shd->hts', q_block, k_bf, preferred_element_type=jnp.floa...  14.5 us
    dot_general x8, matrix products, block_step(): jnp.einsum('thd,hde->the', q_float, carried, precision=PRECISE)  10.3 us
    squeeze x10, local copies, waits for them, and re-layouts, run_blocks(): lax.scan(jax.checkpoint(make_step(key_gain, head_width)), start_state, (t...  10.2 us
    dot_general x6, matrix products, block_step(): jnp.einsum('shd,she->hde', k_float * to_end.T[:, :, None], v_float, preci...  9.62 us

profile of v10, /device:TPU:2, one launch (start us, length us, event | category | flops | bytes accessed | tf_op | source)
XLA Modules:
  0.0 233.6 jit_solution(14023949537443611939)
XLA Ops:
  6.6 1.6 copy.255
  8.2 2.1 reshape.591
  11.6 2.0 fusion.107
  15.4 1.3 reshape_squeeze.17
  16.7 2.1 fusion.109
  19.6 67.0 %shard_map.118 = (f32[4,128,128]{2,1,0:T(8,128)S(1)}, f32[4,128,128]{2,1,0:T(8,128)S(1)}) custom-call(f32[4,136,128]{2,1,0:T(8,128)} %get-tuple-element.773.fwd_ref, f32[4,136,128]{2,1,0:T(8,128)} %get-tuple-element.772.bwd_ref), custom_call_target="tpu_custom_call" | custom-call | tf_op jit(solution)/shard_map/pallas_call | solution.py:260
  87.8 1.4 copy.230
  89.2 2.1 reshape_squeeze.20
  91.4 2.3 copy.231
  94.8 2.4 %copy.232 = bf16[2,512,4,128]{3,1,2,0:T(8,128)(2,1)} copy(bf16[2,512,4,128]{3,2,1,0:T(4,128)(2,1)} %reshape_squeeze.21) | data formatting | bytes 2097152
  97.2 25.8 %while.42 = (s32[]{:T(128)}, f32[4,128,128]{2,1,0:T(8,128)S(1)}, bf16[2,512,4,128]{1,3,2,0:T(8,128)(2,1)}, f32[2,4,128,128]{3,2,1,0:T(8,128)}, f32[2,4,512]{2,1,...) while((s32[]{:T(128)}, f32[4,128,128]{2,1,0:T(8,128)S(1)}, ...), condition=%wide.region_11.12_spmd.clone, body=%wide.region_6.11_spmd.clone.sunk | while | flops 949428288 | bytes 9343697 | solution.py:330
  98.1 1.2 reduce-window.144
  100.6 3.3 %fusion.191 = f32[512,4,128]{0,2,1:T(8,128)S(1)} fusion(bf16[512,4,128]{2,0,1:T(8,128)(2,1)S(1)} %fusion.189, f32[4,512]{1,0:T(4,128)S(1)} %bitcast.354, pred[512,512]{1,0:T(8,128)(4,1)S(1)} %fusion.190, bf16[2,512,4,128]{3,1,2,0:T(8,128)(2,1)} %get-tuple-element.1015, s32[]{:T(128)S(6)} %copy.332, bf16[2,512,4,128]{3,1,2,0:T(8,128)(2,1)} %get-tuple-element.1014), kind=kOutput, calls=%fused_computation.3.clone.1 | convolution fusion | flops 543162368 | bytes 2900992 | tf_op jit(solution)/shard_map/jvp()/while/body/eval_jaxpr/hts,she->the/dot_general | solution.py:302
  105.4 2.5 %fusion.192 = bf16[2,512,4,128]{1,3,2,0:T(8,128)(2,1)} fusion(bf16[2,512,4,128]{1,3,2,0:T(8,128)(2,1)} %get-tuple-element.996, s32[]{:T(128)S(6)} %copy.332, f32[512,4,128]{0,2,1:T(8,128)S(1)} %fusion.191, f32[4,128,128]{2,1,0:T(8,128)S(1)} %get-tuple-element.995, f32[512,4]{0,1:T(4,128)S(1)} %bitcast.346, ...), kind=kOutput, calls=%fused_computation.8.clone.1 | convolution fusion | flops 202375168 | bytes 2892800 | tf_op jit(solution)/shard_map/jvp()/while/body/eval_jaxpr/thd,hde->the/dot_general | solution.py:306
  108.0 2.1 convolution_add_fusion.4
  111.0 1.2 reduce-window.144
  113.5 3.3 %fusion.191 = f32[512,4,128]{0,2,1:T(8,128)S(1)} fusion(bf16[512,4,128]{2,0,1:T(8,128)(2,1)S(1)} %fusion.189, f32[4,512]{1,0:T(4,128)S(1)} %bitcast.354, pred[512,512]{1,0:T(8,128)(4,1)S(1)} %fusion.190, bf16[2,512,4,128]{3,1,2,0:T(8,128)(2,1)} %get-tuple-element.1015, s32[]{:T(128)S(6)} %copy.332, bf16[2,512,4,128]{3,1,2,0:T(8,128)(2,1)} %get-tuple-element.1014), kind=kOutput, calls=%fused_computation.3.clone.1 | convolution fusion | flops 543162368 | bytes 2900992 | tf_op jit(solution)/shard_map/jvp()/while/body/eval_jaxpr/hts,she->the/dot_general | solution.py:302
  118.3 2.5 %fusion.192 = bf16[2,512,4,128]{1,3,2,0:T(8,128)(2,1)} fusion(bf16[2,512,4,128]{1,3,2,0:T(8,128)(2,1)} %get-tuple-element.996, s32[]{:T(128)S(6)} %copy.332, f32[512,4,128]{0,2,1:T(8,128)S(1)} %fusion.191, f32[4,128,128]{2,1,0:T(8,128)S(1)} %get-tuple-element.995, f32[512,4]{0,1:T(4,128)S(1)} %bitcast.346, ...), kind=kOutput, calls=%fused_computation.8.clone.1 | convolution fusion | flops 202375168 | bytes 2892800 | tf_op jit(solution)/shard_map/jvp()/while/body/eval_jaxpr/thd,hde->the/dot_general | solution.py:306
  120.9 2.1 convolution_add_fusion.4
  123.0 1.8 copy.233
  124.8 1.2 convert_element_type.304
  126.1 1.7 reshape.602
  127.7 1.2 broadcast.246.clone
  129.0 1.2 broadcast.246.clone2
  130.2 1.2 broadcast.246.clone2.1
  131.5 79.7 %while.43 = (s32[]{:T(128)}, f32[4,128]{1,0:T(4,128)S(1)}, f32[4,128,128]{2,1,0:T(8,128)S(1)}, bf16[2,512,4,128]{3,2,1,0:T(4,128)(2,1)}, bf16[2,512,4,128]{3,2,1...) while((s32[]{:T(128)}, f32[4,128]{1,0:T(4,128)S(1)}, ...), condition=%wide.region_26.27_spmd.clone, body=%wide.region_12.26_spmd.clone.sunk | while | flops 2388230656 | bytes 116524784 | solution.py:330
  131.5 1.3 dynamic-slice_bitcast_fusion.10
  134.8 1.9 dynamic-slice_bitcast_fusion.13
  140.2 1.2 reduce-window.148
  142.1 1.8 fusion.210
  144.9 2.5 %fusion.213 = (f32[4,512]{1,0:T(4,128)S(1)}, f32[4,512]{1,0:T(4,128)S(1)}, bf16[4,512,512]{2,1,0:T(8,128)(2,1)S(1)}) fusion(f32[4,512]{1,0:T(4,128)S(1)} %bitcast.350, f32[4,512,512]{2,1,0:T(8,128)S(1)} %fusion.211, pred[512,512]{1,0:T(8,128)(4,1)S(1)} %fusion.212, bf16[512,4,128]{2,0,1:T(8,128)(2,1)S(1)} %copy-done.1, f32[512,4,128]{0,2,1:T(8,128)S(1)} %bitcast.337), kind=kOutput, calls=%fused_computation.107.clone.1 | convolution fusion | flops 278917120 | bytes 8151040 | tf_op jit(solution)/shard_map/transpose(jvp())/while/body/eval_jaxpr/checkpoint/hts,she->the/dot_general | solution.py:302
  147.4 3.2 %fusion.214 = (bf16[1,512,4,128]{3,1,2,0:T(8,128)(2,1)}, f32[4,128]{1,0:T(4,128)S(1)}) fusion(f32[4,128]{1,0:T(4,128)S(1)} %get-tuple-element.960, bf16[512,4,128]{2,0,1:T(8,128)(2,1)S(1)} %copy-done.2, bf16[512,4,128]{2,0,1:T(8,128)(2,1)S(1)} %get-tuple-element.967, bf16[512,4,128]{2,0,1:T(8,128)(2,1)S(1)} %dynamic-slice_bitcast_fusion.11, ...), kind=kOutput, calls=%fused_computation.110.clone.1 | convolution fusion | flops 276823552 | bytes 4468736 | tf_op jit(solution)/shard_map/transpose(jvp())/while/body/eval_jaxpr/checkpoint/thd,shd->hts/dot_general | solution.py:300
  150.6 3.8 %fusion.220 = bf16[4,128,512]{2,1,0:T(8,128)(2,1)S(1)} fusion(f32[4,512,512]{2,1,0:T(8,128)} %copy-done, f32[4,512]{1,0:T(4,128)S(1)} %bitcast.352, pred[512,512]{1,0:T(8,128)(4,1)S(1)} %fusion.212, f32[512,4,128]{0,2,1:T(8,128)S(1)} %bitcast.338), kind=kOutput, calls=%fused_computation.81.clone.1 | convolution fusion | flops 274726912 | bytes 6037504 | tf_op jit(solution)/shard_map/transpose(jvp())/while/body/eval_jaxpr/checkpoint/hts,she->the/dot_general | solution.py:302
  157.9 3.3 %fusion.218 = bf16[4,512,128]{2,1,0:T(8,128)(2,1)S(1)} fusion(bf16[512,4,128]{2,0,1:T(8,128)(2,1)S(1)} %fusion.209, bf16[4,512,512]{2,1,0:T(8,128)(2,1)} %copy-done.18, f32[4,512]{1,0:T(4,128)S(1)} %bitcast.353, pred[512,512]{1,0:T(8,128)(4,1)S(1)} %fusion.212), kind=kOutput, calls=%fused_computation.85.clone.1 | convolution fusion | flops 274989056 | bytes 3416064 | tf_op jit(solution)/shard_map/transpose(jvp())/while/body/eval_jaxpr/checkpoint/thd,shd->hts/dot_general | solution.py:300
  165.8 5.0 %reduce-window.150 = f32[4,4,128]{2,1,0:T(4,128)S(1)} reduce-window(f32[4,4,128]{2,1,0:T(4,128)S(1)} %reshape.631, f32[]{:T(128)} %constant.142.clone.1..sunk.1), window={size=1x1x128 pad=0_0x0_0x0_127}, to_apply=%region_24.24 | reduce-window | flops 260096 | bytes 16388 | tf_op jit(solution)/shard_map/reduce-window.60
  171.4 1.3 dynamic-slice_bitcast_fusion.10
  174.6 1.9 dynamic-slice_bitcast_fusion.13
  180.1 1.2 reduce-window.148
  182.0 1.8 fusion.210
  184.7 2.5 %fusion.213 = (f32[4,512]{1,0:T(4,128)S(1)}, f32[4,512]{1,0:T(4,128)S(1)}, bf16[4,512,512]{2,1,0:T(8,128)(2,1)S(1)}) fusion(f32[4,512]{1,0:T(4,128)S(1)} %bitcast.350, f32[4,512,512]{2,1,0:T(8,128)S(1)} %fusion.211, pred[512,512]{1,0:T(8,128)(4,1)S(1)} %fusion.212, bf16[512,4,128]{2,0,1:T(8,128)(2,1)S(1)} %copy-done.1, f32[512,4,128]{0,2,1:T(8,128)S(1)} %bitcast.337), kind=kOutput, calls=%fused_computation.107.clone.1 | convolution fusion | flops 278917120 | bytes 8151040 | tf_op jit(solution)/shard_map/transpose(jvp())/while/body/eval_jaxpr/checkpoint/hts,she->the/dot_general | solution.py:302
  187.3 3.2 %fusion.214 = (bf16[1,512,4,128]{3,1,2,0:T(8,128)(2,1)}, f32[4,128]{1,0:T(4,128)S(1)}) fusion(f32[4,128]{1,0:T(4,128)S(1)} %get-tuple-element.960, bf16[512,4,128]{2,0,1:T(8,128)(2,1)S(1)} %copy-done.2, bf16[512,4,128]{2,0,1:T(8,128)(2,1)S(1)} %get-tuple-element.967, bf16[512,4,128]{2,0,1:T(8,128)(2,1)S(1)} %dynamic-slice_bitcast_fusion.11, ...), kind=kOutput, calls=%fused_computation.110.clone.1 | convolution fusion | flops 276823552 | bytes 4468736 | tf_op jit(solution)/shard_map/transpose(jvp())/while/body/eval_jaxpr/checkpoint/thd,shd->hts/dot_general | solution.py:300
  190.5 3.8 %fusion.220 = bf16[4,128,512]{2,1,0:T(8,128)(2,1)S(1)} fusion(f32[4,512,512]{2,1,0:T(8,128)} %copy-done, f32[4,512]{1,0:T(4,128)S(1)} %bitcast.352, pred[512,512]{1,0:T(8,128)(4,1)S(1)} %fusion.212, f32[512,4,128]{0,2,1:T(8,128)S(1)} %bitcast.338), kind=kOutput, calls=%fused_computation.81.clone.1 | convolution fusion | flops 274726912 | bytes 6037504 | tf_op jit(solution)/shard_map/transpose(jvp())/while/body/eval_jaxpr/checkpoint/hts,she->the/dot_general | solution.py:302
  197.8 3.3 %fusion.218 = bf16[4,512,128]{2,1,0:T(8,128)(2,1)S(1)} fusion(bf16[512,4,128]{2,0,1:T(8,128)(2,1)S(1)} %fusion.209, bf16[4,512,512]{2,1,0:T(8,128)(2,1)} %copy-done.18, f32[4,512]{1,0:T(4,128)S(1)} %bitcast.353, pred[512,512]{1,0:T(8,128)(4,1)S(1)} %fusion.212), kind=kOutput, calls=%fused_computation.85.clone.1 | convolution fusion | flops 274989056 | bytes 3416064 | tf_op jit(solution)/shard_map/transpose(jvp())/while/body/eval_jaxpr/checkpoint/thd,shd->hts/dot_general | solution.py:300
  205.7 5.0 %reduce-window.150 = f32[4,4,128]{2,1,0:T(4,128)S(1)} reduce-window(f32[4,4,128]{2,1,0:T(4,128)S(1)} %reshape.631, f32[]{:T(128)} %constant.142.clone.1..sunk.1), window={size=1x1x128 pad=0_0x0_0x0_127}, to_apply=%region_24.24 | reduce-window | flops 260096 | bytes 16388 | tf_op jit(solution)/shard_map/reduce-window.60
  211.2 2.3 reshape.592
  213.6 2.2 reshape.593
  217.7 14.7 %shard_map.119 = f32[4,64]{1,0:T(4,128)} custom-call(f32[2,4,64]{2,1,0:T(4,128)} %bitcast.368), custom_call_target="tpu_custom_call" | custom-call | tf_op jit(solution)/shard_map/pallas_call | solution.py:155
  232.4 1.2 copy.362
  (227 shorter events, 52.4 us)
Async XLA Ops:
  6.6 7.1 %copy-start.7 = (bf16[1,1024,512]{2,1,0:T(8,128)(2,1)S(1)}, bf16[1,1024,512]{2,1,0:T(8,128)(2,1)}, u32[]{:S(2)}) copy-start(bf16[1,1024,512]{2,1,0:T(8,128)(2,1)} %param.12) | copy-start | bytes 3145732
  8.2 6.0 %copy-start.16 = (f32[4,128]{1,0:T(4,128)S(1)}, f32[4,128]{1,0:T(4,128)}, u32[]{:S(2)}) copy-start(f32[4,128]{1,0:T(4,128)} %param.16) | copy-start | bytes 6148
  87.8 5.9 %copy-start.8 = (bf16[1,1024,512]{2,1,0:T(8,128)(2,1)S(1)}, bf16[1,1024,512]{2,1,0:T(8,128)(2,1)}, u32[]{:S(2)}) copy-start(bf16[1,1024,512]{2,1,0:T(8,128)(2,1)} %param.11) | copy-start | bytes 3145732
  89.2 8.0 %copy-start.15 = (f32[1,4,1024]{2,1,0:T(4,128)S(1)}, f32[1,4,1024]{2,1,0:T(4,128)}, u32[]{:S(2)}) copy-start(f32[1,4,1024]{2,1,0:T(4,128)} %param.14) | copy-start | bytes 49156
  123.0 3.0 %copy-start.9 = (bf16[1,1024,512]{2,1,0:T(8,128)(2,1)S(1)}, bf16[1,1024,512]{2,1,0:T(8,128)(2,1)}, u32[]{:S(2)}) copy-start(bf16[1,1024,512]{2,1,0:T(8,128)(2,1)} %param.17) | copy-start | bytes 3145732
  131.5 5.2 %copy-start.3 = (bf16[2,512,4,128]{3,1,2,0:T(8,128)(2,1)}, bf16[2,512,4,128]{3,1,2,0:T(8,128)(2,1)S(1)}, u32[]{:S(2)}) copy-start(bf16[2,512,4,128]{3,1,2,0:T(8,128)(2,1)S(1)} %get-tuple-element.1063) | copy-start | bytes 3145732 | tf_op jit(solution)/shard_map/transpose(jvp())/while
  131.5 5.2 %copy-start.5 = (f32[2,512,4,128]{3,2,1,0:T(4,128)S(1)}, f32[2,512,4,128]{3,2,1,0:T(4,128)}, u32[]{:S(2)}) copy-start(f32[2,512,4,128]{3,2,1,0:T(4,128)} %get-tuple-element.1067) | copy-start | bytes 6291460 | tf_op jit(solution)/shard_map/transpose(jvp())/while
  137.1 7.7 %copy-start.1 = (bf16[512,4,128]{2,0,1:T(8,128)(2,1)S(1)}, bf16[512,4,128]{2,0,1:T(8,128)(2,1)}, u32[]{:S(2)}) copy-start(bf16[512,4,128]{2,0,1:T(8,128)(2,1)} %dynamic-slice_bitcast_fusion.13) | copy-start | bytes 1572868 | tf_op jit(solution)/shard_map/transpose(jvp())/while
  144.6 2.8 %copy-start = (f32[4,512,512]{2,1,0:T(8,128)}, f32[4,512,512]{2,1,0:T(8,128)S(1)}, u32[]{:S(2)}) copy-start(f32[4,512,512]{2,1,0:T(8,128)S(1)} %fusion.211) | copy-start | bytes 12582916 | tf_op jit(solution)/shard_map/transpose(jvp())/while
  144.8 2.6 %copy-start.2 = (bf16[512,4,128]{2,0,1:T(8,128)(2,1)S(1)}, bf16[512,4,128]{2,0,1:T(8,128)(2,1)}, u32[]{:S(2)}) copy-start(bf16[512,4,128]{2,0,1:T(8,128)(2,1)} %dynamic-slice_bitcast_fusion.12) | copy-start | bytes 1572868 | tf_op jit(solution)/shard_map/transpose(jvp())/while
  147.4 3.2 %copy-start.18 = (bf16[4,512,512]{2,1,0:T(8,128)(2,1)}, bf16[4,512,512]{2,1,0:T(8,128)(2,1)S(1)}, u32[]{:S(2)}) copy-start(bf16[4,512,512]{2,1,0:T(8,128)(2,1)S(1)} %get-tuple-element.970) | copy-start | bytes 6291460 | tf_op jit(solution)/shard_map/transpose(jvp())/while
  157.9 4.4 %copy-start.6 = (bf16[1,512,4,128]{3,1,2,0:T(8,128)(2,1)S(1)}, bf16[1,512,4,128]{3,1,2,0:T(8,128)(2,1)}, u32[]{:S(2)}) copy-start(bf16[1,512,4,128]{3,1,2,0:T(8,128)(2,1)} %get-tuple-element.978) | copy-start | bytes 1572868 | tf_op jit(solution)/shard_map/transpose(jvp())/while
  157.9 4.4 %copy-start.10 = (bf16[2,512,4,128]{3,2,1,0:T(4,128)(2,1)S(1)}, bf16[2,512,4,128]{3,2,1,0:T(4,128)(2,1)}, u32[]{:S(2)}) copy-start(bf16[2,512,4,128]{3,2,1,0:T(4,128)(2,1)} %get-tuple-element.1039) | copy-start | bytes 3145732 | tf_op jit(solution)/shard_map/transpose(jvp())/while
  157.9 4.4 %copy-start.12 = (bf16[2,512,4,128]{3,2,1,0:T(4,128)(2,1)S(1)}, bf16[2,512,4,128]{3,2,1,0:T(4,128)(2,1)}, u32[]{:S(2)}) copy-start(bf16[2,512,4,128]{3,2,1,0:T(4,128)(2,1)} %get-tuple-element.1040) | copy-start | bytes 3145732 | tf_op jit(solution)/shard_map/transpose(jvp())/while
  162.3 9.0 %copy-start.4 = (bf16[2,512,4,128]{3,1,2,0:T(8,128)(2,1)S(1)}, bf16[2,512,4,128]{3,1,2,0:T(8,128)(2,1)}, u32[]{:S(2)}) copy-start(bf16[2,512,4,128]{3,1,2,0:T(8,128)(2,1)} %copy-done.3) | copy-start | bytes 3145732 | tf_op jit(solution)/shard_map/transpose(jvp())/while
  163.2 1.0 copy-start.11
  163.2 1.3 copy-start.13
  171.3 5.2 %copy-start.3 = (bf16[2,512,4,128]{3,1,2,0:T(8,128)(2,1)}, bf16[2,512,4,128]{3,1,2,0:T(8,128)(2,1)S(1)}, u32[]{:S(2)}) copy-start(bf16[2,512,4,128]{3,1,2,0:T(8,128)(2,1)S(1)} %get-tuple-element.1063) | copy-start | bytes 3145732 | tf_op jit(solution)/shard_map/transpose(jvp())/while
  171.4 5.2 %copy-start.5 = (f32[2,512,4,128]{3,2,1,0:T(4,128)S(1)}, f32[2,512,4,128]{3,2,1,0:T(4,128)}, u32[]{:S(2)}) copy-start(f32[2,512,4,128]{3,2,1,0:T(4,128)} %get-tuple-element.1067) | copy-start | bytes 6291460 | tf_op jit(solution)/shard_map/transpose(jvp())/while
  177.0 7.7 %copy-start.1 = (bf16[512,4,128]{2,0,1:T(8,128)(2,1)S(1)}, bf16[512,4,128]{2,0,1:T(8,128)(2,1)}, u32[]{:S(2)}) copy-start(bf16[512,4,128]{2,0,1:T(8,128)(2,1)} %dynamic-slice_bitcast_fusion.13) | copy-start | bytes 1572868 | tf_op jit(solution)/shard_map/transpose(jvp())/while
  184.5 2.8 %copy-start = (f32[4,512,512]{2,1,0:T(8,128)}, f32[4,512,512]{2,1,0:T(8,128)S(1)}, u32[]{:S(2)}) copy-start(f32[4,512,512]{2,1,0:T(8,128)S(1)} %fusion.211) | copy-start | bytes 12582916 | tf_op jit(solution)/shard_map/transpose(jvp())/while
  184.7 2.6 %copy-start.2 = (bf16[512,4,128]{2,0,1:T(8,128)(2,1)S(1)}, bf16[512,4,128]{2,0,1:T(8,128)(2,1)}, u32[]{:S(2)}) copy-start(bf16[512,4,128]{2,0,1:T(8,128)(2,1)} %dynamic-slice_bitcast_fusion.12) | copy-start | bytes 1572868 | tf_op jit(solution)/shard_map/transpose(jvp())/while
  187.3 3.2 %copy-start.18 = (bf16[4,512,512]{2,1,0:T(8,128)(2,1)}, bf16[4,512,512]{2,1,0:T(8,128)(2,1)S(1)}, u32[]{:S(2)}) copy-start(bf16[4,512,512]{2,1,0:T(8,128)(2,1)S(1)} %get-tuple-element.970) | copy-start | bytes 6291460 | tf_op jit(solution)/shard_map/transpose(jvp())/while
  197.7 4.4 %copy-start.6 = (bf16[1,512,4,128]{3,1,2,0:T(8,128)(2,1)S(1)}, bf16[1,512,4,128]{3,1,2,0:T(8,128)(2,1)}, u32[]{:S(2)}) copy-start(bf16[1,512,4,128]{3,1,2,0:T(8,128)(2,1)} %get-tuple-element.978) | copy-start | bytes 1572868 | tf_op jit(solution)/shard_map/transpose(jvp())/while
  197.7 4.4 %copy-start.10 = (bf16[2,512,4,128]{3,2,1,0:T(4,128)(2,1)S(1)}, bf16[2,512,4,128]{3,2,1,0:T(4,128)(2,1)}, u32[]{:S(2)}) copy-start(bf16[2,512,4,128]{3,2,1,0:T(4,128)(2,1)} %get-tuple-element.1039) | copy-start | bytes 3145732 | tf_op jit(solution)/shard_map/transpose(jvp())/while
  197.7 4.4 %copy-start.12 = (bf16[2,512,4,128]{3,2,1,0:T(4,128)(2,1)S(1)}, bf16[2,512,4,128]{3,2,1,0:T(4,128)(2,1)}, u32[]{:S(2)}) copy-start(bf16[2,512,4,128]{3,2,1,0:T(4,128)(2,1)} %get-tuple-element.1040) | copy-start | bytes 3145732 | tf_op jit(solution)/shard_map/transpose(jvp())/while
  202.1 9.1 %copy-start.4 = (bf16[2,512,4,128]{3,1,2,0:T(8,128)(2,1)S(1)}, bf16[2,512,4,128]{3,1,2,0:T(8,128)(2,1)}, u32[]{:S(2)}) copy-start(bf16[2,512,4,128]{3,1,2,0:T(8,128)(2,1)} %copy-done.3) | copy-start | bytes 3145732 | tf_op jit(solution)/shard_map/transpose(jvp())/while
  203.1 1.0 copy-start.11
  203.1 1.3 copy-start.13
  211.2 22.4 %copy-start.17 = (f32[2,4,512]{2,1,0:T(4,128)}, f32[2,4,512]{2,1,0:T(4,128)S(1)}, u32[]{:S(2)}) copy-start(f32[2,4,512]{2,1,0:T(4,128)S(1)} %get-tuple-element.447) | copy-start | bytes 49156
  211.2 4.6 %copy-start.14 = (bf16[2,512,4,128]{3,2,1,0:T(4,128)(2,1)S(1)}, bf16[2,512,4,128]{3,2,1,0:T(4,128)(2,1)}, u32[]{:S(2)}) copy-start(bf16[2,512,4,128]{3,2,1,0:T(4,128)(2,1)} %get-tuple-element.446) | copy-start | bytes 3145732

commit v11 on v9

--- a/solution.py
+++ b/solution.py
@@ -8,7 +8,7 @@
 BLOCK = 512
 
 
-PRECISE = lax.Precision.HIGH
+PRECISE = lax.Precision.DEFAULT
 
 
 def passed_along(value, axis, steps):

time: 235 us -> 229 us (0.974)
  matrix products: 57.7 us -> 52 us
    dot_general x8, matrix products: 10.3 us -> 6.68 us  [block_step(): jnp.einsum('thd,hde->the', q_float, carried, precision=PRECISE)]
where the time goes in v11:
time: 229 us; the launch traced here: 227 us
  Pallas kernels  80.6 us (35%)
  local copies, waits for them, and re-layouts  60.6 us (26%)
  matrix products  52 us (23%)
  other arithmetic  32.1 us (14%)
    pallas_call x1, Pallas kernels, both_scans_kernel(): pl.pallas_call(scan_kernel, out_shape=(out, out), in_specs=[pl.BlockSpec(...  67 us
    another operation x27, other arithmetic  20 us
    dot_general x6, matrix products, block_step(): jnp.einsum('hts,she->the', weights, v_block, preferred_element_type=jnp.f...  19.2 us
    dot_general x6, matrix products, block_step(): jnp.einsum('thd,shd->hts', q_block, k_bf, preferred_element_type=jnp.floa...  14.5 us
    pallas_call x1, Pallas kernels, gain_sum(): pl.pallas_call(gain_sum_kernel, out_shape=jax.ShapeDtypeStruct(shape, par...  13.6 us
    squeeze x10, local copies, waits for them, and re-layouts, run_blocks(): lax.scan(jax.checkpoint(make_step(key_gain, head_width)), start_state, (t...  10.2 us
    unnamed x21, local copies, waits for them, and re-layouts  8.32 us
    dot_general x6, matrix products, block_step(): jnp.einsum('shd,she->hde', k_float * to_end.T[:, :, None], v_float, preci...  8.3 us

profile of v11, /device:TPU:2, one launch (start us, length us, event | category | flops | bytes accessed | tf_op | source)
XLA Modules:
  0.0 226.9 jit_solution(11976524985995788082)
XLA Ops:
  6.6 1.6 copy.255
  8.2 2.1 reshape.591
  11.6 1.7 fusion.107
  15.0 1.3 reshape_squeeze.17
  16.4 1.7 fusion.109
  18.9 67.0 %shard_map.118 = (f32[4,128,128]{2,1,0:T(8,128)S(1)}, f32[4,128,128]{2,1,0:T(8,128)S(1)}) custom-call(f32[4,136,128]{2,1,0:T(8,128)} %get-tuple-element.773.fwd_ref, f32[4,136,128]{2,1,0:T(8,128)} %get-tuple-element.772.bwd_ref), custom_call_target="tpu_custom_call" | custom-call | tf_op jit(solution)/shard_map/pallas_call | solution.py:235
  87.1 1.4 copy.230
  88.6 2.1 reshape_squeeze.20
  90.7 2.3 %copy.231 = bf16[2,512,4,128]{3,1,2,0:T(8,128)(2,1)} copy(bf16[2,512,4,128]{3,2,1,0:T(4,128)(2,1)} %reshape_squeeze.20) | data formatting | bytes 2097152
  94.1 2.4 %copy.232 = bf16[2,512,4,128]{3,1,2,0:T(8,128)(2,1)} copy(bf16[2,512,4,128]{3,2,1,0:T(4,128)(2,1)} %reshape_squeeze.21) | data formatting | bytes 2097152
  96.5 24.7 %while.42 = (s32[]{:T(128)}, f32[4,128,128]{2,1,0:T(8,128)S(1)}, bf16[2,512,4,128]{1,3,2,0:T(8,128)(2,1)}, f32[2,4,128,128]{3,2,1,0:T(8,128)}, f32[2,4,512]{2,1,...) while((s32[]{:T(128)}, f32[4,128,128]{2,1,0:T(8,128)S(1)}, ...), condition=%wide.region_11.12_spmd.clone, body=%wide.region_6.11_spmd.clone.sunk | while | flops 680992832 | bytes 9343697 | solution.py:305
  97.4 1.2 reduce-window.144
  99.9 3.3 %fusion.191 = f32[512,4,128]{0,2,1:T(8,128)S(1)} fusion(bf16[512,4,128]{2,0,1:T(8,128)(2,1)S(1)} %fusion.189, f32[4,512]{1,0:T(4,128)S(1)} %bitcast.354, pred[512,512]{1,0:T(8,128)(4,1)S(1)} %fusion.190, bf16[2,512,4,128]{3,1,2,0:T(8,128)(2,1)} %get-tuple-element.1015, s32[]{:T(128)S(6)} %copy.332, bf16[2,512,4,128]{3,1,2,0:T(8,128)(2,1)} %get-tuple-element.1014), kind=kOutput, calls=%fused_computation.3.clone.1 | convolution fusion | flops 543162368 | bytes 2900992 | tf_op jit(solution)/shard_map/jvp()/while/body/eval_jaxpr/hts,she->the/dot_general | solution.py:277
  104.7 2.2 fusion.192
  107.0 1.9 convolution_add_fusion.4
  109.8 1.2 reduce-window.144
  112.3 3.3 %fusion.191 = f32[512,4,128]{0,2,1:T(8,128)S(1)} fusion(bf16[512,4,128]{2,0,1:T(8,128)(2,1)S(1)} %fusion.189, f32[4,512]{1,0:T(4,128)S(1)} %bitcast.354, pred[512,512]{1,0:T(8,128)(4,1)S(1)} %fusion.190, bf16[2,512,4,128]{3,1,2,0:T(8,128)(2,1)} %get-tuple-element.1015, s32[]{:T(128)S(6)} %copy.332, bf16[2,512,4,128]{3,1,2,0:T(8,128)(2,1)} %get-tuple-element.1014), kind=kOutput, calls=%fused_computation.3.clone.1 | convolution fusion | flops 543162368 | bytes 2900992 | tf_op jit(solution)/shard_map/jvp()/while/body/eval_jaxpr/hts,she->the/dot_general | solution.py:277
  117.0 2.2 fusion.192
  119.4 1.9 convolution_add_fusion.4
  121.3 1.8 copy.233
  123.1 1.2 convert_element_type.304
  124.3 1.7 reshape.602
  126.0 1.2 broadcast.246.clone
  127.2 1.2 broadcast.246.clone2
  128.5 1.2 broadcast.246.clone2.1
  129.7 75.8 %while.43 = (s32[]{:T(128)}, f32[4,128]{1,0:T(4,128)S(1)}, f32[4,128,128]{2,1,0:T(8,128)S(1)}, bf16[2,512,4,128]{3,2,1,0:T(4,128)(2,1)}, bf16[2,512,4,128]{3,2,1...) while((s32[]{:T(128)}, f32[4,128]{1,0:T(4,128)S(1)}, ...), condition=%wide.region_26.27_spmd.clone, body=%wide.region_12.26_spmd.clone.sunk | while | flops 1716879872 | bytes 116524784 | solution.py:305
  129.8 1.3 dynamic-slice_bitcast_fusion.10
  133.0 1.9 dynamic-slice_bitcast_fusion.13
  138.5 1.2 reduce-window.148
  140.4 1.7 fusion.210
  143.1 2.5 %fusion.213 = (f32[4,512]{1,0:T(4,128)S(1)}, f32[4,512]{1,0:T(4,128)S(1)}, bf16[4,512,512]{2,1,0:T(8,128)(2,1)S(1)}) fusion(f32[4,512]{1,0:T(4,128)S(1)} %bitcast.350, f32[4,512,512]{2,1,0:T(8,128)S(1)} %fusion.211, pred[512,512]{1,0:T(8,128)(4,1)S(1)} %fusion.212, bf16[512,4,128]{2,0,1:T(8,128)(2,1)S(1)} %copy-done.1, f32[512,4,128]{0,2,1:T(8,128)S(1)} %bitcast.337), kind=kOutput, calls=%fused_computation.107.clone.1 | convolution fusion | flops 278917120 | bytes 8151040 | tf_op jit(solution)/shard_map/transpose(jvp())/while/body/eval_jaxpr/checkpoint/hts,she->the/dot_general | solution.py:277
  145.6 3.2 %fusion.214 = (bf16[1,512,4,128]{3,1,2,0:T(8,128)(2,1)}, f32[4,128]{1,0:T(4,128)S(1)}) fusion(f32[4,128]{1,0:T(4,128)S(1)} %get-tuple-element.960, bf16[512,4,128]{2,0,1:T(8,128)(2,1)S(1)} %copy-done.2, bf16[512,4,128]{2,0,1:T(8,128)(2,1)S(1)} %get-tuple-element.967, bf16[512,4,128]{2,0,1:T(8,128)(2,1)S(1)} %dynamic-slice_bitcast_fusion.11, ...), kind=kOutput, calls=%fused_computation.110.clone.1 | convolution fusion | flops 276823552 | bytes 4468736 | tf_op jit(solution)/shard_map/transpose(jvp())/while/body/eval_jaxpr/checkpoint/thd,shd->hts/dot_general | solution.py:275
  148.8 3.8 %fusion.220 = bf16[4,128,512]{2,1,0:T(8,128)(2,1)S(1)} fusion(f32[4,512,512]{2,1,0:T(8,128)} %copy-done, f32[4,512]{1,0:T(4,128)S(1)} %bitcast.352, pred[512,512]{1,0:T(8,128)(4,1)S(1)} %fusion.212, f32[512,4,128]{0,2,1:T(8,128)S(1)} %bitcast.338), kind=kOutput, calls=%fused_computation.81.clone.1 | convolution fusion | flops 274726912 | bytes 6037504 | tf_op jit(solution)/shard_map/transpose(jvp())/while/body/eval_jaxpr/checkpoint/hts,she->the/dot_general | solution.py:277
  154.8 3.3 %fusion.218 = bf16[4,512,128]{2,1,0:T(8,128)(2,1)S(1)} fusion(bf16[512,4,128]{2,0,1:T(8,128)(2,1)S(1)} %fusion.209, bf16[4,512,512]{2,1,0:T(8,128)(2,1)} %copy-done.18, f32[4,512]{1,0:T(4,128)S(1)} %bitcast.353, pred[512,512]{1,0:T(8,128)(4,1)S(1)} %fusion.212), kind=kOutput, calls=%fused_computation.85.clone.1 | convolution fusion | flops 274989056 | bytes 3416064 | tf_op jit(solution)/shard_map/transpose(jvp())/while/body/eval_jaxpr/checkpoint/thd,shd->hts/dot_general | solution.py:275
  162.1 5.0 %reduce-window.150 = f32[4,4,128]{2,1,0:T(4,128)S(1)} reduce-window(f32[4,4,128]{2,1,0:T(4,128)S(1)} %reshape.631, f32[]{:T(128)} %constant.142.clone.1..sunk.1), window={size=1x1x128 pad=0_0x0_0x0_127}, to_apply=%region_24.24 | reduce-window | flops 260096 | bytes 16388 | tf_op jit(solution)/shard_map/reduce-window.60
  167.7 1.3 dynamic-slice_bitcast_fusion.10
  170.9 1.9 dynamic-slice_bitcast_fusion.13
  176.4 1.2 reduce-window.148
  178.3 1.7 fusion.210
  180.9 2.5 %fusion.213 = (f32[4,512]{1,0:T(4,128)S(1)}, f32[4,512]{1,0:T(4,128)S(1)}, bf16[4,512,512]{2,1,0:T(8,128)(2,1)S(1)}) fusion(f32[4,512]{1,0:T(4,128)S(1)} %bitcast.350, f32[4,512,512]{2,1,0:T(8,128)S(1)} %fusion.211, pred[512,512]{1,0:T(8,128)(4,1)S(1)} %fusion.212, bf16[512,4,128]{2,0,1:T(8,128)(2,1)S(1)} %copy-done.1, f32[512,4,128]{0,2,1:T(8,128)S(1)} %bitcast.337), kind=kOutput, calls=%fused_computation.107.clone.1 | convolution fusion | flops 278917120 | bytes 8151040 | tf_op jit(solution)/shard_map/transpose(jvp())/while/body/eval_jaxpr/checkpoint/hts,she->the/dot_general | solution.py:277
  183.5 3.2 %fusion.214 = (bf16[1,512,4,128]{3,1,2,0:T(8,128)(2,1)}, f32[4,128]{1,0:T(4,128)S(1)}) fusion(f32[4,128]{1,0:T(4,128)S(1)} %get-tuple-element.960, bf16[512,4,128]{2,0,1:T(8,128)(2,1)S(1)} %copy-done.2, bf16[512,4,128]{2,0,1:T(8,128)(2,1)S(1)} %get-tuple-element.967, bf16[512,4,128]{2,0,1:T(8,128)(2,1)S(1)} %dynamic-slice_bitcast_fusion.11, ...), kind=kOutput, calls=%fused_computation.110.clone.1 | convolution fusion | flops 276823552 | bytes 4468736 | tf_op jit(solution)/shard_map/transpose(jvp())/while/body/eval_jaxpr/checkpoint/thd,shd->hts/dot_general | solution.py:275
  186.7 3.8 %fusion.220 = bf16[4,128,512]{2,1,0:T(8,128)(2,1)S(1)} fusion(f32[4,512,512]{2,1,0:T(8,128)} %copy-done, f32[4,512]{1,0:T(4,128)S(1)} %bitcast.352, pred[512,512]{1,0:T(8,128)(4,1)S(1)} %fusion.212, f32[512,4,128]{0,2,1:T(8,128)S(1)} %bitcast.338), kind=kOutput, calls=%fused_computation.81.clone.1 | convolution fusion | flops 274726912 | bytes 6037504 | tf_op jit(solution)/shard_map/transpose(jvp())/while/body/eval_jaxpr/checkpoint/hts,she->the/dot_general | solution.py:277
  192.7 3.3 %fusion.218 = bf16[4,512,128]{2,1,0:T(8,128)(2,1)S(1)} fusion(bf16[512,4,128]{2,0,1:T(8,128)(2,1)S(1)} %fusion.209, bf16[4,512,512]{2,1,0:T(8,128)(2,1)} %copy-done.18, f32[4,512]{1,0:T(4,128)S(1)} %bitcast.353, pred[512,512]{1,0:T(8,128)(4,1)S(1)} %fusion.212), kind=kOutput, calls=%fused_computation.85.clone.1 | convolution fusion | flops 274989056 | bytes 3416064 | tf_op jit(solution)/shard_map/transpose(jvp())/while/body/eval_jaxpr/checkpoint/thd,shd->hts/dot_general | solution.py:275
  200.0 5.0 %reduce-window.150 = f32[4,4,128]{2,1,0:T(4,128)S(1)} reduce-window(f32[4,4,128]{2,1,0:T(4,128)S(1)} %reshape.631, f32[]{:T(128)} %constant.142.clone.1..sunk.1), window={size=1x1x128 pad=0_0x0_0x0_127}, to_apply=%region_24.24 | reduce-window | flops 260096 | bytes 16388 | tf_op jit(solution)/shard_map/reduce-window.60
  205.6 2.3 %reshape.592 = bf16[1,1024,512]{2,1,0:T(8,128)(2,1)} reshape(bf16[2,512,4,128]{3,2,1,0:T(4,128)(2,1)} %get-tuple-element.444) | data formatting | bytes 2097152 | tf_op jit(solution)/shard_map/broadcast_in_dim;transpose(jvp())/reshape | solution.py:346
  207.9 2.2 reshape.593
  212.0 13.6 %shard_map.119 = f32[4,64]{1,0:T(4,128)} custom-call(f32[2,4,64]{2,1,0:T(4,128)} %bitcast.368), custom_call_target="tpu_custom_call" | custom-call | tf_op jit(solution)/shard_map/pallas_call | solution.py:131
  225.6 1.2 copy.362
  (227 shorter events, 48.5 us)
Async XLA Ops:
  6.6 6.7 %copy-start.7 = (bf16[1,1024,512]{2,1,0:T(8,128)(2,1)S(1)}, bf16[1,1024,512]{2,1,0:T(8,128)(2,1)}, u32[]{:S(2)}) copy-start(bf16[1,1024,512]{2,1,0:T(8,128)(2,1)} %param.12) | copy-start | bytes 3145732
  8.2 5.7 %copy-start.16 = (f32[4,128]{1,0:T(4,128)S(1)}, f32[4,128]{1,0:T(4,128)}, u32[]{:S(2)}) copy-start(f32[4,128]{1,0:T(4,128)} %param.16) | copy-start | bytes 6148
  87.1 5.9 %copy-start.8 = (bf16[1,1024,512]{2,1,0:T(8,128)(2,1)S(1)}, bf16[1,1024,512]{2,1,0:T(8,128)(2,1)}, u32[]{:S(2)}) copy-start(bf16[1,1024,512]{2,1,0:T(8,128)(2,1)} %param.11) | copy-start | bytes 3145732
  88.5 8.0 %copy-start.15 = (f32[1,4,1024]{2,1,0:T(4,128)S(1)}, f32[1,4,1024]{2,1,0:T(4,128)}, u32[]{:S(2)}) copy-start(f32[1,4,1024]{2,1,0:T(4,128)} %param.14) | copy-start | bytes 49156
  121.3 3.0 %copy-start.9 = (bf16[1,1024,512]{2,1,0:T(8,128)(2,1)S(1)}, bf16[1,1024,512]{2,1,0:T(8,128)(2,1)}, u32[]{:S(2)}) copy-start(bf16[1,1024,512]{2,1,0:T(8,128)(2,1)} %param.17) | copy-start | bytes 3145732
  129.7 5.2 %copy-start.3 = (bf16[2,512,4,128]{3,1,2,0:T(8,128)(2,1)}, bf16[2,512,4,128]{3,1,2,0:T(8,128)(2,1)S(1)}, u32[]{:S(2)}) copy-start(bf16[2,512,4,128]{3,1,2,0:T(8,128)(2,1)S(1)} %get-tuple-element.1063) | copy-start | bytes 3145732 | tf_op jit(solution)/shard_map/transpose(jvp())/while
  129.7 5.2 %copy-start.5 = (f32[2,512,4,128]{3,2,1,0:T(4,128)S(1)}, f32[2,512,4,128]{3,2,1,0:T(4,128)}, u32[]{:S(2)}) copy-start(f32[2,512,4,128]{3,2,1,0:T(4,128)} %get-tuple-element.1067) | copy-start | bytes 6291460 | tf_op jit(solution)/shard_map/transpose(jvp())/while
  135.4 7.7 %copy-start.1 = (bf16[512,4,128]{2,0,1:T(8,128)(2,1)S(1)}, bf16[512,4,128]{2,0,1:T(8,128)(2,1)}, u32[]{:S(2)}) copy-start(bf16[512,4,128]{2,0,1:T(8,128)(2,1)} %dynamic-slice_bitcast_fusion.13) | copy-start | bytes 1572868 | tf_op jit(solution)/shard_map/transpose(jvp())/while
  142.8 2.8 %copy-start = (f32[4,512,512]{2,1,0:T(8,128)}, f32[4,512,512]{2,1,0:T(8,128)S(1)}, u32[]{:S(2)}) copy-start(f32[4,512,512]{2,1,0:T(8,128)S(1)} %fusion.211) | copy-start | bytes 12582916 | tf_op jit(solution)/shard_map/transpose(jvp())/while
  143.0 2.6 %copy-start.2 = (bf16[512,4,128]{2,0,1:T(8,128)(2,1)S(1)}, bf16[512,4,128]{2,0,1:T(8,128)(2,1)}, u32[]{:S(2)}) copy-start(bf16[512,4,128]{2,0,1:T(8,128)(2,1)} %dynamic-slice_bitcast_fusion.12) | copy-start | bytes 1572868 | tf_op jit(solution)/shard_map/transpose(jvp())/while
  145.6 3.2 %copy-start.18 = (bf16[4,512,512]{2,1,0:T(8,128)(2,1)}, bf16[4,512,512]{2,1,0:T(8,128)(2,1)S(1)}, u32[]{:S(2)}) copy-start(bf16[4,512,512]{2,1,0:T(8,128)(2,1)S(1)} %get-tuple-element.970) | copy-start | bytes 6291460 | tf_op jit(solution)/shard_map/transpose(jvp())/while
  154.8 3.7 %copy-start.6 = (bf16[1,512,4,128]{3,1,2,0:T(8,128)(2,1)S(1)}, bf16[1,512,4,128]{3,1,2,0:T(8,128)(2,1)}, u32[]{:S(2)}) copy-start(bf16[1,512,4,128]{3,1,2,0:T(8,128)(2,1)} %get-tuple-element.978) | copy-start | bytes 1572868 | tf_op jit(solution)/shard_map/transpose(jvp())/while
  154.8 3.7 %copy-start.10 = (bf16[2,512,4,128]{3,2,1,0:T(4,128)(2,1)S(1)}, bf16[2,512,4,128]{3,2,1,0:T(4,128)(2,1)}, u32[]{:S(2)}) copy-start(bf16[2,512,4,128]{3,2,1,0:T(4,128)(2,1)} %get-tuple-element.1039) | copy-start | bytes 3145732 | tf_op jit(solution)/shard_map/transpose(jvp())/while
  154.8 3.7 %copy-start.12 = (bf16[2,512,4,128]{3,2,1,0:T(4,128)(2,1)S(1)}, bf16[2,512,4,128]{3,2,1,0:T(4,128)(2,1)}, u32[]{:S(2)}) copy-start(bf16[2,512,4,128]{3,2,1,0:T(4,128)(2,1)} %get-tuple-element.1040) | copy-start | bytes 3145732 | tf_op jit(solution)/shard_map/transpose(jvp())/while
  158.6 9.0 %copy-start.4 = (bf16[2,512,4,128]{3,1,2,0:T(8,128)(2,1)S(1)}, bf16[2,512,4,128]{3,1,2,0:T(8,128)(2,1)}, u32[]{:S(2)}) copy-start(bf16[2,512,4,128]{3,1,2,0:T(8,128)(2,1)} %copy-done.3) | copy-start | bytes 3145732 | tf_op jit(solution)/shard_map/transpose(jvp())/while
  159.5 1.0 copy-start.11
  159.5 1.3 copy-start.13
  167.6 5.2 %copy-start.3 = (bf16[2,512,4,128]{3,1,2,0:T(8,128)(2,1)}, bf16[2,512,4,128]{3,1,2,0:T(8,128)(2,1)S(1)}, u32[]{:S(2)}) copy-start(bf16[2,512,4,128]{3,1,2,0:T(8,128)(2,1)S(1)} %get-tuple-element.1063) | copy-start | bytes 3145732 | tf_op jit(solution)/shard_map/transpose(jvp())/while
  167.6 5.2 %copy-start.5 = (f32[2,512,4,128]{3,2,1,0:T(4,128)S(1)}, f32[2,512,4,128]{3,2,1,0:T(4,128)}, u32[]{:S(2)}) copy-start(f32[2,512,4,128]{3,2,1,0:T(4,128)} %get-tuple-element.1067) | copy-start | bytes 6291460 | tf_op jit(solution)/shard_map/transpose(jvp())/while
  173.3 7.7 %copy-start.1 = (bf16[512,4,128]{2,0,1:T(8,128)(2,1)S(1)}, bf16[512,4,128]{2,0,1:T(8,128)(2,1)}, u32[]{:S(2)}) copy-start(bf16[512,4,128]{2,0,1:T(8,128)(2,1)} %dynamic-slice_bitcast_fusion.13) | copy-start | bytes 1572868 | tf_op jit(solution)/shard_map/transpose(jvp())/while
  180.7 2.8 %copy-start = (f32[4,512,512]{2,1,0:T(8,128)}, f32[4,512,512]{2,1,0:T(8,128)S(1)}, u32[]{:S(2)}) copy-start(f32[4,512,512]{2,1,0:T(8,128)S(1)} %fusion.211) | copy-start | bytes 12582916 | tf_op jit(solution)/shard_map/transpose(jvp())/while
  180.9 2.6 %copy-start.2 = (bf16[512,4,128]{2,0,1:T(8,128)(2,1)S(1)}, bf16[512,4,128]{2,0,1:T(8,128)(2,1)}, u32[]{:S(2)}) copy-start(bf16[512,4,128]{2,0,1:T(8,128)(2,1)} %dynamic-slice_bitcast_fusion.12) | copy-start | bytes 1572868 | tf_op jit(solution)/shard_map/transpose(jvp())/while
  183.5 3.2 %copy-start.18 = (bf16[4,512,512]{2,1,0:T(8,128)(2,1)}, bf16[4,512,512]{2,1,0:T(8,128)(2,1)S(1)}, u32[]{:S(2)}) copy-start(bf16[4,512,512]{2,1,0:T(8,128)(2,1)S(1)} %get-tuple-element.970) | copy-start | bytes 6291460 | tf_op jit(solution)/shard_map/transpose(jvp())/while
  192.7 3.7 %copy-start.6 = (bf16[1,512,4,128]{3,1,2,0:T(8,128)(2,1)S(1)}, bf16[1,512,4,128]{3,1,2,0:T(8,128)(2,1)}, u32[]{:S(2)}) copy-start(bf16[1,512,4,128]{3,1,2,0:T(8,128)(2,1)} %get-tuple-element.978) | copy-start | bytes 1572868 | tf_op jit(solution)/shard_map/transpose(jvp())/while
  192.7 3.7 %copy-start.10 = (bf16[2,512,4,128]{3,2,1,0:T(4,128)(2,1)S(1)}, bf16[2,512,4,128]{3,2,1,0:T(4,128)(2,1)}, u32[]{:S(2)}) copy-start(bf16[2,512,4,128]{3,2,1,0:T(4,128)(2,1)} %get-tuple-element.1039) | copy-start | bytes 3145732 | tf_op jit(solution)/shard_map/transpose(jvp())/while
  192.7 3.7 %copy-start.12 = (bf16[2,512,4,128]{3,2,1,0:T(4,128)(2,1)S(1)}, bf16[2,512,4,128]{3,2,1,0:T(4,128)(2,1)}, u32[]{:S(2)}) copy-start(bf16[2,512,4,128]{3,2,1,0:T(4,128)(2,1)} %get-tuple-element.1040) | copy-start | bytes 3145732 | tf_op jit(solution)/shard_map/transpose(jvp())/while
  196.5 9.1 %copy-start.4 = (bf16[2,512,4,128]{3,1,2,0:T(8,128)(2,1)S(1)}, bf16[2,512,4,128]{3,1,2,0:T(8,128)(2,1)}, u32[]{:S(2)}) copy-start(bf16[2,512,4,128]{3,1,2,0:T(8,128)(2,1)} %copy-done.3) | copy-start | bytes 3145732 | tf_op jit(solution)/shard_map/transpose(jvp())/while
  197.4 1.0 copy-start.11
  197.4 1.3 copy-start.13
  205.5 21.4 %copy-start.17 = (f32[2,4,512]{2,1,0:T(4,128)}, f32[2,4,512]{2,1,0:T(4,128)S(1)}, u32[]{:S(2)}) copy-start(f32[2,4,512]{2,1,0:T(4,128)S(1)} %get-tuple-element.447) | copy-start | bytes 49156
  205.5 4.6 %copy-start.14 = (bf16[2,512,4,128]{3,2,1,0:T(4,128)(2,1)S(1)}, bf16[2,512,4,128]{3,2,1,0:T(4,128)(2,1)}, u32[]{:S(2)}) copy-start(bf16[2,512,4,128]{3,2,1,0:T(4,128)(2,1)} %get-tuple-element.446) | copy-start | bytes 3145732

commit v12 on v9

--- a/solution.py
+++ b/solution.py
@@ -186,10 +186,13 @@
         targets = (me + shift, me - shift)
         sources = (me - shift, me + shift)
 
+        last = round_index == len(shifts) - 1
+        span = pl.ds(0, rows) if last else slice(None)
+
         def copy_of(side, peer):
             return pltpu.make_async_remote_copy(
-                src_ref=aggs.at[side],
-                dst_ref=slots.at[side, round_index],
+                src_ref=aggs.at[side, :, span, :],
+                dst_ref=slots.at[side, round_index, :, span, :],
                 send_sem=send_sem.at[side, round_index],
                 recv_sem=recv_sem.at[side, round_index],
                 device_id=device(peer),
@@ -210,15 +213,16 @@
             @pl.when(sends[1 - side])
             def _():
                 copy_of(side, sources[side]).wait_recv()
-                got = slots[side, round_index]
+                got = slots[side, round_index, :, span, :]
                 ex = exs[side]
                 agg = aggs[side]
                 ex_a = ex[:, rows:rows + 1, :]
                 agg_a = agg[:, rows:rows + 1, :]
                 exs[side, :, :rows, :] = ex_a * got[:, :rows, :] + ex[:, :rows, :]
-                exs[side, :, rows:, :] = ex[:, rows:, :] * got[:, rows:, :]
-                aggs[side, :, :rows, :] = agg_a * got[:, :rows, :] + agg[:, :rows, :]
-                aggs[side, :, rows:, :] = agg[:, rows:, :] * got[:, rows:, :]
+                if not last:
+                    exs[side, :, rows:, :] = ex[:, rows:, :] * got[:, rows:, :]
+                    aggs[side, :, :rows, :] = agg_a * got[:, :rows, :] + agg[:, :rows, :]
+                    aggs[side, :, rows:, :] = agg[:, rows:, :] * got[:, rows:, :]
 
     fwd_out[...] = exs[0, :, :rows, :]
     bwd_out[...] = exs[1, :, :rows, :]

time: 235 us -> 234 us (level)
  no operation moved by 1% of the time
where the time goes in v12:
time: 234 us; the launch traced here: 232 us
  Pallas kernels  79.9 us (34%)
  local copies, waits for them, and re-layouts  60.6 us (26%)
  matrix products  57.7 us (25%)
  other arithmetic  32.1 us (14%)
    pallas_call x1, Pallas kernels, both_scans_kernel(): pl.pallas_call(scan_kernel, out_shape=(out, out), in_specs=[pl.BlockSpec(...  66.5 us
    another operation x27, other arithmetic  20 us
    dot_general x6, matrix products, block_step(): jnp.einsum('hts,she->the', weights, v_block, preferred_element_type=jnp.f...  19.2 us
    dot_general x6, matrix products, block_step(): jnp.einsum('thd,shd->hts', q_block, k_bf, preferred_element_type=jnp.floa...  14.5 us
    pallas_call x1, Pallas kernels, gain_sum(): pl.pallas_call(gain_sum_kernel, out_shape=jax.ShapeDtypeStruct(shape, par...  13.4 us
    dot_general x8, matrix products, block_step(): jnp.einsum('thd,hde->the', q_float, carried, precision=PRECISE)  10.3 us
    squeeze x10, local copies, waits for them, and re-layouts, run_blocks(): lax.scan(jax.checkpoint(make_step(key_gain, head_width)), start_state, (t...  10.2 us
    dot_general x6, matrix products, block_step(): jnp.einsum('shd,she->hde', k_float * to_end.T[:, :, None], v_float, preci...  9.62 us

profile of v12, /device:TPU:2, one launch (start us, length us, event | category | flops | bytes accessed | tf_op | source)
XLA Modules:
  0.0 231.8 jit_solution(7584640673533715668)
XLA Ops:
  6.6 1.6 copy.255
  8.2 2.1 reshape.591
  11.6 2.0 fusion.107
  15.4 1.3 reshape_squeeze.17
  16.7 2.1 fusion.109
  19.6 66.5 %shard_map.118 = (f32[4,128,128]{2,1,0:T(8,128)S(1)}, f32[4,128,128]{2,1,0:T(8,128)S(1)}) custom-call(f32[4,136,128]{2,1,0:T(8,128)} %get-tuple-element.773.fwd_ref, f32[4,136,128]{2,1,0:T(8,128)} %get-tuple-element.772.bwd_ref), custom_call_target="tpu_custom_call" | custom-call | tf_op jit(solution)/shard_map/pallas_call | solution.py:239
  87.2 1.4 copy.230
  88.7 2.1 reshape_squeeze.20
  90.8 2.3 %copy.231 = bf16[2,512,4,128]{3,1,2,0:T(8,128)(2,1)} copy(bf16[2,512,4,128]{3,2,1,0:T(4,128)(2,1)} %reshape_squeeze.20) | data formatting | bytes 2097152
  94.3 2.4 %copy.232 = bf16[2,512,4,128]{3,1,2,0:T(8,128)(2,1)} copy(bf16[2,512,4,128]{3,2,1,0:T(4,128)(2,1)} %reshape_squeeze.21) | data formatting | bytes 2097152
  96.7 25.8 %while.42 = (s32[]{:T(128)}, f32[4,128,128]{2,1,0:T(8,128)S(1)}, bf16[2,512,4,128]{1,3,2,0:T(8,128)(2,1)}, f32[2,4,128,128]{3,2,1,0:T(8,128)}, f32[2,4,512]{2,1,...) while((s32[]{:T(128)}, f32[4,128,128]{2,1,0:T(8,128)S(1)}, ...), condition=%wide.region_11.12_spmd.clone, body=%wide.region_6.11_spmd.clone.sunk | while | flops 949428288 | bytes 9343697 | solution.py:309
  97.6 1.2 reduce-window.144
  100.0 3.3 %fusion.191 = f32[512,4,128]{0,2,1:T(8,128)S(1)} fusion(bf16[512,4,128]{2,0,1:T(8,128)(2,1)S(1)} %fusion.189, f32[4,512]{1,0:T(4,128)S(1)} %bitcast.354, pred[512,512]{1,0:T(8,128)(4,1)S(1)} %fusion.190, bf16[2,512,4,128]{3,1,2,0:T(8,128)(2,1)} %get-tuple-element.1015, s32[]{:T(128)S(6)} %copy.332, bf16[2,512,4,128]{3,1,2,0:T(8,128)(2,1)} %get-tuple-element.1014), kind=kOutput, calls=%fused_computation.3.clone.1 | convolution fusion | flops 543162368 | bytes 2900992 | tf_op jit(solution)/shard_map/jvp()/while/body/eval_jaxpr/hts,she->the/dot_general | solution.py:281
  104.8 2.5 %fusion.192 = bf16[2,512,4,128]{1,3,2,0:T(8,128)(2,1)} fusion(bf16[2,512,4,128]{1,3,2,0:T(8,128)(2,1)} %get-tuple-element.996, s32[]{:T(128)S(6)} %copy.332, f32[512,4,128]{0,2,1:T(8,128)S(1)} %fusion.191, f32[4,128,128]{2,1,0:T(8,128)S(1)} %get-tuple-element.995, f32[512,4]{0,1:T(4,128)S(1)} %bitcast.346, ...), kind=kOutput, calls=%fused_computation.8.clone.1 | convolution fusion | flops 202375168 | bytes 2892800 | tf_op jit(solution)/shard_map/jvp()/while/body/eval_jaxpr/thd,hde->the/dot_general | solution.py:285
  107.5 2.1 convolution_add_fusion.4
  110.5 1.2 reduce-window.144
  112.9 3.3 %fusion.191 = f32[512,4,128]{0,2,1:T(8,128)S(1)} fusion(bf16[512,4,128]{2,0,1:T(8,128)(2,1)S(1)} %fusion.189, f32[4,512]{1,0:T(4,128)S(1)} %bitcast.354, pred[512,512]{1,0:T(8,128)(4,1)S(1)} %fusion.190, bf16[2,512,4,128]{3,1,2,0:T(8,128)(2,1)} %get-tuple-element.1015, s32[]{:T(128)S(6)} %copy.332, bf16[2,512,4,128]{3,1,2,0:T(8,128)(2,1)} %get-tuple-element.1014), kind=kOutput, calls=%fused_computation.3.clone.1 | convolution fusion | flops 543162368 | bytes 2900992 | tf_op jit(solution)/shard_map/jvp()/while/body/eval_jaxpr/hts,she->the/dot_general | solution.py:281
  117.7 2.5 %fusion.192 = bf16[2,512,4,128]{1,3,2,0:T(8,128)(2,1)} fusion(bf16[2,512,4,128]{1,3,2,0:T(8,128)(2,1)} %get-tuple-element.996, s32[]{:T(128)S(6)} %copy.332, f32[512,4,128]{0,2,1:T(8,128)S(1)} %fusion.191, f32[4,128,128]{2,1,0:T(8,128)S(1)} %get-tuple-element.995, f32[512,4]{0,1:T(4,128)S(1)} %bitcast.346, ...), kind=kOutput, calls=%fused_computation.8.clone.1 | convolution fusion | flops 202375168 | bytes 2892800 | tf_op jit(solution)/shard_map/jvp()/while/body/eval_jaxpr/thd,hde->the/dot_general | solution.py:285
  120.4 2.1 convolution_add_fusion.4
  122.5 1.8 copy.233
  124.3 1.2 convert_element_type.304
  125.5 1.7 reshape.602
  127.2 1.2 broadcast.246.clone
  128.4 1.2 broadcast.246.clone2
  129.7 1.2 broadcast.246.clone2.1
  130.9 79.7 %while.43 = (s32[]{:T(128)}, f32[4,128]{1,0:T(4,128)S(1)}, f32[4,128,128]{2,1,0:T(8,128)S(1)}, bf16[2,512,4,128]{3,2,1,0:T(4,128)(2,1)}, bf16[2,512,4,128]{3,2,1...) while((s32[]{:T(128)}, f32[4,128]{1,0:T(4,128)S(1)}, ...), condition=%wide.region_26.27_spmd.clone, body=%wide.region_12.26_spmd.clone.sunk | while | flops 2388230656 | bytes 116524784 | solution.py:309
  130.9 1.3 dynamic-slice_bitcast_fusion.10
  134.2 1.9 dynamic-slice_bitcast_fusion.13
  139.7 1.2 reduce-window.148
  141.6 1.8 fusion.210
  144.3 2.5 %fusion.213 = (f32[4,512]{1,0:T(4,128)S(1)}, f32[4,512]{1,0:T(4,128)S(1)}, bf16[4,512,512]{2,1,0:T(8,128)(2,1)S(1)}) fusion(f32[4,512]{1,0:T(4,128)S(1)} %bitcast.350, f32[4,512,512]{2,1,0:T(8,128)S(1)} %fusion.211, pred[512,512]{1,0:T(8,128)(4,1)S(1)} %fusion.212, bf16[512,4,128]{2,0,1:T(8,128)(2,1)S(1)} %copy-done.1, f32[512,4,128]{0,2,1:T(8,128)S(1)} %bitcast.337), kind=kOutput, calls=%fused_computation.107.clone.1 | convolution fusion | flops 278917120 | bytes 8151040 | tf_op jit(solution)/shard_map/transpose(jvp())/while/body/eval_jaxpr/checkpoint/hts,she->the/dot_general | solution.py:281
  146.9 3.2 %fusion.214 = (bf16[1,512,4,128]{3,1,2,0:T(8,128)(2,1)}, f32[4,128]{1,0:T(4,128)S(1)}) fusion(f32[4,128]{1,0:T(4,128)S(1)} %get-tuple-element.960, bf16[512,4,128]{2,0,1:T(8,128)(2,1)S(1)} %copy-done.2, bf16[512,4,128]{2,0,1:T(8,128)(2,1)S(1)} %get-tuple-element.967, bf16[512,4,128]{2,0,1:T(8,128)(2,1)S(1)} %dynamic-slice_bitcast_fusion.11, ...), kind=kOutput, calls=%fused_computation.110.clone.1 | convolution fusion | flops 276823552 | bytes 4468736 | tf_op jit(solution)/shard_map/transpose(jvp())/while/body/eval_jaxpr/checkpoint/thd,shd->hts/dot_general | solution.py:279
  150.1 3.8 %fusion.220 = bf16[4,128,512]{2,1,0:T(8,128)(2,1)S(1)} fusion(f32[4,512,512]{2,1,0:T(8,128)} %copy-done, f32[4,512]{1,0:T(4,128)S(1)} %bitcast.352, pred[512,512]{1,0:T(8,128)(4,1)S(1)} %fusion.212, f32[512,4,128]{0,2,1:T(8,128)S(1)} %bitcast.338), kind=kOutput, calls=%fused_computation.81.clone.1 | convolution fusion | flops 274726912 | bytes 6037504 | tf_op jit(solution)/shard_map/transpose(jvp())/while/body/eval_jaxpr/checkpoint/hts,she->the/dot_general | solution.py:281
  157.3 3.3 %fusion.218 = bf16[4,512,128]{2,1,0:T(8,128)(2,1)S(1)} fusion(bf16[512,4,128]{2,0,1:T(8,128)(2,1)S(1)} %fusion.209, bf16[4,512,512]{2,1,0:T(8,128)(2,1)} %copy-done.18, f32[4,512]{1,0:T(4,128)S(1)} %bitcast.353, pred[512,512]{1,0:T(8,128)(4,1)S(1)} %fusion.212), kind=kOutput, calls=%fused_computation.85.clone.1 | convolution fusion | flops 274989056 | bytes 3416064 | tf_op jit(solution)/shard_map/transpose(jvp())/while/body/eval_jaxpr/checkpoint/thd,shd->hts/dot_general | solution.py:279
  165.3 5.0 %reduce-window.150 = f32[4,4,128]{2,1,0:T(4,128)S(1)} reduce-window(f32[4,4,128]{2,1,0:T(4,128)S(1)} %reshape.631, f32[]{:T(128)} %constant.142.clone.1..sunk.1), window={size=1x1x128 pad=0_0x0_0x0_127}, to_apply=%region_24.24 | reduce-window | flops 260096 | bytes 16388 | tf_op jit(solution)/shard_map/reduce-window.60
  170.8 1.3 dynamic-slice_bitcast_fusion.10
  174.1 1.9 dynamic-slice_bitcast_fusion.13
  179.5 1.2 reduce-window.148
  181.4 1.8 fusion.210
  184.2 2.5 %fusion.213 = (f32[4,512]{1,0:T(4,128)S(1)}, f32[4,512]{1,0:T(4,128)S(1)}, bf16[4,512,512]{2,1,0:T(8,128)(2,1)S(1)}) fusion(f32[4,512]{1,0:T(4,128)S(1)} %bitcast.350, f32[4,512,512]{2,1,0:T(8,128)S(1)} %fusion.211, pred[512,512]{1,0:T(8,128)(4,1)S(1)} %fusion.212, bf16[512,4,128]{2,0,1:T(8,128)(2,1)S(1)} %copy-done.1, f32[512,4,128]{0,2,1:T(8,128)S(1)} %bitcast.337), kind=kOutput, calls=%fused_computation.107.clone.1 | convolution fusion | flops 278917120 | bytes 8151040 | tf_op jit(solution)/shard_map/transpose(jvp())/while/body/eval_jaxpr/checkpoint/hts,she->the/dot_general | solution.py:281
  186.7 3.2 %fusion.214 = (bf16[1,512,4,128]{3,1,2,0:T(8,128)(2,1)}, f32[4,128]{1,0:T(4,128)S(1)}) fusion(f32[4,128]{1,0:T(4,128)S(1)} %get-tuple-element.960, bf16[512,4,128]{2,0,1:T(8,128)(2,1)S(1)} %copy-done.2, bf16[512,4,128]{2,0,1:T(8,128)(2,1)S(1)} %get-tuple-element.967, bf16[512,4,128]{2,0,1:T(8,128)(2,1)S(1)} %dynamic-slice_bitcast_fusion.11, ...), kind=kOutput, calls=%fused_computation.110.clone.1 | convolution fusion | flops 276823552 | bytes 4468736 | tf_op jit(solution)/shard_map/transpose(jvp())/while/body/eval_jaxpr/checkpoint/thd,shd->hts/dot_general | solution.py:279
  190.0 3.8 %fusion.220 = bf16[4,128,512]{2,1,0:T(8,128)(2,1)S(1)} fusion(f32[4,512,512]{2,1,0:T(8,128)} %copy-done, f32[4,512]{1,0:T(4,128)S(1)} %bitcast.352, pred[512,512]{1,0:T(8,128)(4,1)S(1)} %fusion.212, f32[512,4,128]{0,2,1:T(8,128)S(1)} %bitcast.338), kind=kOutput, calls=%fused_computation.81.clone.1 | convolution fusion | flops 274726912 | bytes 6037504 | tf_op jit(solution)/shard_map/transpose(jvp())/while/body/eval_jaxpr/checkpoint/hts,she->the/dot_general | solution.py:281
  197.2 3.3 %fusion.218 = bf16[4,512,128]{2,1,0:T(8,128)(2,1)S(1)} fusion(bf16[512,4,128]{2,0,1:T(8,128)(2,1)S(1)} %fusion.209, bf16[4,512,512]{2,1,0:T(8,128)(2,1)} %copy-done.18, f32[4,512]{1,0:T(4,128)S(1)} %bitcast.353, pred[512,512]{1,0:T(8,128)(4,1)S(1)} %fusion.212), kind=kOutput, calls=%fused_computation.85.clone.1 | convolution fusion | flops 274989056 | bytes 3416064 | tf_op jit(solution)/shard_map/transpose(jvp())/while/body/eval_jaxpr/checkpoint/thd,shd->hts/dot_general | solution.py:279
  205.2 5.0 %reduce-window.150 = f32[4,4,128]{2,1,0:T(4,128)S(1)} reduce-window(f32[4,4,128]{2,1,0:T(4,128)S(1)} %reshape.631, f32[]{:T(128)} %constant.142.clone.1..sunk.1), window={size=1x1x128 pad=0_0x0_0x0_127}, to_apply=%region_24.24 | reduce-window | flops 260096 | bytes 16388 | tf_op jit(solution)/shard_map/reduce-window.60
  210.7 2.3 %reshape.592 = bf16[1,1024,512]{2,1,0:T(8,128)(2,1)} reshape(bf16[2,512,4,128]{3,2,1,0:T(4,128)(2,1)} %get-tuple-element.444) | data formatting | bytes 2097152 | tf_op jit(solution)/shard_map/broadcast_in_dim;transpose(jvp())/reshape | solution.py:350
  213.0 2.2 reshape.593
  217.1 13.4 %shard_map.119 = f32[4,64]{1,0:T(4,128)} custom-call(f32[2,4,64]{2,1,0:T(4,128)} %bitcast.368), custom_call_target="tpu_custom_call" | custom-call | tf_op jit(solution)/shard_map/pallas_call | solution.py:131
  230.6 1.2 copy.362
  (227 shorter events, 52.4 us)
Async XLA Ops:
  6.6 7.1 %copy-start.7 = (bf16[1,1024,512]{2,1,0:T(8,128)(2,1)S(1)}, bf16[1,1024,512]{2,1,0:T(8,128)(2,1)}, u32[]{:S(2)}) copy-start(bf16[1,1024,512]{2,1,0:T(8,128)(2,1)} %param.12) | copy-start | bytes 3145732
  8.2 6.0 %copy-start.16 = (f32[4,128]{1,0:T(4,128)S(1)}, f32[4,128]{1,0:T(4,128)}, u32[]{:S(2)}) copy-start(f32[4,128]{1,0:T(4,128)} %param.16) | copy-start | bytes 6148
  87.2 5.9 %copy-start.8 = (bf16[1,1024,512]{2,1,0:T(8,128)(2,1)S(1)}, bf16[1,1024,512]{2,1,0:T(8,128)(2,1)}, u32[]{:S(2)}) copy-start(bf16[1,1024,512]{2,1,0:T(8,128)(2,1)} %param.11) | copy-start | bytes 3145732
  88.7 8.0 %copy-start.15 = (f32[1,4,1024]{2,1,0:T(4,128)S(1)}, f32[1,4,1024]{2,1,0:T(4,128)}, u32[]{:S(2)}) copy-start(f32[1,4,1024]{2,1,0:T(4,128)} %param.14) | copy-start | bytes 49156
  122.5 3.0 %copy-start.9 = (bf16[1,1024,512]{2,1,0:T(8,128)(2,1)S(1)}, bf16[1,1024,512]{2,1,0:T(8,128)(2,1)}, u32[]{:S(2)}) copy-start(bf16[1,1024,512]{2,1,0:T(8,128)(2,1)} %param.17) | copy-start | bytes 3145732
  130.9 5.2 %copy-start.3 = (bf16[2,512,4,128]{3,1,2,0:T(8,128)(2,1)}, bf16[2,512,4,128]{3,1,2,0:T(8,128)(2,1)S(1)}, u32[]{:S(2)}) copy-start(bf16[2,512,4,128]{3,1,2,0:T(8,128)(2,1)S(1)} %get-tuple-element.1063) | copy-start | bytes 3145732 | tf_op jit(solution)/shard_map/transpose(jvp())/while
  130.9 5.2 %copy-start.5 = (f32[2,512,4,128]{3,2,1,0:T(4,128)S(1)}, f32[2,512,4,128]{3,2,1,0:T(4,128)}, u32[]{:S(2)}) copy-start(f32[2,512,4,128]{3,2,1,0:T(4,128)} %get-tuple-element.1067) | copy-start | bytes 6291460 | tf_op jit(solution)/shard_map/transpose(jvp())/while
  136.6 7.7 %copy-start.1 = (bf16[512,4,128]{2,0,1:T(8,128)(2,1)S(1)}, bf16[512,4,128]{2,0,1:T(8,128)(2,1)}, u32[]{:S(2)}) copy-start(bf16[512,4,128]{2,0,1:T(8,128)(2,1)} %dynamic-slice_bitcast_fusion.13) | copy-start | bytes 1572868 | tf_op jit(solution)/shard_map/transpose(jvp())/while
  144.1 2.8 %copy-start = (f32[4,512,512]{2,1,0:T(8,128)}, f32[4,512,512]{2,1,0:T(8,128)S(1)}, u32[]{:S(2)}) copy-start(f32[4,512,512]{2,1,0:T(8,128)S(1)} %fusion.211) | copy-start | bytes 12582916 | tf_op jit(solution)/shard_map/transpose(jvp())/while
  144.3 2.6 %copy-start.2 = (bf16[512,4,128]{2,0,1:T(8,128)(2,1)S(1)}, bf16[512,4,128]{2,0,1:T(8,128)(2,1)}, u32[]{:S(2)}) copy-start(bf16[512,4,128]{2,0,1:T(8,128)(2,1)} %dynamic-slice_bitcast_fusion.12) | copy-start | bytes 1572868 | tf_op jit(solution)/shard_map/transpose(jvp())/while
  146.9 3.2 %copy-start.18 = (bf16[4,512,512]{2,1,0:T(8,128)(2,1)}, bf16[4,512,512]{2,1,0:T(8,128)(2,1)S(1)}, u32[]{:S(2)}) copy-start(bf16[4,512,512]{2,1,0:T(8,128)(2,1)S(1)} %get-tuple-element.970) | copy-start | bytes 6291460 | tf_op jit(solution)/shard_map/transpose(jvp())/while
  157.3 4.4 %copy-start.6 = (bf16[1,512,4,128]{3,1,2,0:T(8,128)(2,1)S(1)}, bf16[1,512,4,128]{3,1,2,0:T(8,128)(2,1)}, u32[]{:S(2)}) copy-start(bf16[1,512,4,128]{3,1,2,0:T(8,128)(2,1)} %get-tuple-element.978) | copy-start | bytes 1572868 | tf_op jit(solution)/shard_map/transpose(jvp())/while
  157.3 4.4 %copy-start.10 = (bf16[2,512,4,128]{3,2,1,0:T(4,128)(2,1)S(1)}, bf16[2,512,4,128]{3,2,1,0:T(4,128)(2,1)}, u32[]{:S(2)}) copy-start(bf16[2,512,4,128]{3,2,1,0:T(4,128)(2,1)} %get-tuple-element.1039) | copy-start | bytes 3145732 | tf_op jit(solution)/shard_map/transpose(jvp())/while
  157.3 4.4 %copy-start.12 = (bf16[2,512,4,128]{3,2,1,0:T(4,128)(2,1)S(1)}, bf16[2,512,4,128]{3,2,1,0:T(4,128)(2,1)}, u32[]{:S(2)}) copy-start(bf16[2,512,4,128]{3,2,1,0:T(4,128)(2,1)} %get-tuple-element.1040) | copy-start | bytes 3145732 | tf_op jit(solution)/shard_map/transpose(jvp())/while
  161.7 9.0 %copy-start.4 = (bf16[2,512,4,128]{3,1,2,0:T(8,128)(2,1)S(1)}, bf16[2,512,4,128]{3,1,2,0:T(8,128)(2,1)}, u32[]{:S(2)}) copy-start(bf16[2,512,4,128]{3,1,2,0:T(8,128)(2,1)} %copy-done.3) | copy-start | bytes 3145732 | tf_op jit(solution)/shard_map/transpose(jvp())/while
  162.6 1.0 copy-start.11
  162.7 1.3 copy-start.13
  170.8 5.2 %copy-start.3 = (bf16[2,512,4,128]{3,1,2,0:T(8,128)(2,1)}, bf16[2,512,4,128]{3,1,2,0:T(8,128)(2,1)S(1)}, u32[]{:S(2)}) copy-start(bf16[2,512,4,128]{3,1,2,0:T(8,128)(2,1)S(1)} %get-tuple-element.1063) | copy-start | bytes 3145732 | tf_op jit(solution)/shard_map/transpose(jvp())/while
  170.8 5.2 %copy-start.5 = (f32[2,512,4,128]{3,2,1,0:T(4,128)S(1)}, f32[2,512,4,128]{3,2,1,0:T(4,128)}, u32[]{:S(2)}) copy-start(f32[2,512,4,128]{3,2,1,0:T(4,128)} %get-tuple-element.1067) | copy-start | bytes 6291460 | tf_op jit(solution)/shard_map/transpose(jvp())/while
  176.4 7.7 %copy-start.1 = (bf16[512,4,128]{2,0,1:T(8,128)(2,1)S(1)}, bf16[512,4,128]{2,0,1:T(8,128)(2,1)}, u32[]{:S(2)}) copy-start(bf16[512,4,128]{2,0,1:T(8,128)(2,1)} %dynamic-slice_bitcast_fusion.13) | copy-start | bytes 1572868 | tf_op jit(solution)/shard_map/transpose(jvp())/while
  183.9 2.8 %copy-start = (f32[4,512,512]{2,1,0:T(8,128)}, f32[4,512,512]{2,1,0:T(8,128)S(1)}, u32[]{:S(2)}) copy-start(f32[4,512,512]{2,1,0:T(8,128)S(1)} %fusion.211) | copy-start | bytes 12582916 | tf_op jit(solution)/shard_map/transpose(jvp())/while
  184.2 2.6 %copy-start.2 = (bf16[512,4,128]{2,0,1:T(8,128)(2,1)S(1)}, bf16[512,4,128]{2,0,1:T(8,128)(2,1)}, u32[]{:S(2)}) copy-start(bf16[512,4,128]{2,0,1:T(8,128)(2,1)} %dynamic-slice_bitcast_fusion.12) | copy-start | bytes 1572868 | tf_op jit(solution)/shard_map/transpose(jvp())/while
  186.7 3.2 %copy-start.18 = (bf16[4,512,512]{2,1,0:T(8,128)(2,1)}, bf16[4,512,512]{2,1,0:T(8,128)(2,1)S(1)}, u32[]{:S(2)}) copy-start(bf16[4,512,512]{2,1,0:T(8,128)(2,1)S(1)} %get-tuple-element.970) | copy-start | bytes 6291460 | tf_op jit(solution)/shard_map/transpose(jvp())/while
  197.2 4.4 %copy-start.6 = (bf16[1,512,4,128]{3,1,2,0:T(8,128)(2,1)S(1)}, bf16[1,512,4,128]{3,1,2,0:T(8,128)(2,1)}, u32[]{:S(2)}) copy-start(bf16[1,512,4,128]{3,1,2,0:T(8,128)(2,1)} %get-tuple-element.978) | copy-start | bytes 1572868 | tf_op jit(solution)/shard_map/transpose(jvp())/while
  197.2 4.4 %copy-start.10 = (bf16[2,512,4,128]{3,2,1,0:T(4,128)(2,1)S(1)}, bf16[2,512,4,128]{3,2,1,0:T(4,128)(2,1)}, u32[]{:S(2)}) copy-start(bf16[2,512,4,128]{3,2,1,0:T(4,128)(2,1)} %get-tuple-element.1039) | copy-start | bytes 3145732 | tf_op jit(solution)/shard_map/transpose(jvp())/while
  197.2 4.4 %copy-start.12 = (bf16[2,512,4,128]{3,2,1,0:T(4,128)(2,1)S(1)}, bf16[2,512,4,128]{3,2,1,0:T(4,128)(2,1)}, u32[]{:S(2)}) copy-start(bf16[2,512,4,128]{3,2,1,0:T(4,128)(2,1)} %get-tuple-element.1040) | copy-start | bytes 3145732 | tf_op jit(solution)/shard_map/transpose(jvp())/while
  201.6 9.1 %copy-start.4 = (bf16[2,512,4,128]{3,1,2,0:T(8,128)(2,1)S(1)}, bf16[2,512,4,128]{3,1,2,0:T(8,128)(2,1)}, u32[]{:S(2)}) copy-start(bf16[2,512,4,128]{3,1,2,0:T(8,128)(2,1)} %copy-done.3) | copy-start | bytes 3145732 | tf_op jit(solution)/shard_map/transpose(jvp())/while
  202.5 1.0 copy-start.11
  202.5 1.3 copy-start.13
  210.7 21.2 %copy-start.17 = (f32[2,4,512]{2,1,0:T(4,128)}, f32[2,4,512]{2,1,0:T(4,128)S(1)}, u32[]{:S(2)}) copy-start(f32[2,4,512]{2,1,0:T(4,128)S(1)} %get-tuple-element.447) | copy-start | bytes 49156
  210.7 4.6 %copy-start.14 = (bf16[2,512,4,128]{3,2,1,0:T(4,128)(2,1)S(1)}, bf16[2,512,4,128]{3,2,1,0:T(4,128)(2,1)}, u32[]{:S(2)}) copy-start(bf16[2,512,4,128]{3,2,1,0:T(4,128)(2,1)} %get-tuple-element.446) | copy-start | bytes 3145732

commit v13 on v12

--- a/solution.py
+++ b/solution.py
@@ -144,7 +144,7 @@
     )(halves)
 
 
-def scan_kernel(fwd_ref, bwd_ref, fwd_out, bwd_out, aggs, exs, slots, send_sem, recv_sem):
+def scan_kernel(fwd_ref, bwd_ref, lane_ref, fwd_out, bwd_out, aggs, exs, slots, send_sem, recv_sem):
     count = lax.axis_size("ctx")
     me = lax.axis_index("ctx")
     row, col = lax.axis_index("dp"), lax.axis_index("head")
@@ -176,8 +176,10 @@
         peers = peers + at_least(shift) + 1 - at_least(count - shift)
     pl.semaphore_wait(barrier, peers)
 
-    aggs[0] = fwd_ref[...]
-    aggs[1] = bwd_ref[...]
+    aggs[0, :, :rows, :] = fwd_ref[...]
+    aggs[1, :, :rows, :] = bwd_ref[...]
+    aggs[0, :, rows:, :] = lane_ref[...]
+    aggs[1, :, rows:, :] = lane_ref[...]
     exs[...] = jnp.zeros_like(exs)
     exs[:, :, rows:, :] = jnp.ones_like(exs[:, :, rows:, :])
 
@@ -232,14 +234,12 @@
     heads, rows, width = fwd_term.shape
     rounds = max(1, (count - 1).bit_length())
     lane = jnp.broadcast_to(decay[:, None, None], (heads, 8, width))
-    fwd = jnp.concatenate([fwd_term, lane], axis=1)
-    bwd = jnp.concatenate([bwd_term, lane], axis=1)
-    packed = fwd.shape
+    packed = (heads, rows + 8, width)
     out = jax.ShapeDtypeStruct(fwd_term.shape, jnp.float32)
     return pl.pallas_call(
         scan_kernel,
         out_shape=(out, out),
-        in_specs=[pl.BlockSpec(memory_space=pltpu.VMEM)] * 2,
+        in_specs=[pl.BlockSpec(memory_space=pltpu.VMEM)] * 3,
         out_specs=(pl.BlockSpec(memory_space=pltpu.VMEM),) * 2,
         scratch_shapes=[
             pltpu.VMEM((2,) + packed, jnp.float32),
@@ -249,7 +249,7 @@
             pltpu.SemaphoreType.DMA((2, rounds)),
         ],
         compiler_params=pltpu.CompilerParams(collective_id=1, has_side_effects=True),
-    )(fwd, bwd)
+    )(fwd_term, bwd_term, lane)
 
 
 def start_flags(doc_lengths, first_pos, num_rows):

time: 234 us -> 234 us (level)
    unnamed x21 -> x25, local copies, waits for them, and re-layouts: 8.32 us -> 7.52 us
where the time goes in v13:
time: 234 us; the launch traced here: 232 us
  Pallas kernels  79.8 us (34%)
  local copies, waits for them, and re-layouts  60.4 us (26%)
  matrix products  59.1 us (25%)
  other arithmetic  30.6 us (13%)
    pallas_call x1, Pallas kernels, both_scans_kernel(): pl.pallas_call(scan_kernel, out_shape=(out, out), in_specs=[pl.BlockSpec(...  66.4 us
    another operation x27, other arithmetic  19.4 us
    dot_general x6, matrix products, block_step(): jnp.einsum('hts,she->the', weights, v_block, preferred_element_type=jnp.f...  19.2 us
    dot_general x6, matrix products, block_step(): jnp.einsum('thd,shd->hts', q_block, k_bf, preferred_element_type=jnp.floa...  14.5 us
    pallas_call x1, Pallas kernels, gain_sum(): pl.pallas_call(gain_sum_kernel, out_shape=jax.ShapeDtypeStruct(shape, par...  13.4 us
    dot_general x8, matrix products, block_step(): jnp.einsum('thd,hde->the', q_float, carried, precision=PRECISE)  10.3 us
    squeeze x10, local copies, waits for them, and re-layouts, run_blocks(): lax.scan(jax.checkpoint(make_step(key_gain, head_width)), start_state, (t...  10.2 us
    dot_general x6, matrix products, block_step(): jnp.einsum('shd,she->hde', k_float * to_end.T[:, :, None], v_float, preci...  9.62 us

profile of v13, /device:TPU:2, one launch (start us, length us, event | category | flops | bytes accessed | tf_op | source)
XLA Modules:
  0.0 231.5 jit_solution(1890822184762650327)
XLA Ops:
  0.7 1.6 copy.254
  2.2 1.8 multiply_convert_fusion.6
  8.3 2.8 %fusion.109.fwd_ref = f32[4,128,128]{2,1,0:T(8,128)} fusion(bf16[1024,4,128]{0,2,1:T(8,128)(2,1)} %multiply_convert_fusion.6, bf16[1024,4,128]{2,1,0:T(4,128)(2,1)S(1)} %reshape_squeeze.17, f32[1024,4]{0,1:T(4,128)S(1)} %get-tuple-element.773), kind=kOutput, calls=%fused_computation.161 | convolution fusion | flops 403701760 | bytes 2375680 | tf_op jit(solution)/shard_map/shd,she->hde/dot_general | solution.py:334
  11.1 1.6 copy.255
  12.7 2.1 reshape.591
  14.8 2.7 %fusion.107.bwd_ref = f32[4,128,128]{2,1,0:T(8,128)} fusion(f32[1024,4,128]{0,2,1:T(8,128)S(1)} %bitcast.342, bf16[1024,4,128]{2,1,0:T(4,128)(2,1)} %reshape.591, f32[1024,4]{0,1:T(4,128)S(1)} %get-tuple-element.772), kind=kOutput, calls=%fused_computation.159 | convolution fusion | flops 403177472 | bytes 3424256 | tf_op jit(solution)/shard_map/thd,the->hde/dot_general | solution.py:29
  19.4 66.4 %shard_map.118 = (f32[4,128,128]{2,1,0:T(8,128)S(1)}, f32[4,128,128]{2,1,0:T(8,128)S(1)}) custom-call(f32[4,128,128]{2,1,0:T(8,128)} %fusion.109.fwd_ref, f32[4,128,128]{2,1,0:T(8,128)} %fusion.107.bwd_ref, f32[4,8,128]{2,1,0:T(8,128)} %broadcast_in_dim.173.lane_ref), custom_call_target="tpu_custom_call" | custom-call | tf_op jit(solution)/shard_map/pallas_call | solution.py:239
  87.0 1.4 copy.230
  88.4 2.1 reshape_squeeze.20
  90.6 2.3 %copy.231 = bf16[2,512,4,128]{3,1,2,0:T(8,128)(2,1)} copy(bf16[2,512,4,128]{3,2,1,0:T(4,128)(2,1)} %reshape_squeeze.20) | data formatting | bytes 2097152
  94.0 2.4 %copy.232 = bf16[2,512,4,128]{3,1,2,0:T(8,128)(2,1)} copy(bf16[2,512,4,128]{3,2,1,0:T(4,128)(2,1)} %reshape_squeeze.21) | data formatting | bytes 2097152
  96.4 25.8 %while.42 = (s32[]{:T(128)}, f32[4,128,128]{2,1,0:T(8,128)S(1)}, bf16[2,512,4,128]{1,3,2,0:T(8,128)(2,1)}, f32[2,4,128,128]{3,2,1,0:T(8,128)}, f32[2,4,512]{2,1,...) while((s32[]{:T(128)}, f32[4,128,128]{2,1,0:T(8,128)S(1)}, ...), condition=%wide.region_11.12_spmd.clone, body=%wide.region_6.11_spmd.clone.sunk | while | flops 949428288 | bytes 9343697 | solution.py:309
  97.3 1.2 reduce-window.144
  99.8 3.3 %fusion.191 = f32[512,4,128]{0,2,1:T(8,128)S(1)} fusion(bf16[512,4,128]{2,0,1:T(8,128)(2,1)S(1)} %fusion.189, f32[4,512]{1,0:T(4,128)S(1)} %bitcast.354, pred[512,512]{1,0:T(8,128)(4,1)S(1)} %fusion.190, bf16[2,512,4,128]{3,1,2,0:T(8,128)(2,1)} %get-tuple-element.1013, s32[]{:T(128)S(6)} %copy.332, bf16[2,512,4,128]{3,1,2,0:T(8,128)(2,1)} %get-tuple-element.1012), kind=kOutput, calls=%fused_computation.3.clone.1 | convolution fusion | flops 543162368 | bytes 2900992 | tf_op jit(solution)/shard_map/jvp()/while/body/eval_jaxpr/hts,she->the/dot_general | solution.py:281
  104.5 2.5 %fusion.192 = bf16[2,512,4,128]{1,3,2,0:T(8,128)(2,1)} fusion(bf16[2,512,4,128]{1,3,2,0:T(8,128)(2,1)} %get-tuple-element.994, s32[]{:T(128)S(6)} %copy.332, f32[512,4,128]{0,2,1:T(8,128)S(1)} %fusion.191, f32[4,128,128]{2,1,0:T(8,128)S(1)} %get-tuple-element.993, f32[512,4]{0,1:T(4,128)S(1)} %bitcast.346, ...), kind=kOutput, calls=%fused_computation.8.clone.1 | convolution fusion | flops 202375168 | bytes 2892800 | tf_op jit(solution)/shard_map/jvp()/while/body/eval_jaxpr/thd,hde->the/dot_general | solution.py:285
  107.2 2.1 convolution_add_fusion.4
  110.2 1.2 reduce-window.144
  112.7 3.3 %fusion.191 = f32[512,4,128]{0,2,1:T(8,128)S(1)} fusion(bf16[512,4,128]{2,0,1:T(8,128)(2,1)S(1)} %fusion.189, f32[4,512]{1,0:T(4,128)S(1)} %bitcast.354, pred[512,512]{1,0:T(8,128)(4,1)S(1)} %fusion.190, bf16[2,512,4,128]{3,1,2,0:T(8,128)(2,1)} %get-tuple-element.1013, s32[]{:T(128)S(6)} %copy.332, bf16[2,512,4,128]{3,1,2,0:T(8,128)(2,1)} %get-tuple-element.1012), kind=kOutput, calls=%fused_computation.3.clone.1 | convolution fusion | flops 543162368 | bytes 2900992 | tf_op jit(solution)/shard_map/jvp()/while/body/eval_jaxpr/hts,she->the/dot_general | solution.py:281
  117.4 2.5 %fusion.192 = bf16[2,512,4,128]{1,3,2,0:T(8,128)(2,1)} fusion(bf16[2,512,4,128]{1,3,2,0:T(8,128)(2,1)} %get-tuple-element.994, s32[]{:T(128)S(6)} %copy.332, f32[512,4,128]{0,2,1:T(8,128)S(1)} %fusion.191, f32[4,128,128]{2,1,0:T(8,128)S(1)} %get-tuple-element.993, f32[512,4]{0,1:T(4,128)S(1)} %bitcast.346, ...), kind=kOutput, calls=%fused_computation.8.clone.1 | convolution fusion | flops 202375168 | bytes 2892800 | tf_op jit(solution)/shard_map/jvp()/while/body/eval_jaxpr/thd,hde->the/dot_general | solution.py:285
  120.1 2.1 convolution_add_fusion.4
  122.2 1.8 copy.233
  125.2 1.7 reshape.602
  126.9 1.2 broadcast.246.clone
  128.2 1.2 broadcast.246.clone2
  129.4 1.2 broadcast.246.clone2.1
  130.7 79.7 %while.43 = (s32[]{:T(128)}, f32[4,128]{1,0:T(4,128)S(1)}, f32[4,128,128]{2,1,0:T(8,128)S(1)}, bf16[2,512,4,128]{3,2,1,0:T(4,128)(2,1)}, bf16[2,512,4,128]{3,2,1...) while((s32[]{:T(128)}, f32[4,128]{1,0:T(4,128)S(1)}, ...), condition=%wide.region_26.27_spmd.clone, body=%wide.region_12.26_spmd.clone.sunk | while | flops 2388230656 | bytes 116524784 | solution.py:309
  130.7 1.3 dynamic-slice_bitcast_fusion.10
  133.9 1.9 dynamic-slice_bitcast_fusion.13
  139.4 1.2 reduce-window.148
  141.3 1.8 fusion.210
  144.0 2.5 %fusion.213 = (f32[4,512]{1,0:T(4,128)S(1)}, f32[4,512]{1,0:T(4,128)S(1)}, bf16[4,512,512]{2,1,0:T(8,128)(2,1)S(1)}) fusion(f32[4,512]{1,0:T(4,128)S(1)} %bitcast.350, f32[4,512,512]{2,1,0:T(8,128)S(1)} %fusion.211, pred[512,512]{1,0:T(8,128)(4,1)S(1)} %fusion.212, bf16[512,4,128]{2,0,1:T(8,128)(2,1)S(1)} %copy-done.1, f32[512,4,128]{0,2,1:T(8,128)S(1)} %bitcast.337), kind=kOutput, calls=%fused_computation.107.clone.1 | convolution fusion | flops 278917120 | bytes 8151040 | tf_op jit(solution)/shard_map/transpose(jvp())/while/body/eval_jaxpr/checkpoint/hts,she->the/dot_general | solution.py:281
  146.6 3.2 %fusion.214 = (bf16[1,512,4,128]{3,1,2,0:T(8,128)(2,1)}, f32[4,128]{1,0:T(4,128)S(1)}) fusion(f32[4,128]{1,0:T(4,128)S(1)} %get-tuple-element.958, bf16[512,4,128]{2,0,1:T(8,128)(2,1)S(1)} %copy-done.2, bf16[512,4,128]{2,0,1:T(8,128)(2,1)S(1)} %get-tuple-element.965, bf16[512,4,128]{2,0,1:T(8,128)(2,1)S(1)} %dynamic-slice_bitcast_fusion.11, ...), kind=kOutput, calls=%fused_computation.110.clone.1 | convolution fusion | flops 276823552 | bytes 4468736 | tf_op jit(solution)/shard_map/transpose(jvp())/while/body/eval_jaxpr/checkpoint/thd,shd->hts/dot_general | solution.py:279
  149.8 3.8 %fusion.220 = bf16[4,128,512]{2,1,0:T(8,128)(2,1)S(1)} fusion(f32[4,512,512]{2,1,0:T(8,128)} %copy-done, f32[4,512]{1,0:T(4,128)S(1)} %bitcast.352, pred[512,512]{1,0:T(8,128)(4,1)S(1)} %fusion.212, f32[512,4,128]{0,2,1:T(8,128)S(1)} %bitcast.338), kind=kOutput, calls=%fused_computation.81.clone.1 | convolution fusion | flops 274726912 | bytes 6037504 | tf_op jit(solution)/shard_map/transpose(jvp())/while/body/eval_jaxpr/checkpoint/hts,she->the/dot_general | solution.py:281
  157.1 3.3 %fusion.218 = bf16[4,512,128]{2,1,0:T(8,128)(2,1)S(1)} fusion(bf16[512,4,128]{2,0,1:T(8,128)(2,1)S(1)} %fusion.209, bf16[4,512,512]{2,1,0:T(8,128)(2,1)} %copy-done.20, f32[4,512]{1,0:T(4,128)S(1)} %bitcast.353, pred[512,512]{1,0:T(8,128)(4,1)S(1)} %fusion.212), kind=kOutput, calls=%fused_computation.85.clone.1 | convolution fusion | flops 274989056 | bytes 3416064 | tf_op jit(solution)/shard_map/transpose(jvp())/while/body/eval_jaxpr/checkpoint/thd,shd->hts/dot_general | solution.py:279
  165.0 5.0 %reduce-window.150 = f32[4,4,128]{2,1,0:T(4,128)S(1)} reduce-window(f32[4,4,128]{2,1,0:T(4,128)S(1)} %reshape.631, f32[]{:T(128)} %constant.142.clone.1..sunk.1), window={size=1x1x128 pad=0_0x0_0x0_127}, to_apply=%region_24.24 | reduce-window | flops 260096 | bytes 16388 | tf_op jit(solution)/shard_map/reduce-window.60
  170.5 1.3 dynamic-slice_bitcast_fusion.10
  173.8 1.9 dynamic-slice_bitcast_fusion.13
  179.2 1.2 reduce-window.148
  181.2 1.8 fusion.210
  183.9 2.5 %fusion.213 = (f32[4,512]{1,0:T(4,128)S(1)}, f32[4,512]{1,0:T(4,128)S(1)}, bf16[4,512,512]{2,1,0:T(8,128)(2,1)S(1)}) fusion(f32[4,512]{1,0:T(4,128)S(1)} %bitcast.350, f32[4,512,512]{2,1,0:T(8,128)S(1)} %fusion.211, pred[512,512]{1,0:T(8,128)(4,1)S(1)} %fusion.212, bf16[512,4,128]{2,0,1:T(8,128)(2,1)S(1)} %copy-done.1, f32[512,4,128]{0,2,1:T(8,128)S(1)} %bitcast.337), kind=kOutput, calls=%fused_computation.107.clone.1 | convolution fusion | flops 278917120 | bytes 8151040 | tf_op jit(solution)/shard_map/transpose(jvp())/while/body/eval_jaxpr/checkpoint/hts,she->the/dot_general | solution.py:281
  186.5 3.2 %fusion.214 = (bf16[1,512,4,128]{3,1,2,0:T(8,128)(2,1)}, f32[4,128]{1,0:T(4,128)S(1)}) fusion(f32[4,128]{1,0:T(4,128)S(1)} %get-tuple-element.958, bf16[512,4,128]{2,0,1:T(8,128)(2,1)S(1)} %copy-done.2, bf16[512,4,128]{2,0,1:T(8,128)(2,1)S(1)} %get-tuple-element.965, bf16[512,4,128]{2,0,1:T(8,128)(2,1)S(1)} %dynamic-slice_bitcast_fusion.11, ...), kind=kOutput, calls=%fused_computation.110.clone.1 | convolution fusion | flops 276823552 | bytes 4468736 | tf_op jit(solution)/shard_map/transpose(jvp())/while/body/eval_jaxpr/checkpoint/thd,shd->hts/dot_general | solution.py:279
  189.7 3.8 %fusion.220 = bf16[4,128,512]{2,1,0:T(8,128)(2,1)S(1)} fusion(f32[4,512,512]{2,1,0:T(8,128)} %copy-done, f32[4,512]{1,0:T(4,128)S(1)} %bitcast.352, pred[512,512]{1,0:T(8,128)(4,1)S(1)} %fusion.212, f32[512,4,128]{0,2,1:T(8,128)S(1)} %bitcast.338), kind=kOutput, calls=%fused_computation.81.clone.1 | convolution fusion | flops 274726912 | bytes 6037504 | tf_op jit(solution)/shard_map/transpose(jvp())/while/body/eval_jaxpr/checkpoint/hts,she->the/dot_general | solution.py:281
  196.9 3.3 %fusion.218 = bf16[4,512,128]{2,1,0:T(8,128)(2,1)S(1)} fusion(bf16[512,4,128]{2,0,1:T(8,128)(2,1)S(1)} %fusion.209, bf16[4,512,512]{2,1,0:T(8,128)(2,1)} %copy-done.20, f32[4,512]{1,0:T(4,128)S(1)} %bitcast.353, pred[512,512]{1,0:T(8,128)(4,1)S(1)} %fusion.212), kind=kOutput, calls=%fused_computation.85.clone.1 | convolution fusion | flops 274989056 | bytes 3416064 | tf_op jit(solution)/shard_map/transpose(jvp())/while/body/eval_jaxpr/checkpoint/thd,shd->hts/dot_general | solution.py:279
  204.9 5.0 %reduce-window.150 = f32[4,4,128]{2,1,0:T(4,128)S(1)} reduce-window(f32[4,4,128]{2,1,0:T(4,128)S(1)} %reshape.631, f32[]{:T(128)} %constant.142.clone.1..sunk.1), window={size=1x1x128 pad=0_0x0_0x0_127}, to_apply=%region_24.24 | reduce-window | flops 260096 | bytes 16388 | tf_op jit(solution)/shard_map/reduce-window.60
  210.4 2.3 %reshape.592 = bf16[1,1024,512]{2,1,0:T(8,128)(2,1)} reshape(bf16[2,512,4,128]{3,2,1,0:T(4,128)(2,1)} %get-tuple-element.444) | data formatting | bytes 2097152 | tf_op jit(solution)/shard_map/broadcast_in_dim;transpose(jvp())/reshape | solution.py:350
  212.7 2.2 reshape.593
  216.9 13.4 %shard_map.119 = f32[4,64]{1,0:T(4,128)} custom-call(f32[2,4,64]{2,1,0:T(4,128)} %bitcast.368), custom_call_target="tpu_custom_call" | custom-call | tf_op jit(solution)/shard_map/pallas_call | solution.py:131
  230.3 1.2 copy.362
  (230 shorter events, 49.9 us)
Async XLA Ops:
  0.6 3.4 %copy-start.10 = (bf16[1,1024,512]{2,1,0:T(8,128)(2,1)S(1)}, bf16[1,1024,512]{2,1,0:T(8,128)(2,1)}, u32[]{:S(2)}) copy-start(bf16[1,1024,512]{2,1,0:T(8,128)(2,1)} %param.13) | copy-start | bytes 3145732
  0.6 3.7 %copy-start.19 = (s32[1,16]{1,0:T(1,128)S(1)}, s32[1,16]{1,0:T(1,128)}, u32[]{:S(2)}) copy-start(s32[1,16]{1,0:T(1,128)} %param.15) | copy-start | bytes 196
  0.7 4.6 %copy-start.16 = (f32[1,4,1024]{2,1,0:T(4,128)S(1)}, f32[1,4,1024]{2,1,0:T(4,128)}, u32[]{:S(2)}) copy-start(f32[1,4,1024]{2,1,0:T(4,128)} %param.14) | copy-start | bytes 49156
  11.1 74.8 %copy-start.7 = (bf16[1,1024,512]{2,1,0:T(8,128)(2,1)S(1)}, bf16[1,1024,512]{2,1,0:T(8,128)(2,1)}, u32[]{:S(2)}) copy-start(bf16[1,1024,512]{2,1,0:T(8,128)(2,1)} %param.12) | copy-start | bytes 3145732
  85.9 7.0 %copy-start.8 = (bf16[1,1024,512]{2,1,0:T(8,128)(2,1)S(1)}, bf16[1,1024,512]{2,1,0:T(8,128)(2,1)}, u32[]{:S(2)}) copy-start(bf16[1,1024,512]{2,1,0:T(8,128)(2,1)} %param.11) | copy-start | bytes 3145732
  88.4 8.0 %copy-start.17 = (f32[4,128]{1,0:T(4,128)S(1)}, f32[4,128]{1,0:T(4,128)}, u32[]{:S(2)}) copy-start(f32[4,128]{1,0:T(4,128)} %param.16) | copy-start | bytes 6148
  122.2 3.0 %copy-start.9 = (bf16[1,1024,512]{2,1,0:T(8,128)(2,1)S(1)}, bf16[1,1024,512]{2,1,0:T(8,128)(2,1)}, u32[]{:S(2)}) copy-start(bf16[1,1024,512]{2,1,0:T(8,128)(2,1)} %param.17) | copy-start | bytes 3145732
  130.7 5.2 %copy-start.3 = (bf16[2,512,4,128]{3,1,2,0:T(8,128)(2,1)}, bf16[2,512,4,128]{3,1,2,0:T(8,128)(2,1)S(1)}, u32[]{:S(2)}) copy-start(bf16[2,512,4,128]{3,1,2,0:T(8,128)(2,1)S(1)} %get-tuple-element.1061) | copy-start | bytes 3145732 | tf_op jit(solution)/shard_map/transpose(jvp())/while
  130.7 5.2 %copy-start.5 = (f32[2,512,4,128]{3,2,1,0:T(4,128)S(1)}, f32[2,512,4,128]{3,2,1,0:T(4,128)}, u32[]{:S(2)}) copy-start(f32[2,512,4,128]{3,2,1,0:T(4,128)} %get-tuple-element.1065) | copy-start | bytes 6291460 | tf_op jit(solution)/shard_map/transpose(jvp())/while
  136.3 7.7 %copy-start.1 = (bf16[512,4,128]{2,0,1:T(8,128)(2,1)S(1)}, bf16[512,4,128]{2,0,1:T(8,128)(2,1)}, u32[]{:S(2)}) copy-start(bf16[512,4,128]{2,0,1:T(8,128)(2,1)} %dynamic-slice_bitcast_fusion.13) | copy-start | bytes 1572868 | tf_op jit(solution)/shard_map/transpose(jvp())/while
  143.8 2.8 %copy-start = (f32[4,512,512]{2,1,0:T(8,128)}, f32[4,512,512]{2,1,0:T(8,128)S(1)}, u32[]{:S(2)}) copy-start(f32[4,512,512]{2,1,0:T(8,128)S(1)} %fusion.211) | copy-start | bytes 12582916 | tf_op jit(solution)/shard_map/transpose(jvp())/while
  144.0 2.6 %copy-start.2 = (bf16[512,4,128]{2,0,1:T(8,128)(2,1)S(1)}, bf16[512,4,128]{2,0,1:T(8,128)(2,1)}, u32[]{:S(2)}) copy-start(bf16[512,4,128]{2,0,1:T(8,128)(2,1)} %dynamic-slice_bitcast_fusion.12) | copy-start | bytes 1572868 | tf_op jit(solution)/shard_map/transpose(jvp())/while
  146.6 3.2 %copy-start.20 = (bf16[4,512,512]{2,1,0:T(8,128)(2,1)}, bf16[4,512,512]{2,1,0:T(8,128)(2,1)S(1)}, u32[]{:S(2)}) copy-start(bf16[4,512,512]{2,1,0:T(8,128)(2,1)S(1)} %get-tuple-element.968) | copy-start | bytes 6291460 | tf_op jit(solution)/shard_map/transpose(jvp())/while
  157.0 4.4 %copy-start.6 = (bf16[1,512,4,128]{3,1,2,0:T(8,128)(2,1)S(1)}, bf16[1,512,4,128]{3,1,2,0:T(8,128)(2,1)}, u32[]{:S(2)}) copy-start(bf16[1,512,4,128]{3,1,2,0:T(8,128)(2,1)} %get-tuple-element.976) | copy-start | bytes 1572868 | tf_op jit(solution)/shard_map/transpose(jvp())/while
  157.0 4.4 %copy-start.11 = (bf16[2,512,4,128]{3,2,1,0:T(4,128)(2,1)S(1)}, bf16[2,512,4,128]{3,2,1,0:T(4,128)(2,1)}, u32[]{:S(2)}) copy-start(bf16[2,512,4,128]{3,2,1,0:T(4,128)(2,1)} %get-tuple-element.1037) | copy-start | bytes 3145732 | tf_op jit(solution)/shard_map/transpose(jvp())/while
  157.1 4.4 %copy-start.13 = (bf16[2,512,4,128]{3,2,1,0:T(4,128)(2,1)S(1)}, bf16[2,512,4,128]{3,2,1,0:T(4,128)(2,1)}, u32[]{:S(2)}) copy-start(bf16[2,512,4,128]{3,2,1,0:T(4,128)(2,1)} %get-tuple-element.1038) | copy-start | bytes 3145732 | tf_op jit(solution)/shard_map/transpose(jvp())/while
  161.5 9.0 %copy-start.4 = (bf16[2,512,4,128]{3,1,2,0:T(8,128)(2,1)S(1)}, bf16[2,512,4,128]{3,1,2,0:T(8,128)(2,1)}, u32[]{:S(2)}) copy-start(bf16[2,512,4,128]{3,1,2,0:T(8,128)(2,1)} %copy-done.3) | copy-start | bytes 3145732 | tf_op jit(solution)/shard_map/transpose(jvp())/while
  162.4 1.0 copy-start.12
  162.4 1.3 copy-start.14
  170.5 5.2 %copy-start.3 = (bf16[2,512,4,128]{3,1,2,0:T(8,128)(2,1)}, bf16[2,512,4,128]{3,1,2,0:T(8,128)(2,1)S(1)}, u32[]{:S(2)}) copy-start(bf16[2,512,4,128]{3,1,2,0:T(8,128)(2,1)S(1)} %get-tuple-element.1061) | copy-start | bytes 3145732 | tf_op jit(solution)/shard_map/transpose(jvp())/while
  170.5 5.2 %copy-start.5 = (f32[2,512,4,128]{3,2,1,0:T(4,128)S(1)}, f32[2,512,4,128]{3,2,1,0:T(4,128)}, u32[]{:S(2)}) copy-start(f32[2,512,4,128]{3,2,1,0:T(4,128)} %get-tuple-element.1065) | copy-start | bytes 6291460 | tf_op jit(solution)/shard_map/transpose(jvp())/while
  176.2 7.7 %copy-start.1 = (bf16[512,4,128]{2,0,1:T(8,128)(2,1)S(1)}, bf16[512,4,128]{2,0,1:T(8,128)(2,1)}, u32[]{:S(2)}) copy-start(bf16[512,4,128]{2,0,1:T(8,128)(2,1)} %dynamic-slice_bitcast_fusion.13) | copy-start | bytes 1572868 | tf_op jit(solution)/shard_map/transpose(jvp())/while
  183.7 2.8 %copy-start = (f32[4,512,512]{2,1,0:T(8,128)}, f32[4,512,512]{2,1,0:T(8,128)S(1)}, u32[]{:S(2)}) copy-start(f32[4,512,512]{2,1,0:T(8,128)S(1)} %fusion.211) | copy-start | bytes 12582916 | tf_op jit(solution)/shard_map/transpose(jvp())/while
  183.9 2.6 %copy-start.2 = (bf16[512,4,128]{2,0,1:T(8,128)(2,1)S(1)}, bf16[512,4,128]{2,0,1:T(8,128)(2,1)}, u32[]{:S(2)}) copy-start(bf16[512,4,128]{2,0,1:T(8,128)(2,1)} %dynamic-slice_bitcast_fusion.12) | copy-start | bytes 1572868 | tf_op jit(solution)/shard_map/transpose(jvp())/while
  186.4 3.2 %copy-start.20 = (bf16[4,512,512]{2,1,0:T(8,128)(2,1)}, bf16[4,512,512]{2,1,0:T(8,128)(2,1)S(1)}, u32[]{:S(2)}) copy-start(bf16[4,512,512]{2,1,0:T(8,128)(2,1)S(1)} %get-tuple-element.968) | copy-start | bytes 6291460 | tf_op jit(solution)/shard_map/transpose(jvp())/while
  196.9 4.4 %copy-start.6 = (bf16[1,512,4,128]{3,1,2,0:T(8,128)(2,1)S(1)}, bf16[1,512,4,128]{3,1,2,0:T(8,128)(2,1)}, u32[]{:S(2)}) copy-start(bf16[1,512,4,128]{3,1,2,0:T(8,128)(2,1)} %get-tuple-element.976) | copy-start | bytes 1572868 | tf_op jit(solution)/shard_map/transpose(jvp())/while
  196.9 4.4 %copy-start.11 = (bf16[2,512,4,128]{3,2,1,0:T(4,128)(2,1)S(1)}, bf16[2,512,4,128]{3,2,1,0:T(4,128)(2,1)}, u32[]{:S(2)}) copy-start(bf16[2,512,4,128]{3,2,1,0:T(4,128)(2,1)} %get-tuple-element.1037) | copy-start | bytes 3145732 | tf_op jit(solution)/shard_map/transpose(jvp())/while
  196.9 4.4 %copy-start.13 = (bf16[2,512,4,128]{3,2,1,0:T(4,128)(2,1)S(1)}, bf16[2,512,4,128]{3,2,1,0:T(4,128)(2,1)}, u32[]{:S(2)}) copy-start(bf16[2,512,4,128]{3,2,1,0:T(4,128)(2,1)} %get-tuple-element.1038) | copy-start | bytes 3145732 | tf_op jit(solution)/shard_map/transpose(jvp())/while
  201.3 9.1 %copy-start.4 = (bf16[2,512,4,128]{3,1,2,0:T(8,128)(2,1)S(1)}, bf16[2,512,4,128]{3,1,2,0:T(8,128)(2,1)}, u32[]{:S(2)}) copy-start(bf16[2,512,4,128]{3,1,2,0:T(8,128)(2,1)} %copy-done.3) | copy-start | bytes 3145732 | tf_op jit(solution)/shard_map/transpose(jvp())/while
  202.2 1.0 copy-start.12
  202.2 1.3 copy-start.14
  210.4 21.2 %copy-start.18 = (f32[2,4,512]{2,1,0:T(4,128)}, f32[2,4,512]{2,1,0:T(4,128)S(1)}, u32[]{:S(2)}) copy-start(f32[2,4,512]{2,1,0:T(4,128)S(1)} %get-tuple-element.447) | copy-start | bytes 49156
  210.4 4.6 %copy-start.15 = (bf16[2,512,4,128]{3,2,1,0:T(4,128)(2,1)S(1)}, bf16[2,512,4,128]{3,2,1,0:T(4,128)(2,1)}, u32[]{:S(2)}) copy-start(bf16[2,512,4,128]{3,2,1,0:T(4,128)(2,1)} %get-tuple-element.446) | copy-start | bytes 3145732
